TPU v7x, 256 devices: a whole 4x4x8 slice. The times are simulated.
256 devices in a mesh: dp: 16 (over y, x), tile: 16 (over z, core).
Axes of the slice: x: 4, y: 4, z: 8, core: 2. Of those that a mesh axis runs over, the one named last changes fastest.
Arguments:
- tokens: bfloat16 [2048, 4096], P('dp', 'tile'), may hold values from -6 to 6
- grad_out: bfloat16 [2048, 4096], P('dp', 'tile'), may hold values from -6 to 6
- up_tiles: bfloat16 [16, 128, 128, 128], P('tile'), may hold values from -0.1875 to 0.1875
- down_tiles: bfloat16 [16, 128, 128, 128], P('tile'), may hold values from -0.09375 to 0.09375
- tile_rows: int32 [16, 128], P('tile'), may hold values from 0 to 7, as said below
- tile_cols: int32 [16, 128], P('tile'), may hold values from 0 to 31
- tile_count: int32 [16], P('tile'), may hold values from 16 to 128, as said below
Outputs:
- mixed: bfloat16 [2048, 4096], P('dp', 'tile')
- grad_in: bfloat16 [2048, 4096], P('dp', 'tile')
- grad_up: float32 [16, 128, 128, 128], P('tile', 'dp')
- grad_down: float32 [16, 128, 128, 128], P('tile', 'dp')
Inputs may be any that keep to these rules, and one draw needn't show every extreme that they name: `tile_count`: some owner holds exactly 128 tiles in every draw. The pairs (tile_rows[i, s], tile_cols[i, s]) of one owner are distinct over all its 128 slots.
All inputs are finite; a program needn't handle non-finite values.
Results may differ from a plain program's by a relative error of at most 0.015.
Values may be sent and summed in bfloat16 or wider, within the bound.
No kernel may reach another device: no remote copies, remote signals or barrier semaphores. Data moves between devices by JAX's collectives and lax.ppermute only.
A program may use at most 128 MiB of HBM per device.

v0:
```python
import functools

import jax
import jax.numpy as jnp
from jax import lax
from jax.experimental import pallas as pl
from jax.experimental.pallas import tpu as pltpu
from jax.sharding import Mesh, PartitionSpec as P

SIDE = 128
COLS = 32
ROWS = 8
SLOTS = 128
GROUP = 16
STEPS = SLOTS // GROUP
VM = pltpu.VMEM
SM = pltpu.SMEM
BF = jnp.bfloat16
F32 = jnp.float32


def whole(*shape):
    return pl.BlockSpec(shape, lambda *i: (0,) * len(shape))


def params(**kw):
    return pltpu.CompilerParams(vmem_limit_bytes=32 << 20, **kw)


def sspec():
    return pl.BlockSpec(memory_space=SM)


def nn(a, b):
    return jnp.dot(a, b, preferred_element_type=F32)


def nt(a, b):
    return lax.dot_general(a, b, (((1,), (1,)), ((), ())), preferred_element_type=F32)


def gelu_pair(pre):
    curve = lax.erf(pre * 0.7071067811865476)
    value = 0.5 * pre * (1.0 + curve)
    slope = 0.5 * (1.0 + curve) + pre * jnp.exp(-0.5 * pre * pre) * 0.3989422804014327
    return value, slope


def other_owner(k):
    z, c = lax.axis_index("z"), lax.axis_index("c")
    ahead = 2 * c - 1
    if k < 2:
        return z * 2 + (c if k == 0 else 1 - c)
    hop = (k - 2) // 4 + 1
    kind = (k - 2) % 4
    chip = z + hop * ahead if kind in (0, 2) else z - hop * ahead
    core = c if kind in (0, 3) else 1 - c
    return lax.rem(chip + 8, 8) * 2 + core


def forward_kernel(rows, cols, count_ref, *refs):
    shards = refs[:16]
    up_ref, down_ref = refs[16:18]
    x_ref, dy_ref, h_ref, ht_ref, d_ref, dt_ref = refs[18:24]
    pre_acc, gh_acc, sem = refs[24:27]
    step = pl.program_id(0)
    count = count_ref[0]

    @pl.when(step == 0)
    def _():
        copies = []
        for k in range(16):
            at = other_owner(k) * 2
            for b in range(2):
                lanes = pl.ds(b * SIDE, SIDE)
                copies.append(pltpu.make_async_copy(shards[k].at[0, :, lanes], x_ref.at[at + b], sem))
                copies.append(pltpu.make_async_copy(shards[k].at[1, :, lanes], dy_ref.at[at + b], sem))
        for copy in copies:
            copy.start()
        pre_acc[...] = jnp.zeros_like(pre_acc)
        gh_acc[...] = jnp.zeros_like(gh_acc)
        for copy in copies:
            copy.wait()

    for s in range(GROUP):
        slot = step * GROUP + s
        live = slot < count
        r = rows[slot]
        c = cols[slot]
        up = up_ref[0, s]
        down = down_ref[0, s]
        up = jnp.where(live, up, jnp.zeros_like(up))
        down = jnp.where(live, down, jnp.zeros_like(down))
        pre_acc[r] += nn(x_ref[c], up)
        gh_acc[r] += nt(dy_ref[c], down)

    @pl.when(step == STEPS - 1)
    def _():
        for r in range(ROWS):
            value, slope = gelu_pair(pre_acc[r])
            grad = gh_acc[r] * slope
            h_ref[r] = value.astype(BF)
            ht_ref[r] = value.T.astype(BF)
            d_ref[r] = grad.astype(BF)
            dt_ref[r] = grad.T.astype(BF)


def forward(rows, cols, count, shards, up_tiles, down_tiles):
    block = pl.BlockSpec((1, GROUP, SIDE, SIDE), lambda i: (0, i, 0, 0))
    tok = jax.ShapeDtypeStruct((COLS, SIDE, SIDE), BF)
    hid = jax.ShapeDtypeStruct((ROWS, SIDE, SIDE), BF)
    return pl.pallas_call(
        forward_kernel,
        grid=(STEPS,),
        in_specs=[sspec()] * 3 + [pl.BlockSpec(memory_space=pl.ANY)] * 16 + [block] * 2,
        out_specs=[whole(COLS, SIDE, SIDE)] * 2 + [whole(ROWS, SIDE, SIDE)] * 4,
        out_shape=[tok, tok, hid, hid, hid, hid],
        scratch_shapes=[VM((ROWS, SIDE, SIDE), F32)] * 2 + [pltpu.SemaphoreType.DMA],
        compiler_params=params(),
        cost_estimate=pl.CostEstimate(flops=1 << 30, bytes_accessed=12 << 20, transcendentals=1 << 18),
        name="forward",
    )(rows, cols, count, *shards, up_tiles, down_tiles)


def ring_slot(j):
    away = (2, 1, 3, 0)
    y = lax.rem(lax.axis_index("y") + away[j // 32], 4)
    x = lax.rem(lax.axis_index("x") + away[j // 8 % 4], 4)
    return (y * 4 + x) * 8 + j % 8


def weight_kernel(sizes, order, rows, cols, x_ref, t_ref, *outs):
    at = 0
    for out, n in zip(outs, sizes):
        for s in range(n):
            slot = order(at + s)
            out[s] = nn(t_ref[rows[slot]], x_ref[cols[slot]]).astype(BF)
        at += n


def weight_parts(rows, cols, x, t, sizes, order):
    return pl.pallas_call(
        functools.partial(weight_kernel, sizes, order),
        grid=(1,),
        in_specs=[sspec()] * 2 + [whole(COLS, SIDE, SIDE), whole(ROWS, SIDE, SIDE)],
        out_specs=[whole(n, SIDE, SIDE) for n in sizes],
        out_shape=[jax.ShapeDtypeStruct((n, SIDE, SIDE), BF) for n in sizes],
        compiler_params=params(),
        cost_estimate=pl.CostEstimate(flops=1 << 29, bytes_accessed=6 << 20, transcendentals=0),
        name="weight_parts",
    )(rows, cols, x, t)


def token_kernel(rows, cols, count_ref, h_ref, d_ref, up_ref, down_ref, send_ref, keep_ref, mix_acc, in_acc):
    step = pl.program_id(0)
    count = count_ref[0]

    @pl.when(step == 0)
    def _():
        mix_acc[...] = jnp.zeros_like(mix_acc)
        in_acc[...] = jnp.zeros_like(in_acc)

    for s in range(GROUP):
        slot = step * GROUP + s
        live = slot < count
        r = rows[slot]
        c = cols[slot]
        up = up_ref[0, s]
        down = down_ref[0, s]
        up = jnp.where(live, up, jnp.zeros_like(up))
        down = jnp.where(live, down, jnp.zeros_like(down))
        mix_acc[c] += nn(h_ref[r], down)
        in_acc[c] += nt(d_ref[r], up)

    @pl.when(step == STEPS - 1)
    def _():
        c = lax.axis_index("c")
        for k in range(8):
            for b in range(2):
                lanes = slice(b * SIDE, (b + 1) * SIDE)
                at = (2 * k + 1 - c) * 2 + b
                send_ref[k, 0, :, lanes] = mix_acc[at].astype(BF)
                send_ref[k, 1, :, lanes] = in_acc[at].astype(BF)
                at = (2 * k + c) * 2 + b
                keep_ref[k, 0, :, lanes] = mix_acc[at].astype(BF)
                keep_ref[k, 1, :, lanes] = in_acc[at].astype(BF)


def token_parts(rows, cols, count, h, d, up_tiles, down_tiles):
    block = pl.BlockSpec((1, GROUP, SIDE, SIDE), lambda i: (0, i, 0, 0))
    part = jax.ShapeDtypeStruct((8, 2, SIDE, 2 * SIDE), BF)
    return pl.pallas_call(
        token_kernel,
        grid=(STEPS,),
        in_specs=[sspec()] * 3 + [whole(ROWS, SIDE, SIDE)] * 2 + [block] * 2,
        out_specs=[whole(8, 2, SIDE, 2 * SIDE)] * 2,
        out_shape=[part] * 2,
        scratch_shapes=[VM((COLS, SIDE, SIDE), F32)] * 2,
        compiler_params=params(),
        cost_estimate=pl.CostEstimate(flops=1 << 30, bytes_accessed=11 << 20, transcendentals=0),
        name="token_parts",
    )(rows, cols, count, h, d, up_tiles, down_tiles)


def ring(n, by):
    return [(i, (i + by) % n) for i in range(n)]


def step_both(x):
    pairs = []
    for z in range(8):
        pairs.append((z * 2, ((z + 1) % 8) * 2))
        pairs.append((z * 2 + 1, ((z - 1) % 8) * 2 + 1))
    return lax.ppermute(x, ("z", "c"), pairs)


def swap(x):
    return lax.ppermute(x, "c", [(0, 1), (1, 0)])


def add(*parts):
    total = parts[0].astype(F32)
    for p in parts[1:]:
        total = total + p.astype(F32)
    return total


def gather_over_tile(own):
    first, second = own, swap(own)
    shards = [first, second]
    for k in range(1, 5):
        first = step_both(first)
        shards += [first, swap(first)]
        if k < 4:
            second = step_both(second)
            shards += [second, swap(second)]
    return shards


def scatter_ring(axis, opp_a, opp_b, right, left):
    n = opp_a.shape[0]
    up, down = ring(4, 1), ring(4, -1)
    from_left = lax.ppermute(opp_a, axis, up)
    from_right = lax.ppermute(opp_b, axis, down)
    right = lax.ppermute(right.at[:n].add(from_left), axis, up)
    left = lax.ppermute(left.at[n:].add(from_right), axis, down)
    return right, left


def body(tokens, grad_out, up_tiles, down_tiles, tile_rows, tile_cols, tile_count):
    rows, cols = tile_rows[0], tile_cols[0]
    shards = gather_over_tile(jnp.stack([tokens, grad_out]))
    x_all, dy_all, h, ht, d, dt = forward(rows, cols, tile_count, shards, up_tiles, down_tiles)
    opp_a, opp_b, right, left, mine = weight_parts(rows, cols, dy_all, ht, (16, 16, 32, 32, 32), ring_slot)
    (up_part,) = weight_parts(rows, cols, x_all, dt, (SLOTS,), lambda j: j)
    up_total = lax.psum_scatter(up_part, ("y", "x"), scatter_dimension=0, tiled=True)
    part = add(mine, *scatter_ring("y", opp_a, opp_b, right, left)).astype(BF)
    got = scatter_ring("x", part[:4], part[4:8], part[8:16], part[16:24])
    down_total = add(part[24:], *got)

    send, keep = token_parts(rows, cols, tile_count, h, d, up_tiles, down_tiles)
    pieces = add(keep, swap(send)).astype(BF)
    terms = lax.all_to_all(pieces, "z", 0, 0, tiled=True)
    total = jnp.sum(terms.astype(F32), axis=0).astype(BF)

    slot = lax.axis_index(("y", "x")) * 8 + jnp.arange(8, dtype=jnp.int32)
    live = (slot < tile_count[0])[:, None, None]
    grad_up = jnp.where(live, jnp.swapaxes(up_total, 1, 2).astype(F32) * (1.0 / 16), 0.0)
    grad_down = jnp.where(live, down_total * (1.0 / 16), 0.0)
    return total[0], total[1], grad_up[None], grad_down[None]


def solution(mesh):
    grid = Mesh(mesh.devices.reshape(4, 4, 8, 2), ("y", "x", "z", "c"))
    dp, tile = ("y", "x"), ("z", "c")
    placed = (
        P(dp, tile),
        P(dp, tile),
        P(tile, None, None, None),
        P(tile, None, None, None),
        P(tile, None),
        P(tile, None),
        P(tile),
    )
    return jax.shard_map(
        body,
        mesh=grid,
        in_specs=placed,
        out_specs=(P(dp, tile), P(dp, tile), P(tile, dp, None, None), P(tile, dp, None, None)),
        check_vma=False,
    )
```

profile of v0, /device:TPU:6, one launch (start us, length us, event | category | flops | bytes accessed | tf_op | source)
XLA Modules:
  0.0 163.0 jit_solution(821700106185786814)
XLA Ops:
  8.1 2.0 %collective-permute-start.1 = (bf16[2,128,256]{2,1,0:T(8,128)(2,1)S(1)}, bf16[2,128,256]{2,1,0:T(8,128)(2,1)S(1)}, u32[]{:S(2)}, u32[]{:S(2)}) collective-permute-start(bf16[2,128,256]{2,1,0:T(8,128)(2,1)S(1)} %pad_maximum_fusion.refs_0_), channel_id=1, source_target_pairs={{0,2},{1,15},{2,4},{3,1},{4,6},{5,3},{6,8},{7,5},{8,10},{9,7},{10,... | collective-permute-start | bytes 393224 | tf_op jit(solution)/shard_map/ppermute | solution.py:214
  10.1 3.5 %collective-permute-start = (bf16[2,128,256]{2,1,0:T(8,128)(2,1)S(1)}, bf16[2,128,256]{2,1,0:T(8,128)(2,1)S(1)}, u32[]{:S(2)}, u32[]{:S(2)}) collective-permute-start(bf16[2,128,256]{2,1,0:T(8,128)(2,1)S(1)} %pad_maximum_fusion.refs_0_), channel_id=1, source_target_pairs={{0,1},{1,0},{2,3},{3,2},{4,5},{5,4},{6,7},{7,6},{8,9},{9,8},{10,11... | collective-permute-start | bytes 393224 | tf_op jit(solution)/shard_map/ppermute | solution.py:218
  13.6 3.4 %collective-permute-done.1.refs_2_ = bf16[2,128,256]{2,1,0:T(8,128)(2,1)S(1)} collective-permute-done((bf16[2,128,256]{2,1,0:T(8,128)(2,1)S(1)}, bf16[2,128,256]{2,1,0:T(8,128)(2,1)S(1)}, u32[]{:S(2)}, u32[]{:S(2)}) %collective-permute-start.1) | collective-permute-done | bytes 131104 | tf_op jit(solution)/shard_map/ppermute | solution.py:214
  17.0 6.2 %collective-permute-done.5.refs_6_ = bf16[2,128,256]{2,1,0:T(8,128)(2,1)S(1)} collective-permute-done((bf16[2,128,256]{2,1,0:T(8,128)(2,1)S(1)}, bf16[2,128,256]{2,1,0:T(8,128)(2,1)S(1)}, u32[]{:S(2)}, u32[]{:S(2)}) %collective-permute-start.5) | collective-permute-done | bytes 131104 | tf_op jit(solution)/shard_map/ppermute | solution.py:214
  23.2 1.4 collective-permute-done.3.refs_4_
  25.1 4.3 %collective-permute-done.9.refs_10_ = bf16[2,128,256]{2,1,0:T(8,128)(2,1)S(1)} collective-permute-done((bf16[2,128,256]{2,1,0:T(8,128)(2,1)S(1)}, bf16[2,128,256]{2,1,0:T(8,128)(2,1)S(1)}, u32[]{:S(2)}, u32[]{:S(2)}) %collective-permute-start.9) | collective-permute-done | bytes 131104 | tf_op jit(solution)/shard_map/ppermute | solution.py:214
  29.3 1.4 collective-permute-done.7.refs_8_
  31.4 4.2 %collective-permute-done.13.refs_14_ = bf16[2,128,256]{2,1,0:T(8,128)(2,1)S(1)} collective-permute-done((bf16[2,128,256]{2,1,0:T(8,128)(2,1)S(1)}, bf16[2,128,256]{2,1,0:T(8,128)(2,1)S(1)}, u32[]{:S(2)}, u32[]{:S(2)}) %collective-permute-start.13) | collective-permute-done | bytes 131104 | tf_op jit(solution)/shard_map/ppermute | solution.py:214
  35.5 1.4 collective-permute-done.11.refs_12_
  38.3 2.2 %copy-done = bf16[1,128,128,128]{3,2,1,0:T(8,128)(2,1)S(1)} copy-done((bf16[1,128,128,128]{3,2,1,0:T(8,128)(2,1)S(1)}, bf16[1,128,128,128]{3,2,1,0:T(8,128)(2,1)}, u32[]{:S(2)}) %copy-start) | copy-done | bytes 4194328
  40.5 2.2 %copy-done.2 = bf16[1,128,128,128]{3,2,1,0:T(8,128)(2,1)S(1)} copy-done((bf16[1,128,128,128]{3,2,1,0:T(8,128)(2,1)S(1)}, bf16[1,128,128,128]{3,2,1,0:T(8,128)(2,1)}, u32[]{:S(2)}) %copy-start.2) | copy-done | bytes 4194328
  44.0 7.6 %forward.1 = (bf16[32,128,128]{2,1,0:T(8,128)(2,1)S(1)}, bf16[32,128,128]{2,1,0:T(8,128)(2,1)S(1)}, bf16[8,128,128]{2,1,0:T(8,128)(2,1)S(1)}, bf16[8,128,128]{2,...) custom-call(s32[128]{0:T(128)S(1)} %bitcast.16, s32[128]{0:T(128)S(1)} %bitcast.20, ...), custom_call_target="tpu_custom_call" | custom-call | flops 1073741824 | bytes 12582912 | tf_op jit(solution)/shard_map/forward/pallas_call | solution.py:112
  54.0 1.8 %weight_parts.2 = bf16[128,128,128]{2,1,0:T(8,128)(2,1)S(1)} custom-call(s32[128]{0:T(128)S(1)} %bitcast.17, s32[128]{0:T(128)S(1)} %bitcast.21, bf16[32,128,128]{2,1,0:T(8,128)(2,1)S(1)} %get-tuple-element.69.x_ref, bf16[8,128,128]{2,1,0:T(8,128)(2,1)S(1)} %get-tuple-element.70.t_ref), custom_call_target="tpu_custom_call" | custom-call | flops 536870912 | bytes 6291456 | tf_op jit(solution)/shard_map/weight_parts/pallas_call | solution.py:142
  55.8 2.0 %copy-done.4 = bf16[128,128,128]{2,1,0:T(8,128)(2,1)} copy-done((bf16[128,128,128]{2,1,0:T(8,128)(2,1)}, bf16[128,128,128]{2,1,0:T(8,128)(2,1)S(1)}, u32[]{:S(2)}) %copy-start.4) | copy-done | bytes 4194328
  60.6 1.8 %weight_parts.3 = (bf16[16,128,128]{2,1,0:T(8,128)(2,1)S(1)}, bf16[16,128,128]{2,1,0:T(8,128)(2,1)S(1)}, bf16[32,128,128]{2,1,0:T(8,128)(2,1)S(1)}, bf16[32,128,...) custom-call(s32[128]{0:T(128)S(1)} %bitcast.18, s32[128]{0:T(128)S(1)} %bitcast.22, bf16[32,128,128]{2,1,0:T(8,128)(2,1)S(1)} %copy-done.12, ...), custom_call_target="tpu_custom_call" | custom-call | flops 536870912 | bytes 6291456 | tf_op jit(solution)/shard_map/weight_parts/pallas_call | solution.py:142
  62.4 3.1 %collective-permute-start.18 = (bf16[16,128,128]{2,1,0:T(8,128)(2,1)S(1)}, bf16[16,128,128]{2,1,0:T(8,128)(2,1)S(1)}, u32[]{:S(2)}, u32[]{:S(2)}) collective-permute-start(bf16[16,128,128]{2,1,0:T(8,128)(2,1)S(1)} %get-tuple-element.77), channel_id=1, source_target_pairs={{0,192},{64,0},{128,64},{192,128},{1,193},{65,1},{129,65},{193,129... | collective-permute-start | bytes 1572872 | tf_op jit(solution)/shard_map/ppermute | solution.py:244
  65.5 2.2 %copy-done.1 = bf16[1,128,128,128]{3,2,1,0:T(8,128)(2,1)S(1)} copy-done((bf16[1,128,128,128]{3,2,1,0:T(8,128)(2,1)S(1)}, bf16[1,128,128,128]{3,2,1,0:T(8,128)(2,1)}, u32[]{:S(2)}) %copy-start.1) | copy-done | bytes 4194328
  67.7 2.2 %copy-done.3 = bf16[1,128,128,128]{3,2,1,0:T(8,128)(2,1)S(1)} copy-done((bf16[1,128,128,128]{3,2,1,0:T(8,128)(2,1)S(1)}, bf16[1,128,128,128]{3,2,1,0:T(8,128)(2,1)}, u32[]{:S(2)}) %copy-start.3) | copy-done | bytes 4194328
  69.9 6.8 %token_parts.1 = (bf16[8,2,128,256]{3,2,1,0:T(8,128)(2,1)S(1)}, bf16[8,2,128,256]{3,2,1,0:T(8,128)(2,1)S(1)}) custom-call(s32[128]{0:T(128)S(1)} %bitcast.19, s32[128]{0:T(128)S(1)} %bitcast.23, s32[1]{0:T(128)} %copy.16.count_ref, bf16[8,128,128]{2,1,0:T(8,128)(2,1)S(1)} %get-tuple-element.65.h_ref, bf16[8,128,128]{2,1,0:T(8,128)(2,1)S(1)} %copy-done.6, ...), custom_call_target="tpu_custom_call" | custom-call | flops 1073741824 | bytes 11534336 | tf_op jit(solution)/shard_map/token_parts/pallas_call | solution.py:192
  76.9 4.8 %collective-permute-done.18 = bf16[16,128,128]{2,1,0:T(8,128)(2,1)S(1)} collective-permute-done((bf16[16,128,128]{2,1,0:T(8,128)(2,1)S(1)}, bf16[16,128,128]{2,1,0:T(8,128)(2,1)S(1)}, u32[]{:S(2)}, u32[]{:S(2)}) %collective-permute-start.18) | collective-permute-done | bytes 524320 | tf_op jit(solution)/shard_map/ppermute | solution.py:244
  82.0 3.8 %collective-permute-start.19 = (bf16[32,128,128]{2,1,0:T(8,128)(2,1)S(1)}, bf16[32,128,128]{2,1,0:T(8,128)(2,1)}, u32[]{:S(2)}, u32[]{:S(2)}) collective-permute-start(bf16[32,128,128]{2,1,0:T(8,128)(2,1)S(1)} %add_dynamic-update-slice_fusion), channel_id=1, source_target_pairs={{0,192},{64,0},{128,64},{192,128},{1,193},{65,1},{129,65},{193,129... | collective-permute-start | bytes 3145736 | tf_op jit(solution)/shard_map/ppermute | solution.py:246
  85.8 13.3 %collective-permute-done.16 = bf16[16,128,128]{2,1,0:T(8,128)(2,1)S(1)} collective-permute-done((bf16[16,128,128]{2,1,0:T(8,128)(2,1)S(1)}, bf16[16,128,128]{2,1,0:T(8,128)(2,1)S(1)}, u32[]{:S(2)}, u32[]{:S(2)}) %collective-permute-start.16) | collective-permute-done | bytes 524320 | tf_op jit(solution)/shard_map/ppermute | solution.py:243
  100.8 5.3 %all-to-all-start = ((bf16[8,2,128,256]{3,2,1,0:T(8,128)(2,1)}), bf16[8,2,128,256]{3,2,1,0:T(8,128)(2,1)}, u32[]{:S(2)}, u32[]{:S(2)}) async-start(bf16[8,2,128,256]{3,2,1,0:T(8,128)(2,1)} %add_convert_fusion.1), calls=%async_computation | async-start | bytes 2097152 | tf_op jit(solution)/shard_map/all_to_all | solution.py:263
  106.1 12.3 %collective-permute-done.19 = bf16[32,128,128]{2,1,0:T(8,128)(2,1)} collective-permute-done((bf16[32,128,128]{2,1,0:T(8,128)(2,1)S(1)}, bf16[32,128,128]{2,1,0:T(8,128)(2,1)}, u32[]{:S(2)}, u32[]{:S(2)}) %collective-permute-start.19) | collective-permute-done | bytes 1048608 | tf_op jit(solution)/shard_map/ppermute | solution.py:246
  118.3 12.4 %collective-permute-done.17 = bf16[32,128,128]{2,1,0:T(8,128)(2,1)} collective-permute-done((bf16[32,128,128]{2,1,0:T(8,128)(2,1)S(1)}, bf16[32,128,128]{2,1,0:T(8,128)(2,1)}, u32[]{:S(2)}, u32[]{:S(2)}) %collective-permute-start.17) | collective-permute-done | bytes 1048608 | tf_op jit(solution)/shard_map/ppermute | solution.py:245
  130.7 2.2 %add_convert_fusion = bf16[32,128,128]{2,1,0:T(8,128)(2,1)S(1)} fusion(bf16[32,128,128]{2,1,0:T(8,128)(2,1)} %collective-permute-done.19, bf16[32,128,128]{2,1,0:T(8,128)(2,1)} %collective-permute-done.17, bf16[32,128,128]{2,1,0:T(8,128)(2,1)S(1)} %get-tuple-element.73), kind=kLoop, calls=%fused_computation | loop fusion | flops 3145728 | bytes 4194304 | tf_op jit(solution)/shard_map/convert_element_type | solution.py:257
  134.2 4.9 %collective-permute-done.20 = bf16[4,128,128]{2,1,0:T(8,128)(2,1)S(1)} collective-permute-done((bf16[4,128,128]{2,1,0:T(8,128)(2,1)S(1)}, bf16[4,128,128]{2,1,0:T(8,128)(2,1)S(1)}, u32[]{:S(2)}, u32[]{:S(2)}) %collective-permute-start.20) | collective-permute-done | bytes 131104 | tf_op jit(solution)/shard_map/ppermute | solution.py:243
  139.7 2.7 %collective-permute-start.21 = (bf16[8,128,128]{2,1,0:T(8,128)(2,1)S(1)}, bf16[8,128,128]{2,1,0:T(8,128)(2,1)S(1)}, u32[]{:S(2)}, u32[]{:S(2)}) collective-permute-start(bf16[8,128,128]{2,1,0:T(8,128)(2,1)S(1)} %get-tuple-element.82), channel_id=1, source_target_pairs={{0,16},{16,32},{32,48},{48,0},{1,17},{17,33},{33,49},{49,1},{2,18}... | collective-permute-start | bytes 786440 | tf_op jit(solution)/shard_map/ppermute | solution.py:245
  142.4 3.1 %collective-permute-done.22 = bf16[4,128,128]{2,1,0:T(8,128)(2,1)S(1)} collective-permute-done((bf16[4,128,128]{2,1,0:T(8,128)(2,1)S(1)}, bf16[4,128,128]{2,1,0:T(8,128)(2,1)S(1)}, u32[]{:S(2)}, u32[]{:S(2)}) %collective-permute-start.22) | collective-permute-done | bytes 131104 | tf_op jit(solution)/shard_map/ppermute | solution.py:244
  145.7 1.4 reduce_sum.12
  147.8 5.5 %collective-permute-done.23 = bf16[8,128,128]{2,1,0:T(8,128)(2,1)S(1)} collective-permute-done((bf16[8,128,128]{2,1,0:T(8,128)(2,1)S(1)}, bf16[8,128,128]{2,1,0:T(8,128)(2,1)S(1)}, u32[]{:S(2)}, u32[]{:S(2)}) %collective-permute-start.23) | collective-permute-done | bytes 262176 | tf_op jit(solution)/shard_map/ppermute | solution.py:246
  153.3 1.9 %select_bitcast_fusion = (f32[1,8,128,128]{3,2,1,0:T(8,128)}, f32[1,8,128,128]{2,3,1,0:T(8,128)S(1)}) fusion(bf16[8,128,128]{2,1,0:T(8,128)(2,1)S(1)} %collective-permute-done.23, bf16[8,128,128]{2,1,0:T(8,128)(2,1)S(1)} %collective-permute-done.21, bf16[32,128,128]{2,1,0:T(8,128)(2,1)S(1)} %add_convert_fusion, pred[8]{0:T(512)(128)(4,1)S(1)} %add_compare_fusion, ...), kind=kLoop, calls=%fused_computation.2 | loop fusion | flops 1310720 | bytes 2097160 | tf_op jit(solution)/shard_map/broadcast_in_dim | solution.py:270
  (69 shorter events, 15.2 us)
Async XLA Ops:
  7.2 146.1 %reduce-scatter.2.cloned.1.call-start = ((), (), s32[]{:S(2)}) async-start(), calls=%async_computation.2 | async-start | bytes 4456448 | tf_op jit(solution)/shard_map/reduce_scatter | solution.py:256
  8.1 8.9 %collective-permute-start.1 = (bf16[2,128,256]{2,1,0:T(8,128)(2,1)S(1)}, bf16[2,128,256]{2,1,0:T(8,128)(2,1)S(1)}, u32[]{:S(2)}, u32[]{:S(2)}) collective-permute-start(bf16[2,128,256]{2,1,0:T(8,128)(2,1)S(1)} %pad_maximum_fusion.refs_0_), channel_id=1, source_target_pairs={{0,2},{1,15},{2,4},{3,1},{4,6},{5,3},{6,8},{7,5},{8,10},{9,7},{10,... | collective-permute-start | bytes 393224 | tf_op jit(solution)/shard_map/ppermute | solution.py:214
  10.1 6.9 %collective-permute-start = (bf16[2,128,256]{2,1,0:T(8,128)(2,1)S(1)}, bf16[2,128,256]{2,1,0:T(8,128)(2,1)S(1)}, u32[]{:S(2)}, u32[]{:S(2)}) collective-permute-start(bf16[2,128,256]{2,1,0:T(8,128)(2,1)S(1)} %pad_maximum_fusion.refs_0_), channel_id=1, source_target_pairs={{0,1},{1,0},{2,3},{3,2},{4,5},{5,4},{6,7},{7,6},{8,9},{9,8},{10,11... | collective-permute-start | bytes 393224 | tf_op jit(solution)/shard_map/ppermute | solution.py:218
  17.0 6.2 %collective-permute-start.5 = (bf16[2,128,256]{2,1,0:T(8,128)(2,1)S(1)}, bf16[2,128,256]{2,1,0:T(8,128)(2,1)S(1)}, u32[]{:S(2)}, u32[]{:S(2)}) collective-permute-start(bf16[2,128,256]{2,1,0:T(8,128)(2,1)S(1)} %collective-permute-done.1.refs_2_), channel_id=1, source_target_pairs={{0,2},{1,15},{2,4},{3,1},{4,6},{5,3},{6,8},{7,5},{8,10},{9,7},{10,... | collective-permute-start | bytes 393224 | tf_op jit(solution)/shard_map/ppermute | solution.py:214
  17.0 7.6 %collective-permute-start.3 = (bf16[2,128,256]{2,1,0:T(8,128)(2,1)S(1)}, bf16[2,128,256]{2,1,0:T(8,128)(2,1)S(1)}, u32[]{:S(2)}, u32[]{:S(2)}) collective-permute-start(bf16[2,128,256]{2,1,0:T(8,128)(2,1)S(1)} %collective-permute-done.refs_1_), channel_id=1, source_target_pairs={{0,2},{1,15},{2,4},{3,1},{4,6},{5,3},{6,8},{7,5},{8,10},{9,7},{10,... | collective-permute-start | bytes 393224 | tf_op jit(solution)/shard_map/ppermute | solution.py:214
  23.2 6.2 %collective-permute-start.9 = (bf16[2,128,256]{2,1,0:T(8,128)(2,1)S(1)}, bf16[2,128,256]{2,1,0:T(8,128)(2,1)S(1)}, u32[]{:S(2)}, u32[]{:S(2)}) collective-permute-start(bf16[2,128,256]{2,1,0:T(8,128)(2,1)S(1)} %collective-permute-done.5.refs_6_), channel_id=1, source_target_pairs={{0,2},{1,15},{2,4},{3,1},{4,6},{5,3},{6,8},{7,5},{8,10},{9,7},{10,... | collective-permute-start | bytes 393224 | tf_op jit(solution)/shard_map/ppermute | solution.py:214
  24.6 6.2 %collective-permute-start.7 = (bf16[2,128,256]{2,1,0:T(8,128)(2,1)S(1)}, bf16[2,128,256]{2,1,0:T(8,128)(2,1)S(1)}, u32[]{:S(2)}, u32[]{:S(2)}) collective-permute-start(bf16[2,128,256]{2,1,0:T(8,128)(2,1)S(1)} %collective-permute-done.3.refs_4_), channel_id=1, source_target_pairs={{0,2},{1,15},{2,4},{3,1},{4,6},{5,3},{6,8},{7,5},{8,10},{9,7},{10,... | collective-permute-start | bytes 393224 | tf_op jit(solution)/shard_map/ppermute | solution.py:214
  24.6 6.2 %collective-permute-start.2 = (bf16[2,128,256]{2,1,0:T(8,128)(2,1)S(1)}, bf16[2,128,256]{2,1,0:T(8,128)(2,1)S(1)}, u32[]{:S(2)}, u32[]{:S(2)}) collective-permute-start(bf16[2,128,256]{2,1,0:T(8,128)(2,1)S(1)} %collective-permute-done.1.refs_2_), channel_id=1, source_target_pairs={{0,1},{1,0},{2,3},{3,2},{4,5},{5,4},{6,7},{7,6},{8,9},{9,8},{10,11... | collective-permute-start | bytes 393224 | tf_op jit(solution)/shard_map/ppermute | solution.py:218
  25.1 6.2 %collective-permute-start.6 = (bf16[2,128,256]{2,1,0:T(8,128)(2,1)S(1)}, bf16[2,128,256]{2,1,0:T(8,128)(2,1)S(1)}, u32[]{:S(2)}, u32[]{:S(2)}) collective-permute-start(bf16[2,128,256]{2,1,0:T(8,128)(2,1)S(1)} %collective-permute-done.5.refs_6_), channel_id=1, source_target_pairs={{0,1},{1,0},{2,3},{3,2},{4,5},{5,4},{6,7},{7,6},{8,9},{9,8},{10,11... | collective-permute-start | bytes 393224 | tf_op jit(solution)/shard_map/ppermute | solution.py:218
  29.3 6.2 %collective-permute-start.13 = (bf16[2,128,256]{2,1,0:T(8,128)(2,1)S(1)}, bf16[2,128,256]{2,1,0:T(8,128)(2,1)S(1)}, u32[]{:S(2)}, u32[]{:S(2)}) collective-permute-start(bf16[2,128,256]{2,1,0:T(8,128)(2,1)S(1)} %collective-permute-done.9.refs_10_), channel_id=1, source_target_pairs={{0,2},{1,15},{2,4},{3,1},{4,6},{5,3},{6,8},{7,5},{8,10},{9,7},{10,... | collective-permute-start | bytes 393224 | tf_op jit(solution)/shard_map/ppermute | solution.py:214
  30.7 6.2 %collective-permute-start.11 = (bf16[2,128,256]{2,1,0:T(8,128)(2,1)S(1)}, bf16[2,128,256]{2,1,0:T(8,128)(2,1)S(1)}, u32[]{:S(2)}, u32[]{:S(2)}) collective-permute-start(bf16[2,128,256]{2,1,0:T(8,128)(2,1)S(1)} %collective-permute-done.7.refs_8_), channel_id=1, source_target_pairs={{0,2},{1,15},{2,4},{3,1},{4,6},{5,3},{6,8},{7,5},{8,10},{9,7},{10,... | collective-permute-start | bytes 393224 | tf_op jit(solution)/shard_map/ppermute | solution.py:214
  30.7 6.8 %collective-permute-start.4 = (bf16[2,128,256]{2,1,0:T(8,128)(2,1)S(1)}, bf16[2,128,256]{2,1,0:T(8,128)(2,1)S(1)}, u32[]{:S(2)}, u32[]{:S(2)}) collective-permute-start(bf16[2,128,256]{2,1,0:T(8,128)(2,1)S(1)} %collective-permute-done.3.refs_4_), channel_id=1, source_target_pairs={{0,1},{1,0},{2,3},{3,2},{4,5},{5,4},{6,7},{7,6},{8,9},{9,8},{10,11... | collective-permute-start | bytes 393224 | tf_op jit(solution)/shard_map/ppermute | solution.py:218
  30.8 6.8 %collective-permute-start.10 = (bf16[2,128,256]{2,1,0:T(8,128)(2,1)S(1)}, bf16[2,128,256]{2,1,0:T(8,128)(2,1)S(1)}, u32[]{:S(2)}, u32[]{:S(2)}) collective-permute-start(bf16[2,128,256]{2,1,0:T(8,128)(2,1)S(1)} %collective-permute-done.9.refs_10_), channel_id=1, source_target_pairs={{0,1},{1,0},{2,3},{3,2},{4,5},{5,4},{6,7},{7,6},{8,9},{9,8},{10,11... | collective-permute-start | bytes 393224 | tf_op jit(solution)/shard_map/ppermute | solution.py:218
  31.3 6.3 %collective-permute-start.8 = (bf16[2,128,256]{2,1,0:T(8,128)(2,1)S(1)}, bf16[2,128,256]{2,1,0:T(8,128)(2,1)S(1)}, u32[]{:S(2)}, u32[]{:S(2)}) collective-permute-start(bf16[2,128,256]{2,1,0:T(8,128)(2,1)S(1)} %collective-permute-done.7.refs_8_), channel_id=1, source_target_pairs={{0,1},{1,0},{2,3},{3,2},{4,5},{5,4},{6,7},{7,6},{8,9},{9,8},{10,11... | collective-permute-start | bytes 393224 | tf_op jit(solution)/shard_map/ppermute | solution.py:218
  35.5 2.1 %collective-permute-start.14 = (bf16[2,128,256]{2,1,0:T(8,128)(2,1)S(1)}, bf16[2,128,256]{2,1,0:T(8,128)(2,1)S(1)}, u32[]{:S(2)}, u32[]{:S(2)}) collective-permute-start(bf16[2,128,256]{2,1,0:T(8,128)(2,1)S(1)} %collective-permute-done.13.refs_14_), channel_id=1, source_target_pairs={{0,1},{1,0},{2,3},{3,2},{4,5},{5,4},{6,7},{7,6},{8,9},{9,8},{10,11... | collective-permute-start | bytes 393224 | tf_op jit(solution)/shard_map/ppermute | solution.py:218
  36.9 1.3 collective-permute-start.12
  38.3 2.2 %copy-start = (bf16[1,128,128,128]{3,2,1,0:T(8,128)(2,1)S(1)}, bf16[1,128,128,128]{3,2,1,0:T(8,128)(2,1)}, u32[]{:S(2)}) copy-start(bf16[1,128,128,128]{3,2,1,0:T(8,128)(2,1)} %up_ref.1) | copy-start | bytes 12582916
  40.5 2.2 %copy-start.2 = (bf16[1,128,128,128]{3,2,1,0:T(8,128)(2,1)S(1)}, bf16[1,128,128,128]{3,2,1,0:T(8,128)(2,1)}, u32[]{:S(2)}) copy-start(bf16[1,128,128,128]{3,2,1,0:T(8,128)(2,1)} %down_ref.1) | copy-start | bytes 12582916
  55.8 2.0 %copy-start.4 = (bf16[128,128,128]{2,1,0:T(8,128)(2,1)}, bf16[128,128,128]{2,1,0:T(8,128)(2,1)S(1)}, u32[]{:S(2)}) copy-start(bf16[128,128,128]{2,1,0:T(8,128)(2,1)S(1)} %weight_parts.2) | copy-start | bytes 12582916
  57.8 7.7 %copy-start.6 = (bf16[8,128,128]{2,1,0:T(8,128)(2,1)S(1)}, bf16[8,128,128]{2,1,0:T(8,128)(2,1)}, u32[]{:S(2)}) copy-start(bf16[8,128,128]{2,1,0:T(8,128)(2,1)} %copy-done.5) | copy-start | bytes 786436
  62.4 19.3 %collective-permute-start.18 = (bf16[16,128,128]{2,1,0:T(8,128)(2,1)S(1)}, bf16[16,128,128]{2,1,0:T(8,128)(2,1)S(1)}, u32[]{:S(2)}, u32[]{:S(2)}) collective-permute-start(bf16[16,128,128]{2,1,0:T(8,128)(2,1)S(1)} %get-tuple-element.77), channel_id=1, source_target_pairs={{0,192},{64,0},{128,64},{192,128},{1,193},{65,1},{129,65},{193,129... | collective-permute-start | bytes 1572872 | tf_op jit(solution)/shard_map/ppermute | solution.py:244
  65.5 2.2 %copy-start.1 = (bf16[1,128,128,128]{3,2,1,0:T(8,128)(2,1)S(1)}, bf16[1,128,128,128]{3,2,1,0:T(8,128)(2,1)}, u32[]{:S(2)}) copy-start(bf16[1,128,128,128]{3,2,1,0:T(8,128)(2,1)} %up_ref.1) | copy-start | bytes 12582916
  67.7 2.2 %copy-start.3 = (bf16[1,128,128,128]{3,2,1,0:T(8,128)(2,1)S(1)}, bf16[1,128,128,128]{3,2,1,0:T(8,128)(2,1)}, u32[]{:S(2)}) copy-start(bf16[1,128,128,128]{3,2,1,0:T(8,128)(2,1)} %down_ref.1) | copy-start | bytes 12582916
  76.7 22.8 %collective-permute-start.15 = (bf16[8,2,128,256]{3,2,1,0:T(8,128)(2,1)S(1)}, bf16[8,2,128,256]{3,2,1,0:T(8,128)(2,1)S(1)}, u32[]{:S(2)}, u32[]{:S(2)}) collective-permute-start(bf16[8,2,128,256]{3,2,1,0:T(8,128)(2,1)S(1)} %get-tuple-element.68), channel_id=1, source_target_pairs={{0,1},{1,0},{2,3},{3,2},{4,5},{5,4},{6,7},{7,6},{8,9},{9,8},{10,11... | collective-permute-start | bytes 3145736 | tf_op jit(solution)/shard_map/ppermute | solution.py:218
  76.8 22.3 %collective-permute-start.16 = (bf16[16,128,128]{2,1,0:T(8,128)(2,1)S(1)}, bf16[16,128,128]{2,1,0:T(8,128)(2,1)S(1)}, u32[]{:S(2)}, u32[]{:S(2)}) collective-permute-start(bf16[16,128,128]{2,1,0:T(8,128)(2,1)S(1)} %get-tuple-element.75), channel_id=1, source_target_pairs={{0,64},{64,128},{128,192},{192,0},{1,65},{65,129},{129,193},{193,1... | collective-permute-start | bytes 1572872 | tf_op jit(solution)/shard_map/ppermute | solution.py:243
  82.0 36.3 %collective-permute-start.19 = (bf16[32,128,128]{2,1,0:T(8,128)(2,1)S(1)}, bf16[32,128,128]{2,1,0:T(8,128)(2,1)}, u32[]{:S(2)}, u32[]{:S(2)}) collective-permute-start(bf16[32,128,128]{2,1,0:T(8,128)(2,1)S(1)} %add_dynamic-update-slice_fusion), channel_id=1, source_target_pairs={{0,192},{64,0},{128,64},{192,128},{1,193},{65,1},{129,65},{193,129... | collective-permute-start | bytes 3145736 | tf_op jit(solution)/shard_map/ppermute | solution.py:246
  99.4 31.3 %collective-permute-start.17 = (bf16[32,128,128]{2,1,0:T(8,128)(2,1)S(1)}, bf16[32,128,128]{2,1,0:T(8,128)(2,1)}, u32[]{:S(2)}, u32[]{:S(2)}) collective-permute-start(bf16[32,128,128]{2,1,0:T(8,128)(2,1)S(1)} %add_dynamic-update-slice_fusion.1), channel_id=1, source_target_pairs={{0,64},{64,128},{128,192},{192,0},{1,65},{65,129},{129,193},{193,1... | collective-permute-start | bytes 3145736 | tf_op jit(solution)/shard_map/ppermute | solution.py:245
  100.8 44.9 %all-to-all-start = ((bf16[8,2,128,256]{3,2,1,0:T(8,128)(2,1)}), bf16[8,2,128,256]{3,2,1,0:T(8,128)(2,1)}, u32[]{:S(2)}, u32[]{:S(2)}) async-start(bf16[8,2,128,256]{3,2,1,0:T(8,128)(2,1)} %add_convert_fusion.1), calls=%async_computation | async-start | bytes 2097152 | tf_op jit(solution)/shard_map/all_to_all | solution.py:263
  132.9 6.2 %collective-permute-start.20 = (bf16[4,128,128]{2,1,0:T(8,128)(2,1)S(1)}, bf16[4,128,128]{2,1,0:T(8,128)(2,1)S(1)}, u32[]{:S(2)}, u32[]{:S(2)}) collective-permute-start(bf16[4,128,128]{2,1,0:T(8,128)(2,1)S(1)} %slice.135), channel_id=1, source_target_pairs={{0,16},{16,32},{32,48},{48,0},{1,17},{17,33},{33,49},{49,1},{2,18}... | collective-permute-start | bytes 393224 | tf_op jit(solution)/shard_map/ppermute | solution.py:243
  139.1 6.4 %collective-permute-start.22 = (bf16[4,128,128]{2,1,0:T(8,128)(2,1)S(1)}, bf16[4,128,128]{2,1,0:T(8,128)(2,1)S(1)}, u32[]{:S(2)}, u32[]{:S(2)}) collective-permute-start(bf16[4,128,128]{2,1,0:T(8,128)(2,1)S(1)} %get-tuple-element.83), channel_id=1, source_target_pairs={{0,48},{16,0},{32,16},{48,32},{1,49},{17,1},{33,17},{49,33},{2,50}... | collective-permute-start | bytes 393224 | tf_op jit(solution)/shard_map/ppermute | solution.py:244
  139.7 8.0 %collective-permute-start.21 = (bf16[8,128,128]{2,1,0:T(8,128)(2,1)S(1)}, bf16[8,128,128]{2,1,0:T(8,128)(2,1)S(1)}, u32[]{:S(2)}, u32[]{:S(2)}) collective-permute-start(bf16[8,128,128]{2,1,0:T(8,128)(2,1)S(1)} %get-tuple-element.82), channel_id=1, source_target_pairs={{0,16},{16,32},{32,48},{48,0},{1,17},{17,33},{33,49},{49,1},{2,18}... | collective-permute-start | bytes 786440 | tf_op jit(solution)/shard_map/ppermute | solution.py:245
  145.6 7.7 %collective-permute-start.23 = (bf16[8,128,128]{2,1,0:T(8,128)(2,1)S(1)}, bf16[8,128,128]{2,1,0:T(8,128)(2,1)S(1)}, u32[]{:S(2)}, u32[]{:S(2)}) collective-permute-start(bf16[8,128,128]{2,1,0:T(8,128)(2,1)S(1)} %fusion), channel_id=1, source_target_pairs={{0,48},{16,0},{32,16},{48,32},{1,49},{17,1},{33,17},{49,33},{2,50}... | collective-permute-start | bytes 786440 | tf_op jit(solution)/shard_map/ppermute | solution.py:246
  (9 other events, 7.2 us)
Sparse Core Ops, SparseCore 0:
  57.9 87.6 reduce-scatter.1
where the time goes:
time: 164 us; the launch traced here: 163 us
  waiting for transfers between devices  79.2 us (48%)
  starting transfers between devices  23.6 us (14%)
  local copies, waits for them, and re-layouts  18.9 us (12%)
  Pallas kernels  18 us (11%)
  between operations  14.9 us (9%)
  other arithmetic  8.38 us (5%)
    ppermute x7, waiting for transfers between devices, step_both(): return lax.ppermute(x, ('z', 'c'), pairs)  22.2 us
    unnamed x31, local copies, waits for them, and re-layouts  18.2 us
    ppermute x2, waiting for transfers between devices, scatter_ring(): from_left = lax.ppermute(opp_a, axis, up)  18.2 us
    ppermute x2, waiting for transfers between devices, scatter_ring(): left = lax.ppermute(left.at[n:].add(from_right), axis, down)  17.8 us
    ppermute x2, waiting for transfers between devices, scatter_ring(): right = lax.ppermute(right.at[:n].add(from_left), axis, up)  12.4 us
    ppermute x2, waiting for transfers between devices, scatter_ring(): from_right = lax.ppermute(opp_b, axis, down)  7.95 us
    pallas_call x1, Pallas kernels, forward(): pl.pallas_call(forward_kernel, grid=(STEPS,), in_specs=[sspec()] * 3 + [p...  7.59 us
    pallas_call x1, Pallas kernels, token_parts(): pl.pallas_call(token_kernel, grid=(STEPS,), in_specs=[sspec()] * 3 + [who...  6.83 us
  transfers between devices with their start and end apart: 26, of which 15 were waited for; matrix products, arithmetic and copies ran while one was open for 4% of the time, Pallas kernels for 5%

commit v1 on v0

--- a/solution.py
+++ b/solution.py
@@ -23,8 +23,8 @@
     return pl.BlockSpec(shape, lambda *i: (0,) * len(shape))
 
 
-def params(**kw):
-    return pltpu.CompilerParams(vmem_limit_bytes=32 << 20, **kw)
+def params(mib):
+    return pltpu.CompilerParams(vmem_limit_bytes=mib << 20)
 
 
 def sspec():
@@ -116,39 +116,47 @@
         out_specs=[whole(COLS, SIDE, SIDE)] * 2 + [whole(ROWS, SIDE, SIDE)] * 4,
         out_shape=[tok, tok, hid, hid, hid, hid],
         scratch_shapes=[VM((ROWS, SIDE, SIDE), F32)] * 2 + [pltpu.SemaphoreType.DMA],
-        compiler_params=params(),
+        compiler_params=params(48),
         cost_estimate=pl.CostEstimate(flops=1 << 30, bytes_accessed=12 << 20, transcendentals=1 << 18),
         name="forward",
     )(rows, cols, count, *shards, up_tiles, down_tiles)
 
 
-def ring_slot(j):
+def ring_slot(j, first, second):
     away = (2, 1, 3, 0)
-    y = lax.rem(lax.axis_index("y") + away[j // 32], 4)
-    x = lax.rem(lax.axis_index("x") + away[j // 8 % 4], 4)
-    return (y * 4 + x) * 8 + j % 8
-
-
-def weight_kernel(sizes, order, rows, cols, x_ref, t_ref, *outs):
-    at = 0
-    for out, n in zip(outs, sizes):
-        for s in range(n):
-            slot = order(at + s)
-            out[s] = nn(t_ref[rows[slot]], x_ref[cols[slot]]).astype(BF)
-        at += n
-
-
-def weight_parts(rows, cols, x, t, sizes, order):
-    return pl.pallas_call(
-        functools.partial(weight_kernel, sizes, order),
+    at = {
+        first: lax.rem(lax.axis_index(first) + away[j // 32], 4),
+        second: lax.rem(lax.axis_index(second) + away[j // 8 % 4], 4),
+    }
+    return (at["y"] * 4 + at["x"]) * 8 + j % 8
+
+
+def weight_kernel(rows, cols, x_ref, dt_ref, dy_ref, ht_ref, *outs):
+    up_outs, down_outs = outs[:7], outs[7:]
+
+    def piece(axes, t_ref, v_ref, out, at):
+        for s in range(out.shape[0]):
+            slot = ring_slot(at + s, *axes)
+            out[s] = nn(t_ref[rows[slot]], v_ref[cols[slot]]).astype(BF)
+
+    for k in range(7):
+        piece(("x", "y"), dt_ref, x_ref, up_outs[k], 16 * k)
+        piece(("y", "x"), ht_ref, dy_ref, down_outs[k], 16 * k)
+
+
+def weight_parts(rows, cols, x, dt, dy, ht):
+    sizes = [16] * 6 + [32]
+    outs = pl.pallas_call(
+        weight_kernel,
         grid=(1,),
-        in_specs=[sspec()] * 2 + [whole(COLS, SIDE, SIDE), whole(ROWS, SIDE, SIDE)],
-        out_specs=[whole(n, SIDE, SIDE) for n in sizes],
-        out_shape=[jax.ShapeDtypeStruct((n, SIDE, SIDE), BF) for n in sizes],
-        compiler_params=params(),
-        cost_estimate=pl.CostEstimate(flops=1 << 29, bytes_accessed=6 << 20, transcendentals=0),
+        in_specs=[sspec()] * 2 + [whole(COLS, SIDE, SIDE), whole(ROWS, SIDE, SIDE)] * 2,
+        out_specs=[whole(n, SIDE, SIDE) for n in sizes * 2],
+        out_shape=[jax.ShapeDtypeStruct((n, SIDE, SIDE), BF) for n in sizes * 2],
+        compiler_params=params(32),
+        cost_estimate=pl.CostEstimate(flops=1 << 30, bytes_accessed=12 << 20, transcendentals=0),
         name="weight_parts",
-    )(rows, cols, x, t)
+    )(rows, cols, x, dt, dy, ht)
+    return outs[:7], outs[7:]
 
 
 def token_kernel(rows, cols, count_ref, h_ref, d_ref, up_ref, down_ref, send_ref, keep_ref, mix_acc, in_acc):
@@ -159,6 +167,7 @@
     def _():
         mix_acc[...] = jnp.zeros_like(mix_acc)
         in_acc[...] = jnp.zeros_like(in_acc)
+
 
     for s in range(GROUP):
         slot = step * GROUP + s
@@ -196,7 +205,7 @@
         out_specs=[whole(8, 2, SIDE, 2 * SIDE)] * 2,
         out_shape=[part] * 2,
         scratch_shapes=[VM((COLS, SIDE, SIDE), F32)] * 2,
-        compiler_params=params(),
+        compiler_params=params(48),
         cost_estimate=pl.CostEstimate(flops=1 << 30, bytes_accessed=11 << 20, transcendentals=0),
         name="token_parts",
     )(rows, cols, count, h, d, up_tiles, down_tiles)
@@ -237,26 +246,39 @@
     return shards
 
 
-def scatter_ring(axis, opp_a, opp_b, right, left):
-    n = opp_a.shape[0]
-    up, down = ring(4, 1), ring(4, -1)
-    from_left = lax.ppermute(opp_a, axis, up)
-    from_right = lax.ppermute(opp_b, axis, down)
-    right = lax.ppermute(right.at[:n].add(from_left), axis, up)
-    left = lax.ppermute(left.at[n:].add(from_right), axis, down)
-    return right, left
+def hop(x, axis, by):
+    return lax.ppermute(x, axis, ring(4, by))
+
+
+def first_stage(axis, parts):
+    far_a, far_b, next_a, next_b, before_a, before_b, own = parts
+    from_left = hop(far_a, axis, 1)
+    from_right = hop(far_b, axis, -1)
+    left_b = hop(next_b, axis, 1)
+    right_a = hop(before_a, axis, -1)
+    left_a = hop(add(next_a, from_left).astype(BF), axis, 1)
+    right_b = hop(add(before_b, from_right).astype(BF), axis, -1)
+    return add(own[:16], left_a, right_a).astype(BF), add(own[16:], left_b, right_b).astype(BF)
+
+
+def second_stage(axis, a, b):
+    from_left = hop(a[:4], axis, 1)
+    from_right = hop(a[4:8], axis, -1)
+    left = hop(a[8:].at[:4].add(from_left), axis, 1)
+    right = hop(b[:8].at[4:].add(from_right), axis, -1)
+    return add(b[8:], left, right)
 
 
 def body(tokens, grad_out, up_tiles, down_tiles, tile_rows, tile_cols, tile_count):
     rows, cols = tile_rows[0], tile_cols[0]
     shards = gather_over_tile(jnp.stack([tokens, grad_out]))
     x_all, dy_all, h, ht, d, dt = forward(rows, cols, tile_count, shards, up_tiles, down_tiles)
-    opp_a, opp_b, right, left, mine = weight_parts(rows, cols, dy_all, ht, (16, 16, 32, 32, 32), ring_slot)
-    (up_part,) = weight_parts(rows, cols, x_all, dt, (SLOTS,), lambda j: j)
-    up_total = lax.psum_scatter(up_part, ("y", "x"), scatter_dimension=0, tiled=True)
-    part = add(mine, *scatter_ring("y", opp_a, opp_b, right, left)).astype(BF)
-    got = scatter_ring("x", part[:4], part[4:8], part[8:16], part[16:24])
-    down_total = add(part[24:], *got)
+    up_parts, down_parts = weight_parts(rows, cols, x_all, dt, dy_all, ht)
+    up_half = first_stage("x", up_parts)
+    down_half = first_stage("y", down_parts)
+    up_total = second_stage("y", *up_half)
+    down_total = second_stage("x", *down_half)
+    h, d, _, _ = lax.optimization_barrier((h, d, up_parts[0], down_parts[0]))
 
     send, keep = token_parts(rows, cols, tile_count, h, d, up_tiles, down_tiles)
     pieces = add(keep, swap(send)).astype(BF)
@@ -265,7 +287,7 @@
 
     slot = lax.axis_index(("y", "x")) * 8 + jnp.arange(8, dtype=jnp.int32)
     live = (slot < tile_count[0])[:, None, None]
-    grad_up = jnp.where(live, jnp.swapaxes(up_total, 1, 2).astype(F32) * (1.0 / 16), 0.0)
+    grad_up = jnp.where(live, jnp.swapaxes(up_total, 1, 2) * (1.0 / 16), 0.0)
     grad_down = jnp.where(live, down_total * (1.0 / 16), 0.0)
     return total[0], total[1], grad_up[None], grad_down[None]
 

time: 164 us -> 136 us (0.83)
  waiting for transfers between devices: 79.2 us -> 58.5 us
  local copies, waits for them, and re-layouts: 18.9 us -> 3.08 us
  starting transfers between devices: 23.6 us -> 37.3 us
  between operations: 14.9 us -> 1.57 us
  other arithmetic: 8.38 us -> 12.8 us
  Pallas kernels: 18 us -> 22 us
    ppermute x8 -> x20, waiting for transfers between devices: 56.3 us -> 35.6 us  [hop(): return lax.ppermute(x, axis, ring(4, by))]
    unnamed x31 -> x13, local copies, waits for them, and re-layouts: 18.2 us -> 2.32 us
    ppermute x8 -> x20, starting transfers between devices: 11.6 us -> 24.8 us  [hop(): return lax.ppermute(x, axis, ring(4, by))]
    convert_element_type x1 -> x6, other arithmetic: 2.17 us -> 6.95 us  [the longest x2 3.99 us: first_stage(): add(own[:16], left_a, right_a).astype(BF)]
    pallas_call x1, Pallas kernels: 6.83 us -> 9.31 us  [token_parts(): pl.pallas_call(token_kernel, grid=(STEPS,), in_specs=[sspec()] * 3 + [who...]
    pallas_call x1, Pallas kernels: 7.59 us -> 9.68 us  [forward(): pl.pallas_call(forward_kernel, grid=(STEPS,), in_specs=[sspec()] * 3 + [p...]
    pallas_call x2 -> x1, Pallas kernels: 3.6 us -> 3.04 us  [weight_parts(): pl.pallas_call(weight_kernel, grid=(1,), in_specs=[sspec()] * 2 + [whole(...]
  transfers between devices with their start and end apart: 26 -> 37, of which waited for: 15 -> 19; matrix products, arithmetic and copies ran while one was open for 4% -> 9% of each run, Pallas kernels for 5% -> 7%
where the time goes in v1:
time: 136 us; the launch traced here: 135 us
  waiting for transfers between devices  58.5 us (43%)
  starting transfers between devices  37.3 us (27%)
  Pallas kernels  22 us (16%)
  other arithmetic  12.8 us (9%)
  local copies, waits for them, and re-layouts  3.08 us (2%)
  between operations  1.57 us (1%)
    ppermute x20, waiting for transfers between devices, hop(): return lax.ppermute(x, axis, ring(4, by))  35.6 us
    ppermute x20, starting transfers between devices, hop(): return lax.ppermute(x, axis, ring(4, by))  24.8 us
    ppermute x7, waiting for transfers between devices, step_both(): return lax.ppermute(x, ('z', 'c'), pairs)  22.2 us
    pallas_call x1, Pallas kernels, forward(): pl.pallas_call(forward_kernel, grid=(STEPS,), in_specs=[sspec()] * 3 + [p...  9.68 us
    pallas_call x1, Pallas kernels, token_parts(): pl.pallas_call(token_kernel, grid=(STEPS,), in_specs=[sspec()] * 3 + [who...  9.31 us
    all_to_all x1, starting transfers between devices, body(): terms = lax.all_to_all(pieces, 'z', 0, 0, tiled=True)  5.82 us
    ppermute x9, starting transfers between devices, swap(): return lax.ppermute(x, 'c', [(0, 1), (1, 0)])  4.7 us
    convert_element_type x2, other arithmetic, first_stage(): add(own[:16], left_a, right_a).astype(BF)  3.99 us
  transfers between devices with their start and end apart: 37, of which 19 were waited for; matrix products, arithmetic and copies ran while one was open for 9% of the time, Pallas kernels for 7%

profile of v1, /device:TPU:6, one launch (start us, length us, event | category | flops | bytes accessed | tf_op | source)
XLA Modules:
  0.0 135.3 jit_solution(7394507266825329551)
XLA Ops:
  1.5 2.0 %collective-permute-start.1 = (bf16[2,128,256]{2,1,0:T(8,128)(2,1)S(1)}, bf16[2,128,256]{2,1,0:T(8,128)(2,1)S(1)}, u32[]{:S(2)}, u32[]{:S(2)}) collective-permute-start(bf16[2,128,256]{2,1,0:T(8,128)(2,1)S(1)} %pad_maximum_fusion.refs_0_), channel_id=1, source_target_pairs={{0,2},{1,15},{2,4},{3,1},{4,6},{5,3},{6,8},{7,5},{8,10},{9,7},{10,... | collective-permute-start | bytes 393224 | tf_op jit(solution)/shard_map/ppermute | solution.py:223
  3.5 3.5 %collective-permute-start = (bf16[2,128,256]{2,1,0:T(8,128)(2,1)S(1)}, bf16[2,128,256]{2,1,0:T(8,128)(2,1)S(1)}, u32[]{:S(2)}, u32[]{:S(2)}) collective-permute-start(bf16[2,128,256]{2,1,0:T(8,128)(2,1)S(1)} %pad_maximum_fusion.refs_0_), channel_id=1, source_target_pairs={{0,1},{1,0},{2,3},{3,2},{4,5},{5,4},{6,7},{7,6},{8,9},{9,8},{10,11... | collective-permute-start | bytes 393224 | tf_op jit(solution)/shard_map/ppermute | solution.py:227
  7.0 3.4 %collective-permute-done.1.refs_2_ = bf16[2,128,256]{2,1,0:T(8,128)(2,1)S(1)} collective-permute-done((bf16[2,128,256]{2,1,0:T(8,128)(2,1)S(1)}, bf16[2,128,256]{2,1,0:T(8,128)(2,1)S(1)}, u32[]{:S(2)}, u32[]{:S(2)}) %collective-permute-start.1) | collective-permute-done | bytes 131104 | tf_op jit(solution)/shard_map/ppermute | solution.py:223
  10.4 6.2 %collective-permute-done.5.refs_6_ = bf16[2,128,256]{2,1,0:T(8,128)(2,1)S(1)} collective-permute-done((bf16[2,128,256]{2,1,0:T(8,128)(2,1)S(1)}, bf16[2,128,256]{2,1,0:T(8,128)(2,1)S(1)}, u32[]{:S(2)}, u32[]{:S(2)}) %collective-permute-start.5) | collective-permute-done | bytes 131104 | tf_op jit(solution)/shard_map/ppermute | solution.py:223
  18.5 4.3 %collective-permute-done.9.refs_10_ = bf16[2,128,256]{2,1,0:T(8,128)(2,1)S(1)} collective-permute-done((bf16[2,128,256]{2,1,0:T(8,128)(2,1)S(1)}, bf16[2,128,256]{2,1,0:T(8,128)(2,1)S(1)}, u32[]{:S(2)}, u32[]{:S(2)}) %collective-permute-start.9) | collective-permute-done | bytes 131104 | tf_op jit(solution)/shard_map/ppermute | solution.py:223
  24.8 4.2 %collective-permute-done.13.refs_14_ = bf16[2,128,256]{2,1,0:T(8,128)(2,1)S(1)} collective-permute-done((bf16[2,128,256]{2,1,0:T(8,128)(2,1)S(1)}, bf16[2,128,256]{2,1,0:T(8,128)(2,1)S(1)}, u32[]{:S(2)}, u32[]{:S(2)}) %collective-permute-start.13) | collective-permute-done | bytes 131104 | tf_op jit(solution)/shard_map/ppermute | solution.py:223
  28.9 1.4 %collective-permute-done.11.refs_12_ = bf16[2,128,256]{2,1,0:T(8,128)(2,1)S(1)} collective-permute-done((bf16[2,128,256]{2,1,0:T(8,128)(2,1)S(1)}, bf16[2,128,256]{2,1,0:T(8,128)(2,1)S(1)}, u32[]{:S(2)}, u32[]{:S(2)}) %collective-permute-start.11) | collective-permute-done | bytes 131104 | tf_op jit(solution)/shard_map/ppermute | solution.py:223
  33.0 9.7 %forward.1 = (bf16[32,128,128]{2,1,0:T(8,128)(2,1)S(1)}, bf16[32,128,128]{2,1,0:T(8,128)(2,1)S(1)}, bf16[8,128,128]{2,1,0:T(8,128)(2,1)S(1)}, bf16[8,128,128]{2,...) custom-call(s32[128]{0:T(128)S(1)} %bitcast.16, s32[128]{0:T(128)S(1)} %bitcast.19, ...), custom_call_target="tpu_custom_call" | custom-call | flops 1073741824 | bytes 12582912 | tf_op jit(solution)/shard_map/forward/pallas_call | solution.py:112
  42.7 3.0 %weight_parts.1 = (bf16[16,128,128]{2,1,0:T(8,128)(2,1)S(1)}, bf16[16,128,128]{2,1,0:T(8,128)(2,1)S(1)}, bf16[16,128,128]{2,1,0:T(8,128)(2,1)S(1)}, bf16[16,128,...) custom-call(s32[128]{0:T(128)S(1)} %bitcast.17, ...), custom_call_target="tpu_custom_call" | custom-call | flops 1073741824 | bytes 12582912 | tf_op jit(solution)/shard_map/weight_parts/pallas_call | solution.py:149
  46.7 2.4 %collective-permute-start.19 = (bf16[16,128,128]{2,1,0:T(8,128)(2,1)S(1)}, bf16[16,128,128]{2,1,0:T(8,128)(2,1)S(1)}, u32[]{:S(2)}, u32[]{:S(2)}) collective-permute-start(bf16[16,128,128]{2,1,0:T(8,128)(2,1)S(1)} %get-tuple-element.82), channel_id=1, source_target_pairs={{0,16},{16,32},{32,48},{48,0},{1,17},{17,33},{33,49},{49,1},{2,18}... | collective-permute-start | bytes 1572872 | tf_op jit(solution)/shard_map/ppermute | solution.py:250
  49.1 3.0 %collective-permute-start.27 = (bf16[16,128,128]{2,1,0:T(8,128)(2,1)S(1)}, bf16[16,128,128]{2,1,0:T(8,128)(2,1)S(1)}, u32[]{:S(2)}, u32[]{:S(2)}) collective-permute-start(bf16[16,128,128]{2,1,0:T(8,128)(2,1)S(1)} %get-tuple-element.97), channel_id=1, source_target_pairs={{0,192},{64,0},{128,64},{192,128},{1,193},{65,1},{129,65},{193,129... | collective-permute-start | bytes 1572872 | tf_op jit(solution)/shard_map/ppermute | solution.py:250
  52.1 9.3 %token_parts.1 = (bf16[8,2,128,256]{3,2,1,0:T(8,128)(2,1)S(1)}, bf16[8,2,128,256]{3,2,1,0:T(8,128)(2,1)S(1)}) custom-call(s32[128]{0:T(128)S(1)} %bitcast.18, s32[128]{0:T(128)S(1)} %bitcast.21, s32[1]{0:T(128)} %copy.16.count_ref, bf16[8,128,128]{2,1,0:T(8,128)(2,1)S(1)} %get-tuple-element.84.h_ref, bf16[8,128,128]{2,1,0:T(8,128)(2,1)S(1)} %get-tuple-element.85.d_ref, ...), custom_call_target="tpu_custom_call" | custom-call | flops 1073741824 | bytes 11534336 | tf_op jit(solution)/shard_map/token_parts/pallas_call | solution.py:201
  61.7 2.1 %collective-permute-start.21 = (bf16[16,128,128]{2,1,0:T(8,128)(2,1)S(1)}, bf16[16,128,128]{2,1,0:T(8,128)(2,1)S(1)}, u32[]{:S(2)}, u32[]{:S(2)}) collective-permute-start(bf16[16,128,128]{2,1,0:T(8,128)(2,1)S(1)} %get-tuple-element.93), channel_id=1, source_target_pairs={{0,48},{16,0},{32,16},{48,32},{1,49},{17,1},{33,17},{49,33},{2,50}... | collective-permute-start | bytes 1572872 | tf_op jit(solution)/shard_map/ppermute | solution.py:250
  66.5 2.5 %collective-permute-start.20 = (bf16[16,128,128]{2,1,0:T(8,128)(2,1)}, bf16[16,128,128]{2,1,0:T(8,128)(2,1)}, u32[]{:S(2)}, u32[]{:S(2)}) collective-permute-start(bf16[16,128,128]{2,1,0:T(8,128)(2,1)} %add_convert_fusion.6), channel_id=1, source_target_pairs={{0,16},{16,32},{32,48},{48,0},{1,17},{17,33},{33,49},{49,1},{2,18}... | collective-permute-start | bytes 1572872 | tf_op jit(solution)/shard_map/ppermute | solution.py:250
  69.9 2.8 %collective-permute-done.16 = bf16[16,128,128]{2,1,0:T(8,128)(2,1)S(1)} collective-permute-done((bf16[16,128,128]{2,1,0:T(8,128)(2,1)S(1)}, bf16[16,128,128]{2,1,0:T(8,128)(2,1)S(1)}, u32[]{:S(2)}, u32[]{:S(2)}) %collective-permute-start.16) | collective-permute-done | bytes 524320 | tf_op jit(solution)/shard_map/ppermute | solution.py:250
  72.7 1.6 %collective-permute-start.26 = (bf16[16,128,128]{2,1,0:T(8,128)(2,1)S(1)}, bf16[16,128,128]{2,1,0:T(8,128)(2,1)}, u32[]{:S(2)}, u32[]{:S(2)}) collective-permute-start(bf16[16,128,128]{2,1,0:T(8,128)(2,1)S(1)} %get-tuple-element.95), channel_id=1, source_target_pairs={{0,64},{64,128},{128,192},{192,0},{1,65},{65,129},{129,193},{193,1... | collective-permute-start | bytes 1572872 | tf_op jit(solution)/shard_map/ppermute | solution.py:250
  74.3 3.5 %collective-permute-done.21 = bf16[16,128,128]{2,1,0:T(8,128)(2,1)S(1)} collective-permute-done((bf16[16,128,128]{2,1,0:T(8,128)(2,1)S(1)}, bf16[16,128,128]{2,1,0:T(8,128)(2,1)S(1)}, u32[]{:S(2)}, u32[]{:S(2)}) %collective-permute-start.21) | collective-permute-done | bytes 524320 | tf_op jit(solution)/shard_map/ppermute | solution.py:250
  77.8 3.2 %collective-permute-start.31 = (bf16[16,128,128]{2,1,0:T(8,128)(2,1)S(1)}, bf16[16,128,128]{2,1,0:T(8,128)(2,1)}, u32[]{:S(2)}, u32[]{:S(2)}) collective-permute-start(bf16[16,128,128]{2,1,0:T(8,128)(2,1)S(1)} %get-tuple-element.99), channel_id=1, source_target_pairs={{0,192},{64,0},{128,64},{192,128},{1,193},{65,1},{129,65},{193,129... | collective-permute-start | bytes 1572872 | tf_op jit(solution)/shard_map/ppermute | solution.py:250
  81.0 7.6 %collective-permute-done.18 = bf16[16,128,128]{2,1,0:T(8,128)(2,1)S(1)} collective-permute-done((bf16[16,128,128]{2,1,0:T(8,128)(2,1)S(1)}, bf16[16,128,128]{2,1,0:T(8,128)(2,1)S(1)}, u32[]{:S(2)}, u32[]{:S(2)}) %collective-permute-start.18) | collective-permute-done | bytes 524320 | tf_op jit(solution)/shard_map/ppermute | solution.py:250
  88.6 3.2 %collective-permute-start.28 = (bf16[16,128,128]{2,1,0:T(8,128)(2,1)}, bf16[16,128,128]{2,1,0:T(8,128)(2,1)}, u32[]{:S(2)}, u32[]{:S(2)}) collective-permute-start(bf16[16,128,128]{2,1,0:T(8,128)(2,1)} %add_convert_fusion.4), channel_id=1, source_target_pairs={{0,192},{64,0},{128,64},{192,128},{1,193},{65,1},{129,65},{193,129... | collective-permute-start | bytes 1572872 | tf_op jit(solution)/shard_map/ppermute | solution.py:250
  93.2 5.8 %all-to-all-start = ((bf16[8,2,128,256]{3,2,1,0:T(8,128)(2,1)}), bf16[8,2,128,256]{3,2,1,0:T(8,128)(2,1)}, u32[]{:S(2)}, u32[]{:S(2)}) async-start(bf16[8,2,128,256]{3,2,1,0:T(8,128)(2,1)} %add_convert_fusion), calls=%async_computation | async-start | bytes 2097152 | tf_op jit(solution)/shard_map/all_to_all | solution.py:285
  99.0 2.0 %add_convert_fusion.5 = (bf16[16,128,128]{2,1,0:T(8,128)(2,1)S(1)}, bf16[16,128,128]{2,1,0:T(8,128)(2,1)S(1)}) fusion(bf16[16,128,128]{2,1,0:T(8,128)(2,1)} %copy-done.4, bf16[16,128,128]{2,1,0:T(8,128)(2,1)} %collective-permute-done.20, bf16[32,128,128]{2,1,0:T(8,128)(2,1)S(1)} %get-tuple-element.88, bf16[16,128,128]{2,1,0:T(8,128)(2,1)} %copy-done.5, ...), kind=kLoop, calls=%fused_computation.5 | loop fusion | flops 3145728 | bytes 4194304 | tf_op jit(solution)/shard_map/convert_element_type | solution.py:261
  101.1 2.2 %collective-permute-done.28 = bf16[16,128,128]{2,1,0:T(8,128)(2,1)} collective-permute-done((bf16[16,128,128]{2,1,0:T(8,128)(2,1)}, bf16[16,128,128]{2,1,0:T(8,128)(2,1)}, u32[]{:S(2)}, u32[]{:S(2)}) %collective-permute-start.28) | collective-permute-done | bytes 524320 | tf_op jit(solution)/shard_map/ppermute | solution.py:250
  103.3 4.8 %collective-permute-done.30 = bf16[16,128,128]{2,1,0:T(8,128)(2,1)} collective-permute-done((bf16[16,128,128]{2,1,0:T(8,128)(2,1)}, bf16[16,128,128]{2,1,0:T(8,128)(2,1)}, u32[]{:S(2)}, u32[]{:S(2)}) %collective-permute-start.30) | collective-permute-done | bytes 524320 | tf_op jit(solution)/shard_map/ppermute | solution.py:250
  108.1 2.0 %add_convert_fusion.1 = (bf16[16,128,128]{2,1,0:T(8,128)(2,1)S(1)}, bf16[16,128,128]{2,1,0:T(8,128)(2,1)S(1)}) fusion(bf16[16,128,128]{2,1,0:T(8,128)(2,1)} %collective-permute-done.31, bf16[16,128,128]{2,1,0:T(8,128)(2,1)} %collective-permute-done.30, bf16[32,128,128]{2,1,0:T(8,128)(2,1)S(1)} %get-tuple-element.94, ...), kind=kLoop, calls=%fused_computation.1 | loop fusion | flops 3145728 | bytes 4194304 | tf_op jit(solution)/shard_map/convert_element_type | solution.py:261
  110.5 2.0 %collective-permute-start.23 = (bf16[8,128,128]{2,1,0:T(8,128)(2,1)S(1)}, bf16[8,128,128]{2,1,0:T(8,128)(2,1)S(1)}, u32[]{:S(2)}, u32[]{:S(2)}) collective-permute-start(bf16[8,128,128]{2,1,0:T(8,128)(2,1)S(1)} %get-tuple-element.110), channel_id=1, source_target_pairs={{0,64},{64,128},{128,192},{192,0},{1,65},{65,129},{129,193},{193,1... | collective-permute-start | bytes 786440 | tf_op jit(solution)/shard_map/ppermute | solution.py:250
  112.5 3.0 %collective-permute-done.32 = bf16[4,128,128]{2,1,0:T(8,128)(2,1)S(1)} collective-permute-done((bf16[4,128,128]{2,1,0:T(8,128)(2,1)S(1)}, bf16[4,128,128]{2,1,0:T(8,128)(2,1)S(1)}, u32[]{:S(2)}, u32[]{:S(2)}) %collective-permute-start.32) | collective-permute-done | bytes 131104 | tf_op jit(solution)/shard_map/ppermute | solution.py:250
  116.5 2.4 %collective-permute-start.33 = (bf16[8,128,128]{2,1,0:T(8,128)(2,1)S(1)}, bf16[8,128,128]{2,1,0:T(8,128)(2,1)S(1)}, u32[]{:S(2)}, u32[]{:S(2)}) collective-permute-start(bf16[8,128,128]{2,1,0:T(8,128)(2,1)S(1)} %get-tuple-element.108), channel_id=1, source_target_pairs={{0,16},{16,32},{32,48},{48,0},{1,17},{17,33},{33,49},{49,1},{2,18}... | collective-permute-start | bytes 786440 | tf_op jit(solution)/shard_map/ppermute | solution.py:250
  119.1 3.4 %collective-permute-done.34 = bf16[4,128,128]{2,1,0:T(8,128)(2,1)S(1)} collective-permute-done((bf16[4,128,128]{2,1,0:T(8,128)(2,1)S(1)}, bf16[4,128,128]{2,1,0:T(8,128)(2,1)S(1)}, u32[]{:S(2)}, u32[]{:S(2)}) %collective-permute-start.34) | collective-permute-done | bytes 131104 | tf_op jit(solution)/shard_map/ppermute | solution.py:250
  122.9 2.5 %collective-permute-done.25 = bf16[8,128,128]{2,1,0:T(8,128)(2,1)S(1)} collective-permute-done((bf16[8,128,128]{2,1,0:T(8,128)(2,1)S(1)}, bf16[8,128,128]{2,1,0:T(8,128)(2,1)S(1)}, u32[]{:S(2)}, u32[]{:S(2)}) %collective-permute-start.25) | collective-permute-done | bytes 262176 | tf_op jit(solution)/shard_map/ppermute | solution.py:250
  125.4 4.8 %collective-permute-done.35 = bf16[8,128,128]{2,1,0:T(8,128)(2,1)S(1)} collective-permute-done((bf16[8,128,128]{2,1,0:T(8,128)(2,1)S(1)}, bf16[8,128,128]{2,1,0:T(8,128)(2,1)S(1)}, u32[]{:S(2)}, u32[]{:S(2)}) %collective-permute-start.35) | collective-permute-done | bytes 262176 | tf_op jit(solution)/shard_map/ppermute | solution.py:250
  130.2 2.0 %select_bitcast_fusion = (f32[1,8,128,128]{3,2,1,0:T(8,128)}, f32[1,8,128,128]{2,3,1,0:T(8,128)S(1)}) fusion(bf16[8,128,128]{2,1,0:T(8,128)(2,1)S(1)} %collective-permute-done.35, bf16[8,128,128]{2,1,0:T(8,128)(2,1)S(1)} %collective-permute-done.33, bf16[16,128,128]{2,1,0:T(8,128)(2,1)S(1)} %get-tuple-element.105, pred[8]{0:T(512)(128)(4,1)S(1)} %add_compare_fusion, ...), kind=kLoop, calls=%fused_computation.9 | loop fusion | flops 1835008 | bytes 2621448 | tf_op jit(solution)/shard_map/broadcast_in_dim | solution.py:292
  (80 shorter events, 17.9 us)
Async XLA Ops:
  1.5 8.9 %collective-permute-start.1 = (bf16[2,128,256]{2,1,0:T(8,128)(2,1)S(1)}, bf16[2,128,256]{2,1,0:T(8,128)(2,1)S(1)}, u32[]{:S(2)}, u32[]{:S(2)}) collective-permute-start(bf16[2,128,256]{2,1,0:T(8,128)(2,1)S(1)} %pad_maximum_fusion.refs_0_), channel_id=1, source_target_pairs={{0,2},{1,15},{2,4},{3,1},{4,6},{5,3},{6,8},{7,5},{8,10},{9,7},{10,... | collective-permute-start | bytes 393224 | tf_op jit(solution)/shard_map/ppermute | solution.py:223
  3.5 6.9 %collective-permute-start = (bf16[2,128,256]{2,1,0:T(8,128)(2,1)S(1)}, bf16[2,128,256]{2,1,0:T(8,128)(2,1)S(1)}, u32[]{:S(2)}, u32[]{:S(2)}) collective-permute-start(bf16[2,128,256]{2,1,0:T(8,128)(2,1)S(1)} %pad_maximum_fusion.refs_0_), channel_id=1, source_target_pairs={{0,1},{1,0},{2,3},{3,2},{4,5},{5,4},{6,7},{7,6},{8,9},{9,8},{10,11... | collective-permute-start | bytes 393224 | tf_op jit(solution)/shard_map/ppermute | solution.py:227
  10.4 6.2 %collective-permute-start.5 = (bf16[2,128,256]{2,1,0:T(8,128)(2,1)S(1)}, bf16[2,128,256]{2,1,0:T(8,128)(2,1)S(1)}, u32[]{:S(2)}, u32[]{:S(2)}) collective-permute-start(bf16[2,128,256]{2,1,0:T(8,128)(2,1)S(1)} %collective-permute-done.1.refs_2_), channel_id=1, source_target_pairs={{0,2},{1,15},{2,4},{3,1},{4,6},{5,3},{6,8},{7,5},{8,10},{9,7},{10,... | collective-permute-start | bytes 393224 | tf_op jit(solution)/shard_map/ppermute | solution.py:223
  10.4 7.6 %collective-permute-start.3 = (bf16[2,128,256]{2,1,0:T(8,128)(2,1)S(1)}, bf16[2,128,256]{2,1,0:T(8,128)(2,1)S(1)}, u32[]{:S(2)}, u32[]{:S(2)}) collective-permute-start(bf16[2,128,256]{2,1,0:T(8,128)(2,1)S(1)} %collective-permute-done.refs_1_), channel_id=1, source_target_pairs={{0,2},{1,15},{2,4},{3,1},{4,6},{5,3},{6,8},{7,5},{8,10},{9,7},{10,... | collective-permute-start | bytes 393224 | tf_op jit(solution)/shard_map/ppermute | solution.py:223
  16.6 6.2 %collective-permute-start.9 = (bf16[2,128,256]{2,1,0:T(8,128)(2,1)S(1)}, bf16[2,128,256]{2,1,0:T(8,128)(2,1)S(1)}, u32[]{:S(2)}, u32[]{:S(2)}) collective-permute-start(bf16[2,128,256]{2,1,0:T(8,128)(2,1)S(1)} %collective-permute-done.5.refs_6_), channel_id=1, source_target_pairs={{0,2},{1,15},{2,4},{3,1},{4,6},{5,3},{6,8},{7,5},{8,10},{9,7},{10,... | collective-permute-start | bytes 393224 | tf_op jit(solution)/shard_map/ppermute | solution.py:223
  18.0 6.2 %collective-permute-start.7 = (bf16[2,128,256]{2,1,0:T(8,128)(2,1)S(1)}, bf16[2,128,256]{2,1,0:T(8,128)(2,1)S(1)}, u32[]{:S(2)}, u32[]{:S(2)}) collective-permute-start(bf16[2,128,256]{2,1,0:T(8,128)(2,1)S(1)} %collective-permute-done.3.refs_4_), channel_id=1, source_target_pairs={{0,2},{1,15},{2,4},{3,1},{4,6},{5,3},{6,8},{7,5},{8,10},{9,7},{10,... | collective-permute-start | bytes 393224 | tf_op jit(solution)/shard_map/ppermute | solution.py:223
  18.0 6.2 %collective-permute-start.2 = (bf16[2,128,256]{2,1,0:T(8,128)(2,1)S(1)}, bf16[2,128,256]{2,1,0:T(8,128)(2,1)S(1)}, u32[]{:S(2)}, u32[]{:S(2)}) collective-permute-start(bf16[2,128,256]{2,1,0:T(8,128)(2,1)S(1)} %collective-permute-done.1.refs_2_), channel_id=1, source_target_pairs={{0,1},{1,0},{2,3},{3,2},{4,5},{5,4},{6,7},{7,6},{8,9},{9,8},{10,11... | collective-permute-start | bytes 393224 | tf_op jit(solution)/shard_map/ppermute | solution.py:227
  18.5 6.2 %collective-permute-start.6 = (bf16[2,128,256]{2,1,0:T(8,128)(2,1)S(1)}, bf16[2,128,256]{2,1,0:T(8,128)(2,1)S(1)}, u32[]{:S(2)}, u32[]{:S(2)}) collective-permute-start(bf16[2,128,256]{2,1,0:T(8,128)(2,1)S(1)} %collective-permute-done.5.refs_6_), channel_id=1, source_target_pairs={{0,1},{1,0},{2,3},{3,2},{4,5},{5,4},{6,7},{7,6},{8,9},{9,8},{10,11... | collective-permute-start | bytes 393224 | tf_op jit(solution)/shard_map/ppermute | solution.py:227
  24.2 6.8 %collective-permute-start.4 = (bf16[2,128,256]{2,1,0:T(8,128)(2,1)S(1)}, bf16[2,128,256]{2,1,0:T(8,128)(2,1)S(1)}, u32[]{:S(2)}, u32[]{:S(2)}) collective-permute-start(bf16[2,128,256]{2,1,0:T(8,128)(2,1)S(1)} %collective-permute-done.3.refs_4_), channel_id=1, source_target_pairs={{0,1},{1,0},{2,3},{3,2},{4,5},{5,4},{6,7},{7,6},{8,9},{9,8},{10,11... | collective-permute-start | bytes 393224 | tf_op jit(solution)/shard_map/ppermute | solution.py:227
  24.2 6.8 %collective-permute-start.10 = (bf16[2,128,256]{2,1,0:T(8,128)(2,1)S(1)}, bf16[2,128,256]{2,1,0:T(8,128)(2,1)S(1)}, u32[]{:S(2)}, u32[]{:S(2)}) collective-permute-start(bf16[2,128,256]{2,1,0:T(8,128)(2,1)S(1)} %collective-permute-done.9.refs_10_), channel_id=1, source_target_pairs={{0,1},{1,0},{2,3},{3,2},{4,5},{5,4},{6,7},{7,6},{8,9},{9,8},{10,11... | collective-permute-start | bytes 393224 | tf_op jit(solution)/shard_map/ppermute | solution.py:227
  24.7 6.3 %collective-permute-start.8 = (bf16[2,128,256]{2,1,0:T(8,128)(2,1)S(1)}, bf16[2,128,256]{2,1,0:T(8,128)(2,1)S(1)}, u32[]{:S(2)}, u32[]{:S(2)}) collective-permute-start(bf16[2,128,256]{2,1,0:T(8,128)(2,1)S(1)} %collective-permute-done.7.refs_8_), channel_id=1, source_target_pairs={{0,1},{1,0},{2,3},{3,2},{4,5},{5,4},{6,7},{7,6},{8,9},{9,8},{10,11... | collective-permute-start | bytes 393224 | tf_op jit(solution)/shard_map/ppermute | solution.py:227
  45.7 15.7 %collective-permute-start.17 = (bf16[16,128,128]{2,1,0:T(8,128)(2,1)S(1)}, bf16[16,128,128]{2,1,0:T(8,128)(2,1)S(1)}, u32[]{:S(2)}, u32[]{:S(2)}) collective-permute-start(bf16[16,128,128]{2,1,0:T(8,128)(2,1)S(1)} %get-tuple-element.91), channel_id=1, source_target_pairs={{0,48},{16,0},{32,16},{48,32},{1,49},{17,1},{33,17},{49,33},{2,50}... | collective-permute-start | bytes 1572872 | tf_op jit(solution)/shard_map/ppermute | solution.py:250
  46.7 15.1 %collective-permute-start.19 = (bf16[16,128,128]{2,1,0:T(8,128)(2,1)S(1)}, bf16[16,128,128]{2,1,0:T(8,128)(2,1)S(1)}, u32[]{:S(2)}, u32[]{:S(2)}) collective-permute-start(bf16[16,128,128]{2,1,0:T(8,128)(2,1)S(1)} %get-tuple-element.82), channel_id=1, source_target_pairs={{0,16},{16,32},{32,48},{48,0},{1,17},{17,33},{33,49},{49,1},{2,18}... | collective-permute-start | bytes 1572872 | tf_op jit(solution)/shard_map/ppermute | solution.py:250
  49.1 23.6 %collective-permute-start.16 = (bf16[16,128,128]{2,1,0:T(8,128)(2,1)S(1)}, bf16[16,128,128]{2,1,0:T(8,128)(2,1)S(1)}, u32[]{:S(2)}, u32[]{:S(2)}) collective-permute-start(bf16[16,128,128]{2,1,0:T(8,128)(2,1)S(1)} %get-tuple-element.89), channel_id=1, source_target_pairs={{0,16},{16,32},{32,48},{48,0},{1,17},{17,33},{33,49},{49,1},{2,18}... | collective-permute-start | bytes 1572872 | tf_op jit(solution)/shard_map/ppermute | solution.py:250
  49.1 15.6 %collective-permute-start.27 = (bf16[16,128,128]{2,1,0:T(8,128)(2,1)S(1)}, bf16[16,128,128]{2,1,0:T(8,128)(2,1)S(1)}, u32[]{:S(2)}, u32[]{:S(2)}) collective-permute-start(bf16[16,128,128]{2,1,0:T(8,128)(2,1)S(1)} %get-tuple-element.97), channel_id=1, source_target_pairs={{0,192},{64,0},{128,64},{192,128},{1,193},{65,1},{129,65},{193,129... | collective-permute-start | bytes 1572872 | tf_op jit(solution)/shard_map/ppermute | solution.py:250
  52.1 14.3 %collective-permute-start.29 = (bf16[16,128,128]{2,1,0:T(8,128)(2,1)S(1)}, bf16[16,128,128]{2,1,0:T(8,128)(2,1)S(1)}, u32[]{:S(2)}, u32[]{:S(2)}) collective-permute-start(bf16[16,128,128]{2,1,0:T(8,128)(2,1)S(1)} %get-tuple-element.83), channel_id=1, source_target_pairs={{0,64},{64,128},{128,192},{192,0},{1,65},{65,129},{129,193},{193,1... | collective-permute-start | bytes 1572872 | tf_op jit(solution)/shard_map/ppermute | solution.py:250
  61.5 30.3 %collective-permute-start.15 = (bf16[8,2,128,256]{3,2,1,0:T(8,128)(2,1)S(1)}, bf16[8,2,128,256]{3,2,1,0:T(8,128)(2,1)S(1)}, u32[]{:S(2)}, u32[]{:S(2)}) collective-permute-start(bf16[8,2,128,256]{3,2,1,0:T(8,128)(2,1)S(1)} %get-tuple-element.87), channel_id=1, source_target_pairs={{0,1},{1,0},{2,3},{3,2},{4,5},{5,4},{6,7},{7,6},{8,9},{9,8},{10,11... | collective-permute-start | bytes 3145736 | tf_op jit(solution)/shard_map/ppermute | solution.py:227
  61.7 16.1 %collective-permute-start.21 = (bf16[16,128,128]{2,1,0:T(8,128)(2,1)S(1)}, bf16[16,128,128]{2,1,0:T(8,128)(2,1)S(1)}, u32[]{:S(2)}, u32[]{:S(2)}) collective-permute-start(bf16[16,128,128]{2,1,0:T(8,128)(2,1)S(1)} %get-tuple-element.93), channel_id=1, source_target_pairs={{0,48},{16,0},{32,16},{48,32},{1,49},{17,1},{33,17},{49,33},{2,50}... | collective-permute-start | bytes 1572872 | tf_op jit(solution)/shard_map/ppermute | solution.py:250
  64.7 23.8 %collective-permute-start.18 = (bf16[16,128,128]{2,1,0:T(8,128)(2,1)S(1)}, bf16[16,128,128]{2,1,0:T(8,128)(2,1)S(1)}, u32[]{:S(2)}, u32[]{:S(2)}) collective-permute-start(bf16[16,128,128]{2,1,0:T(8,128)(2,1)S(1)} %add_convert_fusion.8), channel_id=1, source_target_pairs={{0,48},{16,0},{32,16},{48,32},{1,49},{17,1},{33,17},{49,33},{2,50}... | collective-permute-start | bytes 1572872 | tf_op jit(solution)/shard_map/ppermute | solution.py:250
  66.5 32.5 %collective-permute-start.20 = (bf16[16,128,128]{2,1,0:T(8,128)(2,1)}, bf16[16,128,128]{2,1,0:T(8,128)(2,1)}, u32[]{:S(2)}, u32[]{:S(2)}) collective-permute-start(bf16[16,128,128]{2,1,0:T(8,128)(2,1)} %add_convert_fusion.6), channel_id=1, source_target_pairs={{0,16},{16,32},{32,48},{48,0},{1,17},{17,33},{33,49},{49,1},{2,18}... | collective-permute-start | bytes 1572872 | tf_op jit(solution)/shard_map/ppermute | solution.py:250
  72.7 28.4 %collective-permute-start.26 = (bf16[16,128,128]{2,1,0:T(8,128)(2,1)S(1)}, bf16[16,128,128]{2,1,0:T(8,128)(2,1)}, u32[]{:S(2)}, u32[]{:S(2)}) collective-permute-start(bf16[16,128,128]{2,1,0:T(8,128)(2,1)S(1)} %get-tuple-element.95), channel_id=1, source_target_pairs={{0,64},{64,128},{128,192},{192,0},{1,65},{65,129},{129,193},{193,1... | collective-permute-start | bytes 1572872 | tf_op jit(solution)/shard_map/ppermute | solution.py:250
  77.8 23.3 %collective-permute-start.31 = (bf16[16,128,128]{2,1,0:T(8,128)(2,1)S(1)}, bf16[16,128,128]{2,1,0:T(8,128)(2,1)}, u32[]{:S(2)}, u32[]{:S(2)}) collective-permute-start(bf16[16,128,128]{2,1,0:T(8,128)(2,1)S(1)} %get-tuple-element.99), channel_id=1, source_target_pairs={{0,192},{64,0},{128,64},{192,128},{1,193},{65,1},{129,65},{193,129... | collective-permute-start | bytes 1572872 | tf_op jit(solution)/shard_map/ppermute | solution.py:250
  88.6 14.7 %collective-permute-start.28 = (bf16[16,128,128]{2,1,0:T(8,128)(2,1)}, bf16[16,128,128]{2,1,0:T(8,128)(2,1)}, u32[]{:S(2)}, u32[]{:S(2)}) collective-permute-start(bf16[16,128,128]{2,1,0:T(8,128)(2,1)} %add_convert_fusion.4), channel_id=1, source_target_pairs={{0,192},{64,0},{128,64},{192,128},{1,193},{65,1},{129,65},{193,129... | collective-permute-start | bytes 1572872 | tf_op jit(solution)/shard_map/ppermute | solution.py:250
  91.8 16.3 %collective-permute-start.30 = (bf16[16,128,128]{2,1,0:T(8,128)(2,1)}, bf16[16,128,128]{2,1,0:T(8,128)(2,1)}, u32[]{:S(2)}, u32[]{:S(2)}) collective-permute-start(bf16[16,128,128]{2,1,0:T(8,128)(2,1)} %add_convert_fusion.2), channel_id=1, source_target_pairs={{0,64},{64,128},{128,192},{192,0},{1,65},{65,129},{129,193},{193,1... | collective-permute-start | bytes 1572872 | tf_op jit(solution)/shard_map/ppermute | solution.py:250
  93.2 40.1 %all-to-all-start = ((bf16[8,2,128,256]{3,2,1,0:T(8,128)(2,1)}), bf16[8,2,128,256]{3,2,1,0:T(8,128)(2,1)}, u32[]{:S(2)}, u32[]{:S(2)}) async-start(bf16[8,2,128,256]{3,2,1,0:T(8,128)(2,1)} %add_convert_fusion), calls=%async_computation | async-start | bytes 2097152 | tf_op jit(solution)/shard_map/all_to_all | solution.py:285
  101.0 9.3 %collective-permute-start.22 = (bf16[4,128,128]{2,1,0:T(8,128)(2,1)S(1)}, bf16[4,128,128]{2,1,0:T(8,128)(2,1)S(1)}, u32[]{:S(2)}, u32[]{:S(2)}) collective-permute-start(bf16[4,128,128]{2,1,0:T(8,128)(2,1)S(1)} %slice.173), channel_id=1, source_target_pairs={{0,64},{64,128},{128,192},{192,0},{1,65},{65,129},{129,193},{193,1... | collective-permute-start | bytes 393224 | tf_op jit(solution)/shard_map/ppermute | solution.py:250
  110.4 8.5 %collective-permute-start.24 = (bf16[4,128,128]{2,1,0:T(8,128)(2,1)S(1)}, bf16[4,128,128]{2,1,0:T(8,128)(2,1)S(1)}, u32[]{:S(2)}, u32[]{:S(2)}) collective-permute-start(bf16[4,128,128]{2,1,0:T(8,128)(2,1)S(1)} %get-tuple-element.111), channel_id=1, source_target_pairs={{0,192},{64,0},{128,64},{192,128},{1,193},{65,1},{129,65},{193,129... | collective-permute-start | bytes 393224 | tf_op jit(solution)/shard_map/ppermute | solution.py:250
  110.5 12.3 %collective-permute-start.23 = (bf16[8,128,128]{2,1,0:T(8,128)(2,1)S(1)}, bf16[8,128,128]{2,1,0:T(8,128)(2,1)S(1)}, u32[]{:S(2)}, u32[]{:S(2)}) collective-permute-start(bf16[8,128,128]{2,1,0:T(8,128)(2,1)S(1)} %get-tuple-element.110), channel_id=1, source_target_pairs={{0,64},{64,128},{128,192},{192,0},{1,65},{65,129},{129,193},{193,1... | collective-permute-start | bytes 786440 | tf_op jit(solution)/shard_map/ppermute | solution.py:250
  115.6 6.9 %collective-permute-start.34 = (bf16[4,128,128]{2,1,0:T(8,128)(2,1)S(1)}, bf16[4,128,128]{2,1,0:T(8,128)(2,1)S(1)}, u32[]{:S(2)}, u32[]{:S(2)}) collective-permute-start(bf16[4,128,128]{2,1,0:T(8,128)(2,1)S(1)} %get-tuple-element.109), channel_id=1, source_target_pairs={{0,48},{16,0},{32,16},{48,32},{1,49},{17,1},{33,17},{49,33},{2,50}... | collective-permute-start | bytes 393224 | tf_op jit(solution)/shard_map/ppermute | solution.py:250
  116.5 6.4 %collective-permute-start.33 = (bf16[8,128,128]{2,1,0:T(8,128)(2,1)S(1)}, bf16[8,128,128]{2,1,0:T(8,128)(2,1)S(1)}, u32[]{:S(2)}, u32[]{:S(2)}) collective-permute-start(bf16[8,128,128]{2,1,0:T(8,128)(2,1)S(1)} %get-tuple-element.108), channel_id=1, source_target_pairs={{0,16},{16,32},{32,48},{48,0},{1,17},{17,33},{33,49},{49,1},{2,18}... | collective-permute-start | bytes 786440 | tf_op jit(solution)/shard_map/ppermute | solution.py:250
  119.0 6.4 %collective-permute-start.25 = (bf16[8,128,128]{2,1,0:T(8,128)(2,1)S(1)}, bf16[8,128,128]{2,1,0:T(8,128)(2,1)S(1)}, u32[]{:S(2)}, u32[]{:S(2)}) collective-permute-start(bf16[8,128,128]{2,1,0:T(8,128)(2,1)S(1)} %fusion.2), channel_id=1, source_target_pairs={{0,192},{64,0},{128,64},{192,128},{1,193},{65,1},{129,65},{193,129... | collective-permute-start | bytes 786440 | tf_op jit(solution)/shard_map/ppermute | solution.py:250
  122.6 7.7 %collective-permute-start.35 = (bf16[8,128,128]{2,1,0:T(8,128)(2,1)S(1)}, bf16[8,128,128]{2,1,0:T(8,128)(2,1)S(1)}, u32[]{:S(2)}, u32[]{:S(2)}) collective-permute-start(bf16[8,128,128]{2,1,0:T(8,128)(2,1)S(1)} %fusion), channel_id=1, source_target_pairs={{0,48},{16,0},{32,16},{48,32},{1,49},{17,1},{33,17},{49,33},{2,50}... | collective-permute-start | bytes 786440 | tf_op jit(solution)/shard_map/ppermute | solution.py:250
  (11 other events, 76.8 us)

commit v2 on v0

--- a/solution.py
+++ b/solution.py
@@ -23,8 +23,8 @@
     return pl.BlockSpec(shape, lambda *i: (0,) * len(shape))
 
 
-def params(**kw):
-    return pltpu.CompilerParams(vmem_limit_bytes=32 << 20, **kw)
+def params(mib):
+    return pltpu.CompilerParams(vmem_limit_bytes=mib << 20)
 
 
 def sspec():
@@ -116,39 +116,51 @@
         out_specs=[whole(COLS, SIDE, SIDE)] * 2 + [whole(ROWS, SIDE, SIDE)] * 4,
         out_shape=[tok, tok, hid, hid, hid, hid],
         scratch_shapes=[VM((ROWS, SIDE, SIDE), F32)] * 2 + [pltpu.SemaphoreType.DMA],
-        compiler_params=params(),
+        compiler_params=params(48),
         cost_estimate=pl.CostEstimate(flops=1 << 30, bytes_accessed=12 << 20, transcendentals=1 << 18),
         name="forward",
     )(rows, cols, count, *shards, up_tiles, down_tiles)
 
 
 def ring_slot(j):
-    away = (2, 1, 3, 0)
-    y = lax.rem(lax.axis_index("y") + away[j // 32], 4)
-    x = lax.rem(lax.axis_index("x") + away[j // 8 % 4], 4)
-    return (y * 4 + x) * 8 + j % 8
-
-
-def weight_kernel(sizes, order, rows, cols, x_ref, t_ref, *outs):
+    first = ((2, 0), (2, 16), (1, 16), (3, 0), (1, 0), (3, 16), (0, 0), (0, 16))
+    second = ((2, 0), (1, 4), (2, 4), (3, 0), (1, 0), (3, 4), (0, 0), (0, 4))
+    away1, base = first[j // 16]
+    place = base + j % 16
+    away2, near = second[place // 4]
+    c = lax.axis_index("c")
+    away_x = away1 + c * (away2 - away1)
+    away_y = away2 + c * (away1 - away2)
+    y = lax.rem(lax.axis_index("y") + away_y, 4)
+    x = lax.rem(lax.axis_index("x") + away_x, 4)
+    return (y * 4 + x) * 8 + near + place % 4
+
+
+SIZES = (16, 16, 16, 16, 16, 16, 32)
+
+
+def weight_kernel(rows, cols, x_ref, dt_ref, dy_ref, ht_ref, *outs):
     at = 0
-    for out, n in zip(outs, sizes):
+    for out, n in zip(outs, SIZES):
         for s in range(n):
-            slot = order(at + s)
-            out[s] = nn(t_ref[rows[slot]], x_ref[cols[slot]]).astype(BF)
+            slot = ring_slot(at + s)
+            row, col = rows[slot], cols[slot]
+            out[0, s] = nn(dt_ref[row], x_ref[col]).astype(BF)
+            out[1, s] = nn(ht_ref[row], dy_ref[col]).astype(BF)
         at += n
 
 
-def weight_parts(rows, cols, x, t, sizes, order):
+def weight_parts(rows, cols, x, dt, dy, ht):
     return pl.pallas_call(
-        functools.partial(weight_kernel, sizes, order),
+        weight_kernel,
         grid=(1,),
-        in_specs=[sspec()] * 2 + [whole(COLS, SIDE, SIDE), whole(ROWS, SIDE, SIDE)],
-        out_specs=[whole(n, SIDE, SIDE) for n in sizes],
-        out_shape=[jax.ShapeDtypeStruct((n, SIDE, SIDE), BF) for n in sizes],
-        compiler_params=params(),
-        cost_estimate=pl.CostEstimate(flops=1 << 29, bytes_accessed=6 << 20, transcendentals=0),
+        in_specs=[sspec()] * 2 + [whole(COLS, SIDE, SIDE), whole(ROWS, SIDE, SIDE)] * 2,
+        out_specs=[whole(2, n, SIDE, SIDE) for n in SIZES],
+        out_shape=[jax.ShapeDtypeStruct((2, n, SIDE, SIDE), BF) for n in SIZES],
+        compiler_params=params(32),
+        cost_estimate=pl.CostEstimate(flops=1 << 30, bytes_accessed=12 << 20, transcendentals=0),
         name="weight_parts",
-    )(rows, cols, x, t)
+    )(rows, cols, x, dt, dy, ht)
 
 
 def token_kernel(rows, cols, count_ref, h_ref, d_ref, up_ref, down_ref, send_ref, keep_ref, mix_acc, in_acc):
@@ -159,6 +171,7 @@
     def _():
         mix_acc[...] = jnp.zeros_like(mix_acc)
         in_acc[...] = jnp.zeros_like(in_acc)
+
 
     for s in range(GROUP):
         slot = step * GROUP + s
@@ -196,7 +209,7 @@
         out_specs=[whole(8, 2, SIDE, 2 * SIDE)] * 2,
         out_shape=[part] * 2,
         scratch_shapes=[VM((COLS, SIDE, SIDE), F32)] * 2,
-        compiler_params=params(),
+        compiler_params=params(48),
         cost_estimate=pl.CostEstimate(flops=1 << 30, bytes_accessed=11 << 20, transcendentals=0),
         name="token_parts",
     )(rows, cols, count, h, d, up_tiles, down_tiles)
@@ -237,36 +250,60 @@
     return shards
 
 
-def scatter_ring(axis, opp_a, opp_b, right, left):
-    n = opp_a.shape[0]
-    up, down = ring(4, 1), ring(4, -1)
-    from_left = lax.ppermute(opp_a, axis, up)
-    from_right = lax.ppermute(opp_b, axis, down)
-    right = lax.ppermute(right.at[:n].add(from_left), axis, up)
-    left = lax.ppermute(left.at[n:].add(from_right), axis, down)
-    return right, left
+def hop(t, stage, by):
+    pairs = []
+    for y in range(4):
+        for x in range(4):
+            for c in range(2):
+                along_x = (stage + c) % 2 == 0
+                to_y = y if along_x else (y + by) % 4
+                to_x = (x + by) % 4 if along_x else x
+                pairs.append(((y * 4 + x) * 2 + c, (to_y * 4 + to_x) * 2 + c))
+    return lax.ppermute(t, ("y", "x", "c"), pairs)
+
+
+def send_far(parts):
+    far_a, far_b, next_b, before_a = parts[:4]
+    return hop(far_a, 0, 1), hop(far_b, 0, -1), hop(next_b, 0, 1), hop(before_a, 0, -1)
+
+
+def two_stages(far, next_a, before_b, own):
+    from_left, from_right, left_b, right_a = far
+    left_a = hop(add(next_a, from_left).astype(BF), 0, 1)
+    right_b = hop(add(before_b, from_right).astype(BF), 0, -1)
+
+    def total(k, n):
+        left, right = (left_a, right_a) if k < 16 else (left_b, right_b)
+        at = slice(k % 16, k % 16 + n)
+        return add(own[:, k : k + n], left[:, at], right[:, at])
+
+    from_left = hop(total(0, 8).astype(BF), 1, 1)
+    from_right = hop(total(8, 8).astype(BF), 1, -1)
+    end_a = hop(add(total(16, 4), from_left[:, :4]).astype(BF), 1, 1)
+    end_b = hop(add(total(20, 4), from_right[:, :4]).astype(BF), 1, -1)
+    half_a = add(total(24, 4), end_a, from_right[:, 4:])
+    half_b = add(total(28, 4), from_left[:, 4:], end_b)
+    return jnp.concatenate([half_a, half_b], axis=1)
 
 
 def body(tokens, grad_out, up_tiles, down_tiles, tile_rows, tile_cols, tile_count):
     rows, cols = tile_rows[0], tile_cols[0]
     shards = gather_over_tile(jnp.stack([tokens, grad_out]))
     x_all, dy_all, h, ht, d, dt = forward(rows, cols, tile_count, shards, up_tiles, down_tiles)
-    opp_a, opp_b, right, left, mine = weight_parts(rows, cols, dy_all, ht, (16, 16, 32, 32, 32), ring_slot)
-    (up_part,) = weight_parts(rows, cols, x_all, dt, (SLOTS,), lambda j: j)
-    up_total = lax.psum_scatter(up_part, ("y", "x"), scatter_dimension=0, tiled=True)
-    part = add(mine, *scatter_ring("y", opp_a, opp_b, right, left)).astype(BF)
-    got = scatter_ring("x", part[:4], part[4:8], part[8:16], part[16:24])
-    down_total = add(part[24:], *got)
-
+    parts = weight_parts(rows, cols, x_all, dt, dy_all, ht)
+    far = send_far(parts)
+    h, d, _ = lax.optimization_barrier((h, d, parts[0]))
     send, keep = token_parts(rows, cols, tile_count, h, d, up_tiles, down_tiles)
     pieces = add(keep, swap(send)).astype(BF)
+    pieces, next_a, before_b = lax.optimization_barrier((pieces, parts[4], parts[5]))
+    weights = two_stages(far, next_a, before_b, parts[6]) * (1.0 / 16)
     terms = lax.all_to_all(pieces, "z", 0, 0, tiled=True)
     total = jnp.sum(terms.astype(F32), axis=0).astype(BF)
 
     slot = lax.axis_index(("y", "x")) * 8 + jnp.arange(8, dtype=jnp.int32)
     live = (slot < tile_count[0])[:, None, None]
-    grad_up = jnp.where(live, jnp.swapaxes(up_total, 1, 2).astype(F32) * (1.0 / 16), 0.0)
-    grad_down = jnp.where(live, down_total * (1.0 / 16), 0.0)
+    grad_up = jnp.where(live, jnp.swapaxes(weights[0], 1, 2), 0.0)
+    grad_down = jnp.where(live, weights[1], 0.0)
     return total[0], total[1], grad_up[None], grad_down[None]
 
 

time: 164 us -> 129 us (0.79)
  waiting for transfers between devices: 79.2 us -> 59.8 us
  local copies, waits for them, and re-layouts: 18.9 us -> 3.76 us
  between operations: 14.9 us -> 1.4 us
  other arithmetic: 8.38 us -> 15.1 us
  Pallas kernels: 18 us -> 22.8 us
    ppermute x8 -> x10, waiting for transfers between devices: 56.3 us -> 37 us  [hop(): return lax.ppermute(t, ('y', 'x', 'c'), pairs)]
    unnamed x31 -> x9, local copies, waits for them, and re-layouts: 18.2 us -> 3.1 us
    convert_element_type x1 -> x4, other arithmetic: 2.17 us -> 6.8 us  [the longest x1 2.79 us: two_stages(): from_left = hop(total(0, 8).astype(BF), 1, 1)]
    add x0 -> x2, other arithmetic: none -> 3.61 us  [add(): total = total + p.astype(F32)]
    pallas_call x1, Pallas kernels: 6.83 us -> 9.31 us  [token_parts(): pl.pallas_call(token_kernel, grid=(STEPS,), in_specs=[sspec()] * 3 + [who...]
    pallas_call x1, Pallas kernels: 7.59 us -> 9.77 us  [forward(): pl.pallas_call(forward_kernel, grid=(STEPS,), in_specs=[sspec()] * 3 + [p...]
    broadcast_in_dim x1, other arithmetic: 1.94 us -> 0.1 us  [body(): return (total[0], total[1], grad_up[None], grad_down[None])]
    ppermute x8 -> x10, starting transfers between devices: 11.6 us -> 11.5 us  [hop(): return lax.ppermute(t, ('y', 'x', 'c'), pairs)]
  transfers between devices with their start and end apart: 26 -> 27, of which waited for: 15 -> 15; matrix products, arithmetic and copies ran while one was open for 4% -> 10% of each run, Pallas kernels for 5% -> 0%
where the time goes in v2:
time: 129 us; the launch traced here: 127 us
  waiting for transfers between devices  59.8 us (46%)
  starting transfers between devices  24.2 us (19%)
  Pallas kernels  22.8 us (18%)
  other arithmetic  15.1 us (12%)
  local copies, waits for them, and re-layouts  3.76 us (3%)
  between operations  1.4 us (1%)
    ppermute x10, waiting for transfers between devices, hop(): return lax.ppermute(t, ('y', 'x', 'c'), pairs)  37 us
    ppermute x7, waiting for transfers between devices, step_both(): return lax.ppermute(x, ('z', 'c'), pairs)  22.2 us
    ppermute x10, starting transfers between devices, hop(): return lax.ppermute(t, ('y', 'x', 'c'), pairs)  11.5 us
    pallas_call x1, Pallas kernels, forward(): pl.pallas_call(forward_kernel, grid=(STEPS,), in_specs=[sspec()] * 3 + [p...  9.77 us
    pallas_call x1, Pallas kernels, token_parts(): pl.pallas_call(token_kernel, grid=(STEPS,), in_specs=[sspec()] * 3 + [who...  9.31 us
    all_to_all x1, starting transfers between devices, body(): terms = lax.all_to_all(pieces, 'z', 0, 0, tiled=True)  5.85 us
    ppermute x9, starting transfers between devices, swap(): return lax.ppermute(x, 'c', [(0, 1), (1, 0)])  4.84 us
    pallas_call x1, Pallas kernels, weight_parts(): pl.pallas_call(weight_kernel, grid=(1,), in_specs=[sspec()] * 2 + [whole(...  3.73 us
  transfers between devices with their start and end apart: 27, of which 15 were waited for; matrix products, arithmetic and copies ran while one was open for 10% of the time, Pallas kernels for 0%

profile of v2, /device:TPU:6, one launch (start us, length us, event | category | flops | bytes accessed | tf_op | source)
XLA Modules:
  0.0 127.1 jit_solution(4866392960093110119)
XLA Ops:
  1.5 2.0 %collective-permute-start.1 = (bf16[2,128,256]{2,1,0:T(8,128)(2,1)S(1)}, bf16[2,128,256]{2,1,0:T(8,128)(2,1)S(1)}, u32[]{:S(2)}, u32[]{:S(2)}) collective-permute-start(bf16[2,128,256]{2,1,0:T(8,128)(2,1)S(1)} %pad_maximum_fusion.refs_0_), channel_id=1, source_target_pairs={{0,2},{1,15},{2,4},{3,1},{4,6},{5,3},{6,8},{7,5},{8,10},{9,7},{10,... | collective-permute-start | bytes 393224 | tf_op jit(solution)/shard_map/ppermute | solution.py:227
  3.5 3.5 %collective-permute-start = (bf16[2,128,256]{2,1,0:T(8,128)(2,1)S(1)}, bf16[2,128,256]{2,1,0:T(8,128)(2,1)S(1)}, u32[]{:S(2)}, u32[]{:S(2)}) collective-permute-start(bf16[2,128,256]{2,1,0:T(8,128)(2,1)S(1)} %pad_maximum_fusion.refs_0_), channel_id=1, source_target_pairs={{0,1},{1,0},{2,3},{3,2},{4,5},{5,4},{6,7},{7,6},{8,9},{9,8},{10,11... | collective-permute-start | bytes 393224 | tf_op jit(solution)/shard_map/ppermute | solution.py:231
  7.0 3.4 %collective-permute-done.1.refs_2_ = bf16[2,128,256]{2,1,0:T(8,128)(2,1)S(1)} collective-permute-done((bf16[2,128,256]{2,1,0:T(8,128)(2,1)S(1)}, bf16[2,128,256]{2,1,0:T(8,128)(2,1)S(1)}, u32[]{:S(2)}, u32[]{:S(2)}) %collective-permute-start.1) | collective-permute-done | bytes 131104 | tf_op jit(solution)/shard_map/ppermute | solution.py:227
  10.4 6.2 %collective-permute-done.5.refs_6_ = bf16[2,128,256]{2,1,0:T(8,128)(2,1)S(1)} collective-permute-done((bf16[2,128,256]{2,1,0:T(8,128)(2,1)S(1)}, bf16[2,128,256]{2,1,0:T(8,128)(2,1)S(1)}, u32[]{:S(2)}, u32[]{:S(2)}) %collective-permute-start.5) | collective-permute-done | bytes 131104 | tf_op jit(solution)/shard_map/ppermute | solution.py:227
  16.6 1.4 %collective-permute-done.3.refs_4_ = bf16[2,128,256]{2,1,0:T(8,128)(2,1)S(1)} collective-permute-done((bf16[2,128,256]{2,1,0:T(8,128)(2,1)S(1)}, bf16[2,128,256]{2,1,0:T(8,128)(2,1)S(1)}, u32[]{:S(2)}, u32[]{:S(2)}) %collective-permute-start.3) | collective-permute-done | bytes 131104 | tf_op jit(solution)/shard_map/ppermute | solution.py:227
  18.5 4.3 %collective-permute-done.9.refs_10_ = bf16[2,128,256]{2,1,0:T(8,128)(2,1)S(1)} collective-permute-done((bf16[2,128,256]{2,1,0:T(8,128)(2,1)S(1)}, bf16[2,128,256]{2,1,0:T(8,128)(2,1)S(1)}, u32[]{:S(2)}, u32[]{:S(2)}) %collective-permute-start.9) | collective-permute-done | bytes 131104 | tf_op jit(solution)/shard_map/ppermute | solution.py:227
  22.8 1.4 %collective-permute-done.7.refs_8_ = bf16[2,128,256]{2,1,0:T(8,128)(2,1)S(1)} collective-permute-done((bf16[2,128,256]{2,1,0:T(8,128)(2,1)S(1)}, bf16[2,128,256]{2,1,0:T(8,128)(2,1)S(1)}, u32[]{:S(2)}, u32[]{:S(2)}) %collective-permute-start.7) | collective-permute-done | bytes 131104 | tf_op jit(solution)/shard_map/ppermute | solution.py:227
  24.8 4.2 %collective-permute-done.13.refs_14_ = bf16[2,128,256]{2,1,0:T(8,128)(2,1)S(1)} collective-permute-done((bf16[2,128,256]{2,1,0:T(8,128)(2,1)S(1)}, bf16[2,128,256]{2,1,0:T(8,128)(2,1)S(1)}, u32[]{:S(2)}, u32[]{:S(2)}) %collective-permute-start.13) | collective-permute-done | bytes 131104 | tf_op jit(solution)/shard_map/ppermute | solution.py:227
  28.9 1.4 %collective-permute-done.11.refs_12_ = bf16[2,128,256]{2,1,0:T(8,128)(2,1)S(1)} collective-permute-done((bf16[2,128,256]{2,1,0:T(8,128)(2,1)S(1)}, bf16[2,128,256]{2,1,0:T(8,128)(2,1)S(1)}, u32[]{:S(2)}, u32[]{:S(2)}) %collective-permute-start.11) | collective-permute-done | bytes 131104 | tf_op jit(solution)/shard_map/ppermute | solution.py:227
  33.0 9.8 %forward.1 = (bf16[32,128,128]{2,1,0:T(8,128)(2,1)S(1)}, bf16[32,128,128]{2,1,0:T(8,128)(2,1)S(1)}, bf16[8,128,128]{2,1,0:T(8,128)(2,1)S(1)}, bf16[8,128,128]{2,...) custom-call(s32[128]{0:T(128)S(1)} %bitcast.20, s32[128]{0:T(128)S(1)} %bitcast.23, ...), custom_call_target="tpu_custom_call" | custom-call | flops 1073741824 | bytes 12582912 | tf_op jit(solution)/shard_map/forward/pallas_call | solution.py:112
  42.8 3.7 %weight_parts.1 = (bf16[2,16,128,128]{3,2,1,0:T(8,128)(2,1)S(1)}, bf16[2,16,128,128]{3,2,1,0:T(8,128)(2,1)S(1)}, bf16[2,16,128,128]{3,2,1,0:T(8,128)(2,1)S(1)}, ...) custom-call(s32[128]{0:T(128)S(1)} %bitcast.21, ...), custom_call_target="tpu_custom_call" | custom-call | flops 1073741824 | bytes 12582912 | tf_op jit(solution)/shard_map/weight_parts/pallas_call | solution.py:154
  46.5 9.3 %token_parts.1 = (bf16[8,2,128,256]{3,2,1,0:T(8,128)(2,1)S(1)}, bf16[8,2,128,256]{3,2,1,0:T(8,128)(2,1)S(1)}) custom-call(s32[128]{0:T(128)S(1)} %bitcast.22, s32[128]{0:T(128)S(1)} %bitcast.25, s32[1]{0:T(128)} %copy.12.count_ref, bf16[8,128,128]{2,1,0:T(8,128)(2,1)S(1)} %get-tuple-element.31.h_ref, bf16[8,128,128]{2,1,0:T(8,128)(2,1)S(1)} %get-tuple-element.32.d_ref, ...), custom_call_target="tpu_custom_call" | custom-call | flops 1073741824 | bytes 11534336 | tf_op jit(solution)/shard_map/token_parts/pallas_call | solution.py:205
  56.5 1.5 %collective-permute-start.17 = (bf16[2,16,128,128]{3,2,1,0:T(8,128)(2,1)S(1)}, bf16[2,16,128,128]{3,2,1,0:T(8,128)(2,1)S(1)}, u32[]{:S(2)}, u32[]{:S(2)}) collective-permute-start(bf16[2,16,128,128]{3,2,1,0:T(8,128)(2,1)S(1)} %get-tuple-element.41), channel_id=1, source_target_pairs={{0,48},{1,193},{16,0},{17,209},{32,16},{33,225},{48,32},{49,241},{... | collective-permute-start | bytes 3145736 | tf_op jit(solution)/shard_map/ppermute | solution.py:262
  58.9 1.3 %add_convert_fusion.2 = bf16[8,2,128,256]{3,2,1,0:T(8,128)(2,1)} fusion(bf16[8,2,128,256]{3,2,1,0:T(8,128)(2,1)S(1)} %collective-permute-done.15, bf16[8,2,128,256]{3,2,1,0:T(8,128)(2,1)S(1)} %get-tuple-element.33), kind=kLoop, calls=%fused_computation.2 | loop fusion | flops 2097152 | bytes 3145728 | tf_op jit(solution)/shard_map/convert_element_type | solution.py:297
  60.2 10.6 %collective-permute-done.19 = bf16[2,16,128,128]{3,2,1,0:T(8,128)(2,1)S(1)} collective-permute-done((bf16[2,16,128,128]{3,2,1,0:T(8,128)(2,1)S(1)}, bf16[2,16,128,128]{3,2,1,0:T(8,128)(2,1)S(1)}, u32[]{:S(2)}, u32[]{:S(2)}) %collective-permute-start.19) | collective-permute-done | bytes 1048608 | tf_op jit(solution)/shard_map/ppermute | solution.py:262
  70.9 1.4 %add_convert_fusion = bf16[2,16,128,128]{3,2,1,0:T(8,128)(2,1)} fusion(bf16[2,16,128,128]{3,2,1,0:T(8,128)(2,1)S(1)} %collective-permute-done.19, bf16[2,16,128,128]{3,2,1,0:T(8,128)(2,1)S(1)} %get-tuple-element.42), kind=kLoop, calls=%fused_computation | loop fusion | flops 2097152 | bytes 3145728 | tf_op jit(solution)/shard_map/convert_element_type | solution.py:272
  72.3 1.7 %collective-permute-start.20 = (bf16[2,16,128,128]{3,2,1,0:T(8,128)(2,1)}, bf16[2,16,128,128]{3,2,1,0:T(8,128)(2,1)}, u32[]{:S(2)}, u32[]{:S(2)}) collective-permute-start(bf16[2,16,128,128]{3,2,1,0:T(8,128)(2,1)} %add_convert_fusion), channel_id=1, source_target_pairs={{0,16},{1,65},{16,32},{17,81},{32,48},{33,97},{48,0},{49,113},{64,... | collective-permute-start | bytes 3145736 | tf_op jit(solution)/shard_map/ppermute | solution.py:262
  74.2 1.4 %add_convert_fusion.1 = bf16[2,16,128,128]{3,2,1,0:T(8,128)(2,1)} fusion(bf16[2,16,128,128]{3,2,1,0:T(8,128)(2,1)S(1)} %collective-permute-done.17, bf16[2,16,128,128]{3,2,1,0:T(8,128)(2,1)S(1)} %get-tuple-element.40), kind=kLoop, calls=%fused_computation.1 | loop fusion | flops 2097152 | bytes 3145728 | tf_op jit(solution)/shard_map/convert_element_type | solution.py:273
  75.7 1.7 %collective-permute-start.18 = (bf16[2,16,128,128]{3,2,1,0:T(8,128)(2,1)}, bf16[2,16,128,128]{3,2,1,0:T(8,128)(2,1)}, u32[]{:S(2)}, u32[]{:S(2)}) collective-permute-start(bf16[2,16,128,128]{3,2,1,0:T(8,128)(2,1)} %add_convert_fusion.1), channel_id=1, source_target_pairs={{0,48},{1,193},{16,0},{17,209},{32,16},{33,225},{48,32},{49,241},{... | collective-permute-start | bytes 3145736 | tf_op jit(solution)/shard_map/ppermute | solution.py:262
  77.4 5.9 %all-to-all-start = ((bf16[8,2,128,256]{3,2,1,0:T(8,128)(2,1)}), bf16[8,2,128,256]{3,2,1,0:T(8,128)(2,1)}, u32[]{:S(2)}, u32[]{:S(2)}) async-start(bf16[8,2,128,256]{3,2,1,0:T(8,128)(2,1)} %add_convert_fusion.2), calls=%async_computation | async-start | bytes 2097152 | tf_op jit(solution)/shard_map/all_to_all | solution.py:300
  83.9 3.5 %collective-permute-done.20 = bf16[2,16,128,128]{3,2,1,0:T(8,128)(2,1)} collective-permute-done((bf16[2,16,128,128]{3,2,1,0:T(8,128)(2,1)}, bf16[2,16,128,128]{3,2,1,0:T(8,128)(2,1)}, u32[]{:S(2)}, u32[]{:S(2)}) %collective-permute-start.20) | collective-permute-done | bytes 1048608 | tf_op jit(solution)/shard_map/ppermute | solution.py:262
  87.4 2.8 %add_convert_fusion.4 = (bf16[2,8,128,128]{3,2,1,0:T(8,128)(2,1)S(1)}, bf16[2,8,128,128]{3,2,1,0:T(8,128)(2,1)}) fusion(bf16[2,16,128,128]{3,2,1,0:T(8,128)(2,1)} %collective-permute-done.21, bf16[2,16,128,128]{3,2,1,0:T(8,128)(2,1)} %collective-permute-done.20, bf16[2,32,128,128]{3,2,1,0:T(8,128)(2,1)S(1)} %get-tuple-element.38), kind=kLoop, calls=%fused_computation.5 | loop fusion | flops 3145728 | bytes 4194304 | tf_op jit(solution)/shard_map/convert_element_type | solution.py:280
  90.2 1.6 %collective-permute-start.22 = (bf16[2,8,128,128]{3,2,1,0:T(8,128)(2,1)S(1)}, bf16[2,8,128,128]{3,2,1,0:T(8,128)(2,1)S(1)}, u32[]{:S(2)}, u32[]{:S(2)}) collective-permute-start(bf16[2,8,128,128]{3,2,1,0:T(8,128)(2,1)S(1)} %get-tuple-element.50), channel_id=1, source_target_pairs={{0,64},{1,17},{16,80},{17,33},{32,96},{33,49},{48,112},{49,1},{64,... | collective-permute-start | bytes 1572872 | tf_op jit(solution)/shard_map/ppermute | solution.py:262
  91.8 1.6 %collective-permute-start.24 = (bf16[2,8,128,128]{3,2,1,0:T(8,128)(2,1)}, bf16[2,8,128,128]{3,2,1,0:T(8,128)(2,1)}, u32[]{:S(2)}, u32[]{:S(2)}) collective-permute-start(bf16[2,8,128,128]{3,2,1,0:T(8,128)(2,1)} %get-tuple-element.51), channel_id=1, source_target_pairs={{0,192},{1,49},{16,208},{17,1},{32,224},{33,17},{48,240},{49,33},{... | collective-permute-start | bytes 1572872 | tf_op jit(solution)/shard_map/ppermute | solution.py:262
  93.4 9.9 %collective-permute-done.16 = bf16[2,16,128,128]{3,2,1,0:T(8,128)(2,1)} collective-permute-done((bf16[2,16,128,128]{3,2,1,0:T(8,128)(2,1)S(1)}, bf16[2,16,128,128]{3,2,1,0:T(8,128)(2,1)}, u32[]{:S(2)}, u32[]{:S(2)}) %collective-permute-start.16) | collective-permute-done | bytes 1048608 | tf_op jit(solution)/shard_map/ppermute | solution.py:262
  103.3 1.8 %collective-permute-done.22 = bf16[2,8,128,128]{3,2,1,0:T(8,128)(2,1)S(1)} collective-permute-done((bf16[2,8,128,128]{3,2,1,0:T(8,128)(2,1)S(1)}, bf16[2,8,128,128]{3,2,1,0:T(8,128)(2,1)S(1)}, u32[]{:S(2)}, u32[]{:S(2)}) %collective-permute-start.22) | collective-permute-done | bytes 524320 | tf_op jit(solution)/shard_map/ppermute | solution.py:262
  105.9 1.2 add_convert_fusion.6
  107.9 6.9 %collective-permute-done.23 = bf16[2,4,128,128]{3,2,1,0:T(8,128)(2,1)S(1)} collective-permute-done((bf16[2,4,128,128]{3,2,1,0:T(8,128)(2,1)S(1)}, bf16[2,4,128,128]{3,2,1,0:T(8,128)(2,1)S(1)}, u32[]{:S(2)}, u32[]{:S(2)}) %collective-permute-start.23) | collective-permute-done | bytes 262176 | tf_op jit(solution)/shard_map/ppermute | solution.py:262
  114.8 2.4 %convert_add_fusion.1 = (f32[2,4,128,128]{3,2,1,0:T(8,128)S(1)}, bf16[2,4,128,128]{3,2,1,0:T(8,128)(2,1)}) fusion(bf16[2,4,128,128]{3,2,1,0:T(8,128)(2,1)S(1)} %collective-permute-done.23, bf16[2,8,128,128]{3,2,1,0:T(8,128)(2,1)} %collective-permute-done.24, bf16[2,16,128,128]{3,2,1,0:T(8,128)(2,1)} %collective-permute-done.18, ...), kind=kLoop, calls=%fused_computation.12 | loop fusion | flops 2228224 | bytes 3145728 | tf_op jit(solution)/shard_map/add | solution.py:237
  118.1 1.4 %reduce_sum.12 = bf16[2,128,256]{2,1,0:T(8,128)(2,1)S(1)} reduce(bf16[8,2,128,256]{3,2,1,0:T(8,128)(2,1)} %all-to-all-done, bf16[]{:T(256)} %constant.5.clone.1), dimensions={0}, to_apply=%region_0.0 | reduce | flops 458752 | bytes 1179650 | tf_op jit(solution)/shard_map/reduce_sum | solution.py:301
  120.2 3.6 %collective-permute-done.25 = bf16[2,4,128,128]{3,2,1,0:T(8,128)(2,1)S(1)} collective-permute-done((bf16[2,4,128,128]{3,2,1,0:T(8,128)(2,1)}, bf16[2,4,128,128]{3,2,1,0:T(8,128)(2,1)S(1)}, u32[]{:S(2)}, u32[]{:S(2)}) %collective-permute-start.25) | collective-permute-done | bytes 262176 | tf_op jit(solution)/shard_map/ppermute | solution.py:262
  123.8 1.2 convert_add_fusion
  (48 shorter events, 11.7 us)
Async XLA Ops:
  1.5 8.9 %collective-permute-start.1 = (bf16[2,128,256]{2,1,0:T(8,128)(2,1)S(1)}, bf16[2,128,256]{2,1,0:T(8,128)(2,1)S(1)}, u32[]{:S(2)}, u32[]{:S(2)}) collective-permute-start(bf16[2,128,256]{2,1,0:T(8,128)(2,1)S(1)} %pad_maximum_fusion.refs_0_), channel_id=1, source_target_pairs={{0,2},{1,15},{2,4},{3,1},{4,6},{5,3},{6,8},{7,5},{8,10},{9,7},{10,... | collective-permute-start | bytes 393224 | tf_op jit(solution)/shard_map/ppermute | solution.py:227
  3.5 6.9 %collective-permute-start = (bf16[2,128,256]{2,1,0:T(8,128)(2,1)S(1)}, bf16[2,128,256]{2,1,0:T(8,128)(2,1)S(1)}, u32[]{:S(2)}, u32[]{:S(2)}) collective-permute-start(bf16[2,128,256]{2,1,0:T(8,128)(2,1)S(1)} %pad_maximum_fusion.refs_0_), channel_id=1, source_target_pairs={{0,1},{1,0},{2,3},{3,2},{4,5},{5,4},{6,7},{7,6},{8,9},{9,8},{10,11... | collective-permute-start | bytes 393224 | tf_op jit(solution)/shard_map/ppermute | solution.py:231
  10.4 6.2 %collective-permute-start.5 = (bf16[2,128,256]{2,1,0:T(8,128)(2,1)S(1)}, bf16[2,128,256]{2,1,0:T(8,128)(2,1)S(1)}, u32[]{:S(2)}, u32[]{:S(2)}) collective-permute-start(bf16[2,128,256]{2,1,0:T(8,128)(2,1)S(1)} %collective-permute-done.1.refs_2_), channel_id=1, source_target_pairs={{0,2},{1,15},{2,4},{3,1},{4,6},{5,3},{6,8},{7,5},{8,10},{9,7},{10,... | collective-permute-start | bytes 393224 | tf_op jit(solution)/shard_map/ppermute | solution.py:227
  10.4 7.6 %collective-permute-start.3 = (bf16[2,128,256]{2,1,0:T(8,128)(2,1)S(1)}, bf16[2,128,256]{2,1,0:T(8,128)(2,1)S(1)}, u32[]{:S(2)}, u32[]{:S(2)}) collective-permute-start(bf16[2,128,256]{2,1,0:T(8,128)(2,1)S(1)} %collective-permute-done.refs_1_), channel_id=1, source_target_pairs={{0,2},{1,15},{2,4},{3,1},{4,6},{5,3},{6,8},{7,5},{8,10},{9,7},{10,... | collective-permute-start | bytes 393224 | tf_op jit(solution)/shard_map/ppermute | solution.py:227
  16.6 6.2 %collective-permute-start.9 = (bf16[2,128,256]{2,1,0:T(8,128)(2,1)S(1)}, bf16[2,128,256]{2,1,0:T(8,128)(2,1)S(1)}, u32[]{:S(2)}, u32[]{:S(2)}) collective-permute-start(bf16[2,128,256]{2,1,0:T(8,128)(2,1)S(1)} %collective-permute-done.5.refs_6_), channel_id=1, source_target_pairs={{0,2},{1,15},{2,4},{3,1},{4,6},{5,3},{6,8},{7,5},{8,10},{9,7},{10,... | collective-permute-start | bytes 393224 | tf_op jit(solution)/shard_map/ppermute | solution.py:227
  18.0 6.2 %collective-permute-start.7 = (bf16[2,128,256]{2,1,0:T(8,128)(2,1)S(1)}, bf16[2,128,256]{2,1,0:T(8,128)(2,1)S(1)}, u32[]{:S(2)}, u32[]{:S(2)}) collective-permute-start(bf16[2,128,256]{2,1,0:T(8,128)(2,1)S(1)} %collective-permute-done.3.refs_4_), channel_id=1, source_target_pairs={{0,2},{1,15},{2,4},{3,1},{4,6},{5,3},{6,8},{7,5},{8,10},{9,7},{10,... | collective-permute-start | bytes 393224 | tf_op jit(solution)/shard_map/ppermute | solution.py:227
  18.0 6.2 %collective-permute-start.2 = (bf16[2,128,256]{2,1,0:T(8,128)(2,1)S(1)}, bf16[2,128,256]{2,1,0:T(8,128)(2,1)S(1)}, u32[]{:S(2)}, u32[]{:S(2)}) collective-permute-start(bf16[2,128,256]{2,1,0:T(8,128)(2,1)S(1)} %collective-permute-done.1.refs_2_), channel_id=1, source_target_pairs={{0,1},{1,0},{2,3},{3,2},{4,5},{5,4},{6,7},{7,6},{8,9},{9,8},{10,11... | collective-permute-start | bytes 393224 | tf_op jit(solution)/shard_map/ppermute | solution.py:231
  18.5 6.2 %collective-permute-start.6 = (bf16[2,128,256]{2,1,0:T(8,128)(2,1)S(1)}, bf16[2,128,256]{2,1,0:T(8,128)(2,1)S(1)}, u32[]{:S(2)}, u32[]{:S(2)}) collective-permute-start(bf16[2,128,256]{2,1,0:T(8,128)(2,1)S(1)} %collective-permute-done.5.refs_6_), channel_id=1, source_target_pairs={{0,1},{1,0},{2,3},{3,2},{4,5},{5,4},{6,7},{7,6},{8,9},{9,8},{10,11... | collective-permute-start | bytes 393224 | tf_op jit(solution)/shard_map/ppermute | solution.py:231
  22.8 6.2 %collective-permute-start.13 = (bf16[2,128,256]{2,1,0:T(8,128)(2,1)S(1)}, bf16[2,128,256]{2,1,0:T(8,128)(2,1)S(1)}, u32[]{:S(2)}, u32[]{:S(2)}) collective-permute-start(bf16[2,128,256]{2,1,0:T(8,128)(2,1)S(1)} %collective-permute-done.9.refs_10_), channel_id=1, source_target_pairs={{0,2},{1,15},{2,4},{3,1},{4,6},{5,3},{6,8},{7,5},{8,10},{9,7},{10,... | collective-permute-start | bytes 393224 | tf_op jit(solution)/shard_map/ppermute | solution.py:227
  24.2 6.2 %collective-permute-start.11 = (bf16[2,128,256]{2,1,0:T(8,128)(2,1)S(1)}, bf16[2,128,256]{2,1,0:T(8,128)(2,1)S(1)}, u32[]{:S(2)}, u32[]{:S(2)}) collective-permute-start(bf16[2,128,256]{2,1,0:T(8,128)(2,1)S(1)} %collective-permute-done.7.refs_8_), channel_id=1, source_target_pairs={{0,2},{1,15},{2,4},{3,1},{4,6},{5,3},{6,8},{7,5},{8,10},{9,7},{10,... | collective-permute-start | bytes 393224 | tf_op jit(solution)/shard_map/ppermute | solution.py:227
  24.2 6.8 %collective-permute-start.4 = (bf16[2,128,256]{2,1,0:T(8,128)(2,1)S(1)}, bf16[2,128,256]{2,1,0:T(8,128)(2,1)S(1)}, u32[]{:S(2)}, u32[]{:S(2)}) collective-permute-start(bf16[2,128,256]{2,1,0:T(8,128)(2,1)S(1)} %collective-permute-done.3.refs_4_), channel_id=1, source_target_pairs={{0,1},{1,0},{2,3},{3,2},{4,5},{5,4},{6,7},{7,6},{8,9},{9,8},{10,11... | collective-permute-start | bytes 393224 | tf_op jit(solution)/shard_map/ppermute | solution.py:231
  24.2 6.8 %collective-permute-start.10 = (bf16[2,128,256]{2,1,0:T(8,128)(2,1)S(1)}, bf16[2,128,256]{2,1,0:T(8,128)(2,1)S(1)}, u32[]{:S(2)}, u32[]{:S(2)}) collective-permute-start(bf16[2,128,256]{2,1,0:T(8,128)(2,1)S(1)} %collective-permute-done.9.refs_10_), channel_id=1, source_target_pairs={{0,1},{1,0},{2,3},{3,2},{4,5},{5,4},{6,7},{7,6},{8,9},{9,8},{10,11... | collective-permute-start | bytes 393224 | tf_op jit(solution)/shard_map/ppermute | solution.py:231
  24.7 6.3 %collective-permute-start.8 = (bf16[2,128,256]{2,1,0:T(8,128)(2,1)S(1)}, bf16[2,128,256]{2,1,0:T(8,128)(2,1)S(1)}, u32[]{:S(2)}, u32[]{:S(2)}) collective-permute-start(bf16[2,128,256]{2,1,0:T(8,128)(2,1)S(1)} %collective-permute-done.7.refs_8_), channel_id=1, source_target_pairs={{0,1},{1,0},{2,3},{3,2},{4,5},{5,4},{6,7},{7,6},{8,9},{9,8},{10,11... | collective-permute-start | bytes 393224 | tf_op jit(solution)/shard_map/ppermute | solution.py:231
  28.9 2.1 %collective-permute-start.14 = (bf16[2,128,256]{2,1,0:T(8,128)(2,1)S(1)}, bf16[2,128,256]{2,1,0:T(8,128)(2,1)S(1)}, u32[]{:S(2)}, u32[]{:S(2)}) collective-permute-start(bf16[2,128,256]{2,1,0:T(8,128)(2,1)S(1)} %collective-permute-done.13.refs_14_), channel_id=1, source_target_pairs={{0,1},{1,0},{2,3},{3,2},{4,5},{5,4},{6,7},{7,6},{8,9},{9,8},{10,11... | collective-permute-start | bytes 393224 | tf_op jit(solution)/shard_map/ppermute | solution.py:231
  30.3 1.3 %collective-permute-start.12 = (bf16[2,128,256]{2,1,0:T(8,128)(2,1)S(1)}, bf16[2,128,256]{2,1,0:T(8,128)(2,1)S(1)}, u32[]{:S(2)}, u32[]{:S(2)}) collective-permute-start(bf16[2,128,256]{2,1,0:T(8,128)(2,1)S(1)} %collective-permute-done.11.refs_12_), channel_id=1, source_target_pairs={{0,1},{1,0},{2,3},{3,2},{4,5},{5,4},{6,7},{7,6},{8,9},{9,8},{10,11... | collective-permute-start | bytes 393224 | tf_op jit(solution)/shard_map/ppermute | solution.py:231
  31.7 0.7 copy-start
  32.3 0.7 copy-start.1
  55.8 3.1 %collective-permute-start.15 = (bf16[8,2,128,256]{3,2,1,0:T(8,128)(2,1)S(1)}, bf16[8,2,128,256]{3,2,1,0:T(8,128)(2,1)S(1)}, u32[]{:S(2)}, u32[]{:S(2)}) collective-permute-start(bf16[8,2,128,256]{3,2,1,0:T(8,128)(2,1)S(1)} %get-tuple-element.34), channel_id=1, source_target_pairs={{0,1},{1,0},{2,3},{3,2},{4,5},{5,4},{6,7},{7,6},{8,9},{9,8},{10,11... | collective-permute-start | bytes 3145736 | tf_op jit(solution)/shard_map/ppermute | solution.py:231
  56.1 14.8 %collective-permute-start.19 = (bf16[2,16,128,128]{3,2,1,0:T(8,128)(2,1)S(1)}, bf16[2,16,128,128]{3,2,1,0:T(8,128)(2,1)S(1)}, u32[]{:S(2)}, u32[]{:S(2)}) collective-permute-start(bf16[2,16,128,128]{3,2,1,0:T(8,128)(2,1)S(1)} %get-tuple-element.30), channel_id=1, source_target_pairs={{0,16},{1,65},{16,32},{17,81},{32,48},{33,97},{48,0},{49,113},{64,... | collective-permute-start | bytes 3145736 | tf_op jit(solution)/shard_map/ppermute | solution.py:262
  56.5 17.7 %collective-permute-start.17 = (bf16[2,16,128,128]{3,2,1,0:T(8,128)(2,1)S(1)}, bf16[2,16,128,128]{3,2,1,0:T(8,128)(2,1)S(1)}, u32[]{:S(2)}, u32[]{:S(2)}) collective-permute-start(bf16[2,16,128,128]{3,2,1,0:T(8,128)(2,1)S(1)} %get-tuple-element.41), channel_id=1, source_target_pairs={{0,48},{1,193},{16,0},{17,209},{32,16},{33,225},{48,32},{49,241},{... | collective-permute-start | bytes 3145736 | tf_op jit(solution)/shard_map/ppermute | solution.py:262
  58.1 25.8 %collective-permute-start.21 = (bf16[2,16,128,128]{3,2,1,0:T(8,128)(2,1)}, bf16[2,16,128,128]{3,2,1,0:T(8,128)(2,1)}, u32[]{:S(2)}, u32[]{:S(2)}) collective-permute-start(bf16[2,16,128,128]{3,2,1,0:T(8,128)(2,1)} %get-tuple-element.43), channel_id=1, source_target_pairs={{0,48},{1,193},{16,0},{17,209},{32,16},{33,225},{48,32},{49,241},{... | collective-permute-start | bytes 3145736 | tf_op jit(solution)/shard_map/ppermute | solution.py:262
  72.3 15.1 %collective-permute-start.20 = (bf16[2,16,128,128]{3,2,1,0:T(8,128)(2,1)}, bf16[2,16,128,128]{3,2,1,0:T(8,128)(2,1)}, u32[]{:S(2)}, u32[]{:S(2)}) collective-permute-start(bf16[2,16,128,128]{3,2,1,0:T(8,128)(2,1)} %add_convert_fusion), channel_id=1, source_target_pairs={{0,16},{1,65},{16,32},{17,81},{32,48},{33,97},{48,0},{49,113},{64,... | collective-permute-start | bytes 3145736 | tf_op jit(solution)/shard_map/ppermute | solution.py:262
  74.0 29.4 %collective-permute-start.16 = (bf16[2,16,128,128]{3,2,1,0:T(8,128)(2,1)S(1)}, bf16[2,16,128,128]{3,2,1,0:T(8,128)(2,1)}, u32[]{:S(2)}, u32[]{:S(2)}) collective-permute-start(bf16[2,16,128,128]{3,2,1,0:T(8,128)(2,1)S(1)} %get-tuple-element.39), channel_id=1, source_target_pairs={{0,16},{1,65},{16,32},{17,81},{32,48},{33,97},{48,0},{49,113},{64,... | collective-permute-start | bytes 3145736 | tf_op jit(solution)/shard_map/ppermute | solution.py:262
  75.7 27.7 %collective-permute-start.18 = (bf16[2,16,128,128]{3,2,1,0:T(8,128)(2,1)}, bf16[2,16,128,128]{3,2,1,0:T(8,128)(2,1)}, u32[]{:S(2)}, u32[]{:S(2)}) collective-permute-start(bf16[2,16,128,128]{3,2,1,0:T(8,128)(2,1)} %add_convert_fusion.1), channel_id=1, source_target_pairs={{0,48},{1,193},{16,0},{17,209},{32,16},{33,225},{48,32},{49,241},{... | collective-permute-start | bytes 3145736 | tf_op jit(solution)/shard_map/ppermute | solution.py:262
  77.4 40.7 %all-to-all-start = ((bf16[8,2,128,256]{3,2,1,0:T(8,128)(2,1)}), bf16[8,2,128,256]{3,2,1,0:T(8,128)(2,1)}, u32[]{:S(2)}, u32[]{:S(2)}) async-start(bf16[8,2,128,256]{3,2,1,0:T(8,128)(2,1)} %add_convert_fusion.2), calls=%async_computation | async-start | bytes 2097152 | tf_op jit(solution)/shard_map/all_to_all | solution.py:300
  90.2 15.0 %collective-permute-start.22 = (bf16[2,8,128,128]{3,2,1,0:T(8,128)(2,1)S(1)}, bf16[2,8,128,128]{3,2,1,0:T(8,128)(2,1)S(1)}, u32[]{:S(2)}, u32[]{:S(2)}) collective-permute-start(bf16[2,8,128,128]{3,2,1,0:T(8,128)(2,1)S(1)} %get-tuple-element.50), channel_id=1, source_target_pairs={{0,64},{1,17},{16,80},{17,33},{32,96},{33,49},{48,112},{49,1},{64,... | collective-permute-start | bytes 1572872 | tf_op jit(solution)/shard_map/ppermute | solution.py:262
  91.8 16.1 %collective-permute-start.24 = (bf16[2,8,128,128]{3,2,1,0:T(8,128)(2,1)}, bf16[2,8,128,128]{3,2,1,0:T(8,128)(2,1)}, u32[]{:S(2)}, u32[]{:S(2)}) collective-permute-start(bf16[2,8,128,128]{3,2,1,0:T(8,128)(2,1)} %get-tuple-element.51), channel_id=1, source_target_pairs={{0,192},{1,49},{16,208},{17,1},{32,224},{33,17},{48,240},{49,33},{... | collective-permute-start | bytes 1572872 | tf_op jit(solution)/shard_map/ppermute | solution.py:262
  105.2 0.8 copy-start.2
  107.1 7.7 %collective-permute-start.23 = (bf16[2,4,128,128]{3,2,1,0:T(8,128)(2,1)S(1)}, bf16[2,4,128,128]{3,2,1,0:T(8,128)(2,1)S(1)}, u32[]{:S(2)}, u32[]{:S(2)}) collective-permute-start(bf16[2,4,128,128]{3,2,1,0:T(8,128)(2,1)S(1)} %add_convert_fusion.6), channel_id=1, source_target_pairs={{0,64},{1,17},{16,80},{17,33},{32,96},{33,49},{48,112},{49,1},{64,... | collective-permute-start | bytes 786440 | tf_op jit(solution)/shard_map/ppermute | solution.py:262
  107.9 15.9 %copy-start.3 = (bf16[2,8,128,128]{3,2,1,0:T(8,128)(2,1)S(1)}, bf16[2,8,128,128]{3,2,1,0:T(8,128)(2,1)}, u32[]{:S(2)}) copy-start(bf16[2,8,128,128]{3,2,1,0:T(8,128)(2,1)} %copy-done.2) | copy-start | bytes 1572868
  117.2 6.6 %collective-permute-start.25 = (bf16[2,4,128,128]{3,2,1,0:T(8,128)(2,1)}, bf16[2,4,128,128]{3,2,1,0:T(8,128)(2,1)S(1)}, u32[]{:S(2)}, u32[]{:S(2)}) collective-permute-start(bf16[2,4,128,128]{3,2,1,0:T(8,128)(2,1)} %get-tuple-element.49), channel_id=1, source_target_pairs={{0,192},{1,49},{16,208},{17,1},{32,224},{33,17},{48,240},{49,33},{... | collective-permute-start | bytes 786440 | tf_op jit(solution)/shard_map/ppermute | solution.py:262

commit v3 on v2

v3 whole, which is shorter than its diff:
```python
import functools

import jax
import jax.numpy as jnp
from jax import lax
from jax.experimental import pallas as pl
from jax.experimental.pallas import tpu as pltpu
from jax.sharding import Mesh, PartitionSpec as P

SIDE = 128
COLS = 32
ROWS = 8
DENSE_MIB, FORWARD_MIB, TOKEN_MIB = 16, 16, 16
VM = pltpu.VMEM
SM = pltpu.SMEM
BF = jnp.bfloat16
F32 = jnp.float32


def whole(*shape):
    return pl.BlockSpec(shape, lambda *i: (0,) * len(shape))


def params(mib):
    return pltpu.CompilerParams(vmem_limit_bytes=mib << 20)


def sspec():
    return pl.BlockSpec(memory_space=SM)


def nn(a, b):
    return jnp.dot(a, b, preferred_element_type=F32)


def nt(a, b):
    return lax.dot_general(a, b, (((1,), (1,)), ((), ())), preferred_element_type=F32)


def gelu_pair(pre):
    curve = lax.erf(pre * 0.7071067811865476)
    value = 0.5 * pre * (1.0 + curve)
    slope = 0.5 * (1.0 + curve) + pre * jnp.exp(-0.5 * pre * pre) * 0.3989422804014327
    return value, slope


def other_owner(k):
    z, c = lax.axis_index("z"), lax.axis_index("c")
    ahead = 2 * c - 1
    if k < 2:
        return z * 2 + (c if k == 0 else 1 - c)
    hop = (k - 2) // 4 + 1
    kind = (k - 2) % 4
    chip = z + hop * ahead if kind in (0, 2) else z - hop * ahead
    core = c if kind in (0, 3) else 1 - c
    return lax.rem(chip + 8, 8) * 2 + core


def dense_kernel(rows, cols, count_ref, up_ref, down_ref, wu_ref, wd_ref, sem):
    count = count_ref[0]
    wu_ref[...] = jnp.zeros_like(wu_ref)
    wd_ref[...] = jnp.zeros_like(wd_ref)

    def copies(s):
        row = pl.ds(pl.multiple_of(rows[s] * SIDE, SIDE), SIDE)
        col = pl.ds(pl.multiple_of(cols[s] * SIDE, SIDE), SIDE)
        return (
            pltpu.make_async_copy(up_ref.at[0, s], wu_ref.at[col, row], sem),
            pltpu.make_async_copy(down_ref.at[0, s], wd_ref.at[row, col], sem),
        )

    @pl.loop(0, count)
    def _(s):
        for copy in copies(s):
            copy.start()

    @pl.loop(0, count)
    def _(s):
        for copy in copies(s):
            copy.wait()


def dense(rows, cols, count, up_tiles, down_tiles):
    return pl.pallas_call(
        dense_kernel,
        in_specs=[sspec()] * 3 + [pl.BlockSpec(memory_space=pltpu.HBM)] * 2,
        out_specs=[pl.BlockSpec(memory_space=VM)] * 2,
        out_shape=[
            jax.ShapeDtypeStruct((COLS * SIDE, ROWS * SIDE), BF),
            jax.ShapeDtypeStruct((ROWS * SIDE, COLS * SIDE), BF),
        ],
        scratch_shapes=[pltpu.SemaphoreType.DMA],
        compiler_params=params(DENSE_MIB),
        cost_estimate=pl.CostEstimate(flops=0, bytes_accessed=24 << 20, transcendentals=0),
        name="dense",
    )(rows, cols, count, up_tiles, down_tiles)


def lanes(k, n):
    return pl.ds(pl.multiple_of(k * n, n), n)


def forward_kernel(rows, cols, *refs):
    shards = refs[:16]
    wu_ref, wd_ref, h_ref, d_ref = refs[16:20]
    parts = refs[20:27]
    x_ref, dy_ref, ht_ref, dt_ref, sem = refs[27:32]
    wide = 2 * SIDE
    copies = []
    for k in range(16):
        at = lanes(other_owner(k), wide)
        copies.append(pltpu.make_async_copy(shards[k].at[0], x_ref.at[:, at], sem))
        copies.append(pltpu.make_async_copy(shards[k].at[1], dy_ref.at[:, at], sem))
    for copy in copies:
        copy.start()
    for copy in copies:
        copy.wait()
    for n in range(ROWS // 2):
        at = slice(n * wide, (n + 1) * wide)
        pre = nn(x_ref[...], wu_ref[:, at])
        grad_hidden = nt(dy_ref[...], wd_ref[at, :])
        value, slope = gelu_pair(pre)
        grad = grad_hidden * slope
        h_ref[:, at] = value.astype(BF)
        d_ref[:, at] = grad.astype(BF)
        for b in range(2):
            half = slice(b * SIDE, (b + 1) * SIDE)
            ht_ref[2 * n + b] = value[:, half].T.astype(BF)
            dt_ref[2 * n + b] = grad[:, half].T.astype(BF)
    at = 0
    for out, n in zip(parts, SIZES):
        for s in range(n):
            slot = ring_slot(at + s)
            row, col = rows[slot], lanes(cols[slot], SIDE)
            out[0, s] = nn(dt_ref[row], x_ref[:, col]).astype(BF)
            out[1, s] = nn(ht_ref[row], dy_ref[:, col]).astype(BF)
        at += n


def forward(rows, cols, shards, wu, wd):
    hid = jax.ShapeDtypeStruct((SIDE, ROWS * SIDE), BF)
    anywhere = pl.BlockSpec(memory_space=pl.ANY)
    return pl.pallas_call(
        forward_kernel,
        in_specs=[sspec()] * 2 + [anywhere] * 16 + [pl.BlockSpec(memory_space=VM)] * 2,
        out_specs=[pl.BlockSpec(memory_space=VM)] * 9,
        out_shape=[hid, hid] + [jax.ShapeDtypeStruct((2, n, SIDE, SIDE), BF) for n in SIZES],
        scratch_shapes=[VM((SIDE, COLS * SIDE), BF)] * 2
        + [VM((ROWS, SIDE, SIDE), BF)] * 2
        + [pltpu.SemaphoreType.DMA],
        compiler_params=params(FORWARD_MIB),
        cost_estimate=pl.CostEstimate(flops=3 << 30, bytes_accessed=28 << 20, transcendentals=1 << 18),
        name="forward",
    )(rows, cols, *shards, wu, wd)


def ring_slot(j):
    first = ((2, 0), (2, 16), (1, 16), (3, 0), (1, 0), (3, 16), (0, 0), (0, 16))
    second = ((2, 0), (1, 4), (2, 4), (3, 0), (1, 0), (3, 4), (0, 0), (0, 4))
    away1, base = first[j // 16]
    place = base + j % 16
    away2, near = second[place // 4]
    c = lax.axis_index("c")
    away_x = away1 + c * (away2 - away1)
    away_y = away2 + c * (away1 - away2)
    y = lax.rem(lax.axis_index("y") + away_y, 4)
    x = lax.rem(lax.axis_index("x") + away_x, 4)
    return (y * 4 + x) * 8 + near + place % 4


SIZES = (16, 16, 16, 16, 16, 16, 32)


def token_kernel(h_ref, d_ref, wu_ref, wd_ref, send_ref, keep_ref):
    wide = 2 * SIDE
    c = lax.axis_index("c")
    for out, core in ((send_ref, 1 - c), (keep_ref, c)):
        for k in range(8):
            at = lanes(2 * k + core, wide)
            out[k, 0] = nn(h_ref[...], wd_ref[:, at]).astype(BF)
            out[k, 1] = nt(d_ref[...], wu_ref[at, :]).astype(BF)


def token_parts(h, d, wu, wd):
    part = jax.ShapeDtypeStruct((8, 2, SIDE, 2 * SIDE), BF)
    return pl.pallas_call(
        token_kernel,
        in_specs=[pl.BlockSpec(memory_space=VM)] * 4,
        out_specs=[pl.BlockSpec(memory_space=VM)] * 2,
        out_shape=[part] * 2,
        compiler_params=params(TOKEN_MIB),
        cost_estimate=pl.CostEstimate(flops=2 << 30, bytes_accessed=19 << 20, transcendentals=0),
        name="token_parts",
    )(h, d, wu, wd)


def ring(n, by):
    return [(i, (i + by) % n) for i in range(n)]


def step_both(x):
    pairs = []
    for z in range(8):
        pairs.append((z * 2, ((z + 1) % 8) * 2))
        pairs.append((z * 2 + 1, ((z - 1) % 8) * 2 + 1))
    return lax.ppermute(x, ("z", "c"), pairs)


def swap(x):
    return lax.ppermute(x, "c", [(0, 1), (1, 0)])


def add(*parts):
    total = parts[0].astype(F32)
    for p in parts[1:]:
        total = total + p.astype(F32)
    return total


def gather_over_tile(own, wu, wd):
    first, second = own, swap(own)
    shards = [first, second]
    for k in range(1, 5):
        if k == 3:
            first, wu, wd = lax.optimization_barrier((first, wu, wd))
        first = step_both(first)
        shards += [first, swap(first)]
        if k < 4:
            second = step_both(second)
            shards += [second, swap(second)]
    return shards, wu, wd


def hop(t, stage, by):
    pairs = []
    for y in range(4):
        for x in range(4):
            for c in range(2):
                along_x = (stage + c) % 2 == 0
                to_y = y if along_x else (y + by) % 4
                to_x = (x + by) % 4 if along_x else x
                pairs.append(((y * 4 + x) * 2 + c, (to_y * 4 + to_x) * 2 + c))
    return lax.ppermute(t, ("y", "x", "c"), pairs)


def send_far(parts):
    far_a, far_b, next_b, before_a = parts[:4]
    return hop(far_a, 0, 1), hop(far_b, 0, -1), hop(next_b, 0, 1), hop(before_a, 0, -1)


def two_stages(far, next_a, before_b, own, pieces):
    from_left, from_right, left_b, right_a = far
    left_a = hop(add(next_a, from_left).astype(BF), 0, 1)
    right_b = hop(add(before_b, from_right).astype(BF), 0, -1)

    def total(k, n):
        left, right = (left_a, right_a) if k < 16 else (left_b, right_b)
        at = slice(k % 16, k % 16 + n)
        return add(own[:, k : k + n], left[:, at], right[:, at])

    start = total(0, 8).astype(BF)
    start, pieces = lax.optimization_barrier((start, pieces))
    from_left = hop(start, 1, 1)
    from_right = hop(total(8, 8).astype(BF), 1, -1)
    end_a = hop(add(total(16, 4), from_left[:, :4]).astype(BF), 1, 1)
    end_b = hop(add(total(20, 4), from_right[:, :4]).astype(BF), 1, -1)
    half_a = add(total(24, 4), end_a, from_right[:, 4:])
    half_b = add(total(28, 4), from_left[:, 4:], end_b)
    return jnp.concatenate([half_a, half_b], axis=1), pieces


def body(tokens, grad_out, up_tiles, down_tiles, tile_rows, tile_cols, tile_count):
    rows, cols = tile_rows[0], tile_cols[0]
    wu, wd = dense(rows, cols, tile_count, up_tiles, down_tiles)
    shards, wu, wd = gather_over_tile(jnp.stack([tokens, grad_out]), wu, wd)
    h, d, *parts = forward(rows, cols, shards, wu, wd)
    far = send_far(parts)
    h, d, _ = lax.optimization_barrier((h, d, parts[0]))
    send, keep = token_parts(h, d, wu, wd)
    pieces = add(keep, swap(send)).astype(BF)
    weights, pieces = two_stages(far, parts[4], parts[5], parts[6], pieces)
    weights = weights * (1.0 / 16)
    terms = lax.all_to_all(pieces, "z", 0, 0, tiled=True)
    total = jnp.sum(terms.astype(F32), axis=0).astype(BF)

    slot = lax.axis_index(("y", "x")) * 8 + jnp.arange(8, dtype=jnp.int32)
    live = (slot < tile_count[0])[:, None, None]
    grad_up = jnp.where(live, jnp.swapaxes(weights[0], 1, 2), 0.0)
    grad_down = jnp.where(live, weights[1], 0.0)
    return total[0], total[1], grad_up[None], grad_down[None]


def solution(mesh):
    grid = Mesh(mesh.devices.reshape(4, 4, 8, 2), ("y", "x", "z", "c"))
    dp, tile = ("y", "x"), ("z", "c")
    placed = (
        P(dp, tile),
        P(dp, tile),
        P(tile, None, None, None),
        P(tile, None, None, None),
        P(tile, None),
        P(tile, None),
        P(tile),
    )
    return jax.shard_map(
        body,
        mesh=grid,
        in_specs=placed,
        out_specs=(P(dp, tile), P(dp, tile), P(tile, dp, None, None), P(tile, dp, None, None)),
        check_vma=False,
    )
```

time: 129 us -> 118 us (0.915); the launches traced: 127 us -> 118 us
  waiting for transfers between devices: 59.8 us -> 45 us
  starting transfers between devices: 24.2 us -> 36.8 us
  Pallas kernels: 22.8 us -> 14.7 us
  local copies, waits for them, and re-layouts: 3.76 us -> 7.34 us
  other arithmetic: 15.1 us -> 12.2 us
    ppermute x7, waiting for transfers between devices: 22.2 us -> 8.56 us  [step_both(): return lax.ppermute(x, ('z', 'c'), pairs)]
    ppermute x7, starting transfers between devices: 2.01 us -> 11.9 us  [step_both(): return lax.ppermute(x, ('z', 'c'), pairs)]
    pallas_call x3, Pallas kernels: 22.8 us -> 14.7 us  [the longest x1 8.41 us: forward(): pl.pallas_call(forward_kernel, in_specs=[sspec()] * 2 + [anywhere] * 16 +...]
    ppermute x10, waiting for transfers between devices: 37 us -> 33 us  [hop(): return lax.ppermute(t, ('y', 'x', 'c'), pairs)]
    unnamed x9, local copies, waits for them, and re-layouts: 3.1 us -> 6.68 us
    all_to_all x1, waiting for transfers between devices: 0.01 us -> 2.12 us  [body(): terms = lax.all_to_all(pieces, 'z', 0, 0, tiled=True)]
    all_to_all x1, starting transfers between devices: 5.85 us -> 7.38 us  [body(): terms = lax.all_to_all(pieces, 'z', 0, 0, tiled=True)]
    convert_element_type x1, other arithmetic: 2.79 us -> 1.46 us  [two_stages(): from_right = hop(total(8, 8).astype(BF), 1, -1)]
  transfers between devices with their start and end apart: 27 -> 27, of which waited for: 15 -> 13; matrix products, arithmetic and copies ran while one was open for 10% -> 9% of each run, Pallas kernels for 0% -> 5%
where the time goes in v3:
time: 118 us
  waiting for transfers between devices  45 us (38%)
  starting transfers between devices  36.8 us (31%)
  Pallas kernels  14.7 us (12%)
  other arithmetic  12.2 us (10%)
  local copies, waits for them, and re-layouts  7.34 us (6%)
  between operations  1.42 us (1%)
    ppermute x10, waiting for transfers between devices, hop(): return lax.ppermute(t, ('y', 'x', 'c'), pairs)  33 us
    ppermute x10, starting transfers between devices, hop(): return lax.ppermute(t, ('y', 'x', 'c'), pairs)  11.9 us
    ppermute x7, starting transfers between devices, step_both(): return lax.ppermute(x, ('z', 'c'), pairs)  11.9 us
    ppermute x7, waiting for transfers between devices, step_both(): return lax.ppermute(x, ('z', 'c'), pairs)  8.56 us
    pallas_call x1, Pallas kernels, forward(): pl.pallas_call(forward_kernel, in_specs=[sspec()] * 2 + [anywhere] * 16 +...  8.41 us
    all_to_all x1, starting transfers between devices, body(): terms = lax.all_to_all(pieces, 'z', 0, 0, tiled=True)  7.38 us
    unnamed x9, local copies, waits for them, and re-layouts  6.68 us
    ppermute x9, starting transfers between devices, swap(): return lax.ppermute(x, 'c', [(0, 1), (1, 0)])  5.62 us
  transfers between devices with their start and end apart: 27, of which 13 were waited for; matrix products, arithmetic and copies ran while one was open for 9% of the time, Pallas kernels for 5%

profile of v3, /device:TPU:6, one launch (start us, length us, event | category | flops | bytes accessed | tf_op | source)
XLA Modules:
  0.0 117.5 jit_solution(11555502266673562550)
XLA Ops:
  1.5 2.0 %collective-permute-start.1 = (bf16[2,128,256]{2,1,0:T(8,128)(2,1)S(1)}, bf16[2,128,256]{2,1,0:T(8,128)(2,1)S(1)}, u32[]{:S(2)}, u32[]{:S(2)}) collective-permute-start(bf16[2,128,256]{2,1,0:T(8,128)(2,1)S(1)} %pad_maximum_fusion.refs_0_), channel_id=1, source_target_pairs={{0,2},{1,15},{2,4},{3,1},{4,6},{5,3},{6,8},{7,5},{8,10},{9,7},{10,... | collective-permute-start | bytes 393224 | tf_op jit(solution)/shard_map/ppermute | solution.py:206
  3.5 3.5 %collective-permute-start = (bf16[2,128,256]{2,1,0:T(8,128)(2,1)S(1)}, bf16[2,128,256]{2,1,0:T(8,128)(2,1)S(1)}, u32[]{:S(2)}, u32[]{:S(2)}) collective-permute-start(bf16[2,128,256]{2,1,0:T(8,128)(2,1)S(1)} %pad_maximum_fusion.refs_0_), channel_id=1, source_target_pairs={{0,1},{1,0},{2,3},{3,2},{4,5},{5,4},{6,7},{7,6},{8,9},{9,8},{10,11... | collective-permute-start | bytes 393224 | tf_op jit(solution)/shard_map/ppermute | solution.py:210
  7.0 3.4 %collective-permute-done.1.refs_2_ = bf16[2,128,256]{2,1,0:T(8,128)(2,1)S(1)} collective-permute-done((bf16[2,128,256]{2,1,0:T(8,128)(2,1)S(1)}, bf16[2,128,256]{2,1,0:T(8,128)(2,1)S(1)}, u32[]{:S(2)}, u32[]{:S(2)}) %collective-permute-start.1) | collective-permute-done | bytes 131104 | tf_op jit(solution)/shard_map/ppermute | solution.py:206
  11.1 2.2 %copy-done = bf16[1,128,128,128]{3,2,1,0:T(8,128)(2,1)S(1)} copy-done((bf16[1,128,128,128]{3,2,1,0:T(8,128)(2,1)S(1)}, bf16[1,128,128,128]{3,2,1,0:T(8,128)(2,1)}, u32[]{:S(2)}) %copy-start) | copy-done | bytes 4194328
  13.3 2.2 %copy-done.1 = bf16[1,128,128,128]{3,2,1,0:T(8,128)(2,1)S(1)} copy-done((bf16[1,128,128,128]{3,2,1,0:T(8,128)(2,1)S(1)}, bf16[1,128,128,128]{3,2,1,0:T(8,128)(2,1)}, u32[]{:S(2)}) %copy-start.1) | copy-done | bytes 4194328
  16.8 2.2 %dense.1 = (bf16[4096,1024]{1,0:T(8,128)(2,1)S(1)}, bf16[1024,4096]{1,0:T(8,128)(2,1)S(1)}) custom-call(s32[128]{0:T(128)S(1)} %bitcast.20, s32[128]{0:T(128)S(1)} %bitcast.22, s32[1]{0:T(128)} %copy.12.count_ref, bf16[1,128,128,128]{3,2,1,0:T(8,128)(2,1)S(1)} %copy-done, bf16[1,128,128,128]{3,2,1,0:T(8,128)(2,1)S(1)} %copy-done.1), custom_call_target="tpu_custom_call" | custom-call | bytes 25165824 | tf_op jit(solution)/shard_map/dense/pallas_call | solution.py:84
  19.0 3.8 %collective-permute-start.7 = (bf16[2,128,256]{2,1,0:T(8,128)(2,1)S(1)}, bf16[2,128,256]{2,1,0:T(8,128)(2,1)S(1)}, u32[]{:S(2)}, u32[]{:S(2)}) collective-permute-start(bf16[2,128,256]{2,1,0:T(8,128)(2,1)S(1)} %collective-permute-done.3.refs_4_), channel_id=1, source_target_pairs={{0,2},{1,15},{2,4},{3,1},{4,6},{5,3},{6,8},{7,5},{8,10},{9,7},{10,... | collective-permute-start | bytes 393224 | tf_op jit(solution)/shard_map/ppermute | solution.py:206
  22.8 2.6 %collective-permute-start.9 = (bf16[2,128,256]{2,1,0:T(8,128)(2,1)S(1)}, bf16[2,128,256]{2,1,0:T(8,128)(2,1)S(1)}, u32[]{:S(2)}, u32[]{:S(2)}) collective-permute-start(bf16[2,128,256]{2,1,0:T(8,128)(2,1)S(1)} %collective-permute-done.5.refs_6_), channel_id=1, source_target_pairs={{0,2},{1,15},{2,4},{3,1},{4,6},{5,3},{6,8},{7,5},{8,10},{9,7},{10,... | collective-permute-start | bytes 393224 | tf_op jit(solution)/shard_map/ppermute | solution.py:206
  26.0 2.0 %collective-permute-start.11 = (bf16[2,128,256]{2,1,0:T(8,128)(2,1)S(1)}, bf16[2,128,256]{2,1,0:T(8,128)(2,1)S(1)}, u32[]{:S(2)}, u32[]{:S(2)}) collective-permute-start(bf16[2,128,256]{2,1,0:T(8,128)(2,1)S(1)} %collective-permute-done.7.refs_8_), channel_id=1, source_target_pairs={{0,2},{1,15},{2,4},{3,1},{4,6},{5,3},{6,8},{7,5},{8,10},{9,7},{10,... | collective-permute-start | bytes 393224 | tf_op jit(solution)/shard_map/ppermute | solution.py:206
  29.0 1.4 %collective-permute-start.13 = (bf16[2,128,256]{2,1,0:T(8,128)(2,1)S(1)}, bf16[2,128,256]{2,1,0:T(8,128)(2,1)S(1)}, u32[]{:S(2)}, u32[]{:S(2)}) collective-permute-start(bf16[2,128,256]{2,1,0:T(8,128)(2,1)S(1)} %collective-permute-done.9.refs_10_), channel_id=1, source_target_pairs={{0,2},{1,15},{2,4},{3,1},{4,6},{5,3},{6,8},{7,5},{8,10},{9,7},{10,... | collective-permute-start | bytes 393224 | tf_op jit(solution)/shard_map/ppermute | solution.py:206
  32.1 3.0 %collective-permute-done.13.refs_14_ = bf16[2,128,256]{2,1,0:T(8,128)(2,1)S(1)} collective-permute-done((bf16[2,128,256]{2,1,0:T(8,128)(2,1)S(1)}, bf16[2,128,256]{2,1,0:T(8,128)(2,1)S(1)}, u32[]{:S(2)}, u32[]{:S(2)}) %collective-permute-start.13) | collective-permute-done | bytes 131104 | tf_op jit(solution)/shard_map/ppermute | solution.py:206
  35.2 1.3 %collective-permute-done.14.refs_15_ = bf16[2,128,256]{2,1,0:T(8,128)(2,1)S(1)} collective-permute-done((bf16[2,128,256]{2,1,0:T(8,128)(2,1)S(1)}, bf16[2,128,256]{2,1,0:T(8,128)(2,1)S(1)}, u32[]{:S(2)}, u32[]{:S(2)}) %collective-permute-start.14) | collective-permute-done | bytes 131104 | tf_op jit(solution)/shard_map/ppermute | solution.py:210
  36.5 8.4 %forward.1 = (bf16[128,1024]{1,0:T(8,128)(2,1)S(1)}, bf16[128,1024]{1,0:T(8,128)(2,1)S(1)}, bf16[2,16,128,128]{3,2,1,0:T(8,128)(2,1)S(1)}, bf16[2,16,128,128]{3,...) custom-call(s32[128]{0:T(128)S(1)} %bitcast.21, ...), custom_call_target="tpu_custom_call" | custom-call | flops 3221225472 | bytes 29360128 | tf_op jit(solution)/shard_map/forward/pallas_call | solution.py:143
  45.5 1.6 %collective-permute-start.20 = (bf16[2,16,128,128]{3,2,1,0:T(8,128)(2,1)S(1)}, bf16[2,16,128,128]{3,2,1,0:T(8,128)(2,1)S(1)}, u32[]{:S(2)}, u32[]{:S(2)}) collective-permute-start(bf16[2,16,128,128]{3,2,1,0:T(8,128)(2,1)S(1)} %get-tuple-element.42), channel_id=1, source_target_pairs={{0,48},{1,193},{16,0},{17,209},{32,16},{33,225},{48,32},{49,241},{... | collective-permute-start | bytes 3145736 | tf_op jit(solution)/shard_map/ppermute | solution.py:243
  47.0 4.1 %token_parts.1 = (bf16[8,2,128,256]{3,2,1,0:T(8,128)(2,1)S(1)}, bf16[8,2,128,256]{3,2,1,0:T(8,128)(2,1)S(1)}) custom-call(bf16[128,1024]{1,0:T(8,128)(2,1)S(1)} %get-tuple-element.35.h_ref, bf16[128,1024]{1,0:T(8,128)(2,1)S(1)} %get-tuple-element.36.d_ref, bf16[4096,1024]{1,0:T(8,128)(2,1)S(1)} %get-tuple-element.27.refs_16_.wu_ref, ...), custom_call_target="tpu_custom_call" | custom-call | flops 2147483648 | bytes 19922944 | tf_op jit(solution)/shard_map/token_parts/pallas_call | solution.py:186
  53.0 6.8 %collective-permute-done.15 = bf16[2,16,128,128]{3,2,1,0:T(8,128)(2,1)S(1)} collective-permute-done((bf16[2,16,128,128]{3,2,1,0:T(8,128)(2,1)S(1)}, bf16[2,16,128,128]{3,2,1,0:T(8,128)(2,1)S(1)}, u32[]{:S(2)}, u32[]{:S(2)}) %collective-permute-start.15) | collective-permute-done | bytes 1048608 | tf_op jit(solution)/shard_map/ppermute | solution.py:243
  60.3 1.8 %collective-permute-start.16 = (bf16[2,16,128,128]{3,2,1,0:T(8,128)(2,1)S(1)}, bf16[2,16,128,128]{3,2,1,0:T(8,128)(2,1)S(1)}, u32[]{:S(2)}, u32[]{:S(2)}) collective-permute-start(bf16[2,16,128,128]{3,2,1,0:T(8,128)(2,1)S(1)} %add_convert_fusion.2), channel_id=1, source_target_pairs={{0,16},{1,65},{16,32},{17,81},{32,48},{33,97},{48,0},{49,113},{64,... | collective-permute-start | bytes 3145736 | tf_op jit(solution)/shard_map/ppermute | solution.py:243
  62.3 1.4 %add_convert_fusion = bf16[2,16,128,128]{3,2,1,0:T(8,128)(2,1)} fusion(bf16[2,16,128,128]{3,2,1,0:T(8,128)(2,1)S(1)} %collective-permute-done.20, bf16[2,16,128,128]{3,2,1,0:T(8,128)(2,1)S(1)} %get-tuple-element.41), kind=kLoop, calls=%fused_computation | loop fusion | flops 2097152 | bytes 3145728 | tf_op jit(solution)/shard_map/convert_element_type | solution.py:254
  63.7 1.7 %collective-permute-start.21 = (bf16[2,16,128,128]{3,2,1,0:T(8,128)(2,1)}, bf16[2,16,128,128]{3,2,1,0:T(8,128)(2,1)}, u32[]{:S(2)}, u32[]{:S(2)}) collective-permute-start(bf16[2,16,128,128]{3,2,1,0:T(8,128)(2,1)} %add_convert_fusion), channel_id=1, source_target_pairs={{0,48},{1,193},{16,0},{17,209},{32,16},{33,225},{48,32},{49,241},{... | collective-permute-start | bytes 3145736 | tf_op jit(solution)/shard_map/ppermute | solution.py:243
  65.5 1.3 %add_convert_fusion.1 = bf16[8,2,128,256]{3,2,1,0:T(8,128)(2,1)} fusion(bf16[8,2,128,256]{3,2,1,0:T(8,128)(2,1)S(1)} %collective-permute-done.18, bf16[8,2,128,256]{3,2,1,0:T(8,128)(2,1)S(1)} %get-tuple-element.37), kind=kLoop, calls=%fused_computation.1 | loop fusion | flops 2097152 | bytes 3145728 | tf_op jit(solution)/shard_map/convert_element_type | solution.py:280
  66.8 5.9 %collective-permute-done.17 = bf16[2,16,128,128]{3,2,1,0:T(8,128)(2,1)S(1)} collective-permute-done((bf16[2,16,128,128]{3,2,1,0:T(8,128)(2,1)S(1)}, bf16[2,16,128,128]{3,2,1,0:T(8,128)(2,1)S(1)}, u32[]{:S(2)}, u32[]{:S(2)}) %collective-permute-start.17) | collective-permute-done | bytes 1048608 | tf_op jit(solution)/shard_map/ppermute | solution.py:243
  72.7 2.4 %collective-permute-done.16 = bf16[2,16,128,128]{3,2,1,0:T(8,128)(2,1)S(1)} collective-permute-done((bf16[2,16,128,128]{3,2,1,0:T(8,128)(2,1)S(1)}, bf16[2,16,128,128]{3,2,1,0:T(8,128)(2,1)S(1)}, u32[]{:S(2)}, u32[]{:S(2)}) %collective-permute-start.16) | collective-permute-done | bytes 1048608 | tf_op jit(solution)/shard_map/ppermute | solution.py:243
  75.2 1.5 %add_convert_fusion.3 = (bf16[2,8,128,128]{3,2,1,0:T(8,128)(2,1)}, bf16[2,8,128,128]{3,2,1,0:T(8,128)(2,1)}) fusion(bf16[2,16,128,128]{3,2,1,0:T(8,128)(2,1)S(1)} %collective-permute-done.17, bf16[2,16,128,128]{3,2,1,0:T(8,128)(2,1)S(1)} %collective-permute-done.16, bf16[2,32,128,128]{3,2,1,0:T(8,128)(2,1)S(1)} %get-tuple-element.29), kind=kLoop, calls=%fused_computation.4 | loop fusion | flops 3145728 | bytes 4194304 | tf_op jit(solution)/shard_map/convert_element_type | solution.py:264
  76.6 1.6 %collective-permute-start.22 = (bf16[2,8,128,128]{3,2,1,0:T(8,128)(2,1)}, bf16[2,8,128,128]{3,2,1,0:T(8,128)(2,1)}, u32[]{:S(2)}, u32[]{:S(2)}) collective-permute-start(bf16[2,8,128,128]{3,2,1,0:T(8,128)(2,1)} %get-tuple-element.43), channel_id=1, source_target_pairs={{0,64},{1,17},{16,80},{17,33},{32,96},{33,49},{48,112},{49,1},{64,... | collective-permute-start | bytes 1572872 | tf_op jit(solution)/shard_map/ppermute | solution.py:243
  78.2 1.7 %collective-permute-start.24 = (bf16[2,8,128,128]{3,2,1,0:T(8,128)(2,1)}, bf16[2,8,128,128]{3,2,1,0:T(8,128)(2,1)}, u32[]{:S(2)}, u32[]{:S(2)}) collective-permute-start(bf16[2,8,128,128]{3,2,1,0:T(8,128)(2,1)} %get-tuple-element.50), channel_id=1, source_target_pairs={{0,192},{1,49},{16,208},{17,1},{32,224},{33,17},{48,240},{49,33},{... | collective-permute-start | bytes 1572872 | tf_op jit(solution)/shard_map/ppermute | solution.py:243
  79.9 7.4 %all-to-all-start = ((bf16[8,2,128,256]{3,2,1,0:T(8,128)(2,1)}), bf16[8,2,128,256]{3,2,1,0:T(8,128)(2,1)}, u32[]{:S(2)}, u32[]{:S(2)}) async-start(bf16[8,2,128,256]{3,2,1,0:T(8,128)(2,1)} %add_convert_fusion.1), calls=%async_computation | async-start | bytes 2097152 | tf_op jit(solution)/shard_map/all_to_all | solution.py:283
  87.2 4.9 %collective-permute-done.19 = bf16[2,16,128,128]{3,2,1,0:T(8,128)(2,1)} collective-permute-done((bf16[2,16,128,128]{3,2,1,0:T(8,128)(2,1)S(1)}, bf16[2,16,128,128]{3,2,1,0:T(8,128)(2,1)}, u32[]{:S(2)}, u32[]{:S(2)}) %collective-permute-start.19) | collective-permute-done | bytes 1048608 | tf_op jit(solution)/shard_map/ppermute | solution.py:243
  95.0 6.8 %collective-permute-done.23 = bf16[2,4,128,128]{3,2,1,0:T(8,128)(2,1)S(1)} collective-permute-done((bf16[2,4,128,128]{3,2,1,0:T(8,128)(2,1)S(1)}, bf16[2,4,128,128]{3,2,1,0:T(8,128)(2,1)S(1)}, u32[]{:S(2)}, u32[]{:S(2)}) %collective-permute-start.23) | collective-permute-done | bytes 262176 | tf_op jit(solution)/shard_map/ppermute | solution.py:243
  101.8 1.7 %convert_add_fusion.1 = (f32[2,4,128,128]{3,2,1,0:T(8,128)S(1)}, bf16[2,4,128,128]{3,2,1,0:T(8,128)(2,1)S(1)}) fusion(bf16[2,4,128,128]{3,2,1,0:T(8,128)(2,1)S(1)} %collective-permute-done.23, bf16[2,8,128,128]{3,2,1,0:T(8,128)(2,1)} %collective-permute-done.24, bf16[2,16,128,128]{3,2,1,0:T(8,128)(2,1)} %collective-permute-done.21, ...), kind=kLoop, calls=%fused_computation.12 | loop fusion | flops 2228224 | bytes 3145728 | tf_op jit(solution)/shard_map/add | solution.py:216
  104.6 5.4 %collective-permute-done.25 = bf16[2,4,128,128]{3,2,1,0:T(8,128)(2,1)S(1)} collective-permute-done((bf16[2,4,128,128]{3,2,1,0:T(8,128)(2,1)S(1)}, bf16[2,4,128,128]{3,2,1,0:T(8,128)(2,1)S(1)}, u32[]{:S(2)}, u32[]{:S(2)}) %collective-permute-start.25) | collective-permute-done | bytes 262176 | tf_op jit(solution)/shard_map/ppermute | solution.py:243
  113.4 2.1 %all-to-all-done = bf16[8,2,128,256]{3,2,1,0:T(8,128)(2,1)} async-done(((bf16[8,2,128,256]{3,2,1,0:T(8,128)(2,1)}), bf16[8,2,128,256]{3,2,1,0:T(8,128)(2,1)}, u32[]{:S(2)}, u32[]{:S(2)}) %all-to-all-start) | async-done | bytes 1048608 | tf_op jit(solution)/shard_map/all_to_all | solution.py:283
  115.5 1.4 %reduce_sum.12 = bf16[2,128,256]{2,1,0:T(8,128)(2,1)S(1)} reduce(bf16[8,2,128,256]{3,2,1,0:T(8,128)(2,1)} %all-to-all-done, bf16[]{:T(256)} %constant.5.clone.1), dimensions={0}, to_apply=%region_0.0 | reduce | flops 458752 | bytes 1179650 | tf_op jit(solution)/shard_map/reduce_sum | solution.py:284
  (48 shorter events, 16.6 us)
Async XLA Ops:
  1.5 8.9 %collective-permute-start.1 = (bf16[2,128,256]{2,1,0:T(8,128)(2,1)S(1)}, bf16[2,128,256]{2,1,0:T(8,128)(2,1)S(1)}, u32[]{:S(2)}, u32[]{:S(2)}) collective-permute-start(bf16[2,128,256]{2,1,0:T(8,128)(2,1)S(1)} %pad_maximum_fusion.refs_0_), channel_id=1, source_target_pairs={{0,2},{1,15},{2,4},{3,1},{4,6},{5,3},{6,8},{7,5},{8,10},{9,7},{10,... | collective-permute-start | bytes 393224 | tf_op jit(solution)/shard_map/ppermute | solution.py:206
  3.5 6.9 %collective-permute-start = (bf16[2,128,256]{2,1,0:T(8,128)(2,1)S(1)}, bf16[2,128,256]{2,1,0:T(8,128)(2,1)S(1)}, u32[]{:S(2)}, u32[]{:S(2)}) collective-permute-start(bf16[2,128,256]{2,1,0:T(8,128)(2,1)S(1)} %pad_maximum_fusion.refs_0_), channel_id=1, source_target_pairs={{0,1},{1,0},{2,3},{3,2},{4,5},{5,4},{6,7},{7,6},{8,9},{9,8},{10,11... | collective-permute-start | bytes 393224 | tf_op jit(solution)/shard_map/ppermute | solution.py:210
  10.4 8.6 %collective-permute-start.5 = (bf16[2,128,256]{2,1,0:T(8,128)(2,1)S(1)}, bf16[2,128,256]{2,1,0:T(8,128)(2,1)S(1)}, u32[]{:S(2)}, u32[]{:S(2)}) collective-permute-start(bf16[2,128,256]{2,1,0:T(8,128)(2,1)S(1)} %collective-permute-done.1.refs_2_), channel_id=1, source_target_pairs={{0,2},{1,15},{2,4},{3,1},{4,6},{5,3},{6,8},{7,5},{8,10},{9,7},{10,... | collective-permute-start | bytes 393224 | tf_op jit(solution)/shard_map/ppermute | solution.py:206
  10.4 8.6 %collective-permute-start.3 = (bf16[2,128,256]{2,1,0:T(8,128)(2,1)S(1)}, bf16[2,128,256]{2,1,0:T(8,128)(2,1)S(1)}, u32[]{:S(2)}, u32[]{:S(2)}) collective-permute-start(bf16[2,128,256]{2,1,0:T(8,128)(2,1)S(1)} %collective-permute-done.refs_1_), channel_id=1, source_target_pairs={{0,2},{1,15},{2,4},{3,1},{4,6},{5,3},{6,8},{7,5},{8,10},{9,7},{10,... | collective-permute-start | bytes 393224 | tf_op jit(solution)/shard_map/ppermute | solution.py:206
  11.1 2.2 %copy-start = (bf16[1,128,128,128]{3,2,1,0:T(8,128)(2,1)S(1)}, bf16[1,128,128,128]{3,2,1,0:T(8,128)(2,1)}, u32[]{:S(2)}) copy-start(bf16[1,128,128,128]{3,2,1,0:T(8,128)(2,1)} %up_ref.1) | copy-start | bytes 12582916
  13.3 2.2 %copy-start.1 = (bf16[1,128,128,128]{3,2,1,0:T(8,128)(2,1)S(1)}, bf16[1,128,128,128]{3,2,1,0:T(8,128)(2,1)}, u32[]{:S(2)}) copy-start(bf16[1,128,128,128]{3,2,1,0:T(8,128)(2,1)} %down_ref.1) | copy-start | bytes 12582916
  15.4 0.7 copy-start.2
  16.1 0.7 copy-start.3
  19.0 7.0 %collective-permute-start.7 = (bf16[2,128,256]{2,1,0:T(8,128)(2,1)S(1)}, bf16[2,128,256]{2,1,0:T(8,128)(2,1)S(1)}, u32[]{:S(2)}, u32[]{:S(2)}) collective-permute-start(bf16[2,128,256]{2,1,0:T(8,128)(2,1)S(1)} %collective-permute-done.3.refs_4_), channel_id=1, source_target_pairs={{0,2},{1,15},{2,4},{3,1},{4,6},{5,3},{6,8},{7,5},{8,10},{9,7},{10,... | collective-permute-start | bytes 393224 | tf_op jit(solution)/shard_map/ppermute | solution.py:206
  22.8 6.2 %collective-permute-start.9 = (bf16[2,128,256]{2,1,0:T(8,128)(2,1)S(1)}, bf16[2,128,256]{2,1,0:T(8,128)(2,1)S(1)}, u32[]{:S(2)}, u32[]{:S(2)}) collective-permute-start(bf16[2,128,256]{2,1,0:T(8,128)(2,1)S(1)} %collective-permute-done.5.refs_6_), channel_id=1, source_target_pairs={{0,2},{1,15},{2,4},{3,1},{4,6},{5,3},{6,8},{7,5},{8,10},{9,7},{10,... | collective-permute-start | bytes 393224 | tf_op jit(solution)/shard_map/ppermute | solution.py:206
  25.4 5.0 %collective-permute-start.2 = (bf16[2,128,256]{2,1,0:T(8,128)(2,1)S(1)}, bf16[2,128,256]{2,1,0:T(8,128)(2,1)S(1)}, u32[]{:S(2)}, u32[]{:S(2)}) collective-permute-start(bf16[2,128,256]{2,1,0:T(8,128)(2,1)S(1)} %collective-permute-done.1.refs_2_), channel_id=1, source_target_pairs={{0,1},{1,0},{2,3},{3,2},{4,5},{5,4},{6,7},{7,6},{8,9},{9,8},{10,11... | collective-permute-start | bytes 393224 | tf_op jit(solution)/shard_map/ppermute | solution.py:210
  25.5 5.5 %collective-permute-start.6 = (bf16[2,128,256]{2,1,0:T(8,128)(2,1)S(1)}, bf16[2,128,256]{2,1,0:T(8,128)(2,1)S(1)}, u32[]{:S(2)}, u32[]{:S(2)}) collective-permute-start(bf16[2,128,256]{2,1,0:T(8,128)(2,1)S(1)} %collective-permute-done.5.refs_6_), channel_id=1, source_target_pairs={{0,1},{1,0},{2,3},{3,2},{4,5},{5,4},{6,7},{7,6},{8,9},{9,8},{10,11... | collective-permute-start | bytes 393224 | tf_op jit(solution)/shard_map/ppermute | solution.py:210
  26.0 6.2 %collective-permute-start.11 = (bf16[2,128,256]{2,1,0:T(8,128)(2,1)S(1)}, bf16[2,128,256]{2,1,0:T(8,128)(2,1)S(1)}, u32[]{:S(2)}, u32[]{:S(2)}) collective-permute-start(bf16[2,128,256]{2,1,0:T(8,128)(2,1)S(1)} %collective-permute-done.7.refs_8_), channel_id=1, source_target_pairs={{0,2},{1,15},{2,4},{3,1},{4,6},{5,3},{6,8},{7,5},{8,10},{9,7},{10,... | collective-permute-start | bytes 393224 | tf_op jit(solution)/shard_map/ppermute | solution.py:206
  29.0 6.2 %collective-permute-start.13 = (bf16[2,128,256]{2,1,0:T(8,128)(2,1)S(1)}, bf16[2,128,256]{2,1,0:T(8,128)(2,1)S(1)}, u32[]{:S(2)}, u32[]{:S(2)}) collective-permute-start(bf16[2,128,256]{2,1,0:T(8,128)(2,1)S(1)} %collective-permute-done.9.refs_10_), channel_id=1, source_target_pairs={{0,2},{1,15},{2,4},{3,1},{4,6},{5,3},{6,8},{7,5},{8,10},{9,7},{10,... | collective-permute-start | bytes 393224 | tf_op jit(solution)/shard_map/ppermute | solution.py:206
  30.4 4.8 %collective-permute-start.4 = (bf16[2,128,256]{2,1,0:T(8,128)(2,1)S(1)}, bf16[2,128,256]{2,1,0:T(8,128)(2,1)S(1)}, u32[]{:S(2)}, u32[]{:S(2)}) collective-permute-start(bf16[2,128,256]{2,1,0:T(8,128)(2,1)S(1)} %collective-permute-done.3.refs_4_), channel_id=1, source_target_pairs={{0,1},{1,0},{2,3},{3,2},{4,5},{5,4},{6,7},{7,6},{8,9},{9,8},{10,11... | collective-permute-start | bytes 393224 | tf_op jit(solution)/shard_map/ppermute | solution.py:210
  30.4 4.8 %collective-permute-start.8 = (bf16[2,128,256]{2,1,0:T(8,128)(2,1)S(1)}, bf16[2,128,256]{2,1,0:T(8,128)(2,1)S(1)}, u32[]{:S(2)}, u32[]{:S(2)}) collective-permute-start(bf16[2,128,256]{2,1,0:T(8,128)(2,1)S(1)} %collective-permute-done.7.refs_8_), channel_id=1, source_target_pairs={{0,1},{1,0},{2,3},{3,2},{4,5},{5,4},{6,7},{7,6},{8,9},{9,8},{10,11... | collective-permute-start | bytes 393224 | tf_op jit(solution)/shard_map/ppermute | solution.py:210
  30.9 4.2 %collective-permute-start.10 = (bf16[2,128,256]{2,1,0:T(8,128)(2,1)S(1)}, bf16[2,128,256]{2,1,0:T(8,128)(2,1)S(1)}, u32[]{:S(2)}, u32[]{:S(2)}) collective-permute-start(bf16[2,128,256]{2,1,0:T(8,128)(2,1)S(1)} %collective-permute-done.9.refs_10_), channel_id=1, source_target_pairs={{0,1},{1,0},{2,3},{3,2},{4,5},{5,4},{6,7},{7,6},{8,9},{9,8},{10,11... | collective-permute-start | bytes 393224 | tf_op jit(solution)/shard_map/ppermute | solution.py:210
  32.1 3.1 %collective-permute-start.12 = (bf16[2,128,256]{2,1,0:T(8,128)(2,1)S(1)}, bf16[2,128,256]{2,1,0:T(8,128)(2,1)S(1)}, u32[]{:S(2)}, u32[]{:S(2)}) collective-permute-start(bf16[2,128,256]{2,1,0:T(8,128)(2,1)S(1)} %collective-permute-done.11.refs_12_), channel_id=1, source_target_pairs={{0,1},{1,0},{2,3},{3,2},{4,5},{5,4},{6,7},{7,6},{8,9},{9,8},{10,11... | collective-permute-start | bytes 393224 | tf_op jit(solution)/shard_map/ppermute | solution.py:210
  35.2 1.3 %collective-permute-start.14 = (bf16[2,128,256]{2,1,0:T(8,128)(2,1)S(1)}, bf16[2,128,256]{2,1,0:T(8,128)(2,1)S(1)}, u32[]{:S(2)}, u32[]{:S(2)}) collective-permute-start(bf16[2,128,256]{2,1,0:T(8,128)(2,1)S(1)} %collective-permute-done.13.refs_14_), channel_id=1, source_target_pairs={{0,1},{1,0},{2,3},{3,2},{4,5},{5,4},{6,7},{7,6},{8,9},{9,8},{10,11... | collective-permute-start | bytes 393224 | tf_op jit(solution)/shard_map/ppermute | solution.py:210
  44.9 14.9 %collective-permute-start.15 = (bf16[2,16,128,128]{3,2,1,0:T(8,128)(2,1)S(1)}, bf16[2,16,128,128]{3,2,1,0:T(8,128)(2,1)S(1)}, u32[]{:S(2)}, u32[]{:S(2)}) collective-permute-start(bf16[2,16,128,128]{3,2,1,0:T(8,128)(2,1)S(1)} %get-tuple-element.31), channel_id=1, source_target_pairs={{0,16},{1,65},{16,32},{17,81},{32,48},{33,97},{48,0},{49,113},{64,... | collective-permute-start | bytes 3145736 | tf_op jit(solution)/shard_map/ppermute | solution.py:243
  45.5 16.8 %collective-permute-start.20 = (bf16[2,16,128,128]{3,2,1,0:T(8,128)(2,1)S(1)}, bf16[2,16,128,128]{3,2,1,0:T(8,128)(2,1)S(1)}, u32[]{:S(2)}, u32[]{:S(2)}) collective-permute-start(bf16[2,16,128,128]{3,2,1,0:T(8,128)(2,1)S(1)} %get-tuple-element.42), channel_id=1, source_target_pairs={{0,48},{1,193},{16,0},{17,209},{32,16},{33,225},{48,32},{49,241},{... | collective-permute-start | bytes 3145736 | tf_op jit(solution)/shard_map/ppermute | solution.py:243
  51.1 14.4 %collective-permute-start.18 = (bf16[8,2,128,256]{3,2,1,0:T(8,128)(2,1)S(1)}, bf16[8,2,128,256]{3,2,1,0:T(8,128)(2,1)S(1)}, u32[]{:S(2)}, u32[]{:S(2)}) collective-permute-start(bf16[8,2,128,256]{3,2,1,0:T(8,128)(2,1)S(1)} %get-tuple-element.38), channel_id=1, source_target_pairs={{0,1},{1,0},{2,3},{3,2},{4,5},{5,4},{6,7},{7,6},{8,9},{9,8},{10,11... | collective-permute-start | bytes 3145736 | tf_op jit(solution)/shard_map/ppermute | solution.py:210
  52.1 20.6 %collective-permute-start.17 = (bf16[2,16,128,128]{3,2,1,0:T(8,128)(2,1)S(1)}, bf16[2,16,128,128]{3,2,1,0:T(8,128)(2,1)S(1)}, u32[]{:S(2)}, u32[]{:S(2)}) collective-permute-start(bf16[2,16,128,128]{3,2,1,0:T(8,128)(2,1)S(1)} %get-tuple-element.32), channel_id=1, source_target_pairs={{0,48},{1,193},{16,0},{17,209},{32,16},{33,225},{48,32},{49,241},{... | collective-permute-start | bytes 3145736 | tf_op jit(solution)/shard_map/ppermute | solution.py:243
  60.3 14.9 %collective-permute-start.16 = (bf16[2,16,128,128]{3,2,1,0:T(8,128)(2,1)S(1)}, bf16[2,16,128,128]{3,2,1,0:T(8,128)(2,1)S(1)}, u32[]{:S(2)}, u32[]{:S(2)}) collective-permute-start(bf16[2,16,128,128]{3,2,1,0:T(8,128)(2,1)S(1)} %add_convert_fusion.2), channel_id=1, source_target_pairs={{0,16},{1,65},{16,32},{17,81},{32,48},{33,97},{48,0},{49,113},{64,... | collective-permute-start | bytes 3145736 | tf_op jit(solution)/shard_map/ppermute | solution.py:243
  62.0 30.1 %collective-permute-start.19 = (bf16[2,16,128,128]{3,2,1,0:T(8,128)(2,1)S(1)}, bf16[2,16,128,128]{3,2,1,0:T(8,128)(2,1)}, u32[]{:S(2)}, u32[]{:S(2)}) collective-permute-start(bf16[2,16,128,128]{3,2,1,0:T(8,128)(2,1)S(1)} %get-tuple-element.40), channel_id=1, source_target_pairs={{0,16},{1,65},{16,32},{17,81},{32,48},{33,97},{48,0},{49,113},{64,... | collective-permute-start | bytes 3145736 | tf_op jit(solution)/shard_map/ppermute | solution.py:243
  63.7 28.4 %collective-permute-start.21 = (bf16[2,16,128,128]{3,2,1,0:T(8,128)(2,1)}, bf16[2,16,128,128]{3,2,1,0:T(8,128)(2,1)}, u32[]{:S(2)}, u32[]{:S(2)}) collective-permute-start(bf16[2,16,128,128]{3,2,1,0:T(8,128)(2,1)} %add_convert_fusion), channel_id=1, source_target_pairs={{0,48},{1,193},{16,0},{17,209},{32,16},{33,225},{48,32},{49,241},{... | collective-permute-start | bytes 3145736 | tf_op jit(solution)/shard_map/ppermute | solution.py:243
  76.6 16.3 %collective-permute-start.22 = (bf16[2,8,128,128]{3,2,1,0:T(8,128)(2,1)}, bf16[2,8,128,128]{3,2,1,0:T(8,128)(2,1)}, u32[]{:S(2)}, u32[]{:S(2)}) collective-permute-start(bf16[2,8,128,128]{3,2,1,0:T(8,128)(2,1)} %get-tuple-element.43), channel_id=1, source_target_pairs={{0,64},{1,17},{16,80},{17,33},{32,96},{33,49},{48,112},{49,1},{64,... | collective-permute-start | bytes 1572872 | tf_op jit(solution)/shard_map/ppermute | solution.py:243
  78.2 16.8 %collective-permute-start.24 = (bf16[2,8,128,128]{3,2,1,0:T(8,128)(2,1)}, bf16[2,8,128,128]{3,2,1,0:T(8,128)(2,1)}, u32[]{:S(2)}, u32[]{:S(2)}) collective-permute-start(bf16[2,8,128,128]{3,2,1,0:T(8,128)(2,1)} %get-tuple-element.50), channel_id=1, source_target_pairs={{0,192},{1,49},{16,208},{17,1},{32,224},{33,17},{48,240},{49,33},{... | collective-permute-start | bytes 1572872 | tf_op jit(solution)/shard_map/ppermute | solution.py:243
  79.9 35.6 %all-to-all-start = ((bf16[8,2,128,256]{3,2,1,0:T(8,128)(2,1)}), bf16[8,2,128,256]{3,2,1,0:T(8,128)(2,1)}, u32[]{:S(2)}, u32[]{:S(2)}) async-start(bf16[8,2,128,256]{3,2,1,0:T(8,128)(2,1)} %add_convert_fusion.1), calls=%async_computation | async-start | bytes 2097152 | tf_op jit(solution)/shard_map/all_to_all | solution.py:283
  94.2 7.7 %collective-permute-start.23 = (bf16[2,4,128,128]{3,2,1,0:T(8,128)(2,1)S(1)}, bf16[2,4,128,128]{3,2,1,0:T(8,128)(2,1)S(1)}, u32[]{:S(2)}, u32[]{:S(2)}) collective-permute-start(bf16[2,4,128,128]{3,2,1,0:T(8,128)(2,1)S(1)} %add_convert_fusion.6), channel_id=1, source_target_pairs={{0,64},{1,17},{16,80},{17,33},{32,96},{33,49},{48,112},{49,1},{64,... | collective-permute-start | bytes 786440 | tf_op jit(solution)/shard_map/ppermute | solution.py:243
  103.6 6.4 %collective-permute-start.25 = (bf16[2,4,128,128]{3,2,1,0:T(8,128)(2,1)S(1)}, bf16[2,4,128,128]{3,2,1,0:T(8,128)(2,1)S(1)}, u32[]{:S(2)}, u32[]{:S(2)}) collective-permute-start(bf16[2,4,128,128]{3,2,1,0:T(8,128)(2,1)S(1)} %get-tuple-element.49), channel_id=1, source_target_pairs={{0,192},{1,49},{16,208},{17,1},{32,224},{33,17},{48,240},{49,33},{... | collective-permute-start | bytes 786440 | tf_op jit(solution)/shard_map/ppermute | solution.py:243

commit v4 on v3

v4 whole, which is shorter than its diff:
```python
import functools

import jax
import jax.numpy as jnp
from jax import lax
from jax.experimental import pallas as pl
from jax.experimental.pallas import tpu as pltpu
from jax.sharding import Mesh, PartitionSpec as P

SIDE = 128
COLS = 32
ROWS = 8
VM = pltpu.VMEM
SM = pltpu.SMEM
BF = jnp.bfloat16
F32 = jnp.float32


def whole(*shape):
    return pl.BlockSpec(shape, lambda *i: (0,) * len(shape))


def vspec():
    return pl.BlockSpec(memory_space=VM)


def params(mib):
    return pltpu.CompilerParams(vmem_limit_bytes=mib << 20)


def sspec():
    return pl.BlockSpec(memory_space=SM)


def nn(a, b):
    return jnp.dot(a, b, preferred_element_type=F32)


def nt(a, b):
    return lax.dot_general(a, b, (((1,), (1,)), ((), ())), preferred_element_type=F32)


def gelu_pair(pre):
    curve = lax.erf(pre * 0.7071067811865476)
    value = 0.5 * pre * (1.0 + curve)
    slope = 0.5 * (1.0 + curve) + pre * jnp.exp(-0.5 * pre * pre) * 0.3989422804014327
    return value, slope


def other_owner(k):
    z, c = lax.axis_index("z"), lax.axis_index("c")
    ahead = 2 * c - 1
    if k < 2:
        return z * 2 + (c if k == 0 else 1 - c)
    hop = (k - 2) // 4 + 1
    kind = (k - 2) % 4
    chip = z + hop * ahead if kind in (0, 2) else z - hop * ahead
    core = c if kind in (0, 3) else 1 - c
    return lax.rem(chip + 8, 8) * 2 + core


def split(code):
    return code // COLS, lax.rem(code, COLS)


def dense_kernel(up, where, count_ref, tiles_ref, out_ref, sem):
    count = count_ref[0]
    out_ref[...] = jnp.zeros_like(out_ref)

    def copy(s):
        row, col = (lanes(k, SIDE) for k in split(where[s]))
        at = (col, row) if up else (row, col)
        return pltpu.make_async_copy(tiles_ref.at[0, s], out_ref.at[at], sem)

    @pl.loop(0, count)
    def _(s):
        copy(s).start()

    @pl.loop(0, count)
    def _(s):
        copy(s).wait()


def dense(where, count, tiles, up):
    features, hidden = COLS * SIDE, ROWS * SIDE
    return pl.pallas_call(
        functools.partial(dense_kernel, up),
        in_specs=[sspec()] * 2 + [pl.BlockSpec(memory_space=pltpu.HBM)],
        out_specs=vspec(),
        out_shape=jax.ShapeDtypeStruct((features, hidden) if up else (hidden, features), BF),
        scratch_shapes=[pltpu.SemaphoreType.DMA],
        compiler_params=params(16),
        cost_estimate=pl.CostEstimate(flops=0, bytes_accessed=12 << 20, transcendentals=0),
        name="dense_up" if up else "dense_down",
    )(where, count, tiles)


def lanes(k, n):
    return pl.ds(pl.multiple_of(k * n, n), n)


def forward_kernel(where, *refs):
    shards = refs[:16]
    wu_ref, wd_ref, h_ref, d_ref, x_ref, dy_ref, dt_ref, ht_ref = refs[16:24]
    parts, sem = refs[24:28], refs[28]
    wide = 2 * SIDE
    copies = []
    for k in range(16):
        at = lanes(other_owner(k), wide)
        copies.append(pltpu.make_async_copy(shards[k].at[0], x_ref.at[:, at], sem))
        copies.append(pltpu.make_async_copy(shards[k].at[1], dy_ref.at[:, at], sem))
    for copy in copies:
        copy.start()
    for copy in copies:
        copy.wait()
    for n in range(ROWS // 2):
        at = slice(n * wide, (n + 1) * wide)
        pre = nn(x_ref[...], wu_ref[:, at])
        grad_hidden = nt(dy_ref[...], wd_ref[at, :])
        value, slope = gelu_pair(pre)
        grad = grad_hidden * slope
        h_ref[:, at] = value.astype(BF)
        d_ref[:, at] = grad.astype(BF)
        for b in range(2):
            half = slice(b * SIDE, (b + 1) * SIDE)
            ht_ref[2 * n + b] = value[:, half].T.astype(BF)
            dt_ref[2 * n + b] = grad[:, half].T.astype(BF)
    fill_parts(where, x_ref, dy_ref, dt_ref, ht_ref, parts, ((2, 0, 2), (2, 2, 2)))


def fill_parts(where, x_ref, dy_ref, dt_ref, ht_ref, outs, blocks):
    for k, (away, start, n) in enumerate(blocks):

        @pl.loop(0, n)
        def _(group):
            first = ring_slot(away, start + group)
            for s in range(8):
                row, col = split(where[first + s])
                at = lanes(col, SIDE)
                outs[2 * k][group * 8 + s] = nn(dt_ref[row], x_ref[:, at]).astype(BF)
                outs[2 * k + 1][group * 8 + s] = nn(ht_ref[row], dy_ref[:, at]).astype(BF)


def forward(where, shards, wu, wd):
    hid = jax.ShapeDtypeStruct((SIDE, ROWS * SIDE), BF)
    tok = jax.ShapeDtypeStruct((SIDE, COLS * SIDE), BF)
    turned = jax.ShapeDtypeStruct((ROWS, SIDE, SIDE), BF)
    part = jax.ShapeDtypeStruct((16, SIDE, SIDE), BF)
    return pl.pallas_call(
        forward_kernel,
        in_specs=[sspec()] + [pl.BlockSpec(memory_space=pl.ANY)] * 16 + [vspec()] * 2,
        out_specs=[vspec()] * 10,
        out_shape=[hid, hid, tok, tok, turned, turned] + [part] * 4,
        scratch_shapes=[pltpu.SemaphoreType.DMA],
        compiler_params=params(16),
        cost_estimate=pl.CostEstimate(flops=3 << 30, bytes_accessed=22 << 20, transcendentals=1 << 18),
        name="forward",
    )(where, *shards, wu, wd)


def rest_kernel(where, x_ref, dy_ref, dt_ref, ht_ref, *outs):
    fill_parts(where, x_ref, dy_ref, dt_ref, ht_ref, outs, ((1, 0, 4), (3, 0, 4), (0, 0, 4)))


def rest_parts(where, x, dy, dt, ht):
    return pl.pallas_call(
        rest_kernel,
        in_specs=[sspec()] + [vspec()] * 4,
        out_specs=[vspec()] * 6,
        out_shape=[jax.ShapeDtypeStruct((32, SIDE, SIDE), BF)] * 6,
        compiler_params=params(16),
        cost_estimate=pl.CostEstimate(flops=1 << 30, bytes_accessed=9 << 20, transcendentals=0),
        name="rest_parts",
    )(where, x, dy, dt, ht)


def ring_slot(away1, group):
    away2 = jnp.where(group == 0, 2, jnp.where(group == 1, 1, jnp.where(group == 2, 3, 0)))
    c = lax.axis_index("c")
    away_x = away1 + c * (away2 - away1)
    away_y = away2 + c * (away1 - away2)
    y = lax.rem(lax.axis_index("y") + away_y, 4)
    x = lax.rem(lax.axis_index("x") + away_x, 4)
    return (y * 4 + x) * 8


def token_kernel(h_ref, d_ref, wu_ref, wd_ref, send_ref, keep_ref):
    wide = 2 * SIDE
    c = lax.axis_index("c")
    for out, core in ((send_ref, 1 - c), (keep_ref, c)):
        for k in range(8):
            at = lanes(2 * k + core, wide)
            out[k, 0] = nn(h_ref[...], wd_ref[:, at]).astype(BF)
            out[k, 1] = nt(d_ref[...], wu_ref[at, :]).astype(BF)


def token_parts(h, d, wu, wd):
    part = jax.ShapeDtypeStruct((8, 2, SIDE, 2 * SIDE), BF)
    return pl.pallas_call(
        token_kernel,
        in_specs=[vspec()] * 4,
        out_specs=[vspec()] * 2,
        out_shape=[part] * 2,
        compiler_params=params(16),
        cost_estimate=pl.CostEstimate(flops=2 << 30, bytes_accessed=19 << 20, transcendentals=0),
        name="token_parts",
    )(h, d, wu, wd)


def ring(n, by):
    return [(i, (i + by) % n) for i in range(n)]


def step_both(x):
    pairs = []
    for z in range(8):
        pairs.append((z * 2, ((z + 1) % 8) * 2))
        pairs.append((z * 2 + 1, ((z - 1) % 8) * 2 + 1))
    return lax.ppermute(x, ("z", "c"), pairs)


def swap(x):
    return lax.ppermute(x, "c", [(0, 1), (1, 0)])


def add(*parts):
    total = parts[0].astype(F32)
    for p in parts[1:]:
        total = total + p.astype(F32)
    return total


def gather_over_tile(own, wu, wd):
    first, second = own, swap(own)
    shards = [first, second]
    for k in range(1, 5):
        if k == 3:
            first, wu = lax.optimization_barrier((first, wu))
        if k == 4:
            first, wd = lax.optimization_barrier((first, wd))
        first = step_both(first)
        shards += [first, swap(first)]
        if k < 4:
            second = step_both(second)
            shards += [second, swap(second)]
    return shards, wu, wd


def hop(t, stage, by):
    pairs = []
    for y in range(4):
        for x in range(4):
            for c in range(2):
                along_x = (stage + c) % 2 == 0
                to_y = y if along_x else (y + by) % 4
                to_x = (x + by) % 4 if along_x else x
                pairs.append(((y * 4 + x) * 2 + c, (to_y * 4 + to_x) * 2 + c))
    return lax.ppermute(t, ("y", "x", "c"), pairs)


def send_two_ways(far_a, far_b, nearer, before, stage):
    n = far_a.shape[0]
    from_left = hop(far_a, stage, 1)
    from_right = hop(far_b, stage, -1)
    left = hop(nearer.at[:n].add(from_left), stage, 1)
    right = hop(before.at[n:].add(from_right), stage, -1)
    return left, right


def ring_sum(far_a, far_b, nearer, before, own):
    left, right = send_two_ways(far_a, far_b, nearer, before, 0)

    def total(k, n):
        return add(own[k : k + n], left[k : k + n], right[k : k + n])

    sent = (total(k, n).astype(BF) for k, n in ((0, 4), (4, 4), (8, 8), (16, 8)))
    return total(24, 8), *send_two_ways(*sent, 1)


def finish_kernel(count_ref, *refs):
    first = lax.axis_index(("y", "x")) * 8
    for k in range(2):
        base, left, right = refs[3 * k : 3 * k + 3]
        out = refs[6 + k]
        for s in range(8):
            total = base[s] + left[s].astype(F32) + right[s].astype(F32)
            total = jnp.where(first + s < count_ref[0], total * (1.0 / 16), 0.0)
            out[0, s] = total.T if k == 0 else total


def finish(count, up, down):
    shape = (1, 8, SIDE, SIDE)
    return pl.pallas_call(
        finish_kernel,
        grid=(1,),
        in_specs=[sspec()] + [whole(8, SIDE, SIDE)] * 6,
        out_specs=[whole(*shape)] * 2,
        out_shape=[jax.ShapeDtypeStruct(shape, F32)] * 2,
        compiler_params=params(16),
        cost_estimate=pl.CostEstimate(flops=1 << 20, bytes_accessed=3 << 20, transcendentals=0),
        name="finish",
    )(count, *up, *down)


def owner_sum_kernel(terms_ref, mixed_ref, grad_in_ref):
    for k, out in enumerate((mixed_ref, grad_in_ref)):
        total = terms_ref[0, k].astype(F32)
        for z in range(1, 8):
            total = total + terms_ref[z, k].astype(F32)
        out[...] = total.astype(BF)


def owner_sum(terms):
    shape = terms.shape[2:]
    return pl.pallas_call(
        owner_sum_kernel,
        grid=(1,),
        in_specs=[whole(*terms.shape)],
        out_specs=[whole(*shape)] * 2,
        out_shape=[jax.ShapeDtypeStruct(shape, BF)] * 2,
        compiler_params=params(16),
        cost_estimate=pl.CostEstimate(flops=1 << 19, bytes_accessed=1 << 20, transcendentals=0),
        name="owner_sum",
    )(terms)


def body(tokens, grad_out, up_tiles, down_tiles, tile_rows, tile_cols, tile_count):
    where = tile_rows[0] * COLS + tile_cols[0]
    wu = dense(where, tile_count, up_tiles, True)
    wd = dense(where, tile_count, down_tiles, False)
    shards, wu, wd = gather_over_tile(jnp.stack([tokens, grad_out]), wu, wd)
    h, d, x, dy, dt, ht, *far = forward(where, shards, wu, wd)
    rest = rest_parts(where, x, dy, dt, ht)
    h, d, _ = lax.optimization_barrier((h, d, rest[0]))
    send, keep = token_parts(h, d, wu, wd)
    pieces = add(keep, swap(send)).astype(BF)
    up = ring_sum(far[0], far[2], *rest[0::2])
    pieces, down_next = lax.optimization_barrier((pieces, rest[1]))
    down = ring_sum(far[1], far[3], down_next, rest[3], rest[5])
    mixed, grad_in = owner_sum(lax.all_to_all(pieces, "z", 0, 0, tiled=True))
    grad_up, grad_down = finish(tile_count, up, down)
    return mixed, grad_in, grad_up, grad_down


def solution(mesh):
    grid = Mesh(mesh.devices.reshape(4, 4, 8, 2), ("y", "x", "z", "c"))
    dp, tile = ("y", "x"), ("z", "c")
    placed = (
        P(dp, tile),
        P(dp, tile),
        P(tile, None, None, None),
        P(tile, None, None, None),
        P(tile, None),
        P(tile, None),
        P(tile),
    )
    return jax.shard_map(
        body,
        mesh=grid,
        in_specs=placed,
        out_specs=(P(dp, tile), P(dp, tile), P(tile, dp, None, None), P(tile, dp, None, None)),
        check_vma=False,
    )
```

time: 118 us -> 124 us (1.051)
  waiting for transfers between devices: 45 us -> 35.7 us
  starting transfers between devices: 36.8 us -> 44.1 us
  Pallas kernels: 14.7 us -> 21.9 us
  local copies, waits for them, and re-layouts: 7.34 us -> 2.19 us
  other arithmetic: 12.2 us -> 17.1 us
    ppermute x10 -> x16, starting transfers between devices: 11.9 us -> 24.2 us  [hop(): return lax.ppermute(t, ('y', 'x', 'c'), pairs)]
    scatter-add x0 -> x8, other arithmetic: none -> 8.37 us  [the longest x4 4.21 us: send_two_ways(): left = hop(nearer.at[:n].add(from_left), stage, 1)]
    ppermute x10 -> x16, waiting for transfers between devices: 33 us -> 24.8 us  [hop(): return lax.ppermute(t, ('y', 'x', 'c'), pairs)]
    pallas_call x3 -> x7, Pallas kernels: 14.7 us -> 21.9 us  [the longest x1 6.53 us: rest_parts(): pl.pallas_call(rest_kernel, in_specs=[sspec()] + [vspec()] * 4, out_specs...]
    unnamed x9 -> x4, local copies, waits for them, and re-layouts: 6.68 us -> 2.19 us
    all_to_all x1, starting transfers between devices: 7.38 us -> 5.06 us  [body(): mixed, grad_in = owner_sum(lax.all_to_all(pieces, 'z', 0, 0, tiled=True))]
    add x2 -> x1, other arithmetic: 2.99 us -> 0.68 us  [body(): where = tile_rows[0] * COLS + tile_cols[0]]
    all_to_all x1, waiting for transfers between devices: 2.12 us -> 0.01 us  [body(): mixed, grad_in = owner_sum(lax.all_to_all(pieces, 'z', 0, 0, tiled=True))]
  transfers between devices with their start and end apart: 27 -> 33, of which waited for: 13 -> 11; matrix products, arithmetic and copies ran while one was open for 9% -> 13% of each run, Pallas kernels for 5% -> 12%
where the time goes in v4:
time: 124 us; the launch traced here: 122 us
  starting transfers between devices  44.1 us (36%)
  waiting for transfers between devices  35.7 us (29%)
  Pallas kernels  21.9 us (18%)
  other arithmetic  17.1 us (14%)
  local copies, waits for them, and re-layouts  2.19 us (2%)
  between operations  1.44 us (1%)
    ppermute x16, waiting for transfers between devices, hop(): return lax.ppermute(t, ('y', 'x', 'c'), pairs)  24.8 us
    ppermute x16, starting transfers between devices, hop(): return lax.ppermute(t, ('y', 'x', 'c'), pairs)  24.2 us
    ppermute x7, starting transfers between devices, step_both(): return lax.ppermute(x, ('z', 'c'), pairs)  10 us
    ppermute x7, waiting for transfers between devices, step_both(): return lax.ppermute(x, ('z', 'c'), pairs)  9.59 us
    pallas_call x1, Pallas kernels, rest_parts(): pl.pallas_call(rest_kernel, in_specs=[sspec()] + [vspec()] * 4, out_specs...  6.53 us
    pallas_call x1, Pallas kernels, forward(): pl.pallas_call(forward_kernel, in_specs=[sspec()] + [pl.BlockSpec(memory_...  6.15 us
    convert_element_type x4, other arithmetic, ring_sum(): total(k, n).astype(BF)  5.82 us
    all_to_all x1, starting transfers between devices, body(): mixed, grad_in = owner_sum(lax.all_to_all(pieces, 'z', 0, 0, tiled=True))  5.06 us
  transfers between devices with their start and end apart: 33, of which 11 were waited for; matrix products, arithmetic and copies ran while one was open for 13% of the time, Pallas kernels for 12%

profile of v4, /device:TPU:6, one launch (start us, length us, event | category | flops | bytes accessed | tf_op | source)
XLA Modules:
  0.0 122.4 jit_solution(17717580315443270254)
XLA Ops:
  1.5 2.0 %collective-permute-start.1 = (bf16[2,128,256]{2,1,0:T(8,128)(2,1)S(1)}, bf16[2,128,256]{2,1,0:T(8,128)(2,1)S(1)}, u32[]{:S(2)}, u32[]{:S(2)}) collective-permute-start(bf16[2,128,256]{2,1,0:T(8,128)(2,1)S(1)} %pad_maximum_fusion.refs_0_), channel_id=1, source_target_pairs={{0,2},{1,15},{2,4},{3,1},{4,6},{5,3},{6,8},{7,5},{8,10},{9,7},{10,... | collective-permute-start | bytes 393224 | tf_op jit(solution)/shard_map/ppermute | solution.py:219
  3.5 3.5 %collective-permute-start = (bf16[2,128,256]{2,1,0:T(8,128)(2,1)S(1)}, bf16[2,128,256]{2,1,0:T(8,128)(2,1)S(1)}, u32[]{:S(2)}, u32[]{:S(2)}) collective-permute-start(bf16[2,128,256]{2,1,0:T(8,128)(2,1)S(1)} %pad_maximum_fusion.refs_0_), channel_id=1, source_target_pairs={{0,1},{1,0},{2,3},{3,2},{4,5},{5,4},{6,7},{7,6},{8,9},{9,8},{10,11... | collective-permute-start | bytes 393224 | tf_op jit(solution)/shard_map/ppermute | solution.py:223
  7.7 2.7 %collective-permute-done.1.refs_2_ = bf16[2,128,256]{2,1,0:T(8,128)(2,1)S(1)} collective-permute-done((bf16[2,128,256]{2,1,0:T(8,128)(2,1)S(1)}, bf16[2,128,256]{2,1,0:T(8,128)(2,1)S(1)}, u32[]{:S(2)}, u32[]{:S(2)}) %collective-permute-start.1) | collective-permute-done | bytes 131104 | tf_op jit(solution)/shard_map/ppermute | solution.py:219
  11.1 2.2 %copy-done = bf16[1,128,128,128]{3,2,1,0:T(8,128)(2,1)S(1)} copy-done((bf16[1,128,128,128]{3,2,1,0:T(8,128)(2,1)S(1)}, bf16[1,128,128,128]{3,2,1,0:T(8,128)(2,1)}, u32[]{:S(2)}) %copy-start) | copy-done | bytes 4194328
  14.9 1.7 %collective-permute-done.5.refs_6_ = bf16[2,128,256]{2,1,0:T(8,128)(2,1)S(1)} collective-permute-done((bf16[2,128,256]{2,1,0:T(8,128)(2,1)S(1)}, bf16[2,128,256]{2,1,0:T(8,128)(2,1)S(1)}, u32[]{:S(2)}, u32[]{:S(2)}) %collective-permute-start.5) | collective-permute-done | bytes 131104 | tf_op jit(solution)/shard_map/ppermute | solution.py:219
  16.6 1.9 %collective-permute-start.9 = (bf16[2,128,256]{2,1,0:T(8,128)(2,1)S(1)}, bf16[2,128,256]{2,1,0:T(8,128)(2,1)S(1)}, u32[]{:S(2)}, u32[]{:S(2)}) collective-permute-start(bf16[2,128,256]{2,1,0:T(8,128)(2,1)S(1)} %collective-permute-done.5.refs_6_), channel_id=1, source_target_pairs={{0,2},{1,15},{2,4},{3,1},{4,6},{5,3},{6,8},{7,5},{8,10},{9,7},{10,... | collective-permute-start | bytes 393224 | tf_op jit(solution)/shard_map/ppermute | solution.py:219
  18.5 3.0 %collective-permute-start.7 = (bf16[2,128,256]{2,1,0:T(8,128)(2,1)S(1)}, bf16[2,128,256]{2,1,0:T(8,128)(2,1)S(1)}, u32[]{:S(2)}, u32[]{:S(2)}) collective-permute-start(bf16[2,128,256]{2,1,0:T(8,128)(2,1)S(1)} %collective-permute-done.3.refs_4_), channel_id=1, source_target_pairs={{0,2},{1,15},{2,4},{3,1},{4,6},{5,3},{6,8},{7,5},{8,10},{9,7},{10,... | collective-permute-start | bytes 393224 | tf_op jit(solution)/shard_map/ppermute | solution.py:219
  24.7 1.7 %collective-permute-start.11 = (bf16[2,128,256]{2,1,0:T(8,128)(2,1)S(1)}, bf16[2,128,256]{2,1,0:T(8,128)(2,1)S(1)}, u32[]{:S(2)}, u32[]{:S(2)}) collective-permute-start(bf16[2,128,256]{2,1,0:T(8,128)(2,1)S(1)} %collective-permute-done.7.refs_8_), channel_id=1, source_target_pairs={{0,2},{1,15},{2,4},{3,1},{4,6},{5,3},{6,8},{7,5},{8,10},{9,7},{10,... | collective-permute-start | bytes 393224 | tf_op jit(solution)/shard_map/ppermute | solution.py:219
  28.4 2.4 %collective-permute-done.11.refs_12_ = bf16[2,128,256]{2,1,0:T(8,128)(2,1)S(1)} collective-permute-done((bf16[2,128,256]{2,1,0:T(8,128)(2,1)S(1)}, bf16[2,128,256]{2,1,0:T(8,128)(2,1)S(1)}, u32[]{:S(2)}, u32[]{:S(2)}) %collective-permute-start.11) | collective-permute-done | bytes 131104 | tf_op jit(solution)/shard_map/ppermute | solution.py:219
  30.8 1.7 %collective-permute-done.13.refs_14_ = bf16[2,128,256]{2,1,0:T(8,128)(2,1)S(1)} collective-permute-done((bf16[2,128,256]{2,1,0:T(8,128)(2,1)S(1)}, bf16[2,128,256]{2,1,0:T(8,128)(2,1)S(1)}, u32[]{:S(2)}, u32[]{:S(2)}) %collective-permute-start.13) | collective-permute-done | bytes 131104 | tf_op jit(solution)/shard_map/ppermute | solution.py:219
  33.9 6.1 %forward.1 = (bf16[128,1024]{1,0:T(8,128)(2,1)S(1)}, bf16[128,1024]{1,0:T(8,128)(2,1)S(1)}, bf16[128,4096]{1,0:T(8,128)(2,1)S(1)}, bf16[128,4096]{1,0:T(8,128)(2...) custom-call(s32[128]{0:T(128)S(1)} %add_bitcast_fusion.where, ...), custom_call_target="tpu_custom_call" | custom-call | flops 3221225472 | bytes 23068672 | tf_op jit(solution)/shard_map/forward/pallas_call | solution.py:149
  41.0 2.4 %collective-permute-start.16 = (bf16[16,128,128]{2,1,0:T(8,128)(2,1)S(1)}, bf16[16,128,128]{2,1,0:T(8,128)(2,1)S(1)}, u32[]{:S(2)}, u32[]{:S(2)}) collective-permute-start(bf16[16,128,128]{2,1,0:T(8,128)(2,1)S(1)} %get-tuple-element.150), channel_id=1, source_target_pairs={{0,16},{1,65},{16,32},{17,81},{32,48},{33,97},{48,0},{49,113},{64,... | collective-permute-start | bytes 1572872 | tf_op jit(solution)/shard_map/ppermute | solution.py:258
  43.4 6.5 %rest_parts.1 = (bf16[32,128,128]{2,1,0:T(8,128)(2,1)}, bf16[32,128,128]{2,1,0:T(8,128)(2,1)}, bf16[32,128,128]{2,1,0:T(8,128)(2,1)}, bf16[32,128,128]{2,1,0:T(8...) custom-call(s32[128]{0:T(128)S(1)} %add_bitcast_fusion.where, ...), custom_call_target="tpu_custom_call" | custom-call | flops 1073741824 | bytes 9437184 | tf_op jit(solution)/shard_map/rest_parts/pallas_call | solution.py:166
  49.9 4.1 %token_parts.1 = (bf16[8,2,128,256]{3,2,1,0:T(8,128)(2,1)S(1)}, bf16[8,2,128,256]{3,2,1,0:T(8,128)(2,1)S(1)}) custom-call(bf16[128,1024]{1,0:T(8,128)(2,1)S(1)} %get-tuple-element.141.h_ref, bf16[128,1024]{1,0:T(8,128)(2,1)S(1)} %get-tuple-element.142.d_ref, bf16[4096,1024]{1,0:T(8,128)(2,1)S(1)} %dense_up.1.refs_16_.wu_ref, ...), custom_call_target="tpu_custom_call" | custom-call | flops 2147483648 | bytes 19922944 | tf_op jit(solution)/shard_map/token_parts/pallas_call | solution.py:199
  54.6 2.0 %add_dynamic-update-slice_fusion.2 = bf16[32,128,128]{2,1,0:T(8,128)(2,1)} fusion(bf16[32,128,128]{2,1,0:T(8,128)(2,1)} %get-tuple-element.151, bf16[16,128,128]{2,1,0:T(8,128)(2,1)S(1)} %collective-permute-done.18), kind=kLoop, calls=%fused_computation.9 | loop fusion | flops 1048576 | bytes 1572864 | tf_op jit(solution)/shard_map/scatter-add | solution.py:266
  57.1 2.0 %add_dynamic-update-slice_fusion.3 = bf16[32,128,128]{2,1,0:T(8,128)(2,1)} fusion(bf16[32,128,128]{2,1,0:T(8,128)(2,1)} %get-tuple-element.140, bf16[16,128,128]{2,1,0:T(8,128)(2,1)S(1)} %collective-permute-done.16), kind=kLoop, calls=%fused_computation.10 | loop fusion | flops 1048576 | bytes 1572864 | tf_op jit(solution)/shard_map/scatter-add | solution.py:265
  59.1 2.7 %collective-permute-start.17 = (bf16[32,128,128]{2,1,0:T(8,128)(2,1)}, bf16[32,128,128]{2,1,0:T(8,128)(2,1)}, u32[]{:S(2)}, u32[]{:S(2)}) collective-permute-start(bf16[32,128,128]{2,1,0:T(8,128)(2,1)} %add_dynamic-update-slice_fusion.3), channel_id=1, source_target_pairs={{0,16},{1,65},{16,32},{17,81},{32,48},{33,97},{48,0},{49,113},{64,... | collective-permute-start | bytes 3145736 | tf_op jit(solution)/shard_map/ppermute | solution.py:258
  61.9 1.7 %collective-permute-start.24 = (bf16[16,128,128]{2,1,0:T(8,128)(2,1)S(1)}, bf16[16,128,128]{2,1,0:T(8,128)(2,1)S(1)}, u32[]{:S(2)}, u32[]{:S(2)}) collective-permute-start(bf16[16,128,128]{2,1,0:T(8,128)(2,1)S(1)} %get-tuple-element.155), channel_id=1, source_target_pairs={{0,16},{1,65},{16,32},{17,81},{32,48},{33,97},{48,0},{49,113},{64,... | collective-permute-start | bytes 1572872 | tf_op jit(solution)/shard_map/ppermute | solution.py:258
  64.6 2.0 %add_dynamic-update-slice_fusion = bf16[32,128,128]{2,1,0:T(8,128)(2,1)} fusion(bf16[32,128,128]{2,1,0:T(8,128)(2,1)} %get-tuple-element.156, bf16[16,128,128]{2,1,0:T(8,128)(2,1)S(1)} %collective-permute-done.26), kind=kLoop, calls=%fused_computation.4 | loop fusion | flops 1048576 | bytes 1572864 | tf_op jit(solution)/shard_map/scatter-add | solution.py:266
  67.9 12.1 %collective-permute-done.24 = bf16[16,128,128]{2,1,0:T(8,128)(2,1)S(1)} collective-permute-done((bf16[16,128,128]{2,1,0:T(8,128)(2,1)S(1)}, bf16[16,128,128]{2,1,0:T(8,128)(2,1)S(1)}, u32[]{:S(2)}, u32[]{:S(2)}) %collective-permute-start.24) | collective-permute-done | bytes 524320 | tf_op jit(solution)/shard_map/ppermute | solution.py:258
  80.0 2.0 %add_dynamic-update-slice_fusion.1 = bf16[32,128,128]{2,1,0:T(8,128)(2,1)} fusion(bf16[32,128,128]{2,1,0:T(8,128)(2,1)} %get-tuple-element.154, bf16[16,128,128]{2,1,0:T(8,128)(2,1)S(1)} %collective-permute-done.24), kind=kLoop, calls=%fused_computation.5 | loop fusion | flops 1048576 | bytes 1572864 | tf_op jit(solution)/shard_map/scatter-add | solution.py:265
  82.0 3.7 %collective-permute-start.25 = (bf16[32,128,128]{2,1,0:T(8,128)(2,1)}, bf16[32,128,128]{2,1,0:T(8,128)(2,1)}, u32[]{:S(2)}, u32[]{:S(2)}) collective-permute-start(bf16[32,128,128]{2,1,0:T(8,128)(2,1)} %add_dynamic-update-slice_fusion.1), channel_id=1, source_target_pairs={{0,16},{1,65},{16,32},{17,81},{32,48},{33,97},{48,0},{49,113},{64,... | collective-permute-start | bytes 3145736 | tf_op jit(solution)/shard_map/ppermute | solution.py:258
  85.7 5.1 %all-to-all-start = ((bf16[8,2,128,256]{3,2,1,0:T(8,128)(2,1)}), bf16[8,2,128,256]{3,2,1,0:T(8,128)(2,1)S(1)}, u32[]{:S(2)}, u32[]{:S(2)}) async-start(bf16[8,2,128,256]{3,2,1,0:T(8,128)(2,1)} %add_convert_fusion), calls=%async_computation | async-start | bytes 2097152 | tf_op jit(solution)/shard_map/all_to_all | solution.py:340
  92.0 3.0 %collective-permute-start.22 = (bf16[4,128,128]{2,1,0:T(8,128)(2,1)S(1)}, bf16[4,128,128]{2,1,0:T(8,128)(2,1)S(1)}, u32[]{:S(2)}, u32[]{:S(2)}) collective-permute-start(bf16[4,128,128]{2,1,0:T(8,128)(2,1)S(1)} %get-tuple-element.165), channel_id=1, source_target_pairs={{0,192},{1,49},{16,208},{17,1},{32,224},{33,17},{48,240},{49,33},{... | collective-permute-start | bytes 393224 | tf_op jit(solution)/shard_map/ppermute | solution.py:258
  95.0 1.7 %add_convert_fusion.3 = (bf16[8,128,128]{2,1,0:T(8,128)(2,1)S(1)}, bf16[8,128,128]{2,1,0:T(8,128)(2,1)S(1)}, f32[8,128,128]{2,1,0:T(8,128)S(1)}) fusion(bf16[32,128,128]{2,1,0:T(8,128)(2,1)} %collective-permute-done.19, bf16[32,128,128]{2,1,0:T(8,128)(2,1)} %collective-permute-done.17, bf16[32,128,128]{2,1,0:T(8,128)(2,1)S(1)} %get-tuple-element.149), kind=kLoop, calls=%fused_computation.6 | loop fusion | flops 2228224 | bytes 3407872 | tf_op jit(solution)/shard_map/convert_element_type | solution.py:276
  96.7 4.9 %collective-permute-done.20 = bf16[4,128,128]{2,1,0:T(8,128)(2,1)S(1)} collective-permute-done((bf16[4,128,128]{2,1,0:T(8,128)(2,1)S(1)}, bf16[4,128,128]{2,1,0:T(8,128)(2,1)S(1)}, u32[]{:S(2)}, u32[]{:S(2)}) %collective-permute-start.20) | collective-permute-done | bytes 131104 | tf_op jit(solution)/shard_map/ppermute | solution.py:258
  101.9 3.3 %collective-permute-start.23 = (bf16[8,128,128]{2,1,0:T(8,128)(2,1)S(1)}, bf16[8,128,128]{2,1,0:T(8,128)(2,1)S(1)}, u32[]{:S(2)}, u32[]{:S(2)}) collective-permute-start(bf16[8,128,128]{2,1,0:T(8,128)(2,1)S(1)} %fusion.2), channel_id=1, source_target_pairs={{0,192},{1,49},{16,208},{17,1},{32,224},{33,17},{48,240},{49,33},{... | collective-permute-start | bytes 786440 | tf_op jit(solution)/shard_map/ppermute | solution.py:258
  106.5 2.0 %collective-permute-start.28 = (bf16[4,128,128]{2,1,0:T(8,128)(2,1)S(1)}, bf16[4,128,128]{2,1,0:T(8,128)(2,1)S(1)}, u32[]{:S(2)}, u32[]{:S(2)}) collective-permute-start(bf16[4,128,128]{2,1,0:T(8,128)(2,1)S(1)} %get-tuple-element.161), channel_id=1, source_target_pairs={{0,64},{1,17},{16,80},{17,33},{32,96},{33,49},{48,112},{49,1},{64,... | collective-permute-start | bytes 393224 | tf_op jit(solution)/shard_map/ppermute | solution.py:258
  108.5 1.7 %add_convert_fusion.1 = (bf16[8,128,128]{2,1,0:T(8,128)(2,1)S(1)}, bf16[8,128,128]{2,1,0:T(8,128)(2,1)S(1)}, f32[8,128,128]{2,1,0:T(8,128)S(1)}) fusion(bf16[32,128,128]{2,1,0:T(8,128)(2,1)} %collective-permute-done.27, bf16[32,128,128]{2,1,0:T(8,128)(2,1)} %collective-permute-done.25, bf16[32,128,128]{2,1,0:T(8,128)(2,1)S(1)} %get-tuple-element.153), kind=kLoop, calls=%fused_computation.1 | loop fusion | flops 2228224 | bytes 3407872 | tf_op jit(solution)/shard_map/convert_element_type | solution.py:276
  110.2 2.5 %collective-permute-done.28 = bf16[4,128,128]{2,1,0:T(8,128)(2,1)S(1)} collective-permute-done((bf16[4,128,128]{2,1,0:T(8,128)(2,1)S(1)}, bf16[4,128,128]{2,1,0:T(8,128)(2,1)S(1)}, u32[]{:S(2)}, u32[]{:S(2)}) %collective-permute-start.28) | collective-permute-done | bytes 131104 | tf_op jit(solution)/shard_map/ppermute | solution.py:258
  113.7 2.6 %collective-permute-start.31 = (bf16[8,128,128]{2,1,0:T(8,128)(2,1)S(1)}, bf16[8,128,128]{2,1,0:T(8,128)(2,1)S(1)}, u32[]{:S(2)}, u32[]{:S(2)}) collective-permute-start(bf16[8,128,128]{2,1,0:T(8,128)(2,1)S(1)} %fusion), channel_id=1, source_target_pairs={{0,192},{1,49},{16,208},{17,1},{32,224},{33,17},{48,240},{49,33},{... | collective-permute-start | bytes 786440 | tf_op jit(solution)/shard_map/ppermute | solution.py:258
  116.3 4.2 %collective-permute-done.29.refs_4_ = bf16[8,128,128]{2,1,0:T(8,128)(2,1)S(1)} collective-permute-done((bf16[8,128,128]{2,1,0:T(8,128)(2,1)S(1)}, bf16[8,128,128]{2,1,0:T(8,128)(2,1)S(1)}, u32[]{:S(2)}, u32[]{:S(2)}) %collective-permute-start.29) | collective-permute-done | bytes 262176 | tf_op jit(solution)/shard_map/ppermute | solution.py:258
  (60 shorter events, 19.8 us)
Async XLA Ops:
  1.5 8.9 %collective-permute-start.1 = (bf16[2,128,256]{2,1,0:T(8,128)(2,1)S(1)}, bf16[2,128,256]{2,1,0:T(8,128)(2,1)S(1)}, u32[]{:S(2)}, u32[]{:S(2)}) collective-permute-start(bf16[2,128,256]{2,1,0:T(8,128)(2,1)S(1)} %pad_maximum_fusion.refs_0_), channel_id=1, source_target_pairs={{0,2},{1,15},{2,4},{3,1},{4,6},{5,3},{6,8},{7,5},{8,10},{9,7},{10,... | collective-permute-start | bytes 393224 | tf_op jit(solution)/shard_map/ppermute | solution.py:219
  3.5 6.9 %collective-permute-start = (bf16[2,128,256]{2,1,0:T(8,128)(2,1)S(1)}, bf16[2,128,256]{2,1,0:T(8,128)(2,1)S(1)}, u32[]{:S(2)}, u32[]{:S(2)}) collective-permute-start(bf16[2,128,256]{2,1,0:T(8,128)(2,1)S(1)} %pad_maximum_fusion.refs_0_), channel_id=1, source_target_pairs={{0,1},{1,0},{2,3},{3,2},{4,5},{5,4},{6,7},{7,6},{8,9},{9,8},{10,11... | collective-permute-start | bytes 393224 | tf_op jit(solution)/shard_map/ppermute | solution.py:223
  10.4 6.2 %collective-permute-start.5 = (bf16[2,128,256]{2,1,0:T(8,128)(2,1)S(1)}, bf16[2,128,256]{2,1,0:T(8,128)(2,1)S(1)}, u32[]{:S(2)}, u32[]{:S(2)}) collective-permute-start(bf16[2,128,256]{2,1,0:T(8,128)(2,1)S(1)} %collective-permute-done.1.refs_2_), channel_id=1, source_target_pairs={{0,2},{1,15},{2,4},{3,1},{4,6},{5,3},{6,8},{7,5},{8,10},{9,7},{10,... | collective-permute-start | bytes 393224 | tf_op jit(solution)/shard_map/ppermute | solution.py:219
  10.4 8.1 %collective-permute-start.3 = (bf16[2,128,256]{2,1,0:T(8,128)(2,1)S(1)}, bf16[2,128,256]{2,1,0:T(8,128)(2,1)S(1)}, u32[]{:S(2)}, u32[]{:S(2)}) collective-permute-start(bf16[2,128,256]{2,1,0:T(8,128)(2,1)S(1)} %collective-permute-done.refs_1_), channel_id=1, source_target_pairs={{0,2},{1,15},{2,4},{3,1},{4,6},{5,3},{6,8},{7,5},{8,10},{9,7},{10,... | collective-permute-start | bytes 393224 | tf_op jit(solution)/shard_map/ppermute | solution.py:219
  16.6 7.1 %collective-permute-start.9 = (bf16[2,128,256]{2,1,0:T(8,128)(2,1)S(1)}, bf16[2,128,256]{2,1,0:T(8,128)(2,1)S(1)}, u32[]{:S(2)}, u32[]{:S(2)}) collective-permute-start(bf16[2,128,256]{2,1,0:T(8,128)(2,1)S(1)} %collective-permute-done.5.refs_6_), channel_id=1, source_target_pairs={{0,2},{1,15},{2,4},{3,1},{4,6},{5,3},{6,8},{7,5},{8,10},{9,7},{10,... | collective-permute-start | bytes 393224 | tf_op jit(solution)/shard_map/ppermute | solution.py:219
  18.5 6.2 %collective-permute-start.7 = (bf16[2,128,256]{2,1,0:T(8,128)(2,1)S(1)}, bf16[2,128,256]{2,1,0:T(8,128)(2,1)S(1)}, u32[]{:S(2)}, u32[]{:S(2)}) collective-permute-start(bf16[2,128,256]{2,1,0:T(8,128)(2,1)S(1)} %collective-permute-done.3.refs_4_), channel_id=1, source_target_pairs={{0,2},{1,15},{2,4},{3,1},{4,6},{5,3},{6,8},{7,5},{8,10},{9,7},{10,... | collective-permute-start | bytes 393224 | tf_op jit(solution)/shard_map/ppermute | solution.py:219
  23.1 4.7 %collective-permute-start.2 = (bf16[2,128,256]{2,1,0:T(8,128)(2,1)S(1)}, bf16[2,128,256]{2,1,0:T(8,128)(2,1)S(1)}, u32[]{:S(2)}, u32[]{:S(2)}) collective-permute-start(bf16[2,128,256]{2,1,0:T(8,128)(2,1)S(1)} %collective-permute-done.1.refs_2_), channel_id=1, source_target_pairs={{0,1},{1,0},{2,3},{3,2},{4,5},{5,4},{6,7},{7,6},{8,9},{9,8},{10,11... | collective-permute-start | bytes 393224 | tf_op jit(solution)/shard_map/ppermute | solution.py:223
  23.2 5.2 %collective-permute-start.6 = (bf16[2,128,256]{2,1,0:T(8,128)(2,1)S(1)}, bf16[2,128,256]{2,1,0:T(8,128)(2,1)S(1)}, u32[]{:S(2)}, u32[]{:S(2)}) collective-permute-start(bf16[2,128,256]{2,1,0:T(8,128)(2,1)S(1)} %collective-permute-done.5.refs_6_), channel_id=1, source_target_pairs={{0,1},{1,0},{2,3},{3,2},{4,5},{5,4},{6,7},{7,6},{8,9},{9,8},{10,11... | collective-permute-start | bytes 393224 | tf_op jit(solution)/shard_map/ppermute | solution.py:223
  24.7 6.2 %collective-permute-start.11 = (bf16[2,128,256]{2,1,0:T(8,128)(2,1)S(1)}, bf16[2,128,256]{2,1,0:T(8,128)(2,1)S(1)}, u32[]{:S(2)}, u32[]{:S(2)}) collective-permute-start(bf16[2,128,256]{2,1,0:T(8,128)(2,1)S(1)} %collective-permute-done.7.refs_8_), channel_id=1, source_target_pairs={{0,2},{1,15},{2,4},{3,1},{4,6},{5,3},{6,8},{7,5},{8,10},{9,7},{10,... | collective-permute-start | bytes 393224 | tf_op jit(solution)/shard_map/ppermute | solution.py:219
  26.4 6.2 %collective-permute-start.13 = (bf16[2,128,256]{2,1,0:T(8,128)(2,1)S(1)}, bf16[2,128,256]{2,1,0:T(8,128)(2,1)S(1)}, u32[]{:S(2)}, u32[]{:S(2)}) collective-permute-start(bf16[2,128,256]{2,1,0:T(8,128)(2,1)S(1)} %collective-permute-done.9.refs_10_), channel_id=1, source_target_pairs={{0,2},{1,15},{2,4},{3,1},{4,6},{5,3},{6,8},{7,5},{8,10},{9,7},{10,... | collective-permute-start | bytes 393224 | tf_op jit(solution)/shard_map/ppermute | solution.py:219
  27.8 4.8 %collective-permute-start.4 = (bf16[2,128,256]{2,1,0:T(8,128)(2,1)S(1)}, bf16[2,128,256]{2,1,0:T(8,128)(2,1)S(1)}, u32[]{:S(2)}, u32[]{:S(2)}) collective-permute-start(bf16[2,128,256]{2,1,0:T(8,128)(2,1)S(1)} %collective-permute-done.3.refs_4_), channel_id=1, source_target_pairs={{0,1},{1,0},{2,3},{3,2},{4,5},{5,4},{6,7},{7,6},{8,9},{9,8},{10,11... | collective-permute-start | bytes 393224 | tf_op jit(solution)/shard_map/ppermute | solution.py:223
  27.8 4.8 %collective-permute-start.8 = (bf16[2,128,256]{2,1,0:T(8,128)(2,1)S(1)}, bf16[2,128,256]{2,1,0:T(8,128)(2,1)S(1)}, u32[]{:S(2)}, u32[]{:S(2)}) collective-permute-start(bf16[2,128,256]{2,1,0:T(8,128)(2,1)S(1)} %collective-permute-done.7.refs_8_), channel_id=1, source_target_pairs={{0,1},{1,0},{2,3},{3,2},{4,5},{5,4},{6,7},{7,6},{8,9},{9,8},{10,11... | collective-permute-start | bytes 393224 | tf_op jit(solution)/shard_map/ppermute | solution.py:223
  28.3 4.3 %collective-permute-start.10 = (bf16[2,128,256]{2,1,0:T(8,128)(2,1)S(1)}, bf16[2,128,256]{2,1,0:T(8,128)(2,1)S(1)}, u32[]{:S(2)}, u32[]{:S(2)}) collective-permute-start(bf16[2,128,256]{2,1,0:T(8,128)(2,1)S(1)} %collective-permute-done.9.refs_10_), channel_id=1, source_target_pairs={{0,1},{1,0},{2,3},{3,2},{4,5},{5,4},{6,7},{7,6},{8,9},{9,8},{10,11... | collective-permute-start | bytes 393224 | tf_op jit(solution)/shard_map/ppermute | solution.py:223
  30.8 1.8 %collective-permute-start.12 = (bf16[2,128,256]{2,1,0:T(8,128)(2,1)S(1)}, bf16[2,128,256]{2,1,0:T(8,128)(2,1)S(1)}, u32[]{:S(2)}, u32[]{:S(2)}) collective-permute-start(bf16[2,128,256]{2,1,0:T(8,128)(2,1)S(1)} %collective-permute-done.11.refs_12_), channel_id=1, source_target_pairs={{0,1},{1,0},{2,3},{3,2},{4,5},{5,4},{6,7},{7,6},{8,9},{9,8},{10,11... | collective-permute-start | bytes 393224 | tf_op jit(solution)/shard_map/ppermute | solution.py:223
  40.1 14.5 %collective-permute-start.18 = (bf16[16,128,128]{2,1,0:T(8,128)(2,1)S(1)}, bf16[16,128,128]{2,1,0:T(8,128)(2,1)S(1)}, u32[]{:S(2)}, u32[]{:S(2)}) collective-permute-start(bf16[16,128,128]{2,1,0:T(8,128)(2,1)S(1)} %get-tuple-element.152), channel_id=1, source_target_pairs={{0,48},{1,193},{16,0},{17,209},{32,16},{33,225},{48,32},{49,241},{... | collective-permute-start | bytes 1572872 | tf_op jit(solution)/shard_map/ppermute | solution.py:258
  41.0 16.1 %collective-permute-start.16 = (bf16[16,128,128]{2,1,0:T(8,128)(2,1)S(1)}, bf16[16,128,128]{2,1,0:T(8,128)(2,1)S(1)}, u32[]{:S(2)}, u32[]{:S(2)}) collective-permute-start(bf16[16,128,128]{2,1,0:T(8,128)(2,1)S(1)} %get-tuple-element.150), channel_id=1, source_target_pairs={{0,16},{1,65},{16,32},{17,81},{32,48},{33,97},{48,0},{49,113},{64,... | collective-permute-start | bytes 1572872 | tf_op jit(solution)/shard_map/ppermute | solution.py:258
  54.0 12.6 %collective-permute-start.15 = (bf16[8,2,128,256]{3,2,1,0:T(8,128)(2,1)S(1)}, bf16[8,2,128,256]{3,2,1,0:T(8,128)(2,1)S(1)}, u32[]{:S(2)}, u32[]{:S(2)}) collective-permute-start(bf16[8,2,128,256]{3,2,1,0:T(8,128)(2,1)S(1)} %get-tuple-element.144), channel_id=1, source_target_pairs={{0,1},{1,0},{2,3},{3,2},{4,5},{5,4},{6,7},{7,6},{8,9},{9,8},{10,11... | collective-permute-start | bytes 3145736 | tf_op jit(solution)/shard_map/ppermute | solution.py:223
  54.1 10.5 %collective-permute-start.26 = (bf16[16,128,128]{2,1,0:T(8,128)(2,1)S(1)}, bf16[16,128,128]{2,1,0:T(8,128)(2,1)S(1)}, u32[]{:S(2)}, u32[]{:S(2)}) collective-permute-start(bf16[16,128,128]{2,1,0:T(8,128)(2,1)S(1)} %get-tuple-element.157), channel_id=1, source_target_pairs={{0,48},{1,193},{16,0},{17,209},{32,16},{33,225},{48,32},{49,241},{... | collective-permute-start | bytes 1572872 | tf_op jit(solution)/shard_map/ppermute | solution.py:258
  56.6 34.2 %collective-permute-start.19 = (bf16[32,128,128]{2,1,0:T(8,128)(2,1)}, bf16[32,128,128]{2,1,0:T(8,128)(2,1)}, u32[]{:S(2)}, u32[]{:S(2)}) collective-permute-start(bf16[32,128,128]{2,1,0:T(8,128)(2,1)} %add_dynamic-update-slice_fusion.2), channel_id=1, source_target_pairs={{0,48},{1,193},{16,0},{17,209},{32,16},{33,225},{48,32},{49,241},{... | collective-permute-start | bytes 3145736 | tf_op jit(solution)/shard_map/ppermute | solution.py:258
  59.1 31.6 %collective-permute-start.17 = (bf16[32,128,128]{2,1,0:T(8,128)(2,1)}, bf16[32,128,128]{2,1,0:T(8,128)(2,1)}, u32[]{:S(2)}, u32[]{:S(2)}) collective-permute-start(bf16[32,128,128]{2,1,0:T(8,128)(2,1)} %add_dynamic-update-slice_fusion.3), channel_id=1, source_target_pairs={{0,16},{1,65},{16,32},{17,81},{32,48},{33,97},{48,0},{49,113},{64,... | collective-permute-start | bytes 3145736 | tf_op jit(solution)/shard_map/ppermute | solution.py:258
  61.9 18.1 %collective-permute-start.24 = (bf16[16,128,128]{2,1,0:T(8,128)(2,1)S(1)}, bf16[16,128,128]{2,1,0:T(8,128)(2,1)S(1)}, u32[]{:S(2)}, u32[]{:S(2)}) collective-permute-start(bf16[16,128,128]{2,1,0:T(8,128)(2,1)S(1)} %get-tuple-element.155), channel_id=1, source_target_pairs={{0,16},{1,65},{16,32},{17,81},{32,48},{33,97},{48,0},{49,113},{64,... | collective-permute-start | bytes 1572872 | tf_op jit(solution)/shard_map/ppermute | solution.py:258
  66.6 38.6 %collective-permute-start.27 = (bf16[32,128,128]{2,1,0:T(8,128)(2,1)}, bf16[32,128,128]{2,1,0:T(8,128)(2,1)}, u32[]{:S(2)}, u32[]{:S(2)}) collective-permute-start(bf16[32,128,128]{2,1,0:T(8,128)(2,1)} %add_dynamic-update-slice_fusion), channel_id=1, source_target_pairs={{0,48},{1,193},{16,0},{17,209},{32,16},{33,225},{48,32},{49,241},{... | collective-permute-start | bytes 3145736 | tf_op jit(solution)/shard_map/ppermute | solution.py:258
  82.0 23.2 %collective-permute-start.25 = (bf16[32,128,128]{2,1,0:T(8,128)(2,1)}, bf16[32,128,128]{2,1,0:T(8,128)(2,1)}, u32[]{:S(2)}, u32[]{:S(2)}) collective-permute-start(bf16[32,128,128]{2,1,0:T(8,128)(2,1)} %add_dynamic-update-slice_fusion.1), channel_id=1, source_target_pairs={{0,16},{1,65},{16,32},{17,81},{32,48},{33,97},{48,0},{49,113},{64,... | collective-permute-start | bytes 3145736 | tf_op jit(solution)/shard_map/ppermute | solution.py:258
  85.7 36.0 %all-to-all-start = ((bf16[8,2,128,256]{3,2,1,0:T(8,128)(2,1)}), bf16[8,2,128,256]{3,2,1,0:T(8,128)(2,1)S(1)}, u32[]{:S(2)}, u32[]{:S(2)}) async-start(bf16[8,2,128,256]{3,2,1,0:T(8,128)(2,1)} %add_convert_fusion), calls=%async_computation | async-start | bytes 2097152 | tf_op jit(solution)/shard_map/all_to_all | solution.py:340
  92.0 9.8 %collective-permute-start.22 = (bf16[4,128,128]{2,1,0:T(8,128)(2,1)S(1)}, bf16[4,128,128]{2,1,0:T(8,128)(2,1)S(1)}, u32[]{:S(2)}, u32[]{:S(2)}) collective-permute-start(bf16[4,128,128]{2,1,0:T(8,128)(2,1)S(1)} %get-tuple-element.165), channel_id=1, source_target_pairs={{0,192},{1,49},{16,208},{17,1},{32,224},{33,17},{48,240},{49,33},{... | collective-permute-start | bytes 393224 | tf_op jit(solution)/shard_map/ppermute | solution.py:258
  95.0 6.6 %collective-permute-start.20 = (bf16[4,128,128]{2,1,0:T(8,128)(2,1)S(1)}, bf16[4,128,128]{2,1,0:T(8,128)(2,1)S(1)}, u32[]{:S(2)}, u32[]{:S(2)}) collective-permute-start(bf16[4,128,128]{2,1,0:T(8,128)(2,1)S(1)} %get-tuple-element.166), channel_id=1, source_target_pairs={{0,64},{1,17},{16,80},{17,33},{32,96},{33,49},{48,112},{49,1},{64,... | collective-permute-start | bytes 393224 | tf_op jit(solution)/shard_map/ppermute | solution.py:258
  101.7 14.6 %collective-permute-start.21 = (bf16[8,128,128]{2,1,0:T(8,128)(2,1)S(1)}, bf16[8,128,128]{2,1,0:T(8,128)(2,1)S(1)}, u32[]{:S(2)}, u32[]{:S(2)}) collective-permute-start(bf16[8,128,128]{2,1,0:T(8,128)(2,1)S(1)} %fusion.3), channel_id=1, source_target_pairs={{0,64},{1,17},{16,80},{17,33},{32,96},{33,49},{48,112},{49,1},{64,... | collective-permute-start | bytes 786440 | tf_op jit(solution)/shard_map/ppermute | solution.py:258
  101.9 14.4 %collective-permute-start.23 = (bf16[8,128,128]{2,1,0:T(8,128)(2,1)S(1)}, bf16[8,128,128]{2,1,0:T(8,128)(2,1)S(1)}, u32[]{:S(2)}, u32[]{:S(2)}) collective-permute-start(bf16[8,128,128]{2,1,0:T(8,128)(2,1)S(1)} %fusion.2), channel_id=1, source_target_pairs={{0,192},{1,49},{16,208},{17,1},{32,224},{33,17},{48,240},{49,33},{... | collective-permute-start | bytes 786440 | tf_op jit(solution)/shard_map/ppermute | solution.py:258
  106.4 7.2 %collective-permute-start.30 = (bf16[4,128,128]{2,1,0:T(8,128)(2,1)S(1)}, bf16[4,128,128]{2,1,0:T(8,128)(2,1)S(1)}, u32[]{:S(2)}, u32[]{:S(2)}) collective-permute-start(bf16[4,128,128]{2,1,0:T(8,128)(2,1)S(1)} %get-tuple-element.160), channel_id=1, source_target_pairs={{0,192},{1,49},{16,208},{17,1},{32,224},{33,17},{48,240},{49,33},{... | collective-permute-start | bytes 393224 | tf_op jit(solution)/shard_map/ppermute | solution.py:258
  106.5 6.2 %collective-permute-start.28 = (bf16[4,128,128]{2,1,0:T(8,128)(2,1)S(1)}, bf16[4,128,128]{2,1,0:T(8,128)(2,1)S(1)}, u32[]{:S(2)}, u32[]{:S(2)}) collective-permute-start(bf16[4,128,128]{2,1,0:T(8,128)(2,1)S(1)} %get-tuple-element.161), channel_id=1, source_target_pairs={{0,64},{1,17},{16,80},{17,33},{32,96},{33,49},{48,112},{49,1},{64,... | collective-permute-start | bytes 393224 | tf_op jit(solution)/shard_map/ppermute | solution.py:258
  112.8 7.7 %collective-permute-start.29 = (bf16[8,128,128]{2,1,0:T(8,128)(2,1)S(1)}, bf16[8,128,128]{2,1,0:T(8,128)(2,1)S(1)}, u32[]{:S(2)}, u32[]{:S(2)}) collective-permute-start(bf16[8,128,128]{2,1,0:T(8,128)(2,1)S(1)} %fusion.1), channel_id=1, source_target_pairs={{0,64},{1,17},{16,80},{17,33},{32,96},{33,49},{48,112},{49,1},{64,... | collective-permute-start | bytes 786440 | tf_op jit(solution)/shard_map/ppermute | solution.py:258
  113.7 6.8 %collective-permute-start.31 = (bf16[8,128,128]{2,1,0:T(8,128)(2,1)S(1)}, bf16[8,128,128]{2,1,0:T(8,128)(2,1)S(1)}, u32[]{:S(2)}, u32[]{:S(2)}) collective-permute-start(bf16[8,128,128]{2,1,0:T(8,128)(2,1)S(1)} %fusion), channel_id=1, source_target_pairs={{0,192},{1,49},{16,208},{17,1},{32,224},{33,17},{48,240},{49,33},{... | collective-permute-start | bytes 786440 | tf_op jit(solution)/shard_map/ppermute | solution.py:258
  (3 other events, 11.7 us)

commit v5 on v4

--- a/solution.py
+++ b/solution.py
@@ -102,7 +102,7 @@
 def forward_kernel(where, *refs):
     shards = refs[:16]
     wu_ref, wd_ref, h_ref, d_ref, x_ref, dy_ref, dt_ref, ht_ref = refs[16:24]
-    parts, sem = refs[24:28], refs[28]
+    parts, sem = refs[24:26], refs[26]
     wide = 2 * SIDE
     copies = []
     for k in range(16):
@@ -113,8 +113,10 @@
         copy.start()
     for copy in copies:
         copy.wait()
-    for n in range(ROWS // 2):
-        at = slice(n * wide, (n + 1) * wide)
+
+    @pl.loop(0, ROWS // 2)
+    def _(n):
+        at = lanes(n, wide)
         pre = nn(x_ref[...], wu_ref[:, at])
         grad_hidden = nt(dy_ref[...], wd_ref[at, :])
         value, slope = gelu_pair(pre)
@@ -125,32 +127,29 @@
             half = slice(b * SIDE, (b + 1) * SIDE)
             ht_ref[2 * n + b] = value[:, half].T.astype(BF)
             dt_ref[2 * n + b] = grad[:, half].T.astype(BF)
-    fill_parts(where, x_ref, dy_ref, dt_ref, ht_ref, parts, ((2, 0, 2), (2, 2, 2)))
+
+    fill_parts(where, x_ref, dy_ref, dt_ref, ht_ref, parts, ((2, 0, 16), (2, 16, 16)))
 
 
 def fill_parts(where, x_ref, dy_ref, dt_ref, ht_ref, outs, blocks):
-    for k, (away, start, n) in enumerate(blocks):
-
-        @pl.loop(0, n)
-        def _(group):
-            first = ring_slot(away, start + group)
-            for s in range(8):
-                row, col = split(where[first + s])
-                at = lanes(col, SIDE)
-                outs[2 * k][group * 8 + s] = nn(dt_ref[row], x_ref[:, at]).astype(BF)
-                outs[2 * k + 1][group * 8 + s] = nn(ht_ref[row], dy_ref[:, at]).astype(BF)
+    for out, (away, start, n) in zip(outs, blocks):
+        for s in range(n):
+            row, col = split(where[ring_slot(away, start + s)])
+            at = lanes(col, SIDE)
+            out[0, s] = nn(dt_ref[row], x_ref[:, at]).astype(BF)
+            out[1, s] = nn(ht_ref[row], dy_ref[:, at]).astype(BF)
 
 
 def forward(where, shards, wu, wd):
     hid = jax.ShapeDtypeStruct((SIDE, ROWS * SIDE), BF)
     tok = jax.ShapeDtypeStruct((SIDE, COLS * SIDE), BF)
     turned = jax.ShapeDtypeStruct((ROWS, SIDE, SIDE), BF)
-    part = jax.ShapeDtypeStruct((16, SIDE, SIDE), BF)
+    part = jax.ShapeDtypeStruct((2, 16, SIDE, SIDE), BF)
     return pl.pallas_call(
         forward_kernel,
         in_specs=[sspec()] + [pl.BlockSpec(memory_space=pl.ANY)] * 16 + [vspec()] * 2,
-        out_specs=[vspec()] * 10,
-        out_shape=[hid, hid, tok, tok, turned, turned] + [part] * 4,
+        out_specs=[vspec()] * 8,
+        out_shape=[hid, hid, tok, tok, turned, turned, part, part],
         scratch_shapes=[pltpu.SemaphoreType.DMA],
         compiler_params=params(16),
         cost_estimate=pl.CostEstimate(flops=3 << 30, bytes_accessed=22 << 20, transcendentals=1 << 18),
@@ -158,30 +157,33 @@
     )(where, *shards, wu, wd)
 
 
+REST = ((1, 16, 16), (3, 0, 16), (1, 0, 16), (3, 16, 16), (0, 0, 32))
+
+
 def rest_kernel(where, x_ref, dy_ref, dt_ref, ht_ref, *outs):
-    fill_parts(where, x_ref, dy_ref, dt_ref, ht_ref, outs, ((1, 0, 4), (3, 0, 4), (0, 0, 4)))
+    fill_parts(where, x_ref, dy_ref, dt_ref, ht_ref, outs, REST)
 
 
 def rest_parts(where, x, dy, dt, ht):
     return pl.pallas_call(
         rest_kernel,
         in_specs=[sspec()] + [vspec()] * 4,
-        out_specs=[vspec()] * 6,
-        out_shape=[jax.ShapeDtypeStruct((32, SIDE, SIDE), BF)] * 6,
+        out_specs=[vspec()] * len(REST),
+        out_shape=[jax.ShapeDtypeStruct((2, n, SIDE, SIDE), BF) for _, _, n in REST],
         compiler_params=params(16),
         cost_estimate=pl.CostEstimate(flops=1 << 30, bytes_accessed=9 << 20, transcendentals=0),
         name="rest_parts",
     )(where, x, dy, dt, ht)
 
 
-def ring_slot(away1, group):
-    away2 = jnp.where(group == 0, 2, jnp.where(group == 1, 1, jnp.where(group == 2, 3, 0)))
+def ring_slot(away1, place):
+    away2, near = ((2, 0), (1, 4), (2, 4), (3, 0), (1, 0), (3, 4), (0, 0), (0, 4))[place // 4]
     c = lax.axis_index("c")
     away_x = away1 + c * (away2 - away1)
     away_y = away2 + c * (away1 - away2)
     y = lax.rem(lax.axis_index("y") + away_y, 4)
     x = lax.rem(lax.axis_index("x") + away_x, 4)
-    return (y * 4 + x) * 8
+    return (y * 4 + x) * 8 + near + place % 4
 
 
 def token_kernel(h_ref, d_ref, wu_ref, wd_ref, send_ref, keep_ref):
@@ -258,70 +260,56 @@
     return lax.ppermute(t, ("y", "x", "c"), pairs)
 
 
-def send_two_ways(far_a, far_b, nearer, before, stage):
-    n = far_a.shape[0]
-    from_left = hop(far_a, stage, 1)
-    from_right = hop(far_b, stage, -1)
-    left = hop(nearer.at[:n].add(from_left), stage, 1)
-    right = hop(before.at[n:].add(from_right), stage, -1)
-    return left, right
-
-
-def ring_sum(far_a, far_b, nearer, before, own):
-    left, right = send_two_ways(far_a, far_b, nearer, before, 0)
+def ring_sums(far_a, far_b, next_b, before_a, next_a, before_b, own):
+    from_left = hop(far_a, 0, 1)
+    from_right = hop(far_b, 0, -1)
+    left_b = hop(next_b, 0, 1)
+    right_a = hop(before_a, 0, -1)
+    left_a = hop(add(next_a, from_left).astype(BF), 0, 1)
+    right_b = hop(add(before_b, from_right).astype(BF), 0, -1)
+    left_a, left_b, right_a, right_b = lax.optimization_barrier((left_a, left_b, right_a, right_b))
 
     def total(k, n):
-        return add(own[k : k + n], left[k : k + n], right[k : k + n])
-
-    sent = (total(k, n).astype(BF) for k, n in ((0, 4), (4, 4), (8, 8), (16, 8)))
-    return total(24, 8), *send_two_ways(*sent, 1)
-
-
-def finish_kernel(count_ref, *refs):
+        left, right = (left_a, right_a) if k < 16 else (left_b, right_b)
+        at = slice(k % 16, k % 16 + n)
+        return add(own[:, k : k + n], left[:, at], right[:, at])
+
+    from_left = hop(total(0, 8).astype(BF), 1, 1)
+    from_right = hop(total(8, 8).astype(BF), 1, -1)
+    end_a = hop(add(total(16, 4), from_left[:, :4]).astype(BF), 1, 1)
+    end_b = hop(add(total(20, 4), from_right[:, :4]).astype(BF), 1, -1)
+    return (own, left_b, right_b, from_left, from_right, end_a, end_b)
+
+
+def finish_kernel(count_ref, own, left_b, right_b, from_left, from_right, end_a, end_b, up_out, down_out):
     first = lax.axis_index(("y", "x")) * 8
     for k in range(2):
-        base, left, right = refs[3 * k : 3 * k + 3]
-        out = refs[6 + k]
         for s in range(8):
-            total = base[s] + left[s].astype(F32) + right[s].astype(F32)
+            one, two = (end_a[k, s], from_right[k, 4 + s]) if s < 4 else (from_left[k, s], end_b[k, s - 4])
+            total = add(own[k, s], left_b[k, s], right_b[k, s], one, two)
             total = jnp.where(first + s < count_ref[0], total * (1.0 / 16), 0.0)
-            out[0, s] = total.T if k == 0 else total
-
-
-def finish(count, up, down):
+            if k == 0:
+                up_out[0, s] = total.T
+            else:
+                down_out[0, s] = total
+
+
+def finish(count, sums):
     shape = (1, 8, SIDE, SIDE)
+
+    def last(block):
+        return pl.BlockSpec((2, 8, SIDE, SIDE), lambda i: (0, block, 0, 0))
+
     return pl.pallas_call(
         finish_kernel,
         grid=(1,),
-        in_specs=[sspec()] + [whole(8, SIDE, SIDE)] * 6,
+        in_specs=[sspec(), last(3), last(1), last(1)] + [whole(2, n, SIDE, SIDE) for n in (8, 8, 4, 4)],
         out_specs=[whole(*shape)] * 2,
         out_shape=[jax.ShapeDtypeStruct(shape, F32)] * 2,
         compiler_params=params(16),
         cost_estimate=pl.CostEstimate(flops=1 << 20, bytes_accessed=3 << 20, transcendentals=0),
         name="finish",
-    )(count, *up, *down)
-
-
-def owner_sum_kernel(terms_ref, mixed_ref, grad_in_ref):
-    for k, out in enumerate((mixed_ref, grad_in_ref)):
-        total = terms_ref[0, k].astype(F32)
-        for z in range(1, 8):
-            total = total + terms_ref[z, k].astype(F32)
-        out[...] = total.astype(BF)
-
-
-def owner_sum(terms):
-    shape = terms.shape[2:]
-    return pl.pallas_call(
-        owner_sum_kernel,
-        grid=(1,),
-        in_specs=[whole(*terms.shape)],
-        out_specs=[whole(*shape)] * 2,
-        out_shape=[jax.ShapeDtypeStruct(shape, BF)] * 2,
-        compiler_params=params(16),
-        cost_estimate=pl.CostEstimate(flops=1 << 19, bytes_accessed=1 << 20, transcendentals=0),
-        name="owner_sum",
-    )(terms)
+    )(count, *sums)
 
 
 def body(tokens, grad_out, up_tiles, down_tiles, tile_rows, tile_cols, tile_count):
@@ -334,12 +322,10 @@
     h, d, _ = lax.optimization_barrier((h, d, rest[0]))
     send, keep = token_parts(h, d, wu, wd)
     pieces = add(keep, swap(send)).astype(BF)
-    up = ring_sum(far[0], far[2], *rest[0::2])
-    pieces, down_next = lax.optimization_barrier((pieces, rest[1]))
-    down = ring_sum(far[1], far[3], down_next, rest[3], rest[5])
-    mixed, grad_in = owner_sum(lax.all_to_all(pieces, "z", 0, 0, tiled=True))
-    grad_up, grad_down = finish(tile_count, up, down)
-    return mixed, grad_in, grad_up, grad_down
+    sums = ring_sums(*far, *rest)
+    both = lax.psum_scatter(pieces, "z", scatter_dimension=0, tiled=True)[0]
+    grad_up, grad_down = finish(tile_count, sums)
+    return both[0], both[1], grad_up, grad_down
 
 
 def solution(mesh):

time: 124 us -> 122 us (0.984)
  starting transfers between devices: 44.1 us -> 26.8 us
  between operations: 1.44 us -> 14.8 us
  waiting for transfers between devices: 35.7 us -> 47.4 us
  other arithmetic: 17.1 us -> 9.02 us
  Pallas kernels: 21.9 us -> 19.9 us
  local copies, waits for them, and re-layouts: 2.19 us -> 3.72 us
    ppermute x16 -> x10, starting transfers between devices: 24.2 us -> 11.3 us  [hop(): return lax.ppermute(t, ('y', 'x', 'c'), pairs)]
    ppermute x16 -> x10, waiting for transfers between devices: 24.8 us -> 36.3 us  [hop(): return lax.ppermute(t, ('y', 'x', 'c'), pairs)]
    scatter-add x8 -> x0, other arithmetic: 8.37 us -> none  [the longest x4 4.21 us: send_two_ways(): left = hop(nearer.at[:n].add(from_left), stage, 1)]
    all_to_all x1 -> x0, starting transfers between devices: 5.06 us -> none  [body(): mixed, grad_in = owner_sum(lax.all_to_all(pieces, 'z', 0, 0, tiled=True))]
    pallas_call x1, Pallas kernels: 6.53 us -> 4 us  [rest_parts(): pl.pallas_call(rest_kernel, in_specs=[sspec()] + [vspec()] * 4, out_specs...]
    squeeze x0 -> x1, local copies, waits for them, and re-layouts: none -> 1.53 us  [body(): return (both[0], both[1], grad_up, grad_down)]
  transfers between devices with their start and end apart: 33 -> 27, of which waited for: 11 -> 14; matrix products, arithmetic and copies ran while one was open for 13% -> 7% of each run, Pallas kernels for 12% -> 11%
where the time goes in v5:
time: 122 us
  waiting for transfers between devices  47.4 us (39%)
  starting transfers between devices  26.8 us (22%)
  Pallas kernels  19.9 us (16%)
  between operations  14.8 us (12%)
  other arithmetic  9.02 us (7%)
  local copies, waits for them, and re-layouts  3.72 us (3%)
    ppermute x10, waiting for transfers between devices, hop(): return lax.ppermute(t, ('y', 'x', 'c'), pairs)  36.3 us
    ppermute x10, starting transfers between devices, hop(): return lax.ppermute(t, ('y', 'x', 'c'), pairs)  11.3 us
    ppermute x7, waiting for transfers between devices, step_both(): return lax.ppermute(x, ('z', 'c'), pairs)  9.76 us
    ppermute x7, starting transfers between devices, step_both(): return lax.ppermute(x, ('z', 'c'), pairs)  9.71 us
    pallas_call x1, Pallas kernels, forward(): pl.pallas_call(forward_kernel, in_specs=[sspec()] + [pl.BlockSpec(memory_...  6.34 us
    ppermute x9, starting transfers between devices, swap(): return lax.ppermute(x, 'c', [(0, 1), (1, 0)])  5.69 us
    pallas_call x1, Pallas kernels, token_parts(): pl.pallas_call(token_kernel, in_specs=[vspec()] * 4, out_specs=[vspec()]...  4.12 us
    pallas_call x1, Pallas kernels, rest_parts(): pl.pallas_call(rest_kernel, in_specs=[sspec()] + [vspec()] * 4, out_specs...  4 us
  transfers between devices with their start and end apart: 27, of which 14 were waited for; matrix products, arithmetic and copies ran while one was open for 7% of the time, Pallas kernels for 11%

profile of v5, /device:TPU:6, one launch (start us, length us, event | category | flops | bytes accessed | tf_op | source)
XLA Modules:
  0.0 121.6 jit_solution(12367228262897277491)
XLA Ops:
  8.1 2.0 %collective-permute-start.1 = (bf16[2,128,256]{2,1,0:T(8,128)(2,1)S(1)}, bf16[2,128,256]{2,1,0:T(8,128)(2,1)S(1)}, u32[]{:S(2)}, u32[]{:S(2)}) collective-permute-start(bf16[2,128,256]{2,1,0:T(8,128)(2,1)S(1)} %pad_maximum_fusion.refs_0_), channel_id=1, source_target_pairs={{0,2},{1,15},{2,4},{3,1},{4,6},{5,3},{6,8},{7,5},{8,10},{9,7},{10,... | collective-permute-start | bytes 393224 | tf_op jit(solution)/shard_map/ppermute | solution.py:221
  10.1 3.5 %collective-permute-start = (bf16[2,128,256]{2,1,0:T(8,128)(2,1)S(1)}, bf16[2,128,256]{2,1,0:T(8,128)(2,1)S(1)}, u32[]{:S(2)}, u32[]{:S(2)}) collective-permute-start(bf16[2,128,256]{2,1,0:T(8,128)(2,1)S(1)} %pad_maximum_fusion.refs_0_), channel_id=1, source_target_pairs={{0,1},{1,0},{2,3},{3,2},{4,5},{5,4},{6,7},{7,6},{8,9},{9,8},{10,11... | collective-permute-start | bytes 393224 | tf_op jit(solution)/shard_map/ppermute | solution.py:225
  14.2 2.7 %collective-permute-done.1.refs_2_ = bf16[2,128,256]{2,1,0:T(8,128)(2,1)S(1)} collective-permute-done((bf16[2,128,256]{2,1,0:T(8,128)(2,1)S(1)}, bf16[2,128,256]{2,1,0:T(8,128)(2,1)S(1)}, u32[]{:S(2)}, u32[]{:S(2)}) %collective-permute-start.1) | collective-permute-done | bytes 131104 | tf_op jit(solution)/shard_map/ppermute | solution.py:221
  17.7 2.2 %copy-done = bf16[1,128,128,128]{3,2,1,0:T(8,128)(2,1)S(1)} copy-done((bf16[1,128,128,128]{3,2,1,0:T(8,128)(2,1)S(1)}, bf16[1,128,128,128]{3,2,1,0:T(8,128)(2,1)}, u32[]{:S(2)}) %copy-start) | copy-done | bytes 4194328
  19.9 1.5 %dense_up.1.refs_16_.wu_ref = bf16[4096,1024]{1,0:T(8,128)(2,1)S(1)} custom-call(s32[128]{0:T(128)S(1)} %add_bitcast_fusion.where, s32[1]{0:T(128)S(6)} %copy.11.count_ref, bf16[1,128,128,128]{3,2,1,0:T(8,128)(2,1)S(1)} %copy-done), custom_call_target="tpu_custom_call" | custom-call | bytes 12582912 | tf_op jit(solution)/shard_map/dense_up/pallas_call | solution.py:86
  21.4 1.7 %collective-permute-done.5.refs_6_ = bf16[2,128,256]{2,1,0:T(8,128)(2,1)S(1)} collective-permute-done((bf16[2,128,256]{2,1,0:T(8,128)(2,1)S(1)}, bf16[2,128,256]{2,1,0:T(8,128)(2,1)S(1)}, u32[]{:S(2)}, u32[]{:S(2)}) %collective-permute-start.5) | collective-permute-done | bytes 131104 | tf_op jit(solution)/shard_map/ppermute | solution.py:221
  23.2 1.7 %collective-permute-start.9 = (bf16[2,128,256]{2,1,0:T(8,128)(2,1)S(1)}, bf16[2,128,256]{2,1,0:T(8,128)(2,1)S(1)}, u32[]{:S(2)}, u32[]{:S(2)}) collective-permute-start(bf16[2,128,256]{2,1,0:T(8,128)(2,1)S(1)} %collective-permute-done.5.refs_6_), channel_id=1, source_target_pairs={{0,2},{1,15},{2,4},{3,1},{4,6},{5,3},{6,8},{7,5},{8,10},{9,7},{10,... | collective-permute-start | bytes 393224 | tf_op jit(solution)/shard_map/ppermute | solution.py:221
  24.9 2.9 %collective-permute-start.7 = (bf16[2,128,256]{2,1,0:T(8,128)(2,1)S(1)}, bf16[2,128,256]{2,1,0:T(8,128)(2,1)S(1)}, u32[]{:S(2)}, u32[]{:S(2)}) collective-permute-start(bf16[2,128,256]{2,1,0:T(8,128)(2,1)S(1)} %collective-permute-done.3.refs_4_), channel_id=1, source_target_pairs={{0,2},{1,15},{2,4},{3,1},{4,6},{5,3},{6,8},{7,5},{8,10},{9,7},{10,... | collective-permute-start | bytes 393224 | tf_op jit(solution)/shard_map/ppermute | solution.py:221
  27.8 1.6 %dense_down.1.refs_17_.wd_ref = bf16[1024,4096]{1,0:T(8,128)(2,1)S(1)} custom-call(s32[128]{0:T(128)S(1)} %add_bitcast_fusion.where, s32[1]{0:T(128)S(6)} %copy.11.count_ref, bf16[1,128,128,128]{3,2,1,0:T(8,128)(2,1)S(1)} %copy-done.1), custom_call_target="tpu_custom_call" | custom-call | bytes 12582912 | tf_op jit(solution)/shard_map/dense_down/pallas_call | solution.py:86
  31.0 1.7 %collective-permute-start.11 = (bf16[2,128,256]{2,1,0:T(8,128)(2,1)S(1)}, bf16[2,128,256]{2,1,0:T(8,128)(2,1)S(1)}, u32[]{:S(2)}, u32[]{:S(2)}) collective-permute-start(bf16[2,128,256]{2,1,0:T(8,128)(2,1)S(1)} %collective-permute-done.7.refs_8_), channel_id=1, source_target_pairs={{0,2},{1,15},{2,4},{3,1},{4,6},{5,3},{6,8},{7,5},{8,10},{9,7},{10,... | collective-permute-start | bytes 393224 | tf_op jit(solution)/shard_map/ppermute | solution.py:221
  32.7 1.4 %collective-permute-start.13 = (bf16[2,128,256]{2,1,0:T(8,128)(2,1)S(1)}, bf16[2,128,256]{2,1,0:T(8,128)(2,1)S(1)}, u32[]{:S(2)}, u32[]{:S(2)}) collective-permute-start(bf16[2,128,256]{2,1,0:T(8,128)(2,1)S(1)} %collective-permute-done.9.refs_10_), channel_id=1, source_target_pairs={{0,2},{1,15},{2,4},{3,1},{4,6},{5,3},{6,8},{7,5},{8,10},{9,7},{10,... | collective-permute-start | bytes 393224 | tf_op jit(solution)/shard_map/ppermute | solution.py:221
  34.8 2.5 %collective-permute-done.11.refs_12_ = bf16[2,128,256]{2,1,0:T(8,128)(2,1)S(1)} collective-permute-done((bf16[2,128,256]{2,1,0:T(8,128)(2,1)S(1)}, bf16[2,128,256]{2,1,0:T(8,128)(2,1)S(1)}, u32[]{:S(2)}, u32[]{:S(2)}) %collective-permute-start.11) | collective-permute-done | bytes 131104 | tf_op jit(solution)/shard_map/ppermute | solution.py:221
  37.2 1.7 %collective-permute-done.13.refs_14_ = bf16[2,128,256]{2,1,0:T(8,128)(2,1)S(1)} collective-permute-done((bf16[2,128,256]{2,1,0:T(8,128)(2,1)S(1)}, bf16[2,128,256]{2,1,0:T(8,128)(2,1)S(1)}, u32[]{:S(2)}, u32[]{:S(2)}) %collective-permute-start.13) | collective-permute-done | bytes 131104 | tf_op jit(solution)/shard_map/ppermute | solution.py:221
  40.3 6.3 %forward.1 = (bf16[128,1024]{1,0:T(8,128)(2,1)S(1)}, bf16[128,1024]{1,0:T(8,128)(2,1)S(1)}, bf16[128,4096]{1,0:T(8,128)(2,1)S(1)}, bf16[128,4096]{1,0:T(8,128)(2...) custom-call(s32[128]{0:T(128)S(1)} %add_bitcast_fusion.where, ...), custom_call_target="tpu_custom_call" | custom-call | flops 3221225472 | bytes 23068672 | tf_op jit(solution)/shard_map/forward/pallas_call | solution.py:148
  47.2 1.5 %collective-permute-start.20 = (bf16[2,16,128,128]{3,2,1,0:T(8,128)(2,1)S(1)}, bf16[2,16,128,128]{3,2,1,0:T(8,128)(2,1)S(1)}, u32[]{:S(2)}, u32[]{:S(2)}) collective-permute-start(bf16[2,16,128,128]{3,2,1,0:T(8,128)(2,1)S(1)} %get-tuple-element.51), channel_id=1, source_target_pairs={{0,48},{1,193},{16,0},{17,209},{32,16},{33,225},{48,32},{49,241},{... | collective-permute-start | bytes 3145736 | tf_op jit(solution)/shard_map/ppermute | solution.py:260
  48.7 4.0 %rest_parts.1 = (bf16[2,16,128,128]{3,2,1,0:T(8,128)(2,1)}, bf16[2,16,128,128]{3,2,1,0:T(8,128)(2,1)}, bf16[2,16,128,128]{3,2,1,0:T(8,128)(2,1)S(1)}, bf16[2,16,...) custom-call(s32[128]{0:T(128)S(1)} %add_bitcast_fusion.where, bf16[128,4096]{1,0:T(8,128)(2,1)S(1)} %get-tuple-element.37.x_ref, ...), custom_call_target="tpu_custom_call" | custom-call | flops 1073741824 | bytes 9437184 | tf_op jit(solution)/shard_map/rest_parts/pallas_call | solution.py:168
  52.7 4.1 %token_parts.1 = (bf16[8,2,128,256]{3,2,1,0:T(8,128)(2,1)S(1)}, bf16[8,2,128,256]{3,2,1,0:T(8,128)(2,1)S(1)}) custom-call(bf16[128,1024]{1,0:T(8,128)(2,1)S(1)} %get-tuple-element.42.h_ref, bf16[128,1024]{1,0:T(8,128)(2,1)S(1)} %get-tuple-element.43.d_ref, bf16[4096,1024]{1,0:T(8,128)(2,1)S(1)} %dense_up.1.refs_16_.wu_ref, ...), custom_call_target="tpu_custom_call" | custom-call | flops 2147483648 | bytes 19922944 | tf_op jit(solution)/shard_map/token_parts/pallas_call | solution.py:201
  59.9 1.6 %collective-permute-done.16 = bf16[2,16,128,128]{3,2,1,0:T(8,128)(2,1)S(1)} collective-permute-done((bf16[2,16,128,128]{3,2,1,0:T(8,128)(2,1)S(1)}, bf16[2,16,128,128]{3,2,1,0:T(8,128)(2,1)S(1)}, u32[]{:S(2)}, u32[]{:S(2)}) %collective-permute-start.16) | collective-permute-done | bytes 1048608 | tf_op jit(solution)/shard_map/ppermute | solution.py:260
  62.8 1.7 %collective-permute-start.17 = (bf16[2,16,128,128]{3,2,1,0:T(8,128)(2,1)}, bf16[2,16,128,128]{3,2,1,0:T(8,128)(2,1)}, u32[]{:S(2)}, u32[]{:S(2)}) collective-permute-start(bf16[2,16,128,128]{3,2,1,0:T(8,128)(2,1)} %add_convert_fusion.1), channel_id=1, source_target_pairs={{0,16},{1,65},{16,32},{17,81},{32,48},{33,97},{48,0},{49,113},{64,... | collective-permute-start | bytes 3145736 | tf_op jit(solution)/shard_map/ppermute | solution.py:260
  64.5 1.4 %add_convert_fusion = bf16[2,16,128,128]{3,2,1,0:T(8,128)(2,1)} fusion(bf16[2,16,128,128]{3,2,1,0:T(8,128)(2,1)S(1)} %collective-permute-done.20, bf16[2,16,128,128]{3,2,1,0:T(8,128)(2,1)S(1)} %get-tuple-element.50), kind=kLoop, calls=%fused_computation | loop fusion | flops 2097152 | bytes 3145728 | tf_op jit(solution)/shard_map/convert_element_type | solution.py:269
  67.7 7.4 %collective-permute-done.19 = bf16[2,16,128,128]{3,2,1,0:T(8,128)(2,1)} collective-permute-done((bf16[2,16,128,128]{3,2,1,0:T(8,128)(2,1)}, bf16[2,16,128,128]{3,2,1,0:T(8,128)(2,1)}, u32[]{:S(2)}, u32[]{:S(2)}) %collective-permute-start.19) | collective-permute-done | bytes 1048608 | tf_op jit(solution)/shard_map/ppermute | solution.py:260
  75.1 9.1 %collective-permute-done.17 = bf16[2,16,128,128]{3,2,1,0:T(8,128)(2,1)} collective-permute-done((bf16[2,16,128,128]{3,2,1,0:T(8,128)(2,1)}, bf16[2,16,128,128]{3,2,1,0:T(8,128)(2,1)}, u32[]{:S(2)}, u32[]{:S(2)}) %collective-permute-start.17) | collective-permute-done | bytes 1048608 | tf_op jit(solution)/shard_map/ppermute | solution.py:260
  84.2 2.1 %collective-permute-done.21.right_b = bf16[2,16,128,128]{3,2,1,0:T(8,128)(2,1)} collective-permute-done((bf16[2,16,128,128]{3,2,1,0:T(8,128)(2,1)}, bf16[2,16,128,128]{3,2,1,0:T(8,128)(2,1)}, u32[]{:S(2)}, u32[]{:S(2)}) %collective-permute-start.21) | collective-permute-done | bytes 1048608 | tf_op jit(solution)/shard_map/ppermute | solution.py:260
  86.3 2.0 %add_convert_fusion.3 = (bf16[2,8,128,128]{3,2,1,0:T(8,128)(2,1)S(1)}, bf16[2,8,128,128]{3,2,1,0:T(8,128)(2,1)S(1)}) fusion(bf16[2,16,128,128]{3,2,1,0:T(8,128)(2,1)} %collective-permute-done.19, bf16[2,16,128,128]{3,2,1,0:T(8,128)(2,1)} %collective-permute-done.17, bf16[2,32,128,128]{3,2,1,0:T(8,128)(2,1)S(1)} %get-tuple-element.46.own), kind=kLoop, calls=%fused_computation.3 | loop fusion | flops 3145728 | bytes 4194304 | tf_op jit(solution)/shard_map/convert_element_type | solution.py:278
  88.3 3.1 %collective-permute-start.23 = (bf16[2,8,128,128]{3,2,1,0:T(8,128)(2,1)S(1)}, bf16[2,8,128,128]{3,2,1,0:T(8,128)(2,1)S(1)}, u32[]{:S(2)}, u32[]{:S(2)}) collective-permute-start(bf16[2,8,128,128]{3,2,1,0:T(8,128)(2,1)S(1)} %get-tuple-element.60), channel_id=1, source_target_pairs={{0,192},{1,49},{16,208},{17,1},{32,224},{33,17},{48,240},{49,33},{... | collective-permute-start | bytes 1572872 | tf_op jit(solution)/shard_map/ppermute | solution.py:260
  91.4 6.7 %collective-permute-done.23.from_right = bf16[2,8,128,128]{3,2,1,0:T(8,128)(2,1)S(1)} collective-permute-done((bf16[2,8,128,128]{3,2,1,0:T(8,128)(2,1)S(1)}, bf16[2,8,128,128]{3,2,1,0:T(8,128)(2,1)S(1)}, u32[]{:S(2)}, u32[]{:S(2)}) %collective-permute-start.23) | collective-permute-done | bytes 524320 | tf_op jit(solution)/shard_map/ppermute | solution.py:260
  98.1 3.7 %collective-permute-done.22.from_left = bf16[2,8,128,128]{3,2,1,0:T(8,128)(2,1)S(1)} collective-permute-done((bf16[2,8,128,128]{3,2,1,0:T(8,128)(2,1)S(1)}, bf16[2,8,128,128]{3,2,1,0:T(8,128)(2,1)S(1)}, u32[]{:S(2)}, u32[]{:S(2)}) %collective-permute-start.22) | collective-permute-done | bytes 524320 | tf_op jit(solution)/shard_map/ppermute | solution.py:260
  101.8 1.4 %add_convert_fusion.5 = (bf16[2,4,128,128]{3,2,1,0:T(8,128)(2,1)S(1)}, bf16[2,4,128,128]{3,2,1,0:T(8,128)(2,1)S(1)}) fusion(bf16[2,8,128,128]{3,2,1,0:T(8,128)(2,1)S(1)} %collective-permute-done.23.from_right, bf16[2,16,128,128]{3,2,1,0:T(8,128)(2,1)} %collective-permute-done.21.right_b, bf16[2,16,128,128]{3,2,1,0:T(8,128)(2,1)S(1)} %collective-permute-done.18.left_b, ...), kind=kLoop, calls=%fused_computation.5 | loop fusion | flops 2097152 | bytes 2621440 | tf_op jit(solution)/shard_map/convert_element_type | solution.py:280
  103.2 2.0 %collective-permute-start.24 = (bf16[2,4,128,128]{3,2,1,0:T(8,128)(2,1)S(1)}, bf16[2,4,128,128]{3,2,1,0:T(8,128)(2,1)S(1)}, u32[]{:S(2)}, u32[]{:S(2)}) collective-permute-start(bf16[2,4,128,128]{3,2,1,0:T(8,128)(2,1)S(1)} %get-tuple-element.59), channel_id=1, source_target_pairs={{0,64},{1,17},{16,80},{17,33},{32,96},{33,49},{48,112},{49,1},{64,... | collective-permute-start | bytes 786440 | tf_op jit(solution)/shard_map/ppermute | solution.py:260
  105.3 4.3 %collective-permute-done.25.end_b = bf16[2,4,128,128]{3,2,1,0:T(8,128)(2,1)S(1)} collective-permute-done((bf16[2,4,128,128]{3,2,1,0:T(8,128)(2,1)S(1)}, bf16[2,4,128,128]{3,2,1,0:T(8,128)(2,1)S(1)}, u32[]{:S(2)}, u32[]{:S(2)}) %collective-permute-start.25) | collective-permute-done | bytes 262176 | tf_op jit(solution)/shard_map/ppermute | solution.py:260
  110.9 2.3 %finish.1 = (f32[1,8,128,128]{3,2,1,0:T(8,128)}, f32[1,8,128,128]{3,2,1,0:T(8,128)}) custom-call(s32[1]{0:T(128)S(6)} %copy.11.count_ref, bf16[2,32,128,128]{3,2,1,0:T(8,128)(2,1)S(1)} %get-tuple-element.46.own, bf16[2,16,128,128]{3,2,1,0:T(8,128)(2,1)S(1)} %collective-permute-done.18.left_b, bf16[2,16,128,128]{3,2,1,0:T(8,128)(2,1)} %collective-permute-done.21.right_b, ...), custom_call_target="tpu_custom_call" | custom-call | flops 1048576 | bytes 3145728 | tf_op jit(solution)/shard_map/finish/pallas_call | solution.py:303
  113.2 1.5 %slice_bitcast_fusion = (bf16[128,256]{1,0:T(8,128)(2,1)}, bf16[128,256]{1,0:T(8,128)(2,1)}) fusion(bf16[1,2,128,256]{3,2,1,0:T(8,128)(2,1)} %reduce-scatter.2.cloned.1.call-done), kind=kLoop, calls=%fused_computation.8 | loop fusion | bytes 262144 | tf_op jit(solution)/shard_map/squeeze | solution.py:328
  (41 shorter events, 13.2 us)
Async XLA Ops:
  7.2 106.1 %reduce-scatter.2.cloned.1.call-start = ((), (), s32[]{:S(2)}) async-start(), calls=%async_computation.1 | async-start | bytes 1179648 | tf_op jit(solution)/shard_map/reduce_scatter | solution.py:326
  8.1 8.9 %collective-permute-start.1 = (bf16[2,128,256]{2,1,0:T(8,128)(2,1)S(1)}, bf16[2,128,256]{2,1,0:T(8,128)(2,1)S(1)}, u32[]{:S(2)}, u32[]{:S(2)}) collective-permute-start(bf16[2,128,256]{2,1,0:T(8,128)(2,1)S(1)} %pad_maximum_fusion.refs_0_), channel_id=1, source_target_pairs={{0,2},{1,15},{2,4},{3,1},{4,6},{5,3},{6,8},{7,5},{8,10},{9,7},{10,... | collective-permute-start | bytes 393224 | tf_op jit(solution)/shard_map/ppermute | solution.py:221
  10.1 6.9 %collective-permute-start = (bf16[2,128,256]{2,1,0:T(8,128)(2,1)S(1)}, bf16[2,128,256]{2,1,0:T(8,128)(2,1)S(1)}, u32[]{:S(2)}, u32[]{:S(2)}) collective-permute-start(bf16[2,128,256]{2,1,0:T(8,128)(2,1)S(1)} %pad_maximum_fusion.refs_0_), channel_id=1, source_target_pairs={{0,1},{1,0},{2,3},{3,2},{4,5},{5,4},{6,7},{7,6},{8,9},{9,8},{10,11... | collective-permute-start | bytes 393224 | tf_op jit(solution)/shard_map/ppermute | solution.py:225
  17.0 6.2 %collective-permute-start.5 = (bf16[2,128,256]{2,1,0:T(8,128)(2,1)S(1)}, bf16[2,128,256]{2,1,0:T(8,128)(2,1)S(1)}, u32[]{:S(2)}, u32[]{:S(2)}) collective-permute-start(bf16[2,128,256]{2,1,0:T(8,128)(2,1)S(1)} %collective-permute-done.1.refs_2_), channel_id=1, source_target_pairs={{0,2},{1,15},{2,4},{3,1},{4,6},{5,3},{6,8},{7,5},{8,10},{9,7},{10,... | collective-permute-start | bytes 393224 | tf_op jit(solution)/shard_map/ppermute | solution.py:221
  17.0 7.9 %collective-permute-start.3 = (bf16[2,128,256]{2,1,0:T(8,128)(2,1)S(1)}, bf16[2,128,256]{2,1,0:T(8,128)(2,1)S(1)}, u32[]{:S(2)}, u32[]{:S(2)}) collective-permute-start(bf16[2,128,256]{2,1,0:T(8,128)(2,1)S(1)} %collective-permute-done.refs_1_), channel_id=1, source_target_pairs={{0,2},{1,15},{2,4},{3,1},{4,6},{5,3},{6,8},{7,5},{8,10},{9,7},{10,... | collective-permute-start | bytes 393224 | tf_op jit(solution)/shard_map/ppermute | solution.py:221
  17.7 2.2 %copy-start = (bf16[1,128,128,128]{3,2,1,0:T(8,128)(2,1)S(1)}, bf16[1,128,128,128]{3,2,1,0:T(8,128)(2,1)}, u32[]{:S(2)}) copy-start(bf16[1,128,128,128]{3,2,1,0:T(8,128)(2,1)} %tiles_ref.2) | copy-start | bytes 12582916
  19.9 7.9 %copy-start.1 = (bf16[1,128,128,128]{3,2,1,0:T(8,128)(2,1)S(1)}, bf16[1,128,128,128]{3,2,1,0:T(8,128)(2,1)}, u32[]{:S(2)}) copy-start(bf16[1,128,128,128]{3,2,1,0:T(8,128)(2,1)} %tiles_ref.3) | copy-start | bytes 12582916
  23.2 6.8 %collective-permute-start.9 = (bf16[2,128,256]{2,1,0:T(8,128)(2,1)S(1)}, bf16[2,128,256]{2,1,0:T(8,128)(2,1)S(1)}, u32[]{:S(2)}, u32[]{:S(2)}) collective-permute-start(bf16[2,128,256]{2,1,0:T(8,128)(2,1)S(1)} %collective-permute-done.5.refs_6_), channel_id=1, source_target_pairs={{0,2},{1,15},{2,4},{3,1},{4,6},{5,3},{6,8},{7,5},{8,10},{9,7},{10,... | collective-permute-start | bytes 393224 | tf_op jit(solution)/shard_map/ppermute | solution.py:221
  24.9 6.2 %collective-permute-start.7 = (bf16[2,128,256]{2,1,0:T(8,128)(2,1)S(1)}, bf16[2,128,256]{2,1,0:T(8,128)(2,1)S(1)}, u32[]{:S(2)}, u32[]{:S(2)}) collective-permute-start(bf16[2,128,256]{2,1,0:T(8,128)(2,1)S(1)} %collective-permute-done.3.refs_4_), channel_id=1, source_target_pairs={{0,2},{1,15},{2,4},{3,1},{4,6},{5,3},{6,8},{7,5},{8,10},{9,7},{10,... | collective-permute-start | bytes 393224 | tf_op jit(solution)/shard_map/ppermute | solution.py:221
  29.3 4.8 %collective-permute-start.2 = (bf16[2,128,256]{2,1,0:T(8,128)(2,1)S(1)}, bf16[2,128,256]{2,1,0:T(8,128)(2,1)S(1)}, u32[]{:S(2)}, u32[]{:S(2)}) collective-permute-start(bf16[2,128,256]{2,1,0:T(8,128)(2,1)S(1)} %collective-permute-done.1.refs_2_), channel_id=1, source_target_pairs={{0,1},{1,0},{2,3},{3,2},{4,5},{5,4},{6,7},{7,6},{8,9},{9,8},{10,11... | collective-permute-start | bytes 393224 | tf_op jit(solution)/shard_map/ppermute | solution.py:225
  29.7 5.0 %collective-permute-start.6 = (bf16[2,128,256]{2,1,0:T(8,128)(2,1)S(1)}, bf16[2,128,256]{2,1,0:T(8,128)(2,1)S(1)}, u32[]{:S(2)}, u32[]{:S(2)}) collective-permute-start(bf16[2,128,256]{2,1,0:T(8,128)(2,1)S(1)} %collective-permute-done.5.refs_6_), channel_id=1, source_target_pairs={{0,1},{1,0},{2,3},{3,2},{4,5},{5,4},{6,7},{7,6},{8,9},{9,8},{10,11... | collective-permute-start | bytes 393224 | tf_op jit(solution)/shard_map/ppermute | solution.py:225
  31.0 6.2 %collective-permute-start.11 = (bf16[2,128,256]{2,1,0:T(8,128)(2,1)S(1)}, bf16[2,128,256]{2,1,0:T(8,128)(2,1)S(1)}, u32[]{:S(2)}, u32[]{:S(2)}) collective-permute-start(bf16[2,128,256]{2,1,0:T(8,128)(2,1)S(1)} %collective-permute-done.7.refs_8_), channel_id=1, source_target_pairs={{0,2},{1,15},{2,4},{3,1},{4,6},{5,3},{6,8},{7,5},{8,10},{9,7},{10,... | collective-permute-start | bytes 393224 | tf_op jit(solution)/shard_map/ppermute | solution.py:221
  32.7 6.2 %collective-permute-start.13 = (bf16[2,128,256]{2,1,0:T(8,128)(2,1)S(1)}, bf16[2,128,256]{2,1,0:T(8,128)(2,1)S(1)}, u32[]{:S(2)}, u32[]{:S(2)}) collective-permute-start(bf16[2,128,256]{2,1,0:T(8,128)(2,1)S(1)} %collective-permute-done.9.refs_10_), channel_id=1, source_target_pairs={{0,2},{1,15},{2,4},{3,1},{4,6},{5,3},{6,8},{7,5},{8,10},{9,7},{10,... | collective-permute-start | bytes 393224 | tf_op jit(solution)/shard_map/ppermute | solution.py:221
  34.1 4.8 %collective-permute-start.4 = (bf16[2,128,256]{2,1,0:T(8,128)(2,1)S(1)}, bf16[2,128,256]{2,1,0:T(8,128)(2,1)S(1)}, u32[]{:S(2)}, u32[]{:S(2)}) collective-permute-start(bf16[2,128,256]{2,1,0:T(8,128)(2,1)S(1)} %collective-permute-done.3.refs_4_), channel_id=1, source_target_pairs={{0,1},{1,0},{2,3},{3,2},{4,5},{5,4},{6,7},{7,6},{8,9},{9,8},{10,11... | collective-permute-start | bytes 393224 | tf_op jit(solution)/shard_map/ppermute | solution.py:225
  34.1 4.8 %collective-permute-start.8 = (bf16[2,128,256]{2,1,0:T(8,128)(2,1)S(1)}, bf16[2,128,256]{2,1,0:T(8,128)(2,1)S(1)}, u32[]{:S(2)}, u32[]{:S(2)}) collective-permute-start(bf16[2,128,256]{2,1,0:T(8,128)(2,1)S(1)} %collective-permute-done.7.refs_8_), channel_id=1, source_target_pairs={{0,1},{1,0},{2,3},{3,2},{4,5},{5,4},{6,7},{7,6},{8,9},{9,8},{10,11... | collective-permute-start | bytes 393224 | tf_op jit(solution)/shard_map/ppermute | solution.py:225
  34.7 4.3 %collective-permute-start.10 = (bf16[2,128,256]{2,1,0:T(8,128)(2,1)S(1)}, bf16[2,128,256]{2,1,0:T(8,128)(2,1)S(1)}, u32[]{:S(2)}, u32[]{:S(2)}) collective-permute-start(bf16[2,128,256]{2,1,0:T(8,128)(2,1)S(1)} %collective-permute-done.9.refs_10_), channel_id=1, source_target_pairs={{0,1},{1,0},{2,3},{3,2},{4,5},{5,4},{6,7},{7,6},{8,9},{9,8},{10,11... | collective-permute-start | bytes 393224 | tf_op jit(solution)/shard_map/ppermute | solution.py:225
  37.2 1.7 %collective-permute-start.12 = (bf16[2,128,256]{2,1,0:T(8,128)(2,1)S(1)}, bf16[2,128,256]{2,1,0:T(8,128)(2,1)S(1)}, u32[]{:S(2)}, u32[]{:S(2)}) collective-permute-start(bf16[2,128,256]{2,1,0:T(8,128)(2,1)S(1)} %collective-permute-done.11.refs_12_), channel_id=1, source_target_pairs={{0,1},{1,0},{2,3},{3,2},{4,5},{5,4},{6,7},{7,6},{8,9},{9,8},{10,11... | collective-permute-start | bytes 393224 | tf_op jit(solution)/shard_map/ppermute | solution.py:225
  38.9 1.3 %collective-permute-start.14 = (bf16[2,128,256]{2,1,0:T(8,128)(2,1)S(1)}, bf16[2,128,256]{2,1,0:T(8,128)(2,1)S(1)}, u32[]{:S(2)}, u32[]{:S(2)}) collective-permute-start(bf16[2,128,256]{2,1,0:T(8,128)(2,1)S(1)} %collective-permute-done.13.refs_14_), channel_id=1, source_target_pairs={{0,1},{1,0},{2,3},{3,2},{4,5},{5,4},{6,7},{7,6},{8,9},{9,8},{10,11... | collective-permute-start | bytes 393224 | tf_op jit(solution)/shard_map/ppermute | solution.py:225
  46.6 14.9 %collective-permute-start.16 = (bf16[2,16,128,128]{3,2,1,0:T(8,128)(2,1)S(1)}, bf16[2,16,128,128]{3,2,1,0:T(8,128)(2,1)S(1)}, u32[]{:S(2)}, u32[]{:S(2)}) collective-permute-start(bf16[2,16,128,128]{3,2,1,0:T(8,128)(2,1)S(1)} %get-tuple-element.48), channel_id=1, source_target_pairs={{0,16},{1,65},{16,32},{17,81},{32,48},{33,97},{48,0},{49,113},{64,... | collective-permute-start | bytes 3145736 | tf_op jit(solution)/shard_map/ppermute | solution.py:260
  47.2 17.3 %collective-permute-start.20 = (bf16[2,16,128,128]{3,2,1,0:T(8,128)(2,1)S(1)}, bf16[2,16,128,128]{3,2,1,0:T(8,128)(2,1)S(1)}, u32[]{:S(2)}, u32[]{:S(2)}) collective-permute-start(bf16[2,16,128,128]{3,2,1,0:T(8,128)(2,1)S(1)} %get-tuple-element.51), channel_id=1, source_target_pairs={{0,48},{1,193},{16,0},{17,209},{32,16},{33,225},{48,32},{49,241},{... | collective-permute-start | bytes 3145736 | tf_op jit(solution)/shard_map/ppermute | solution.py:260
  56.9 9.4 %collective-permute-start.15 = (bf16[8,2,128,256]{3,2,1,0:T(8,128)(2,1)S(1)}, bf16[8,2,128,256]{3,2,1,0:T(8,128)(2,1)S(1)}, u32[]{:S(2)}, u32[]{:S(2)}) collective-permute-start(bf16[8,2,128,256]{3,2,1,0:T(8,128)(2,1)S(1)} %get-tuple-element.45), channel_id=1, source_target_pairs={{0,1},{1,0},{2,3},{3,2},{4,5},{5,4},{6,7},{7,6},{8,9},{9,8},{10,11... | collective-permute-start | bytes 3145736 | tf_op jit(solution)/shard_map/ppermute | solution.py:225
  57.9 17.2 %collective-permute-start.18 = (bf16[2,16,128,128]{3,2,1,0:T(8,128)(2,1)}, bf16[2,16,128,128]{3,2,1,0:T(8,128)(2,1)S(1)}, u32[]{:S(2)}, u32[]{:S(2)}) collective-permute-start(bf16[2,16,128,128]{3,2,1,0:T(8,128)(2,1)} %get-tuple-element.41), channel_id=1, source_target_pairs={{0,16},{1,65},{16,32},{17,81},{32,48},{33,97},{48,0},{49,113},{64,... | collective-permute-start | bytes 3145736 | tf_op jit(solution)/shard_map/ppermute | solution.py:260
  58.7 16.3 %collective-permute-start.19 = (bf16[2,16,128,128]{3,2,1,0:T(8,128)(2,1)}, bf16[2,16,128,128]{3,2,1,0:T(8,128)(2,1)}, u32[]{:S(2)}, u32[]{:S(2)}) collective-permute-start(bf16[2,16,128,128]{3,2,1,0:T(8,128)(2,1)} %get-tuple-element.49), channel_id=1, source_target_pairs={{0,48},{1,193},{16,0},{17,209},{32,16},{33,225},{48,32},{49,241},{... | collective-permute-start | bytes 3145736 | tf_op jit(solution)/shard_map/ppermute | solution.py:260
  62.8 21.4 %collective-permute-start.17 = (bf16[2,16,128,128]{3,2,1,0:T(8,128)(2,1)}, bf16[2,16,128,128]{3,2,1,0:T(8,128)(2,1)}, u32[]{:S(2)}, u32[]{:S(2)}) collective-permute-start(bf16[2,16,128,128]{3,2,1,0:T(8,128)(2,1)} %add_convert_fusion.1), channel_id=1, source_target_pairs={{0,16},{1,65},{16,32},{17,81},{32,48},{33,97},{48,0},{49,113},{64,... | collective-permute-start | bytes 3145736 | tf_op jit(solution)/shard_map/ppermute | solution.py:260
  66.0 20.3 %collective-permute-start.21 = (bf16[2,16,128,128]{3,2,1,0:T(8,128)(2,1)}, bf16[2,16,128,128]{3,2,1,0:T(8,128)(2,1)}, u32[]{:S(2)}, u32[]{:S(2)}) collective-permute-start(bf16[2,16,128,128]{3,2,1,0:T(8,128)(2,1)} %add_convert_fusion), channel_id=1, source_target_pairs={{0,48},{1,193},{16,0},{17,209},{32,16},{33,225},{48,32},{49,241},{... | collective-permute-start | bytes 3145736 | tf_op jit(solution)/shard_map/ppermute | solution.py:260
  88.3 9.8 %collective-permute-start.23 = (bf16[2,8,128,128]{3,2,1,0:T(8,128)(2,1)S(1)}, bf16[2,8,128,128]{3,2,1,0:T(8,128)(2,1)S(1)}, u32[]{:S(2)}, u32[]{:S(2)}) collective-permute-start(bf16[2,8,128,128]{3,2,1,0:T(8,128)(2,1)S(1)} %get-tuple-element.60), channel_id=1, source_target_pairs={{0,192},{1,49},{16,208},{17,1},{32,224},{33,17},{48,240},{49,33},{... | collective-permute-start | bytes 1572872 | tf_op jit(solution)/shard_map/ppermute | solution.py:260
  91.4 10.4 %collective-permute-start.22 = (bf16[2,8,128,128]{3,2,1,0:T(8,128)(2,1)S(1)}, bf16[2,8,128,128]{3,2,1,0:T(8,128)(2,1)S(1)}, u32[]{:S(2)}, u32[]{:S(2)}) collective-permute-start(bf16[2,8,128,128]{3,2,1,0:T(8,128)(2,1)S(1)} %get-tuple-element.61), channel_id=1, source_target_pairs={{0,64},{1,17},{16,80},{17,33},{32,96},{33,49},{48,112},{49,1},{64,... | collective-permute-start | bytes 1572872 | tf_op jit(solution)/shard_map/ppermute | solution.py:260
  103.1 6.4 %collective-permute-start.25 = (bf16[2,4,128,128]{3,2,1,0:T(8,128)(2,1)S(1)}, bf16[2,4,128,128]{3,2,1,0:T(8,128)(2,1)S(1)}, u32[]{:S(2)}, u32[]{:S(2)}) collective-permute-start(bf16[2,4,128,128]{3,2,1,0:T(8,128)(2,1)S(1)} %get-tuple-element.58), channel_id=1, source_target_pairs={{0,192},{1,49},{16,208},{17,1},{32,224},{33,17},{48,240},{49,33},{... | collective-permute-start | bytes 786440 | tf_op jit(solution)/shard_map/ppermute | solution.py:260
  103.2 7.7 %collective-permute-start.24 = (bf16[2,4,128,128]{3,2,1,0:T(8,128)(2,1)S(1)}, bf16[2,4,128,128]{3,2,1,0:T(8,128)(2,1)S(1)}, u32[]{:S(2)}, u32[]{:S(2)}) collective-permute-start(bf16[2,4,128,128]{3,2,1,0:T(8,128)(2,1)S(1)} %get-tuple-element.59), channel_id=1, source_target_pairs={{0,64},{1,17},{16,80},{17,33},{32,96},{33,49},{48,112},{49,1},{64,... | collective-permute-start | bytes 786440 | tf_op jit(solution)/shard_map/ppermute | solution.py:260
Sparse Core Ops, SparseCore 0:
  67.8 38.3 reduce-scatter.1

commit v6 on v5

--- a/solution.py
+++ b/solution.py
@@ -238,10 +238,10 @@
     for k in range(1, 5):
         if k == 3:
             first, wu = lax.optimization_barrier((first, wu))
-        if k == 4:
-            first, wd = lax.optimization_barrier((first, wd))
         first = step_both(first)
         shards += [first, swap(first)]
+        if k == 3:
+            second, wd = lax.optimization_barrier((second, wd))
         if k < 4:
             second = step_both(second)
             shards += [second, swap(second)]
@@ -260,7 +260,7 @@
     return lax.ppermute(t, ("y", "x", "c"), pairs)
 
 
-def ring_sums(far_a, far_b, next_b, before_a, next_a, before_b, own):
+def ring_sums(far_a, far_b, next_b, before_a, next_a, before_b, own, terms):
     from_left = hop(far_a, 0, 1)
     from_right = hop(far_b, 0, -1)
     left_b = hop(next_b, 0, 1)
@@ -276,9 +276,10 @@
 
     from_left = hop(total(0, 8).astype(BF), 1, 1)
     from_right = hop(total(8, 8).astype(BF), 1, -1)
+    from_left, from_right, terms = lax.optimization_barrier((from_left, from_right, terms))
     end_a = hop(add(total(16, 4), from_left[:, :4]).astype(BF), 1, 1)
     end_b = hop(add(total(20, 4), from_right[:, :4]).astype(BF), 1, -1)
-    return (own, left_b, right_b, from_left, from_right, end_a, end_b)
+    return (own, left_b, right_b, from_left, from_right, end_a, end_b), terms
 
 
 def finish_kernel(count_ref, own, left_b, right_b, from_left, from_right, end_a, end_b, up_out, down_out):
@@ -312,6 +313,28 @@
     )(count, *sums)
 
 
+def owner_sum_kernel(terms_ref, mixed_ref, grad_in_ref):
+    for k, out in enumerate((mixed_ref, grad_in_ref)):
+        total = terms_ref[0, k].astype(F32)
+        for z in range(1, 8):
+            total = total + terms_ref[z, k].astype(F32)
+        out[...] = total.astype(BF)
+
+
+def owner_sum(terms):
+    shape = terms.shape[2:]
+    return pl.pallas_call(
+        owner_sum_kernel,
+        grid=(1,),
+        in_specs=[whole(*terms.shape)],
+        out_specs=[whole(*shape)] * 2,
+        out_shape=[jax.ShapeDtypeStruct(shape, BF)] * 2,
+        compiler_params=params(16),
+        cost_estimate=pl.CostEstimate(flops=1 << 19, bytes_accessed=1 << 20, transcendentals=0),
+        name="owner_sum",
+    )(terms)
+
+
 def body(tokens, grad_out, up_tiles, down_tiles, tile_rows, tile_cols, tile_count):
     where = tile_rows[0] * COLS + tile_cols[0]
     wu = dense(where, tile_count, up_tiles, True)
@@ -322,10 +345,11 @@
     h, d, _ = lax.optimization_barrier((h, d, rest[0]))
     send, keep = token_parts(h, d, wu, wd)
     pieces = add(keep, swap(send)).astype(BF)
-    sums = ring_sums(*far, *rest)
-    both = lax.psum_scatter(pieces, "z", scatter_dimension=0, tiled=True)[0]
+    terms = lax.all_to_all(pieces, "z", 0, 0, tiled=True)
+    sums, terms = ring_sums(*far, *rest, terms)
     grad_up, grad_down = finish(tile_count, sums)
-    return both[0], both[1], grad_up, grad_down
+    mixed, grad_in = owner_sum(terms)
+    return mixed, grad_in, grad_up, grad_down
 
 
 def solution(mesh):

time: 122 us -> 112 us (0.918)
  the two profiles are of different devices: /device:TPU:6 before, /device:TPU:1 now
where the time goes in v6:
time: 112 us; the launch traced here: 111 us
  starting transfers between devices  42.3 us (38%)
  waiting for transfers between devices  34.1 us (30%)
  Pallas kernels  20.9 us (19%)
  other arithmetic  9.41 us (8%)
  local copies, waits for them, and re-layouts  2.99 us (3%)
  between operations  1.39 us (1%)
    ppermute x10, waiting for transfers between devices, hop(): return lax.ppermute(t, ('y', 'x', 'c'), pairs)  26.9 us
    ppermute x10, starting transfers between devices, hop(): return lax.ppermute(t, ('y', 'x', 'c'), pairs)  12.9 us
    ppermute x9, starting transfers between devices, swap(): return lax.ppermute(x, 'c', [(0, 1), (1, 0)])  12.3 us
    ppermute x7, starting transfers between devices, step_both(): return lax.ppermute(x, ('z', 'c'), pairs)  12.2 us
    pallas_call x1, Pallas kernels, forward(): pl.pallas_call(forward_kernel, in_specs=[sspec()] + [pl.BlockSpec(memory_...  6.35 us
    all_to_all x1, starting transfers between devices, body(): terms = lax.all_to_all(pieces, 'z', 0, 0, tiled=True)  4.88 us
    pallas_call x1, Pallas kernels, token_parts(): pl.pallas_call(token_kernel, in_specs=[vspec()] * 4, out_specs=[vspec()]...  4.12 us
    all_to_all x1, waiting for transfers between devices, body(): terms = lax.all_to_all(pieces, 'z', 0, 0, tiled=True)  4.05 us
  transfers between devices with their start and end apart: 27, of which 12 were waited for; matrix products, arithmetic and copies ran while one was open for 6% of the time, Pallas kernels for 11%

profile of v6, /device:TPU:1, one launch (start us, length us, event | category | flops | bytes accessed | tf_op | source)
XLA Modules:
  0.0 111.0 jit_solution(6242032817509122134)
XLA Ops:
  1.5 6.5 %collective-permute-start.1 = (bf16[2,128,256]{2,1,0:T(8,128)(2,1)S(1)}, bf16[2,128,256]{2,1,0:T(8,128)(2,1)S(1)}, u32[]{:S(2)}, u32[]{:S(2)}) collective-permute-start(bf16[2,128,256]{2,1,0:T(8,128)(2,1)S(1)} %pad_maximum_fusion.refs_0_), channel_id=1, source_target_pairs={{0,2},{1,15},{2,4},{3,1},{4,6},{5,3},{6,8},{7,5},{8,10},{9,7},{10,... | collective-permute-start | bytes 393224 | tf_op jit(solution)/shard_map/ppermute | solution.py:221
  10.0 3.1 %collective-permute-start.5 = (bf16[2,128,256]{2,1,0:T(8,128)(2,1)S(1)}, bf16[2,128,256]{2,1,0:T(8,128)(2,1)S(1)}, u32[]{:S(2)}, u32[]{:S(2)}) collective-permute-start(bf16[2,128,256]{2,1,0:T(8,128)(2,1)S(1)} %collective-permute-done.1.refs_2_), channel_id=1, source_target_pairs={{0,2},{1,15},{2,4},{3,1},{4,6},{5,3},{6,8},{7,5},{8,10},{9,7},{10,... | collective-permute-start | bytes 393224 | tf_op jit(solution)/shard_map/ppermute | solution.py:221
  13.7 2.2 %copy-done = bf16[1,128,128,128]{3,2,1,0:T(8,128)(2,1)S(1)} copy-done((bf16[1,128,128,128]{3,2,1,0:T(8,128)(2,1)S(1)}, bf16[1,128,128,128]{3,2,1,0:T(8,128)(2,1)}, u32[]{:S(2)}) %copy-start) | copy-done | bytes 4194328
  15.9 1.5 %dense_up.1.refs_16_.wu_ref = bf16[4096,1024]{1,0:T(8,128)(2,1)S(1)} custom-call(s32[128]{0:T(128)S(1)} %add_bitcast_fusion.where, s32[1]{0:T(128)S(6)} %copy.11.count_ref, bf16[1,128,128,128]{3,2,1,0:T(8,128)(2,1)S(1)} %copy-done), custom_call_target="tpu_custom_call" | custom-call | bytes 12582912 | tf_op jit(solution)/shard_map/dense_up/pallas_call | solution.py:86
  17.5 2.0 %collective-permute-start.7 = (bf16[2,128,256]{2,1,0:T(8,128)(2,1)S(1)}, bf16[2,128,256]{2,1,0:T(8,128)(2,1)S(1)}, u32[]{:S(2)}, u32[]{:S(2)}) collective-permute-start(bf16[2,128,256]{2,1,0:T(8,128)(2,1)S(1)} %collective-permute-done.3.refs_4_), channel_id=1, source_target_pairs={{0,2},{1,15},{2,4},{3,1},{4,6},{5,3},{6,8},{7,5},{8,10},{9,7},{10,... | collective-permute-start | bytes 393224 | tf_op jit(solution)/shard_map/ppermute | solution.py:221
  19.5 1.5 %dense_down.1.refs_17_.wd_ref = bf16[1024,4096]{1,0:T(8,128)(2,1)S(1)} custom-call(s32[128]{0:T(128)S(1)} %add_bitcast_fusion.where, s32[1]{0:T(128)S(6)} %copy.11.count_ref, bf16[1,128,128,128]{3,2,1,0:T(8,128)(2,1)S(1)} %copy-done.1), custom_call_target="tpu_custom_call" | custom-call | bytes 12582912 | tf_op jit(solution)/shard_map/dense_down/pallas_call | solution.py:86
  21.0 4.3 %collective-permute-start.2 = (bf16[2,128,256]{2,1,0:T(8,128)(2,1)S(1)}, bf16[2,128,256]{2,1,0:T(8,128)(2,1)S(1)}, u32[]{:S(2)}, u32[]{:S(2)}) collective-permute-start(bf16[2,128,256]{2,1,0:T(8,128)(2,1)S(1)} %collective-permute-done.1.refs_2_), channel_id=1, source_target_pairs={{0,1},{1,0},{2,3},{3,2},{4,5},{5,4},{6,7},{7,6},{8,9},{9,8},{10,11... | collective-permute-start | bytes 393224 | tf_op jit(solution)/shard_map/ppermute | solution.py:225
  26.7 2.3 %collective-permute-start.4 = (bf16[2,128,256]{2,1,0:T(8,128)(2,1)S(1)}, bf16[2,128,256]{2,1,0:T(8,128)(2,1)S(1)}, u32[]{:S(2)}, u32[]{:S(2)}) collective-permute-start(bf16[2,128,256]{2,1,0:T(8,128)(2,1)S(1)} %collective-permute-done.3.refs_4_), channel_id=1, source_target_pairs={{0,1},{1,0},{2,3},{3,2},{4,5},{5,4},{6,7},{7,6},{8,9},{9,8},{10,11... | collective-permute-start | bytes 393224 | tf_op jit(solution)/shard_map/ppermute | solution.py:225
  29.7 2.3 %collective-permute-start.12 = (bf16[2,128,256]{2,1,0:T(8,128)(2,1)S(1)}, bf16[2,128,256]{2,1,0:T(8,128)(2,1)S(1)}, u32[]{:S(2)}, u32[]{:S(2)}) collective-permute-start(bf16[2,128,256]{2,1,0:T(8,128)(2,1)S(1)} %collective-permute-done.11.refs_12_), channel_id=1, source_target_pairs={{0,1},{1,0},{2,3},{3,2},{4,5},{5,4},{6,7},{7,6},{8,9},{9,8},{10,11... | collective-permute-start | bytes 393224 | tf_op jit(solution)/shard_map/ppermute | solution.py:225
  32.1 1.9 %collective-permute-start.14 = (bf16[2,128,256]{2,1,0:T(8,128)(2,1)S(1)}, bf16[2,128,256]{2,1,0:T(8,128)(2,1)S(1)}, u32[]{:S(2)}, u32[]{:S(2)}) collective-permute-start(bf16[2,128,256]{2,1,0:T(8,128)(2,1)S(1)} %collective-permute-done.13.refs_14_), channel_id=1, source_target_pairs={{0,1},{1,0},{2,3},{3,2},{4,5},{5,4},{6,7},{7,6},{8,9},{9,8},{10,11... | collective-permute-start | bytes 393224 | tf_op jit(solution)/shard_map/ppermute | solution.py:225
  34.9 6.3 %forward.1 = (bf16[128,1024]{1,0:T(8,128)(2,1)S(1)}, bf16[128,1024]{1,0:T(8,128)(2,1)S(1)}, bf16[128,4096]{1,0:T(8,128)(2,1)S(1)}, bf16[128,4096]{1,0:T(8,128)(2...) custom-call(s32[128]{0:T(128)S(1)} %add_bitcast_fusion.where, ...), custom_call_target="tpu_custom_call" | custom-call | flops 3221225472 | bytes 23068672 | tf_op jit(solution)/shard_map/forward/pallas_call | solution.py:148
  41.3 1.4 %collective-permute-start.15 = (bf16[2,16,128,128]{3,2,1,0:T(8,128)(2,1)S(1)}, bf16[2,16,128,128]{3,2,1,0:T(8,128)(2,1)S(1)}, u32[]{:S(2)}, u32[]{:S(2)}) collective-permute-start(bf16[2,16,128,128]{3,2,1,0:T(8,128)(2,1)S(1)} %get-tuple-element.46), channel_id=1, source_target_pairs={{0,16},{1,65},{16,32},{17,81},{32,48},{33,97},{48,0},{49,113},{64,... | collective-permute-start | bytes 3145736 | tf_op jit(solution)/shard_map/ppermute | solution.py:260
  42.7 1.5 %collective-permute-start.19 = (bf16[2,16,128,128]{3,2,1,0:T(8,128)(2,1)S(1)}, bf16[2,16,128,128]{3,2,1,0:T(8,128)(2,1)S(1)}, u32[]{:S(2)}, u32[]{:S(2)}) collective-permute-start(bf16[2,16,128,128]{3,2,1,0:T(8,128)(2,1)S(1)} %get-tuple-element.50), channel_id=1, source_target_pairs={{0,48},{1,193},{16,0},{17,209},{32,16},{33,225},{48,32},{49,241},{... | collective-permute-start | bytes 3145736 | tf_op jit(solution)/shard_map/ppermute | solution.py:260
  44.2 4.0 %rest_parts.1 = (bf16[2,16,128,128]{3,2,1,0:T(8,128)(2,1)}, bf16[2,16,128,128]{3,2,1,0:T(8,128)(2,1)}, bf16[2,16,128,128]{3,2,1,0:T(8,128)(2,1)S(1)}, bf16[2,16,...) custom-call(s32[128]{0:T(128)S(1)} %add_bitcast_fusion.where, bf16[128,4096]{1,0:T(8,128)(2,1)S(1)} %get-tuple-element.40.x_ref, ...), custom_call_target="tpu_custom_call" | custom-call | flops 1073741824 | bytes 9437184 | tf_op jit(solution)/shard_map/rest_parts/pallas_call | solution.py:168
  48.2 4.1 %token_parts.1 = (bf16[8,2,128,256]{3,2,1,0:T(8,128)(2,1)S(1)}, bf16[8,2,128,256]{3,2,1,0:T(8,128)(2,1)S(1)}) custom-call(bf16[128,1024]{1,0:T(8,128)(2,1)S(1)} %get-tuple-element.55.h_ref, bf16[128,1024]{1,0:T(8,128)(2,1)S(1)} %get-tuple-element.56.d_ref, bf16[4096,1024]{1,0:T(8,128)(2,1)S(1)} %dense_up.1.refs_16_.wu_ref, ...), custom_call_target="tpu_custom_call" | custom-call | flops 2147483648 | bytes 19922944 | tf_op jit(solution)/shard_map/token_parts/pallas_call | solution.py:201
  53.1 1.3 %collective-permute-start.17 = (bf16[2,16,128,128]{3,2,1,0:T(8,128)(2,1)}, bf16[2,16,128,128]{3,2,1,0:T(8,128)(2,1)}, u32[]{:S(2)}, u32[]{:S(2)}) collective-permute-start(bf16[2,16,128,128]{3,2,1,0:T(8,128)(2,1)} %get-tuple-element.47), channel_id=1, source_target_pairs={{0,16},{1,65},{16,32},{17,81},{32,48},{33,97},{48,0},{49,113},{64,... | collective-permute-start | bytes 3145736 | tf_op jit(solution)/shard_map/ppermute | solution.py:260
  54.5 1.4 %collective-permute-start.18 = (bf16[2,16,128,128]{3,2,1,0:T(8,128)(2,1)}, bf16[2,16,128,128]{3,2,1,0:T(8,128)(2,1)}, u32[]{:S(2)}, u32[]{:S(2)}) collective-permute-start(bf16[2,16,128,128]{3,2,1,0:T(8,128)(2,1)} %get-tuple-element.48), channel_id=1, source_target_pairs={{0,48},{1,193},{16,0},{17,209},{32,16},{33,225},{48,32},{49,241},{... | collective-permute-start | bytes 3145736 | tf_op jit(solution)/shard_map/ppermute | solution.py:260
  56.6 1.4 %add_convert_fusion.2 = bf16[2,16,128,128]{3,2,1,0:T(8,128)(2,1)} fusion(bf16[2,16,128,128]{3,2,1,0:T(8,128)(2,1)S(1)} %collective-permute-done.15, bf16[2,16,128,128]{3,2,1,0:T(8,128)(2,1)S(1)} %get-tuple-element.45), kind=kLoop, calls=%fused_computation.2 | loop fusion | flops 2097152 | bytes 3145728 | tf_op jit(solution)/shard_map/convert_element_type | solution.py:268
  58.0 1.4 %add_convert_fusion.1 = bf16[2,16,128,128]{3,2,1,0:T(8,128)(2,1)} fusion(bf16[2,16,128,128]{3,2,1,0:T(8,128)(2,1)S(1)} %collective-permute-done.19, bf16[2,16,128,128]{3,2,1,0:T(8,128)(2,1)S(1)} %get-tuple-element.49), kind=kLoop, calls=%fused_computation.1 | loop fusion | flops 2097152 | bytes 3145728 | tf_op jit(solution)/shard_map/convert_element_type | solution.py:269
  59.4 2.6 %collective-permute-start.20 = (bf16[2,16,128,128]{3,2,1,0:T(8,128)(2,1)}, bf16[2,16,128,128]{3,2,1,0:T(8,128)(2,1)}, u32[]{:S(2)}, u32[]{:S(2)}) collective-permute-start(bf16[2,16,128,128]{3,2,1,0:T(8,128)(2,1)} %add_convert_fusion.1), channel_id=1, source_target_pairs={{0,48},{1,193},{16,0},{17,209},{32,16},{33,225},{48,32},{49,241},{... | collective-permute-start | bytes 3145736 | tf_op jit(solution)/shard_map/ppermute | solution.py:260
  63.4 4.9 %all-to-all-start = ((bf16[8,2,128,256]{3,2,1,0:T(8,128)(2,1)}), bf16[8,2,128,256]{3,2,1,0:T(8,128)(2,1)S(1)}, u32[]{:S(2)}, u32[]{:S(2)}) async-start(bf16[8,2,128,256]{3,2,1,0:T(8,128)(2,1)} %add_convert_fusion), calls=%async_computation | async-start | bytes 2097152 | tf_op jit(solution)/shard_map/all_to_all | solution.py:348
  68.7 11.2 %collective-permute-done.16 = bf16[2,16,128,128]{3,2,1,0:T(8,128)(2,1)} collective-permute-done((bf16[2,16,128,128]{3,2,1,0:T(8,128)(2,1)}, bf16[2,16,128,128]{3,2,1,0:T(8,128)(2,1)}, u32[]{:S(2)}, u32[]{:S(2)}) %collective-permute-start.16) | collective-permute-done | bytes 1048608 | tf_op jit(solution)/shard_map/ppermute | solution.py:260
  79.9 2.0 %add_convert_fusion.3 = (bf16[2,8,128,128]{3,2,1,0:T(8,128)(2,1)S(1)}, bf16[2,8,128,128]{3,2,1,0:T(8,128)(2,1)S(1)}) fusion(bf16[2,16,128,128]{3,2,1,0:T(8,128)(2,1)} %collective-permute-done.18, bf16[2,16,128,128]{3,2,1,0:T(8,128)(2,1)} %collective-permute-done.16, bf16[2,32,128,128]{3,2,1,0:T(8,128)(2,1)S(1)} %get-tuple-element.44.own), kind=kLoop, calls=%fused_computation.3 | loop fusion | flops 3145728 | bytes 4194304 | tf_op jit(solution)/shard_map/convert_element_type | solution.py:278
  82.0 1.8 %collective-permute-start.22 = (bf16[2,8,128,128]{3,2,1,0:T(8,128)(2,1)S(1)}, bf16[2,8,128,128]{3,2,1,0:T(8,128)(2,1)S(1)}, u32[]{:S(2)}, u32[]{:S(2)}) collective-permute-start(bf16[2,8,128,128]{3,2,1,0:T(8,128)(2,1)S(1)} %get-tuple-element.70), channel_id=1, source_target_pairs={{0,192},{1,49},{16,208},{17,1},{32,224},{33,17},{48,240},{49,33},{... | collective-permute-start | bytes 1572872 | tf_op jit(solution)/shard_map/ppermute | solution.py:260
  83.8 6.7 %collective-permute-done.22.from_right = bf16[2,8,128,128]{3,2,1,0:T(8,128)(2,1)S(1)} collective-permute-done((bf16[2,8,128,128]{3,2,1,0:T(8,128)(2,1)S(1)}, bf16[2,8,128,128]{3,2,1,0:T(8,128)(2,1)S(1)}, u32[]{:S(2)}, u32[]{:S(2)}) %collective-permute-start.22) | collective-permute-done | bytes 524320 | tf_op jit(solution)/shard_map/ppermute | solution.py:260
  91.3 2.1 %collective-permute-done.21.from_left = bf16[2,8,128,128]{3,2,1,0:T(8,128)(2,1)} collective-permute-done((bf16[2,8,128,128]{3,2,1,0:T(8,128)(2,1)S(1)}, bf16[2,8,128,128]{3,2,1,0:T(8,128)(2,1)}, u32[]{:S(2)}, u32[]{:S(2)}) %collective-permute-start.21) | collective-permute-done | bytes 524320 | tf_op jit(solution)/shard_map/ppermute | solution.py:260
  93.4 4.0 %all-to-all-done.terms_ref = bf16[8,2,128,256]{3,2,1,0:T(8,128)(2,1)S(1)} async-done(((bf16[8,2,128,256]{3,2,1,0:T(8,128)(2,1)}), bf16[8,2,128,256]{3,2,1,0:T(8,128)(2,1)S(1)}, u32[]{:S(2)}, u32[]{:S(2)}) %all-to-all-start) | async-done | bytes 1048608 | tf_op jit(solution)/shard_map/all_to_all | solution.py:348
  97.4 1.7 %add_convert_fusion.5 = (bf16[2,4,128,128]{3,2,1,0:T(8,128)(2,1)S(1)}, bf16[2,4,128,128]{3,2,1,0:T(8,128)(2,1)S(1)}) fusion(bf16[2,8,128,128]{3,2,1,0:T(8,128)(2,1)} %copy-done.2, bf16[2,16,128,128]{3,2,1,0:T(8,128)(2,1)} %collective-permute-done.20.right_b, bf16[2,16,128,128]{3,2,1,0:T(8,128)(2,1)} %collective-permute-done.17.left_b, ...), kind=kLoop, calls=%fused_computation.5 | loop fusion | flops 2097152 | bytes 2621440 | tf_op jit(solution)/shard_map/convert_element_type | solution.py:281
  99.2 2.8 %collective-permute-start.25 = (bf16[2,4,128,128]{3,2,1,0:T(8,128)(2,1)S(1)}, bf16[2,4,128,128]{3,2,1,0:T(8,128)(2,1)S(1)}, u32[]{:S(2)}, u32[]{:S(2)}) collective-permute-start(bf16[2,4,128,128]{3,2,1,0:T(8,128)(2,1)S(1)} %get-tuple-element.68), channel_id=1, source_target_pairs={{0,192},{1,49},{16,208},{17,1},{32,224},{33,17},{48,240},{49,33},{... | collective-permute-start | bytes 786440 | tf_op jit(solution)/shard_map/ppermute | solution.py:260
  102.7 2.5 %collective-permute-done.25.end_b = bf16[2,4,128,128]{3,2,1,0:T(8,128)(2,1)S(1)} collective-permute-done((bf16[2,4,128,128]{3,2,1,0:T(8,128)(2,1)S(1)}, bf16[2,4,128,128]{3,2,1,0:T(8,128)(2,1)S(1)}, u32[]{:S(2)}, u32[]{:S(2)}) %collective-permute-start.25) | collective-permute-done | bytes 262176 | tf_op jit(solution)/shard_map/ppermute | solution.py:260
  105.3 3.1 %collective-permute-done.24.end_a = bf16[2,4,128,128]{3,2,1,0:T(8,128)(2,1)S(1)} collective-permute-done((bf16[2,4,128,128]{3,2,1,0:T(8,128)(2,1)S(1)}, bf16[2,4,128,128]{3,2,1,0:T(8,128)(2,1)S(1)}, u32[]{:S(2)}, u32[]{:S(2)}) %collective-permute-start.24) | collective-permute-done | bytes 262176 | tf_op jit(solution)/shard_map/ppermute | solution.py:260
  108.4 2.6 %finish.1 = (f32[1,8,128,128]{3,2,1,0:T(8,128)}, f32[1,8,128,128]{3,2,1,0:T(8,128)}) custom-call(s32[1]{0:T(128)S(6)} %copy.11.count_ref, bf16[2,32,128,128]{3,2,1,0:T(8,128)(2,1)S(1)} %get-tuple-element.44.own, bf16[2,16,128,128]{3,2,1,0:T(8,128)(2,1)} %collective-permute-done.17.left_b, bf16[2,16,128,128]{3,2,1,0:T(8,128)(2,1)} %collective-permute-done.20.right_b, ...), custom_call_target="tpu_custom_call" | custom-call | flops 1048576 | bytes 3145728 | tf_op jit(solution)/shard_map/finish/pallas_call | solution.py:304
  (44 shorter events, 10.9 us)
Async XLA Ops:
  1.5 8.4 %collective-permute-start.1 = (bf16[2,128,256]{2,1,0:T(8,128)(2,1)S(1)}, bf16[2,128,256]{2,1,0:T(8,128)(2,1)S(1)}, u32[]{:S(2)}, u32[]{:S(2)}) collective-permute-start(bf16[2,128,256]{2,1,0:T(8,128)(2,1)S(1)} %pad_maximum_fusion.refs_0_), channel_id=1, source_target_pairs={{0,2},{1,15},{2,4},{3,1},{4,6},{5,3},{6,8},{7,5},{8,10},{9,7},{10,... | collective-permute-start | bytes 393224 | tf_op jit(solution)/shard_map/ppermute | solution.py:221
  8.0 5.0 %collective-permute-start = (bf16[2,128,256]{2,1,0:T(8,128)(2,1)S(1)}, bf16[2,128,256]{2,1,0:T(8,128)(2,1)S(1)}, u32[]{:S(2)}, u32[]{:S(2)}) collective-permute-start(bf16[2,128,256]{2,1,0:T(8,128)(2,1)S(1)} %pad_maximum_fusion.refs_0_), channel_id=1, source_target_pairs={{0,1},{1,0},{2,3},{3,2},{4,5},{5,4},{6,7},{7,6},{8,9},{9,8},{10,11... | collective-permute-start | bytes 393224 | tf_op jit(solution)/shard_map/ppermute | solution.py:225
  10.0 9.5 %collective-permute-start.5 = (bf16[2,128,256]{2,1,0:T(8,128)(2,1)S(1)}, bf16[2,128,256]{2,1,0:T(8,128)(2,1)S(1)}, u32[]{:S(2)}, u32[]{:S(2)}) collective-permute-start(bf16[2,128,256]{2,1,0:T(8,128)(2,1)S(1)} %collective-permute-done.1.refs_2_), channel_id=1, source_target_pairs={{0,2},{1,15},{2,4},{3,1},{4,6},{5,3},{6,8},{7,5},{8,10},{9,7},{10,... | collective-permute-start | bytes 393224 | tf_op jit(solution)/shard_map/ppermute | solution.py:221
  13.0 4.4 %collective-permute-start.3 = (bf16[2,128,256]{2,1,0:T(8,128)(2,1)S(1)}, bf16[2,128,256]{2,1,0:T(8,128)(2,1)S(1)}, u32[]{:S(2)}, u32[]{:S(2)}) collective-permute-start(bf16[2,128,256]{2,1,0:T(8,128)(2,1)S(1)} %collective-permute-done.refs_1_), channel_id=1, source_target_pairs={{0,2},{1,15},{2,4},{3,1},{4,6},{5,3},{6,8},{7,5},{8,10},{9,7},{10,... | collective-permute-start | bytes 393224 | tf_op jit(solution)/shard_map/ppermute | solution.py:221
  13.7 2.2 %copy-start = (bf16[1,128,128,128]{3,2,1,0:T(8,128)(2,1)S(1)}, bf16[1,128,128,128]{3,2,1,0:T(8,128)(2,1)}, u32[]{:S(2)}) copy-start(bf16[1,128,128,128]{3,2,1,0:T(8,128)(2,1)} %tiles_ref.2) | copy-start | bytes 12582916
  15.9 3.6 %copy-start.1 = (bf16[1,128,128,128]{3,2,1,0:T(8,128)(2,1)S(1)}, bf16[1,128,128,128]{3,2,1,0:T(8,128)(2,1)}, u32[]{:S(2)}) copy-start(bf16[1,128,128,128]{3,2,1,0:T(8,128)(2,1)} %tiles_ref.3) | copy-start | bytes 12582916
  17.5 8.0 %collective-permute-start.7 = (bf16[2,128,256]{2,1,0:T(8,128)(2,1)S(1)}, bf16[2,128,256]{2,1,0:T(8,128)(2,1)S(1)}, u32[]{:S(2)}, u32[]{:S(2)}) collective-permute-start(bf16[2,128,256]{2,1,0:T(8,128)(2,1)S(1)} %collective-permute-done.3.refs_4_), channel_id=1, source_target_pairs={{0,2},{1,15},{2,4},{3,1},{4,6},{5,3},{6,8},{7,5},{8,10},{9,7},{10,... | collective-permute-start | bytes 393224 | tf_op jit(solution)/shard_map/ppermute | solution.py:221
  19.5 6.6 %collective-permute-start.9 = (bf16[2,128,256]{2,1,0:T(8,128)(2,1)S(1)}, bf16[2,128,256]{2,1,0:T(8,128)(2,1)S(1)}, u32[]{:S(2)}, u32[]{:S(2)}) collective-permute-start(bf16[2,128,256]{2,1,0:T(8,128)(2,1)S(1)} %collective-permute-done.5.refs_6_), channel_id=1, source_target_pairs={{0,2},{1,15},{2,4},{3,1},{4,6},{5,3},{6,8},{7,5},{8,10},{9,7},{10,... | collective-permute-start | bytes 393224 | tf_op jit(solution)/shard_map/ppermute | solution.py:221
  21.0 7.9 %collective-permute-start.2 = (bf16[2,128,256]{2,1,0:T(8,128)(2,1)S(1)}, bf16[2,128,256]{2,1,0:T(8,128)(2,1)S(1)}, u32[]{:S(2)}, u32[]{:S(2)}) collective-permute-start(bf16[2,128,256]{2,1,0:T(8,128)(2,1)S(1)} %collective-permute-done.1.refs_2_), channel_id=1, source_target_pairs={{0,1},{1,0},{2,3},{3,2},{4,5},{5,4},{6,7},{7,6},{8,9},{9,8},{10,11... | collective-permute-start | bytes 393224 | tf_op jit(solution)/shard_map/ppermute | solution.py:225
  25.4 3.6 %collective-permute-start.6 = (bf16[2,128,256]{2,1,0:T(8,128)(2,1)S(1)}, bf16[2,128,256]{2,1,0:T(8,128)(2,1)S(1)}, u32[]{:S(2)}, u32[]{:S(2)}) collective-permute-start(bf16[2,128,256]{2,1,0:T(8,128)(2,1)S(1)} %collective-permute-done.5.refs_6_), channel_id=1, source_target_pairs={{0,1},{1,0},{2,3},{3,2},{4,5},{5,4},{6,7},{7,6},{8,9},{9,8},{10,11... | collective-permute-start | bytes 393224 | tf_op jit(solution)/shard_map/ppermute | solution.py:225
  25.5 4.2 %collective-permute-start.11 = (bf16[2,128,256]{2,1,0:T(8,128)(2,1)S(1)}, bf16[2,128,256]{2,1,0:T(8,128)(2,1)S(1)}, u32[]{:S(2)}, u32[]{:S(2)}) collective-permute-start(bf16[2,128,256]{2,1,0:T(8,128)(2,1)S(1)} %collective-permute-done.7.refs_8_), channel_id=1, source_target_pairs={{0,2},{1,15},{2,4},{3,1},{4,6},{5,3},{6,8},{7,5},{8,10},{9,7},{10,... | collective-permute-start | bytes 393224 | tf_op jit(solution)/shard_map/ppermute | solution.py:221
  26.0 6.0 %collective-permute-start.13 = (bf16[2,128,256]{2,1,0:T(8,128)(2,1)S(1)}, bf16[2,128,256]{2,1,0:T(8,128)(2,1)S(1)}, u32[]{:S(2)}, u32[]{:S(2)}) collective-permute-start(bf16[2,128,256]{2,1,0:T(8,128)(2,1)S(1)} %collective-permute-done.9.refs_10_), channel_id=1, source_target_pairs={{0,2},{1,15},{2,4},{3,1},{4,6},{5,3},{6,8},{7,5},{8,10},{9,7},{10,... | collective-permute-start | bytes 393224 | tf_op jit(solution)/shard_map/ppermute | solution.py:221
  26.7 7.3 %collective-permute-start.4 = (bf16[2,128,256]{2,1,0:T(8,128)(2,1)S(1)}, bf16[2,128,256]{2,1,0:T(8,128)(2,1)S(1)}, u32[]{:S(2)}, u32[]{:S(2)}) collective-permute-start(bf16[2,128,256]{2,1,0:T(8,128)(2,1)S(1)} %collective-permute-done.3.refs_4_), channel_id=1, source_target_pairs={{0,1},{1,0},{2,3},{3,2},{4,5},{5,4},{6,7},{7,6},{8,9},{9,8},{10,11... | collective-permute-start | bytes 393224 | tf_op jit(solution)/shard_map/ppermute | solution.py:225
  28.9 5.0 %collective-permute-start.8 = (bf16[2,128,256]{2,1,0:T(8,128)(2,1)S(1)}, bf16[2,128,256]{2,1,0:T(8,128)(2,1)S(1)}, u32[]{:S(2)}, u32[]{:S(2)}) collective-permute-start(bf16[2,128,256]{2,1,0:T(8,128)(2,1)S(1)} %collective-permute-done.7.refs_8_), channel_id=1, source_target_pairs={{0,1},{1,0},{2,3},{3,2},{4,5},{5,4},{6,7},{7,6},{8,9},{9,8},{10,11... | collective-permute-start | bytes 393224 | tf_op jit(solution)/shard_map/ppermute | solution.py:225
  28.9 5.0 %collective-permute-start.10 = (bf16[2,128,256]{2,1,0:T(8,128)(2,1)S(1)}, bf16[2,128,256]{2,1,0:T(8,128)(2,1)S(1)}, u32[]{:S(2)}, u32[]{:S(2)}) collective-permute-start(bf16[2,128,256]{2,1,0:T(8,128)(2,1)S(1)} %collective-permute-done.9.refs_10_), channel_id=1, source_target_pairs={{0,1},{1,0},{2,3},{3,2},{4,5},{5,4},{6,7},{7,6},{8,9},{9,8},{10,11... | collective-permute-start | bytes 393224 | tf_op jit(solution)/shard_map/ppermute | solution.py:225
  29.7 4.2 %collective-permute-start.12 = (bf16[2,128,256]{2,1,0:T(8,128)(2,1)S(1)}, bf16[2,128,256]{2,1,0:T(8,128)(2,1)S(1)}, u32[]{:S(2)}, u32[]{:S(2)}) collective-permute-start(bf16[2,128,256]{2,1,0:T(8,128)(2,1)S(1)} %collective-permute-done.11.refs_12_), channel_id=1, source_target_pairs={{0,1},{1,0},{2,3},{3,2},{4,5},{5,4},{6,7},{7,6},{8,9},{9,8},{10,11... | collective-permute-start | bytes 393224 | tf_op jit(solution)/shard_map/ppermute | solution.py:225
  32.1 2.8 %collective-permute-start.14 = (bf16[2,128,256]{2,1,0:T(8,128)(2,1)S(1)}, bf16[2,128,256]{2,1,0:T(8,128)(2,1)S(1)}, u32[]{:S(2)}, u32[]{:S(2)}) collective-permute-start(bf16[2,128,256]{2,1,0:T(8,128)(2,1)S(1)} %collective-permute-done.13.refs_14_), channel_id=1, source_target_pairs={{0,1},{1,0},{2,3},{3,2},{4,5},{5,4},{6,7},{7,6},{8,9},{9,8},{10,11... | collective-permute-start | bytes 393224 | tf_op jit(solution)/shard_map/ppermute | solution.py:225
  41.3 15.3 %collective-permute-start.15 = (bf16[2,16,128,128]{3,2,1,0:T(8,128)(2,1)S(1)}, bf16[2,16,128,128]{3,2,1,0:T(8,128)(2,1)S(1)}, u32[]{:S(2)}, u32[]{:S(2)}) collective-permute-start(bf16[2,16,128,128]{3,2,1,0:T(8,128)(2,1)S(1)} %get-tuple-element.46), channel_id=1, source_target_pairs={{0,16},{1,65},{16,32},{17,81},{32,48},{33,97},{48,0},{49,113},{64,... | collective-permute-start | bytes 3145736 | tf_op jit(solution)/shard_map/ppermute | solution.py:260
  42.7 15.4 %collective-permute-start.19 = (bf16[2,16,128,128]{3,2,1,0:T(8,128)(2,1)S(1)}, bf16[2,16,128,128]{3,2,1,0:T(8,128)(2,1)S(1)}, u32[]{:S(2)}, u32[]{:S(2)}) collective-permute-start(bf16[2,16,128,128]{3,2,1,0:T(8,128)(2,1)S(1)} %get-tuple-element.50), channel_id=1, source_target_pairs={{0,48},{1,193},{16,0},{17,209},{32,16},{33,225},{48,32},{49,241},{... | collective-permute-start | bytes 3145736 | tf_op jit(solution)/shard_map/ppermute | solution.py:260
  52.3 9.8 %collective-permute-start.23 = (bf16[8,2,128,256]{3,2,1,0:T(8,128)(2,1)S(1)}, bf16[8,2,128,256]{3,2,1,0:T(8,128)(2,1)S(1)}, u32[]{:S(2)}, u32[]{:S(2)}) collective-permute-start(bf16[8,2,128,256]{3,2,1,0:T(8,128)(2,1)S(1)} %get-tuple-element.58), channel_id=1, source_target_pairs={{0,1},{1,0},{2,3},{3,2},{4,5},{5,4},{6,7},{7,6},{8,9},{9,8},{10,11... | collective-permute-start | bytes 3145736 | tf_op jit(solution)/shard_map/ppermute | solution.py:225
  53.1 15.6 %collective-permute-start.17 = (bf16[2,16,128,128]{3,2,1,0:T(8,128)(2,1)}, bf16[2,16,128,128]{3,2,1,0:T(8,128)(2,1)}, u32[]{:S(2)}, u32[]{:S(2)}) collective-permute-start(bf16[2,16,128,128]{3,2,1,0:T(8,128)(2,1)} %get-tuple-element.47), channel_id=1, source_target_pairs={{0,16},{1,65},{16,32},{17,81},{32,48},{33,97},{48,0},{49,113},{64,... | collective-permute-start | bytes 3145736 | tf_op jit(solution)/shard_map/ppermute | solution.py:260
  54.5 14.3 %collective-permute-start.18 = (bf16[2,16,128,128]{3,2,1,0:T(8,128)(2,1)}, bf16[2,16,128,128]{3,2,1,0:T(8,128)(2,1)}, u32[]{:S(2)}, u32[]{:S(2)}) collective-permute-start(bf16[2,16,128,128]{3,2,1,0:T(8,128)(2,1)} %get-tuple-element.48), channel_id=1, source_target_pairs={{0,48},{1,193},{16,0},{17,209},{32,16},{33,225},{48,32},{49,241},{... | collective-permute-start | bytes 3145736 | tf_op jit(solution)/shard_map/ppermute | solution.py:260
  58.0 21.9 %collective-permute-start.16 = (bf16[2,16,128,128]{3,2,1,0:T(8,128)(2,1)}, bf16[2,16,128,128]{3,2,1,0:T(8,128)(2,1)}, u32[]{:S(2)}, u32[]{:S(2)}) collective-permute-start(bf16[2,16,128,128]{3,2,1,0:T(8,128)(2,1)} %add_convert_fusion.2), channel_id=1, source_target_pairs={{0,16},{1,65},{16,32},{17,81},{32,48},{33,97},{48,0},{49,113},{64,... | collective-permute-start | bytes 3145736 | tf_op jit(solution)/shard_map/ppermute | solution.py:260
  59.4 20.5 %collective-permute-start.20 = (bf16[2,16,128,128]{3,2,1,0:T(8,128)(2,1)}, bf16[2,16,128,128]{3,2,1,0:T(8,128)(2,1)}, u32[]{:S(2)}, u32[]{:S(2)}) collective-permute-start(bf16[2,16,128,128]{3,2,1,0:T(8,128)(2,1)} %add_convert_fusion.1), channel_id=1, source_target_pairs={{0,48},{1,193},{16,0},{17,209},{32,16},{33,225},{48,32},{49,241},{... | collective-permute-start | bytes 3145736 | tf_op jit(solution)/shard_map/ppermute | solution.py:260
  63.4 34.1 %all-to-all-start = ((bf16[8,2,128,256]{3,2,1,0:T(8,128)(2,1)}), bf16[8,2,128,256]{3,2,1,0:T(8,128)(2,1)S(1)}, u32[]{:S(2)}, u32[]{:S(2)}) async-start(bf16[8,2,128,256]{3,2,1,0:T(8,128)(2,1)} %add_convert_fusion), calls=%async_computation | async-start | bytes 2097152 | tf_op jit(solution)/shard_map/all_to_all | solution.py:348
  82.0 8.5 %collective-permute-start.22 = (bf16[2,8,128,128]{3,2,1,0:T(8,128)(2,1)S(1)}, bf16[2,8,128,128]{3,2,1,0:T(8,128)(2,1)S(1)}, u32[]{:S(2)}, u32[]{:S(2)}) collective-permute-start(bf16[2,8,128,128]{3,2,1,0:T(8,128)(2,1)S(1)} %get-tuple-element.70), channel_id=1, source_target_pairs={{0,192},{1,49},{16,208},{17,1},{32,224},{33,17},{48,240},{49,33},{... | collective-permute-start | bytes 1572872 | tf_op jit(solution)/shard_map/ppermute | solution.py:260
  83.8 9.6 %collective-permute-start.21 = (bf16[2,8,128,128]{3,2,1,0:T(8,128)(2,1)S(1)}, bf16[2,8,128,128]{3,2,1,0:T(8,128)(2,1)}, u32[]{:S(2)}, u32[]{:S(2)}) collective-permute-start(bf16[2,8,128,128]{3,2,1,0:T(8,128)(2,1)S(1)} %get-tuple-element.71), channel_id=1, source_target_pairs={{0,64},{1,17},{16,80},{17,33},{32,96},{33,49},{48,112},{49,1},{64,... | collective-permute-start | bytes 1572872 | tf_op jit(solution)/shard_map/ppermute | solution.py:260
  90.5 0.8 copy-start.2
  97.4 11.0 %copy-start.3 = (bf16[2,8,128,128]{3,2,1,0:T(8,128)(2,1)S(1)}, bf16[2,8,128,128]{3,2,1,0:T(8,128)(2,1)}, u32[]{:S(2)}) copy-start(bf16[2,8,128,128]{3,2,1,0:T(8,128)(2,1)} %copy-done.2) | copy-start | bytes 1572868
  99.2 6.1 %collective-permute-start.25 = (bf16[2,4,128,128]{3,2,1,0:T(8,128)(2,1)S(1)}, bf16[2,4,128,128]{3,2,1,0:T(8,128)(2,1)S(1)}, u32[]{:S(2)}, u32[]{:S(2)}) collective-permute-start(bf16[2,4,128,128]{3,2,1,0:T(8,128)(2,1)S(1)} %get-tuple-element.68), channel_id=1, source_target_pairs={{0,192},{1,49},{16,208},{17,1},{32,224},{33,17},{48,240},{49,33},{... | collective-permute-start | bytes 786440 | tf_op jit(solution)/shard_map/ppermute | solution.py:260
  102.0 6.4 %collective-permute-start.24 = (bf16[2,4,128,128]{3,2,1,0:T(8,128)(2,1)S(1)}, bf16[2,4,128,128]{3,2,1,0:T(8,128)(2,1)S(1)}, u32[]{:S(2)}, u32[]{:S(2)}) collective-permute-start(bf16[2,4,128,128]{3,2,1,0:T(8,128)(2,1)S(1)} %get-tuple-element.69), channel_id=1, source_target_pairs={{0,64},{1,17},{16,80},{17,33},{32,96},{33,49},{48,112},{49,1},{64,... | collective-permute-start | bytes 786440 | tf_op jit(solution)/shard_map/ppermute | solution.py:260

commit v7 on v6

--- a/solution.py
+++ b/solution.py
@@ -99,14 +99,22 @@
     return pl.ds(pl.multiple_of(k * n, n), n)
 
 
-def forward_kernel(where, *refs):
-    shards = refs[:16]
-    wu_ref, wd_ref, h_ref, d_ref, x_ref, dy_ref, dt_ref, ht_ref = refs[16:24]
-    parts, sem = refs[24:26], refs[26]
+EARLY = 10
+
+
+def early_kernel(*refs):
+    shards, (wu_ref, wd_ref, pre_ref, gh_ref, x_ref, dy_ref, sem) = refs[:EARLY], refs[EARLY:]
+    fetch_shards(shards, range(EARLY), x_ref, dy_ref, sem)
     wide = 2 * SIDE
+    for n in range(ROWS // 2):
+        at = slice(n * wide, (n + 1) * wide)
+        pre_ref[:, at], gh_ref[:, at] = products(range(EARLY), at, x_ref, dy_ref, wu_ref, wd_ref)
+
+
+def fetch_shards(shards, which, x_ref, dy_ref, sem):
     copies = []
-    for k in range(16):
-        at = lanes(other_owner(k), wide)
+    for k in which:
+        at = lanes(other_owner(k), 2 * SIDE)
         copies.append(pltpu.make_async_copy(shards[k].at[0], x_ref.at[:, at], sem))
         copies.append(pltpu.make_async_copy(shards[k].at[1], dy_ref.at[:, at], sem))
     for copy in copies:
@@ -114,20 +122,48 @@
     for copy in copies:
         copy.wait()
 
-    @pl.loop(0, ROWS // 2)
-    def _(n):
-        at = lanes(n, wide)
-        pre = nn(x_ref[...], wu_ref[:, at])
-        grad_hidden = nt(dy_ref[...], wd_ref[at, :])
-        value, slope = gelu_pair(pre)
-        grad = grad_hidden * slope
+
+def products(which, at, x_ref, dy_ref, wu_ref, wd_ref):
+    pre, grad_hidden = 0.0, 0.0
+    for k in which:
+        features = lanes(other_owner(k), 2 * SIDE)
+        pre = pre + nn(x_ref[:, features], wu_ref[features, at])
+        grad_hidden = grad_hidden + nt(dy_ref[:, features], wd_ref[at, features])
+    return pre, grad_hidden
+
+
+def early(shards, wu, wd):
+    acc = jax.ShapeDtypeStruct((SIDE, ROWS * SIDE), F32)
+    return pl.pallas_call(
+        early_kernel,
+        in_specs=[pl.BlockSpec(memory_space=pl.ANY)] * EARLY + [vspec()] * 2,
+        out_specs=[vspec()] * 2,
+        out_shape=[acc, acc],
+        scratch_shapes=[VM((SIDE, COLS * SIDE), BF)] * 2 + [pltpu.SemaphoreType.DMA],
+        compiler_params=params(16),
+        cost_estimate=pl.CostEstimate(flops=5 << 28, bytes_accessed=13 << 20, transcendentals=0),
+        name="early",
+    )(*shards[:EARLY], wu, wd)
+
+
+def forward_kernel(where, *refs):
+    shards = refs[:16]
+    wu_ref, wd_ref, pre_ref, gh_ref = refs[16:20]
+    h_ref, d_ref, x_ref, dy_ref, dt_ref, ht_ref = refs[20:26]
+    parts, sem = refs[26:28], refs[28]
+    wide = 2 * SIDE
+    fetch_shards(shards, range(16), x_ref, dy_ref, sem)
+    for n in range(ROWS // 2):
+        at = slice(n * wide, (n + 1) * wide)
+        pre, grad_hidden = products(range(EARLY, 16), at, x_ref, dy_ref, wu_ref, wd_ref)
+        value, slope = gelu_pair(pre + pre_ref[:, at])
+        grad = (grad_hidden + gh_ref[:, at]) * slope
         h_ref[:, at] = value.astype(BF)
         d_ref[:, at] = grad.astype(BF)
         for b in range(2):
             half = slice(b * SIDE, (b + 1) * SIDE)
             ht_ref[2 * n + b] = value[:, half].T.astype(BF)
             dt_ref[2 * n + b] = grad[:, half].T.astype(BF)
-
     fill_parts(where, x_ref, dy_ref, dt_ref, ht_ref, parts, ((2, 0, 16), (2, 16, 16)))
 
 
@@ -140,21 +176,21 @@
             out[1, s] = nn(ht_ref[row], dy_ref[:, at]).astype(BF)
 
 
-def forward(where, shards, wu, wd):
+def forward(where, shards, wu, wd, first):
     hid = jax.ShapeDtypeStruct((SIDE, ROWS * SIDE), BF)
     tok = jax.ShapeDtypeStruct((SIDE, COLS * SIDE), BF)
     turned = jax.ShapeDtypeStruct((ROWS, SIDE, SIDE), BF)
     part = jax.ShapeDtypeStruct((2, 16, SIDE, SIDE), BF)
     return pl.pallas_call(
         forward_kernel,
-        in_specs=[sspec()] + [pl.BlockSpec(memory_space=pl.ANY)] * 16 + [vspec()] * 2,
+        in_specs=[sspec()] + [pl.BlockSpec(memory_space=pl.ANY)] * 16 + [vspec()] * 4,
         out_specs=[vspec()] * 8,
         out_shape=[hid, hid, tok, tok, turned, turned, part, part],
         scratch_shapes=[pltpu.SemaphoreType.DMA],
         compiler_params=params(16),
         cost_estimate=pl.CostEstimate(flops=3 << 30, bytes_accessed=22 << 20, transcendentals=1 << 18),
         name="forward",
-    )(where, *shards, wu, wd)
+    )(where, *shards, wu, wd, *first)
 
 
 REST = ((1, 16, 16), (3, 0, 16), (1, 0, 16), (3, 16, 16), (0, 0, 32))
@@ -239,13 +275,16 @@
         if k == 3:
             first, wu = lax.optimization_barrier((first, wu))
         first = step_both(first)
+        if k == 4:
+            sums = early(shards, wu, wd)
+            first, *sums = lax.optimization_barrier((first, *sums))
         shards += [first, swap(first)]
         if k == 3:
             second, wd = lax.optimization_barrier((second, wd))
         if k < 4:
             second = step_both(second)
             shards += [second, swap(second)]
-    return shards, wu, wd
+    return shards, wu, wd, sums
 
 
 def hop(t, stage, by):
@@ -276,18 +315,40 @@
 
     from_left = hop(total(0, 8).astype(BF), 1, 1)
     from_right = hop(total(8, 8).astype(BF), 1, -1)
-    from_left, from_right, terms = lax.optimization_barrier((from_left, from_right, terms))
+    from_left, terms = lax.optimization_barrier((from_left, terms))
     end_a = hop(add(total(16, 4), from_left[:, :4]).astype(BF), 1, 1)
     end_b = hop(add(total(20, 4), from_right[:, :4]).astype(BF), 1, -1)
-    return (own, left_b, right_b, from_left, from_right, end_a, end_b), terms
-
-
-def finish_kernel(count_ref, own, left_b, right_b, from_left, from_right, end_a, end_b, up_out, down_out):
+    return (near_sum(own, left_b, right_b), from_left, from_right, end_a, end_b), terms
+
+
+def near_sum_kernel(own, left_b, right_b, out):
+    for k in range(2):
+        for s in range(8):
+            out[k, s] = add(own[k, s], left_b[k, s], right_b[k, s])
+
+
+def near_sum(own, left_b, right_b):
+    def last(block):
+        return pl.BlockSpec((2, 8, SIDE, SIDE), lambda i: (0, block, 0, 0))
+
+    return pl.pallas_call(
+        near_sum_kernel,
+        grid=(1,),
+        in_specs=[last(3), last(1), last(1)],
+        out_specs=whole(2, 8, SIDE, SIDE),
+        out_shape=jax.ShapeDtypeStruct((2, 8, SIDE, SIDE), F32),
+        compiler_params=params(16),
+        cost_estimate=pl.CostEstimate(flops=1 << 19, bytes_accessed=3 << 20, transcendentals=0),
+        name="near_sum",
+    )(own, left_b, right_b)
+
+
+def finish_kernel(count_ref, near, from_left, from_right, end_a, end_b, up_out, down_out):
     first = lax.axis_index(("y", "x")) * 8
     for k in range(2):
         for s in range(8):
             one, two = (end_a[k, s], from_right[k, 4 + s]) if s < 4 else (from_left[k, s], end_b[k, s - 4])
-            total = add(own[k, s], left_b[k, s], right_b[k, s], one, two)
+            total = add(near[k, s], one, two)
             total = jnp.where(first + s < count_ref[0], total * (1.0 / 16), 0.0)
             if k == 0:
                 up_out[0, s] = total.T
@@ -297,14 +358,10 @@
 
 def finish(count, sums):
     shape = (1, 8, SIDE, SIDE)
-
-    def last(block):
-        return pl.BlockSpec((2, 8, SIDE, SIDE), lambda i: (0, block, 0, 0))
-
     return pl.pallas_call(
         finish_kernel,
         grid=(1,),
-        in_specs=[sspec(), last(3), last(1), last(1)] + [whole(2, n, SIDE, SIDE) for n in (8, 8, 4, 4)],
+        in_specs=[sspec()] + [whole(2, n, SIDE, SIDE) for n in (8, 8, 8, 4, 4)],
         out_specs=[whole(*shape)] * 2,
         out_shape=[jax.ShapeDtypeStruct(shape, F32)] * 2,
         compiler_params=params(16),
@@ -339,8 +396,8 @@
     where = tile_rows[0] * COLS + tile_cols[0]
     wu = dense(where, tile_count, up_tiles, True)
     wd = dense(where, tile_count, down_tiles, False)
-    shards, wu, wd = gather_over_tile(jnp.stack([tokens, grad_out]), wu, wd)
-    h, d, x, dy, dt, ht, *far = forward(where, shards, wu, wd)
+    shards, wu, wd, first = gather_over_tile(jnp.stack([tokens, grad_out]), wu, wd)
+    h, d, x, dy, dt, ht, *far = forward(where, shards, wu, wd, first)
     rest = rest_parts(where, x, dy, dt, ht)
     h, d, _ = lax.optimization_barrier((h, d, rest[0]))
     send, keep = token_parts(h, d, wu, wd)

time: 112 us -> 109 us (0.973)
  starting transfers between devices: 42.3 us -> 39.2 us
  waiting for transfers between devices: 34.1 us -> 31.2 us
  Pallas kernels: 20.9 us -> 23.6 us
    pallas_call x1 -> x3, Pallas kernels: 2.63 us -> 6.49 us  [the longest x1 2.7 us: early(): pl.pallas_call(early_kernel, in_specs=[pl.BlockSpec(memory_space=pl.ANY)]...]
    ppermute x10, waiting for transfers between devices: 26.9 us -> 23.1 us  [hop(): return lax.ppermute(t, ('y', 'x', 'c'), pairs)]
    ppermute x9, starting transfers between devices: 12.3 us -> 9.21 us  [swap(): return lax.ppermute(x, 'c', [(0, 1), (1, 0)])]
    pallas_call x1, Pallas kernels: 6.35 us -> 3.75 us  [forward(): pl.pallas_call(forward_kernel, in_specs=[sspec()] + [pl.BlockSpec(memory_...]
    all_to_all x1, waiting for transfers between devices: 4.05 us -> 5.66 us  [body(): terms = lax.all_to_all(pieces, 'z', 0, 0, tiled=True)]
    pallas_call x2, Pallas kernels: 3.04 us -> 4.47 us  [dense(): pl.pallas_call(functools.partial(dense_kernel, up), in_specs=[sspec()] *...]
    ppermute x7, starting transfers between devices: 12.2 us -> 10.8 us  [step_both(): return lax.ppermute(x, ('z', 'c'), pairs)]
    unnamed x8 -> x4, local copies, waits for them, and re-layouts: 2.99 us -> 2.19 us
  transfers between devices with their start and end apart: 27 -> 27, of which waited for: 12 -> 10; matrix products, arithmetic and copies ran while one was open for 6% -> 7% of each run, Pallas kernels for 11% -> 16%
where the time goes in v7:
time: 109 us; the launch traced here: 108 us
  starting transfers between devices  39.2 us (36%)
  waiting for transfers between devices  31.2 us (29%)
  Pallas kernels  23.6 us (22%)
  other arithmetic  10.2 us (9%)
  local copies, waits for them, and re-layouts  2.19 us (2%)
  between operations  1.42 us (1%)
    ppermute x10, waiting for transfers between devices, hop(): return lax.ppermute(t, ('y', 'x', 'c'), pairs)  23.1 us
    ppermute x10, starting transfers between devices, hop(): return lax.ppermute(t, ('y', 'x', 'c'), pairs)  13.8 us
    ppermute x7, starting transfers between devices, step_both(): return lax.ppermute(x, ('z', 'c'), pairs)  10.8 us
    ppermute x9, starting transfers between devices, swap(): return lax.ppermute(x, 'c', [(0, 1), (1, 0)])  9.21 us
    all_to_all x1, waiting for transfers between devices, body(): terms = lax.all_to_all(pieces, 'z', 0, 0, tiled=True)  5.66 us
    all_to_all x1, starting transfers between devices, body(): terms = lax.all_to_all(pieces, 'z', 0, 0, tiled=True)  5.31 us
    pallas_call x2, Pallas kernels, dense(): pl.pallas_call(functools.partial(dense_kernel, up), in_specs=[sspec()] *...  4.47 us
    pallas_call x1, Pallas kernels, token_parts(): pl.pallas_call(token_kernel, in_specs=[vspec()] * 4, out_specs=[vspec()]...  4.13 us
  transfers between devices with their start and end apart: 27, of which 10 were waited for; matrix products, arithmetic and copies ran while one was open for 7% of the time, Pallas kernels for 16%

profile of v7, /device:TPU:1, one launch (start us, length us, event | category | flops | bytes accessed | tf_op | source)
XLA Modules:
  0.0 107.8 jit_solution(4467361253783870131)
XLA Ops:
  1.5 3.3 %collective-permute-start = (bf16[2,128,256]{2,1,0:T(8,128)(2,1)S(1)}, bf16[2,128,256]{2,1,0:T(8,128)(2,1)S(1)}, u32[]{:S(2)}, u32[]{:S(2)}) collective-permute-start(bf16[2,128,256]{2,1,0:T(8,128)(2,1)S(1)} %pad_maximum_fusion.refs_0_), channel_id=1, source_target_pairs={{0,1},{1,0},{2,3},{3,2},{4,5},{5,4},{6,7},{7,6},{8,9},{9,8},{10,11... | collective-permute-start | bytes 393224 | tf_op jit(solution)/shard_map/ppermute | solution.py:261
  4.8 3.8 %collective-permute-start.1 = (bf16[2,128,256]{2,1,0:T(8,128)(2,1)S(1)}, bf16[2,128,256]{2,1,0:T(8,128)(2,1)S(1)}, u32[]{:S(2)}, u32[]{:S(2)}) collective-permute-start(bf16[2,128,256]{2,1,0:T(8,128)(2,1)S(1)} %pad_maximum_fusion.refs_0_), channel_id=1, source_target_pairs={{0,2},{1,15},{2,4},{3,1},{4,6},{5,3},{6,8},{7,5},{8,10},{9,7},{10,... | collective-permute-start | bytes 393224 | tf_op jit(solution)/shard_map/ppermute | solution.py:257
  10.6 3.1 %collective-permute-start.5 = (bf16[2,128,256]{2,1,0:T(8,128)(2,1)S(1)}, bf16[2,128,256]{2,1,0:T(8,128)(2,1)S(1)}, u32[]{:S(2)}, u32[]{:S(2)}) collective-permute-start(bf16[2,128,256]{2,1,0:T(8,128)(2,1)S(1)} %collective-permute-done.1.refs_2_), channel_id=1, source_target_pairs={{0,2},{1,15},{2,4},{3,1},{4,6},{5,3},{6,8},{7,5},{8,10},{9,7},{10,... | collective-permute-start | bytes 393224 | tf_op jit(solution)/shard_map/ppermute | solution.py:257
  13.7 1.4 %collective-permute-start.7 = (bf16[2,128,256]{2,1,0:T(8,128)(2,1)S(1)}, bf16[2,128,256]{2,1,0:T(8,128)(2,1)S(1)}, u32[]{:S(2)}, u32[]{:S(2)}) collective-permute-start(bf16[2,128,256]{2,1,0:T(8,128)(2,1)S(1)} %collective-permute-done.3.refs_4_), channel_id=1, source_target_pairs={{0,2},{1,15},{2,4},{3,1},{4,6},{5,3},{6,8},{7,5},{8,10},{9,7},{10,... | collective-permute-start | bytes 393224 | tf_op jit(solution)/shard_map/ppermute | solution.py:257
  15.8 2.2 %copy-done = bf16[1,128,128,128]{3,2,1,0:T(8,128)(2,1)S(1)} copy-done((bf16[1,128,128,128]{3,2,1,0:T(8,128)(2,1)S(1)}, bf16[1,128,128,128]{3,2,1,0:T(8,128)(2,1)}, u32[]{:S(2)}) %copy-start) | copy-done | bytes 4194328
  18.0 2.2 %dense_up.1.refs_10_.refs_16_.wu_ref = bf16[4096,1024]{1,0:T(8,128)(2,1)S(1)} custom-call(s32[128]{0:T(128)S(1)} %add_bitcast_fusion.where, s32[1]{0:T(128)S(6)} %copy.11.count_ref, bf16[1,128,128,128]{3,2,1,0:T(8,128)(2,1)S(1)} %copy-done), custom_call_target="tpu_custom_call" | custom-call | bytes 12582912 | tf_op jit(solution)/shard_map/dense_up/pallas_call | solution.py:86
  21.4 2.3 %dense_down.1.refs_11_.refs_17_.wd_ref = bf16[1024,4096]{1,0:T(8,128)(2,1)S(1)} custom-call(s32[128]{0:T(128)S(1)} %add_bitcast_fusion.where, s32[1]{0:T(128)S(6)} %copy.11.count_ref, bf16[1,128,128,128]{3,2,1,0:T(8,128)(2,1)S(1)} %copy-done.1), custom_call_target="tpu_custom_call" | custom-call | bytes 12582912 | tf_op jit(solution)/shard_map/dense_down/pallas_call | solution.py:86
  25.9 2.1 %collective-permute-start.10 = (bf16[2,128,256]{2,1,0:T(8,128)(2,1)S(1)}, bf16[2,128,256]{2,1,0:T(8,128)(2,1)S(1)}, u32[]{:S(2)}, u32[]{:S(2)}) collective-permute-start(bf16[2,128,256]{2,1,0:T(8,128)(2,1)S(1)} %collective-permute-done.9.refs_10_), channel_id=1, source_target_pairs={{0,1},{1,0},{2,3},{3,2},{4,5},{5,4},{6,7},{7,6},{8,9},{9,8},{10,11... | collective-permute-start | bytes 393224 | tf_op jit(solution)/shard_map/ppermute | solution.py:261
  27.9 2.7 %early.1 = (f32[128,1024]{1,0:T(8,128)S(1)}, f32[128,1024]{1,0:T(8,128)S(1)}) custom-call(bf16[2,128,256]{2,1,0:T(8,128)(2,1)S(1)} %pad_maximum_fusion.refs_0_, bf16[2,128,256]{2,1,0:T(8,128)(2,1)S(1)} %collective-permute-done.refs_1_, bf16[2,128,256]{2,1,0:T(8,128)(2,1)S(1)} %collective-permute-done.1.refs_2_, ...), custom_call_target="tpu_custom_call" | custom-call | flops 1342177280 | bytes 13631488 | tf_op jit(solution)/shard_map/early/pallas_call | solution.py:137
  30.7 2.3 %collective-permute-start.12 = (bf16[2,128,256]{2,1,0:T(8,128)(2,1)S(1)}, bf16[2,128,256]{2,1,0:T(8,128)(2,1)S(1)}, u32[]{:S(2)}, u32[]{:S(2)}) collective-permute-start(bf16[2,128,256]{2,1,0:T(8,128)(2,1)S(1)} %collective-permute-done.11.refs_12_), channel_id=1, source_target_pairs={{0,1},{1,0},{2,3},{3,2},{4,5},{5,4},{6,7},{7,6},{8,9},{9,8},{10,11... | collective-permute-start | bytes 393224 | tf_op jit(solution)/shard_map/ppermute | solution.py:261
  34.3 3.8 %forward.1 = (bf16[128,1024]{1,0:T(8,128)(2,1)S(1)}, bf16[128,1024]{1,0:T(8,128)(2,1)S(1)}, bf16[128,4096]{1,0:T(8,128)(2,1)S(1)}, bf16[128,4096]{1,0:T(8,128)(2...) custom-call(s32[128]{0:T(128)S(1)} %add_bitcast_fusion.where, ...), custom_call_target="tpu_custom_call" | custom-call | flops 3221225472 | bytes 23068672 | tf_op jit(solution)/shard_map/forward/pallas_call | solution.py:184
  38.1 1.4 %collective-permute-start.15 = (bf16[2,16,128,128]{3,2,1,0:T(8,128)(2,1)S(1)}, bf16[2,16,128,128]{3,2,1,0:T(8,128)(2,1)S(1)}, u32[]{:S(2)}, u32[]{:S(2)}) collective-permute-start(bf16[2,16,128,128]{3,2,1,0:T(8,128)(2,1)S(1)} %get-tuple-element.55), channel_id=1, source_target_pairs={{0,16},{1,65},{16,32},{17,81},{32,48},{33,97},{48,0},{49,113},{64,... | collective-permute-start | bytes 3145736 | tf_op jit(solution)/shard_map/ppermute | solution.py:299
  39.4 1.8 %collective-permute-start.19 = (bf16[2,16,128,128]{3,2,1,0:T(8,128)(2,1)S(1)}, bf16[2,16,128,128]{3,2,1,0:T(8,128)(2,1)S(1)}, u32[]{:S(2)}, u32[]{:S(2)}) collective-permute-start(bf16[2,16,128,128]{3,2,1,0:T(8,128)(2,1)S(1)} %get-tuple-element.59), channel_id=1, source_target_pairs={{0,48},{1,193},{16,0},{17,209},{32,16},{33,225},{48,32},{49,241},{... | collective-permute-start | bytes 3145736 | tf_op jit(solution)/shard_map/ppermute | solution.py:299
  41.2 4.0 %rest_parts.1 = (bf16[2,16,128,128]{3,2,1,0:T(8,128)(2,1)}, bf16[2,16,128,128]{3,2,1,0:T(8,128)(2,1)}, bf16[2,16,128,128]{3,2,1,0:T(8,128)(2,1)S(1)}, bf16[2,16,...) custom-call(s32[128]{0:T(128)S(1)} %add_bitcast_fusion.where, bf16[128,4096]{1,0:T(8,128)(2,1)S(1)} %get-tuple-element.49.x_ref, ...), custom_call_target="tpu_custom_call" | custom-call | flops 1073741824 | bytes 9437184 | tf_op jit(solution)/shard_map/rest_parts/pallas_call | solution.py:204
  45.2 4.1 %token_parts.1 = (bf16[8,2,128,256]{3,2,1,0:T(8,128)(2,1)S(1)}, bf16[8,2,128,256]{3,2,1,0:T(8,128)(2,1)S(1)}) custom-call(bf16[128,1024]{1,0:T(8,128)(2,1)S(1)} %get-tuple-element.64.h_ref, bf16[128,1024]{1,0:T(8,128)(2,1)S(1)} %get-tuple-element.65.d_ref, bf16[4096,1024]{1,0:T(8,128)(2,1)S(1)} %dense_up.1.refs_10_.refs_16_.wu_ref, ...), custom_call_target="tpu_custom_call" | custom-call | flops 2147483648 | bytes 19922944 | tf_op jit(solution)/shard_map/token_parts/pallas_call | solution.py:237
  49.8 1.3 %collective-permute-start.17 = (bf16[2,16,128,128]{3,2,1,0:T(8,128)(2,1)}, bf16[2,16,128,128]{3,2,1,0:T(8,128)(2,1)}, u32[]{:S(2)}, u32[]{:S(2)}) collective-permute-start(bf16[2,16,128,128]{3,2,1,0:T(8,128)(2,1)} %get-tuple-element.56), channel_id=1, source_target_pairs={{0,16},{1,65},{16,32},{17,81},{32,48},{33,97},{48,0},{49,113},{64,... | collective-permute-start | bytes 3145736 | tf_op jit(solution)/shard_map/ppermute | solution.py:299
  51.1 1.4 %collective-permute-start.18 = (bf16[2,16,128,128]{3,2,1,0:T(8,128)(2,1)}, bf16[2,16,128,128]{3,2,1,0:T(8,128)(2,1)}, u32[]{:S(2)}, u32[]{:S(2)}) collective-permute-start(bf16[2,16,128,128]{3,2,1,0:T(8,128)(2,1)} %get-tuple-element.57), channel_id=1, source_target_pairs={{0,48},{1,193},{16,0},{17,209},{32,16},{33,225},{48,32},{49,241},{... | collective-permute-start | bytes 3145736 | tf_op jit(solution)/shard_map/ppermute | solution.py:299
  53.4 1.5 %add_convert_fusion.2 = bf16[2,16,128,128]{3,2,1,0:T(8,128)(2,1)} fusion(bf16[2,16,128,128]{3,2,1,0:T(8,128)(2,1)S(1)} %collective-permute-done.15, bf16[2,16,128,128]{3,2,1,0:T(8,128)(2,1)S(1)} %get-tuple-element.54), kind=kLoop, calls=%fused_computation.2 | loop fusion | flops 2097152 | bytes 3145728 | tf_op jit(solution)/shard_map/convert_element_type | solution.py:307
  54.8 1.4 %add_convert_fusion.1 = bf16[2,16,128,128]{3,2,1,0:T(8,128)(2,1)} fusion(bf16[2,16,128,128]{3,2,1,0:T(8,128)(2,1)S(1)} %collective-permute-done.19, bf16[2,16,128,128]{3,2,1,0:T(8,128)(2,1)S(1)} %get-tuple-element.58), kind=kLoop, calls=%fused_computation.1 | loop fusion | flops 2097152 | bytes 3145728 | tf_op jit(solution)/shard_map/convert_element_type | solution.py:308
  56.2 2.7 %collective-permute-start.20 = (bf16[2,16,128,128]{3,2,1,0:T(8,128)(2,1)}, bf16[2,16,128,128]{3,2,1,0:T(8,128)(2,1)}, u32[]{:S(2)}, u32[]{:S(2)}) collective-permute-start(bf16[2,16,128,128]{3,2,1,0:T(8,128)(2,1)} %add_convert_fusion.1), channel_id=1, source_target_pairs={{0,48},{1,193},{16,0},{17,209},{32,16},{33,225},{48,32},{49,241},{... | collective-permute-start | bytes 3145736 | tf_op jit(solution)/shard_map/ppermute | solution.py:299
  58.9 1.3 %add_convert_fusion = bf16[8,2,128,256]{3,2,1,0:T(8,128)(2,1)} fusion(bf16[8,2,128,256]{3,2,1,0:T(8,128)(2,1)S(1)} %collective-permute-done.22, bf16[8,2,128,256]{3,2,1,0:T(8,128)(2,1)S(1)} %get-tuple-element.66), kind=kLoop, calls=%fused_computation | loop fusion | flops 2097152 | bytes 3145728 | tf_op jit(solution)/shard_map/convert_element_type | solution.py:404
  60.2 5.3 %all-to-all-start = ((bf16[8,2,128,256]{3,2,1,0:T(8,128)(2,1)}), bf16[8,2,128,256]{3,2,1,0:T(8,128)(2,1)S(1)}, u32[]{:S(2)}, u32[]{:S(2)}) async-start(bf16[8,2,128,256]{3,2,1,0:T(8,128)(2,1)} %add_convert_fusion), calls=%async_computation | async-start | bytes 2097152 | tf_op jit(solution)/shard_map/all_to_all | solution.py:405
  65.5 11.0 %collective-permute-done.16 = bf16[2,16,128,128]{3,2,1,0:T(8,128)(2,1)} collective-permute-done((bf16[2,16,128,128]{3,2,1,0:T(8,128)(2,1)}, bf16[2,16,128,128]{3,2,1,0:T(8,128)(2,1)}, u32[]{:S(2)}, u32[]{:S(2)}) %collective-permute-start.16) | collective-permute-done | bytes 1048608 | tf_op jit(solution)/shard_map/ppermute | solution.py:299
  76.6 2.8 %add_convert_fusion.3 = (bf16[2,8,128,128]{3,2,1,0:T(8,128)(2,1)}, bf16[2,8,128,128]{3,2,1,0:T(8,128)(2,1)S(1)}) fusion(bf16[2,16,128,128]{3,2,1,0:T(8,128)(2,1)} %collective-permute-done.18, bf16[2,16,128,128]{3,2,1,0:T(8,128)(2,1)} %collective-permute-done.16, bf16[2,32,128,128]{3,2,1,0:T(8,128)(2,1)S(1)} %get-tuple-element.53.own), kind=kLoop, calls=%fused_computation.3 | loop fusion | flops 3145728 | bytes 4194304 | tf_op jit(solution)/shard_map/convert_element_type | solution.py:317
  80.1 1.9 %collective-permute-start.23 = (bf16[2,8,128,128]{3,2,1,0:T(8,128)(2,1)}, bf16[2,8,128,128]{3,2,1,0:T(8,128)(2,1)}, u32[]{:S(2)}, u32[]{:S(2)}) collective-permute-start(bf16[2,8,128,128]{3,2,1,0:T(8,128)(2,1)} %get-tuple-element.78), channel_id=1, source_target_pairs={{0,192},{1,49},{16,208},{17,1},{32,224},{33,17},{48,240},{49,33},{... | collective-permute-start | bytes 1572872 | tf_op jit(solution)/shard_map/ppermute | solution.py:299
  82.1 7.0 %collective-permute-done.21.from_left = bf16[2,8,128,128]{3,2,1,0:T(8,128)(2,1)} collective-permute-done((bf16[2,8,128,128]{3,2,1,0:T(8,128)(2,1)S(1)}, bf16[2,8,128,128]{3,2,1,0:T(8,128)(2,1)}, u32[]{:S(2)}, u32[]{:S(2)}) %collective-permute-start.21) | collective-permute-done | bytes 524320 | tf_op jit(solution)/shard_map/ppermute | solution.py:299
  89.0 5.7 %all-to-all-done.terms_ref = bf16[8,2,128,256]{3,2,1,0:T(8,128)(2,1)S(1)} async-done(((bf16[8,2,128,256]{3,2,1,0:T(8,128)(2,1)}), bf16[8,2,128,256]{3,2,1,0:T(8,128)(2,1)S(1)}, u32[]{:S(2)}, u32[]{:S(2)}) %all-to-all-start) | async-done | bytes 1048608 | tf_op jit(solution)/shard_map/all_to_all | solution.py:405
  94.7 1.7 %add_convert_fusion.5 = (bf16[2,4,128,128]{3,2,1,0:T(8,128)(2,1)S(1)}, bf16[2,4,128,128]{3,2,1,0:T(8,128)(2,1)S(1)}) fusion(bf16[2,8,128,128]{3,2,1,0:T(8,128)(2,1)} %collective-permute-done.23.from_right, bf16[2,16,128,128]{3,2,1,0:T(8,128)(2,1)} %collective-permute-done.20.right_b, bf16[2,16,128,128]{3,2,1,0:T(8,128)(2,1)} %collective-permute-done.17.left_b, ...), kind=kLoop, calls=%fused_computation.5 | loop fusion | flops 2097152 | bytes 2621440 | tf_op jit(solution)/shard_map/convert_element_type | solution.py:320
  96.4 2.6 %collective-permute-start.25 = (bf16[2,4,128,128]{3,2,1,0:T(8,128)(2,1)S(1)}, bf16[2,4,128,128]{3,2,1,0:T(8,128)(2,1)S(1)}, u32[]{:S(2)}, u32[]{:S(2)}) collective-permute-start(bf16[2,4,128,128]{3,2,1,0:T(8,128)(2,1)S(1)} %get-tuple-element.76), channel_id=1, source_target_pairs={{0,192},{1,49},{16,208},{17,1},{32,224},{33,17},{48,240},{49,33},{... | collective-permute-start | bytes 786440 | tf_op jit(solution)/shard_map/ppermute | solution.py:299
  99.0 1.4 %near_sum.1.near = f32[2,8,128,128]{3,2,1,0:T(8,128)S(1)} custom-call(bf16[2,32,128,128]{3,2,1,0:T(8,128)(2,1)S(1)} %get-tuple-element.53.own, bf16[2,16,128,128]{3,2,1,0:T(8,128)(2,1)} %collective-permute-done.17.left_b, bf16[2,16,128,128]{3,2,1,0:T(8,128)(2,1)} %collective-permute-done.20.right_b), custom_call_target="tpu_custom_call" | custom-call | flops 524288 | bytes 3145728 | tf_op jit(solution)/shard_map/near_sum/pallas_call | solution.py:334
  102.3 3.1 %collective-permute-done.24.end_a = bf16[2,4,128,128]{3,2,1,0:T(8,128)(2,1)S(1)} collective-permute-done((bf16[2,4,128,128]{3,2,1,0:T(8,128)(2,1)S(1)}, bf16[2,4,128,128]{3,2,1,0:T(8,128)(2,1)S(1)}, u32[]{:S(2)}, u32[]{:S(2)}) %collective-permute-start.24) | collective-permute-done | bytes 262176 | tf_op jit(solution)/shard_map/ppermute | solution.py:299
  105.4 2.4 %finish.1 = (f32[1,8,128,128]{3,2,1,0:T(8,128)}, f32[1,8,128,128]{3,2,1,0:T(8,128)}) custom-call(s32[1]{0:T(128)S(6)} %copy.11.count_ref, f32[2,8,128,128]{3,2,1,0:T(8,128)S(1)} %near_sum.1.near, bf16[2,8,128,128]{3,2,1,0:T(8,128)(2,1)} %collective-permute-done.21.from_left, bf16[2,8,128,128]{3,2,1,0:T(8,128)(2,1)} %collective-permute-done.23.from_right, ...), custom_call_target="tpu_custom_call" | custom-call | flops 1048576 | bytes 3145728 | tf_op jit(solution)/shard_map/finish/pallas_call | solution.py:361
  (42 shorter events, 11.6 us)
Async XLA Ops:
  1.5 7.2 %collective-permute-start = (bf16[2,128,256]{2,1,0:T(8,128)(2,1)S(1)}, bf16[2,128,256]{2,1,0:T(8,128)(2,1)S(1)}, u32[]{:S(2)}, u32[]{:S(2)}) collective-permute-start(bf16[2,128,256]{2,1,0:T(8,128)(2,1)S(1)} %pad_maximum_fusion.refs_0_), channel_id=1, source_target_pairs={{0,1},{1,0},{2,3},{3,2},{4,5},{5,4},{6,7},{7,6},{8,9},{9,8},{10,11... | collective-permute-start | bytes 393224 | tf_op jit(solution)/shard_map/ppermute | solution.py:261
  4.8 5.8 %collective-permute-start.1 = (bf16[2,128,256]{2,1,0:T(8,128)(2,1)S(1)}, bf16[2,128,256]{2,1,0:T(8,128)(2,1)S(1)}, u32[]{:S(2)}, u32[]{:S(2)}) collective-permute-start(bf16[2,128,256]{2,1,0:T(8,128)(2,1)S(1)} %pad_maximum_fusion.refs_0_), channel_id=1, source_target_pairs={{0,2},{1,15},{2,4},{3,1},{4,6},{5,3},{6,8},{7,5},{8,10},{9,7},{10,... | collective-permute-start | bytes 393224 | tf_op jit(solution)/shard_map/ppermute | solution.py:257
  8.7 5.0 %collective-permute-start.3 = (bf16[2,128,256]{2,1,0:T(8,128)(2,1)S(1)}, bf16[2,128,256]{2,1,0:T(8,128)(2,1)S(1)}, u32[]{:S(2)}, u32[]{:S(2)}) collective-permute-start(bf16[2,128,256]{2,1,0:T(8,128)(2,1)S(1)} %collective-permute-done.refs_1_), channel_id=1, source_target_pairs={{0,2},{1,15},{2,4},{3,1},{4,6},{5,3},{6,8},{7,5},{8,10},{9,7},{10,... | collective-permute-start | bytes 393224 | tf_op jit(solution)/shard_map/ppermute | solution.py:257
  10.6 9.6 %collective-permute-start.5 = (bf16[2,128,256]{2,1,0:T(8,128)(2,1)S(1)}, bf16[2,128,256]{2,1,0:T(8,128)(2,1)S(1)}, u32[]{:S(2)}, u32[]{:S(2)}) collective-permute-start(bf16[2,128,256]{2,1,0:T(8,128)(2,1)S(1)} %collective-permute-done.1.refs_2_), channel_id=1, source_target_pairs={{0,2},{1,15},{2,4},{3,1},{4,6},{5,3},{6,8},{7,5},{8,10},{9,7},{10,... | collective-permute-start | bytes 393224 | tf_op jit(solution)/shard_map/ppermute | solution.py:257
  13.7 7.3 %collective-permute-start.7 = (bf16[2,128,256]{2,1,0:T(8,128)(2,1)S(1)}, bf16[2,128,256]{2,1,0:T(8,128)(2,1)S(1)}, u32[]{:S(2)}, u32[]{:S(2)}) collective-permute-start(bf16[2,128,256]{2,1,0:T(8,128)(2,1)S(1)} %collective-permute-done.3.refs_4_), channel_id=1, source_target_pairs={{0,2},{1,15},{2,4},{3,1},{4,6},{5,3},{6,8},{7,5},{8,10},{9,7},{10,... | collective-permute-start | bytes 393224 | tf_op jit(solution)/shard_map/ppermute | solution.py:257
  15.8 2.2 %copy-start = (bf16[1,128,128,128]{3,2,1,0:T(8,128)(2,1)S(1)}, bf16[1,128,128,128]{3,2,1,0:T(8,128)(2,1)}, u32[]{:S(2)}) copy-start(bf16[1,128,128,128]{3,2,1,0:T(8,128)(2,1)} %tiles_ref.2) | copy-start | bytes 12582916
  18.0 3.4 %copy-start.1 = (bf16[1,128,128,128]{3,2,1,0:T(8,128)(2,1)S(1)}, bf16[1,128,128,128]{3,2,1,0:T(8,128)(2,1)}, u32[]{:S(2)}) copy-start(bf16[1,128,128,128]{3,2,1,0:T(8,128)(2,1)} %tiles_ref.3) | copy-start | bytes 12582916
  20.2 4.2 %collective-permute-start.9 = (bf16[2,128,256]{2,1,0:T(8,128)(2,1)S(1)}, bf16[2,128,256]{2,1,0:T(8,128)(2,1)S(1)}, u32[]{:S(2)}, u32[]{:S(2)}) collective-permute-start(bf16[2,128,256]{2,1,0:T(8,128)(2,1)S(1)} %collective-permute-done.5.refs_6_), channel_id=1, source_target_pairs={{0,2},{1,15},{2,4},{3,1},{4,6},{5,3},{6,8},{7,5},{8,10},{9,7},{10,... | collective-permute-start | bytes 393224 | tf_op jit(solution)/shard_map/ppermute | solution.py:257
  20.3 5.0 %collective-permute-start.2 = (bf16[2,128,256]{2,1,0:T(8,128)(2,1)S(1)}, bf16[2,128,256]{2,1,0:T(8,128)(2,1)S(1)}, u32[]{:S(2)}, u32[]{:S(2)}) collective-permute-start(bf16[2,128,256]{2,1,0:T(8,128)(2,1)S(1)} %collective-permute-done.1.refs_2_), channel_id=1, source_target_pairs={{0,1},{1,0},{2,3},{3,2},{4,5},{5,4},{6,7},{7,6},{8,9},{9,8},{10,11... | collective-permute-start | bytes 393224 | tf_op jit(solution)/shard_map/ppermute | solution.py:261
  20.4 5.5 %collective-permute-start.6 = (bf16[2,128,256]{2,1,0:T(8,128)(2,1)S(1)}, bf16[2,128,256]{2,1,0:T(8,128)(2,1)S(1)}, u32[]{:S(2)}, u32[]{:S(2)}) collective-permute-start(bf16[2,128,256]{2,1,0:T(8,128)(2,1)S(1)} %collective-permute-done.5.refs_6_), channel_id=1, source_target_pairs={{0,1},{1,0},{2,3},{3,2},{4,5},{5,4},{6,7},{7,6},{8,9},{9,8},{10,11... | collective-permute-start | bytes 393224 | tf_op jit(solution)/shard_map/ppermute | solution.py:261
  20.9 7.0 %collective-permute-start.4 = (bf16[2,128,256]{2,1,0:T(8,128)(2,1)S(1)}, bf16[2,128,256]{2,1,0:T(8,128)(2,1)S(1)}, u32[]{:S(2)}, u32[]{:S(2)}) collective-permute-start(bf16[2,128,256]{2,1,0:T(8,128)(2,1)S(1)} %collective-permute-done.3.refs_4_), channel_id=1, source_target_pairs={{0,1},{1,0},{2,3},{3,2},{4,5},{5,4},{6,7},{7,6},{8,9},{9,8},{10,11... | collective-permute-start | bytes 393224 | tf_op jit(solution)/shard_map/ppermute | solution.py:261
  21.0 6.9 %collective-permute-start.8 = (bf16[2,128,256]{2,1,0:T(8,128)(2,1)S(1)}, bf16[2,128,256]{2,1,0:T(8,128)(2,1)S(1)}, u32[]{:S(2)}, u32[]{:S(2)}) collective-permute-start(bf16[2,128,256]{2,1,0:T(8,128)(2,1)S(1)} %collective-permute-done.7.refs_8_), channel_id=1, source_target_pairs={{0,1},{1,0},{2,3},{3,2},{4,5},{5,4},{6,7},{7,6},{8,9},{9,8},{10,11... | collective-permute-start | bytes 393224 | tf_op jit(solution)/shard_map/ppermute | solution.py:261
  24.4 6.2 %collective-permute-start.13 = (bf16[2,128,256]{2,1,0:T(8,128)(2,1)S(1)}, bf16[2,128,256]{2,1,0:T(8,128)(2,1)S(1)}, u32[]{:S(2)}, u32[]{:S(2)}) collective-permute-start(bf16[2,128,256]{2,1,0:T(8,128)(2,1)S(1)} %collective-permute-done.9.refs_10_), channel_id=1, source_target_pairs={{0,2},{1,15},{2,4},{3,1},{4,6},{5,3},{6,8},{7,5},{8,10},{9,7},{10,... | collective-permute-start | bytes 393224 | tf_op jit(solution)/shard_map/ppermute | solution.py:257
  25.3 5.3 %collective-permute-start.11 = (bf16[2,128,256]{2,1,0:T(8,128)(2,1)S(1)}, bf16[2,128,256]{2,1,0:T(8,128)(2,1)S(1)}, u32[]{:S(2)}, u32[]{:S(2)}) collective-permute-start(bf16[2,128,256]{2,1,0:T(8,128)(2,1)S(1)} %collective-permute-done.7.refs_8_), channel_id=1, source_target_pairs={{0,2},{1,15},{2,4},{3,1},{4,6},{5,3},{6,8},{7,5},{8,10},{9,7},{10,... | collective-permute-start | bytes 393224 | tf_op jit(solution)/shard_map/ppermute | solution.py:257
  25.9 7.1 %collective-permute-start.10 = (bf16[2,128,256]{2,1,0:T(8,128)(2,1)S(1)}, bf16[2,128,256]{2,1,0:T(8,128)(2,1)S(1)}, u32[]{:S(2)}, u32[]{:S(2)}) collective-permute-start(bf16[2,128,256]{2,1,0:T(8,128)(2,1)S(1)} %collective-permute-done.9.refs_10_), channel_id=1, source_target_pairs={{0,1},{1,0},{2,3},{3,2},{4,5},{5,4},{6,7},{7,6},{8,9},{9,8},{10,11... | collective-permute-start | bytes 393224 | tf_op jit(solution)/shard_map/ppermute | solution.py:261
  30.7 3.3 %collective-permute-start.12 = (bf16[2,128,256]{2,1,0:T(8,128)(2,1)S(1)}, bf16[2,128,256]{2,1,0:T(8,128)(2,1)S(1)}, u32[]{:S(2)}, u32[]{:S(2)}) collective-permute-start(bf16[2,128,256]{2,1,0:T(8,128)(2,1)S(1)} %collective-permute-done.11.refs_12_), channel_id=1, source_target_pairs={{0,1},{1,0},{2,3},{3,2},{4,5},{5,4},{6,7},{7,6},{8,9},{9,8},{10,11... | collective-permute-start | bytes 393224 | tf_op jit(solution)/shard_map/ppermute | solution.py:261
  32.9 1.3 %collective-permute-start.14 = (bf16[2,128,256]{2,1,0:T(8,128)(2,1)S(1)}, bf16[2,128,256]{2,1,0:T(8,128)(2,1)S(1)}, u32[]{:S(2)}, u32[]{:S(2)}) collective-permute-start(bf16[2,128,256]{2,1,0:T(8,128)(2,1)S(1)} %collective-permute-done.13.refs_14_), channel_id=1, source_target_pairs={{0,1},{1,0},{2,3},{3,2},{4,5},{5,4},{6,7},{7,6},{8,9},{9,8},{10,11... | collective-permute-start | bytes 393224 | tf_op jit(solution)/shard_map/ppermute | solution.py:261
  38.1 15.3 %collective-permute-start.15 = (bf16[2,16,128,128]{3,2,1,0:T(8,128)(2,1)S(1)}, bf16[2,16,128,128]{3,2,1,0:T(8,128)(2,1)S(1)}, u32[]{:S(2)}, u32[]{:S(2)}) collective-permute-start(bf16[2,16,128,128]{3,2,1,0:T(8,128)(2,1)S(1)} %get-tuple-element.55), channel_id=1, source_target_pairs={{0,16},{1,65},{16,32},{17,81},{32,48},{33,97},{48,0},{49,113},{64,... | collective-permute-start | bytes 3145736 | tf_op jit(solution)/shard_map/ppermute | solution.py:299
  39.4 15.4 %collective-permute-start.19 = (bf16[2,16,128,128]{3,2,1,0:T(8,128)(2,1)S(1)}, bf16[2,16,128,128]{3,2,1,0:T(8,128)(2,1)S(1)}, u32[]{:S(2)}, u32[]{:S(2)}) collective-permute-start(bf16[2,16,128,128]{3,2,1,0:T(8,128)(2,1)S(1)} %get-tuple-element.59), channel_id=1, source_target_pairs={{0,48},{1,193},{16,0},{17,209},{32,16},{33,225},{48,32},{49,241},{... | collective-permute-start | bytes 3145736 | tf_op jit(solution)/shard_map/ppermute | solution.py:299
  49.4 9.5 %collective-permute-start.22 = (bf16[8,2,128,256]{3,2,1,0:T(8,128)(2,1)S(1)}, bf16[8,2,128,256]{3,2,1,0:T(8,128)(2,1)S(1)}, u32[]{:S(2)}, u32[]{:S(2)}) collective-permute-start(bf16[8,2,128,256]{3,2,1,0:T(8,128)(2,1)S(1)} %get-tuple-element.67), channel_id=1, source_target_pairs={{0,1},{1,0},{2,3},{3,2},{4,5},{5,4},{6,7},{7,6},{8,9},{9,8},{10,11... | collective-permute-start | bytes 3145736 | tf_op jit(solution)/shard_map/ppermute | solution.py:261
  49.8 15.7 %collective-permute-start.17 = (bf16[2,16,128,128]{3,2,1,0:T(8,128)(2,1)}, bf16[2,16,128,128]{3,2,1,0:T(8,128)(2,1)}, u32[]{:S(2)}, u32[]{:S(2)}) collective-permute-start(bf16[2,16,128,128]{3,2,1,0:T(8,128)(2,1)} %get-tuple-element.56), channel_id=1, source_target_pairs={{0,16},{1,65},{16,32},{17,81},{32,48},{33,97},{48,0},{49,113},{64,... | collective-permute-start | bytes 3145736 | tf_op jit(solution)/shard_map/ppermute | solution.py:299
  51.1 14.4 %collective-permute-start.18 = (bf16[2,16,128,128]{3,2,1,0:T(8,128)(2,1)}, bf16[2,16,128,128]{3,2,1,0:T(8,128)(2,1)}, u32[]{:S(2)}, u32[]{:S(2)}) collective-permute-start(bf16[2,16,128,128]{3,2,1,0:T(8,128)(2,1)} %get-tuple-element.57), channel_id=1, source_target_pairs={{0,48},{1,193},{16,0},{17,209},{32,16},{33,225},{48,32},{49,241},{... | collective-permute-start | bytes 3145736 | tf_op jit(solution)/shard_map/ppermute | solution.py:299
  54.8 21.8 %collective-permute-start.16 = (bf16[2,16,128,128]{3,2,1,0:T(8,128)(2,1)}, bf16[2,16,128,128]{3,2,1,0:T(8,128)(2,1)}, u32[]{:S(2)}, u32[]{:S(2)}) collective-permute-start(bf16[2,16,128,128]{3,2,1,0:T(8,128)(2,1)} %add_convert_fusion.2), channel_id=1, source_target_pairs={{0,16},{1,65},{16,32},{17,81},{32,48},{33,97},{48,0},{49,113},{64,... | collective-permute-start | bytes 3145736 | tf_op jit(solution)/shard_map/ppermute | solution.py:299
  56.2 20.4 %collective-permute-start.20 = (bf16[2,16,128,128]{3,2,1,0:T(8,128)(2,1)}, bf16[2,16,128,128]{3,2,1,0:T(8,128)(2,1)}, u32[]{:S(2)}, u32[]{:S(2)}) collective-permute-start(bf16[2,16,128,128]{3,2,1,0:T(8,128)(2,1)} %add_convert_fusion.1), channel_id=1, source_target_pairs={{0,48},{1,193},{16,0},{17,209},{32,16},{33,225},{48,32},{49,241},{... | collective-permute-start | bytes 3145736 | tf_op jit(solution)/shard_map/ppermute | solution.py:299
  60.2 34.5 %all-to-all-start = ((bf16[8,2,128,256]{3,2,1,0:T(8,128)(2,1)}), bf16[8,2,128,256]{3,2,1,0:T(8,128)(2,1)S(1)}, u32[]{:S(2)}, u32[]{:S(2)}) async-start(bf16[8,2,128,256]{3,2,1,0:T(8,128)(2,1)} %add_convert_fusion), calls=%async_computation | async-start | bytes 2097152 | tf_op jit(solution)/shard_map/all_to_all | solution.py:405
  79.4 9.6 %collective-permute-start.21 = (bf16[2,8,128,128]{3,2,1,0:T(8,128)(2,1)S(1)}, bf16[2,8,128,128]{3,2,1,0:T(8,128)(2,1)}, u32[]{:S(2)}, u32[]{:S(2)}) collective-permute-start(bf16[2,8,128,128]{3,2,1,0:T(8,128)(2,1)S(1)} %get-tuple-element.79), channel_id=1, source_target_pairs={{0,64},{1,17},{16,80},{17,33},{32,96},{33,49},{48,112},{49,1},{64,... | collective-permute-start | bytes 1572872 | tf_op jit(solution)/shard_map/ppermute | solution.py:299
  80.1 14.6 %collective-permute-start.23 = (bf16[2,8,128,128]{3,2,1,0:T(8,128)(2,1)}, bf16[2,8,128,128]{3,2,1,0:T(8,128)(2,1)}, u32[]{:S(2)}, u32[]{:S(2)}) collective-permute-start(bf16[2,8,128,128]{3,2,1,0:T(8,128)(2,1)} %get-tuple-element.78), channel_id=1, source_target_pairs={{0,192},{1,49},{16,208},{17,1},{32,224},{33,17},{48,240},{49,33},{... | collective-permute-start | bytes 1572872 | tf_op jit(solution)/shard_map/ppermute | solution.py:299
  96.4 5.9 %collective-permute-start.25 = (bf16[2,4,128,128]{3,2,1,0:T(8,128)(2,1)S(1)}, bf16[2,4,128,128]{3,2,1,0:T(8,128)(2,1)S(1)}, u32[]{:S(2)}, u32[]{:S(2)}) collective-permute-start(bf16[2,4,128,128]{3,2,1,0:T(8,128)(2,1)S(1)} %get-tuple-element.76), channel_id=1, source_target_pairs={{0,192},{1,49},{16,208},{17,1},{32,224},{33,17},{48,240},{49,33},{... | collective-permute-start | bytes 786440 | tf_op jit(solution)/shard_map/ppermute | solution.py:299
  99.0 6.4 %collective-permute-start.24 = (bf16[2,4,128,128]{3,2,1,0:T(8,128)(2,1)S(1)}, bf16[2,4,128,128]{3,2,1,0:T(8,128)(2,1)S(1)}, u32[]{:S(2)}, u32[]{:S(2)}) collective-permute-start(bf16[2,4,128,128]{3,2,1,0:T(8,128)(2,1)S(1)} %get-tuple-element.77), channel_id=1, source_target_pairs={{0,64},{1,17},{16,80},{17,33},{32,96},{33,49},{48,112},{49,1},{64,... | collective-permute-start | bytes 786440 | tf_op jit(solution)/shard_map/ppermute | solution.py:299

commit v8 on v7

--- a/solution.py
+++ b/solution.py
@@ -308,47 +308,76 @@
     right_b = hop(add(before_b, from_right).astype(BF), 0, -1)
     left_a, left_b, right_a, right_b = lax.optimization_barrier((left_a, left_b, right_a, right_b))
 
-    def total(k, n):
-        left, right = (left_a, right_a) if k < 16 else (left_b, right_b)
-        at = slice(k % 16, k % 16 + n)
-        return add(own[:, k : k + n], left[:, at], right[:, at])
-
-    from_left = hop(total(0, 8).astype(BF), 1, 1)
-    from_right = hop(total(8, 8).astype(BF), 1, -1)
+    plus, minus = send_sums(own, left_a, right_a)
+    from_left = hop(plus, 1, 1)
+    from_right = hop(minus, 1, -1)
+    mid, near = kept_sums(own, left_b, right_b)
     from_left, terms = lax.optimization_barrier((from_left, terms))
-    end_a = hop(add(total(16, 4), from_left[:, :4]).astype(BF), 1, 1)
-    end_b = hop(add(total(20, 4), from_right[:, :4]).astype(BF), 1, -1)
-    return (near_sum(own, left_b, right_b), from_left, from_right, end_a, end_b), terms
-
-
-def near_sum_kernel(own, left_b, right_b, out):
+    end_a = hop(add(mid[:, :4], from_left[:, :4]).astype(BF), 1, 1)
+    end_b = hop(add(mid[:, 4:], from_right[:, :4]).astype(BF), 1, -1)
+    return (near_sum(near, from_left, from_right), end_a, end_b), terms
+
+
+def three_sum_kernel(own, left, right, one_ref, two_ref):
+    for half, out in enumerate((one_ref, two_ref)):
+
+        @pl.when(pl.program_id(0) == half)
+        def _():
+            for k in range(2):
+                for s in range(8):
+                    out[k, s] = add(own[k, s], left[k, s], right[k, s]).astype(out.dtype)
+
+
+def three_sum(own, left, right, half, dtype, name):
+    block = (2, 8, SIDE, SIDE)
+    return pl.pallas_call(
+        three_sum_kernel,
+        grid=(2,),
+        in_specs=[pl.BlockSpec(block, lambda i: (0, 2 * half + i, 0, 0))]
+        + [pl.BlockSpec(block, lambda i: (0, i, 0, 0))] * 2,
+        out_specs=[whole(*block)] * 2,
+        out_shape=[jax.ShapeDtypeStruct(block, dtype)] * 2,
+        compiler_params=params(16),
+        cost_estimate=pl.CostEstimate(flops=1 << 20, bytes_accessed=4 << 20, transcendentals=0),
+        name=name,
+    )(own, left, right)
+
+
+def send_sums(own, left_a, right_a):
+    return three_sum(own, left_a, right_a, 0, BF, "send_sums")
+
+
+def kept_sums(own, left_b, right_b):
+    return three_sum(own, left_b, right_b, 1, F32, "kept_sums")
+
+
+def near_sum_kernel(near, from_left, from_right, out):
     for k in range(2):
-        for s in range(8):
-            out[k, s] = add(own[k, s], left_b[k, s], right_b[k, s])
-
-
-def near_sum(own, left_b, right_b):
-    def last(block):
-        return pl.BlockSpec((2, 8, SIDE, SIDE), lambda i: (0, block, 0, 0))
-
+        for s in range(4):
+            out[k, s] = add(near[k, s], from_right[k, s])
+            out[k, 4 + s] = add(near[k, 4 + s], from_left[k, s])
+
+
+def near_sum(near, from_left, from_right):
+    block = (2, 8, SIDE, SIDE)
+    half = pl.BlockSpec((2, 4, SIDE, SIDE), lambda i: (0, 1, 0, 0))
     return pl.pallas_call(
         near_sum_kernel,
         grid=(1,),
-        in_specs=[last(3), last(1), last(1)],
-        out_specs=whole(2, 8, SIDE, SIDE),
-        out_shape=jax.ShapeDtypeStruct((2, 8, SIDE, SIDE), F32),
+        in_specs=[whole(*block), half, half],
+        out_specs=whole(*block),
+        out_shape=jax.ShapeDtypeStruct(block, F32),
         compiler_params=params(16),
         cost_estimate=pl.CostEstimate(flops=1 << 19, bytes_accessed=3 << 20, transcendentals=0),
         name="near_sum",
-    )(own, left_b, right_b)
-
-
-def finish_kernel(count_ref, near, from_left, from_right, end_a, end_b, up_out, down_out):
+    )(near, from_left, from_right)
+
+
+def finish_kernel(count_ref, near, end_a, end_b, up_out, down_out):
     first = lax.axis_index(("y", "x")) * 8
     for k in range(2):
         for s in range(8):
-            one, two = (end_a[k, s], from_right[k, 4 + s]) if s < 4 else (from_left[k, s], end_b[k, s - 4])
-            total = add(near[k, s], one, two)
+            total = add(near[k, s], end_a[k, s] if s < 4 else end_b[k, s - 4])
             total = jnp.where(first + s < count_ref[0], total * (1.0 / 16), 0.0)
             if k == 0:
                 up_out[0, s] = total.T
@@ -361,7 +390,7 @@
     return pl.pallas_call(
         finish_kernel,
         grid=(1,),
-        in_specs=[sspec()] + [whole(2, n, SIDE, SIDE) for n in (8, 8, 8, 4, 4)],
+        in_specs=[sspec()] + [whole(2, n, SIDE, SIDE) for n in (8, 4, 4)],
         out_specs=[whole(*shape)] * 2,
         out_shape=[jax.ShapeDtypeStruct(shape, F32)] * 2,
         compiler_params=params(16),

time: 109 us -> 113 us (1.037)
  the two profiles are of different devices: /device:TPU:1 before, /device:TPU:6 now
where the time goes in v8:
time: 113 us
  waiting for transfers between devices  41 us (36%)
  starting transfers between devices  31.6 us (28%)
  Pallas kernels  26.7 us (24%)
  other arithmetic  7.86 us (7%)
  local copies, waits for them, and re-layouts  4.17 us (4%)
  between operations  1.46 us (1%)
    ppermute x10, waiting for transfers between devices, hop(): return lax.ppermute(t, ('y', 'x', 'c'), pairs)  31.2 us
    ppermute x10, starting transfers between devices, hop(): return lax.ppermute(t, ('y', 'x', 'c'), pairs)  12.4 us
    ppermute x7, starting transfers between devices, step_both(): return lax.ppermute(x, ('z', 'c'), pairs)  10 us
    ppermute x7, waiting for transfers between devices, step_both(): return lax.ppermute(x, ('z', 'c'), pairs)  8.78 us
    all_to_all x1, starting transfers between devices, body(): terms = lax.all_to_all(pieces, 'z', 0, 0, tiled=True)  7.01 us
    pallas_call x1, Pallas kernels, forward(): pl.pallas_call(forward_kernel, in_specs=[sspec()] + [pl.BlockSpec(memory_...  4.97 us
    unnamed x16, local copies, waits for them, and re-layouts  4.17 us
    pallas_call x1, Pallas kernels, token_parts(): pl.pallas_call(token_kernel, in_specs=[vspec()] * 4, out_specs=[vspec()]...  4.12 us
  transfers between devices with their start and end apart: 27, of which 14 were waited for; matrix products, arithmetic and copies ran while one was open for 5% of the time, Pallas kernels for 11%

profile of v8, /device:TPU:6, one launch (start us, length us, event | category | flops | bytes accessed | tf_op | source)
XLA Modules:
  0.0 112.8 jit_solution(14640552748169073615)
XLA Ops:
  1.6 2.0 %collective-permute-start.1 = (bf16[2,128,256]{2,1,0:T(8,128)(2,1)S(1)}, bf16[2,128,256]{2,1,0:T(8,128)(2,1)S(1)}, u32[]{:S(2)}, u32[]{:S(2)}) collective-permute-start(bf16[2,128,256]{2,1,0:T(8,128)(2,1)S(1)} %pad_maximum_fusion.refs_0_), channel_id=1, source_target_pairs={{0,2},{1,15},{2,4},{3,1},{4,6},{5,3},{6,8},{7,5},{8,10},{9,7},{10,... | collective-permute-start | bytes 393224 | tf_op jit(solution)/shard_map/ppermute | solution.py:257
  3.6 1.9 %collective-permute-start.3 = (bf16[2,128,256]{2,1,0:T(8,128)(2,1)S(1)}, bf16[2,128,256]{2,1,0:T(8,128)(2,1)S(1)}, u32[]{:S(2)}, u32[]{:S(2)}) collective-permute-start(bf16[2,128,256]{2,1,0:T(8,128)(2,1)S(1)} %collective-permute-done.refs_1_), channel_id=1, source_target_pairs={{0,2},{1,15},{2,4},{3,1},{4,6},{5,3},{6,8},{7,5},{8,10},{9,7},{10,... | collective-permute-start | bytes 393224 | tf_op jit(solution)/shard_map/ppermute | solution.py:257
  6.2 4.3 %collective-permute-done.1.refs_2_ = bf16[2,128,256]{2,1,0:T(8,128)(2,1)S(1)} collective-permute-done((bf16[2,128,256]{2,1,0:T(8,128)(2,1)S(1)}, bf16[2,128,256]{2,1,0:T(8,128)(2,1)S(1)}, u32[]{:S(2)}, u32[]{:S(2)}) %collective-permute-start.1) | collective-permute-done | bytes 131104 | tf_op jit(solution)/shard_map/ppermute | solution.py:257
  12.6 2.2 %copy-done = bf16[1,128,128,128]{3,2,1,0:T(8,128)(2,1)S(1)} copy-done((bf16[1,128,128,128]{3,2,1,0:T(8,128)(2,1)S(1)}, bf16[1,128,128,128]{3,2,1,0:T(8,128)(2,1)}, u32[]{:S(2)}) %copy-start) | copy-done | bytes 4194328
  14.8 2.0 %dense_up.1.refs_10_.refs_16_.wu_ref = bf16[4096,1024]{1,0:T(8,128)(2,1)S(1)} custom-call(s32[128]{0:T(128)S(1)} %add_bitcast_fusion.where, s32[1]{0:T(128)S(6)} %copy.11.count_ref, bf16[1,128,128,128]{3,2,1,0:T(8,128)(2,1)S(1)} %copy-done), custom_call_target="tpu_custom_call" | custom-call | bytes 12582912 | tf_op jit(solution)/shard_map/dense_up/pallas_call | solution.py:86
  16.8 2.1 %collective-permute-start.9 = (bf16[2,128,256]{2,1,0:T(8,128)(2,1)S(1)}, bf16[2,128,256]{2,1,0:T(8,128)(2,1)S(1)}, u32[]{:S(2)}, u32[]{:S(2)}) collective-permute-start(bf16[2,128,256]{2,1,0:T(8,128)(2,1)S(1)} %collective-permute-done.5.refs_6_), channel_id=1, source_target_pairs={{0,2},{1,15},{2,4},{3,1},{4,6},{5,3},{6,8},{7,5},{8,10},{9,7},{10,... | collective-permute-start | bytes 393224 | tf_op jit(solution)/shard_map/ppermute | solution.py:257
  20.0 2.1 %dense_down.1.refs_11_.refs_17_.wd_ref = bf16[1024,4096]{1,0:T(8,128)(2,1)S(1)} custom-call(s32[128]{0:T(128)S(1)} %add_bitcast_fusion.where, s32[1]{0:T(128)S(6)} %copy.11.count_ref, bf16[1,128,128,128]{3,2,1,0:T(8,128)(2,1)S(1)} %copy-done.1), custom_call_target="tpu_custom_call" | custom-call | bytes 12582912 | tf_op jit(solution)/shard_map/dense_down/pallas_call | solution.py:86
  23.1 2.7 %collective-permute-start.13 = (bf16[2,128,256]{2,1,0:T(8,128)(2,1)S(1)}, bf16[2,128,256]{2,1,0:T(8,128)(2,1)S(1)}, u32[]{:S(2)}, u32[]{:S(2)}) collective-permute-start(bf16[2,128,256]{2,1,0:T(8,128)(2,1)S(1)} %collective-permute-done.9.refs_10_), channel_id=1, source_target_pairs={{0,2},{1,15},{2,4},{3,1},{4,6},{5,3},{6,8},{7,5},{8,10},{9,7},{10,... | collective-permute-start | bytes 393224 | tf_op jit(solution)/shard_map/ppermute | solution.py:257
  27.2 2.7 %early.1 = (f32[128,1024]{1,0:T(8,128)S(1)}, f32[128,1024]{1,0:T(8,128)S(1)}) custom-call(bf16[2,128,256]{2,1,0:T(8,128)(2,1)S(1)} %pad_maximum_fusion.refs_0_, bf16[2,128,256]{2,1,0:T(8,128)(2,1)S(1)} %collective-permute-done.refs_1_, bf16[2,128,256]{2,1,0:T(8,128)(2,1)S(1)} %collective-permute-done.1.refs_2_, ...), custom_call_target="tpu_custom_call" | custom-call | flops 1342177280 | bytes 13631488 | tf_op jit(solution)/shard_map/early/pallas_call | solution.py:137
  29.9 2.1 %collective-permute-done.11.refs_12_ = bf16[2,128,256]{2,1,0:T(8,128)(2,1)S(1)} collective-permute-done((bf16[2,128,256]{2,1,0:T(8,128)(2,1)S(1)}, bf16[2,128,256]{2,1,0:T(8,128)(2,1)S(1)}, u32[]{:S(2)}, u32[]{:S(2)}) %collective-permute-start.11) | collective-permute-done | bytes 131104 | tf_op jit(solution)/shard_map/ppermute | solution.py:257
  33.5 5.0 %forward.1 = (bf16[128,1024]{1,0:T(8,128)(2,1)S(1)}, bf16[128,1024]{1,0:T(8,128)(2,1)S(1)}, bf16[128,4096]{1,0:T(8,128)(2,1)S(1)}, bf16[128,4096]{1,0:T(8,128)(2...) custom-call(s32[128]{0:T(128)S(1)} %add_bitcast_fusion.where, ...), custom_call_target="tpu_custom_call" | custom-call | flops 3221225472 | bytes 23068672 | tf_op jit(solution)/shard_map/forward/pallas_call | solution.py:184
  38.5 4.0 %rest_parts.1 = (bf16[2,16,128,128]{3,2,1,0:T(8,128)(2,1)}, bf16[2,16,128,128]{3,2,1,0:T(8,128)(2,1)}, bf16[2,16,128,128]{3,2,1,0:T(8,128)(2,1)S(1)}, bf16[2,16,...) custom-call(s32[128]{0:T(128)S(1)} %add_bitcast_fusion.where, bf16[128,4096]{1,0:T(8,128)(2,1)S(1)} %get-tuple-element.53.x_ref, ...), custom_call_target="tpu_custom_call" | custom-call | flops 1073741824 | bytes 9437184 | tf_op jit(solution)/shard_map/rest_parts/pallas_call | solution.py:204
  42.5 4.1 %token_parts.1 = (bf16[8,2,128,256]{3,2,1,0:T(8,128)(2,1)S(1)}, bf16[8,2,128,256]{3,2,1,0:T(8,128)(2,1)S(1)}) custom-call(bf16[128,1024]{1,0:T(8,128)(2,1)S(1)} %get-tuple-element.69.h_ref, bf16[128,1024]{1,0:T(8,128)(2,1)S(1)} %get-tuple-element.70.d_ref, bf16[4096,1024]{1,0:T(8,128)(2,1)S(1)} %dense_up.1.refs_10_.refs_16_.wu_ref, ...), custom_call_target="tpu_custom_call" | custom-call | flops 2147483648 | bytes 19922944 | tf_op jit(solution)/shard_map/token_parts/pallas_call | solution.py:237
  47.5 1.5 %collective-permute-start.19 = (bf16[2,16,128,128]{3,2,1,0:T(8,128)(2,1)}, bf16[2,16,128,128]{3,2,1,0:T(8,128)(2,1)}, u32[]{:S(2)}, u32[]{:S(2)}) collective-permute-start(bf16[2,16,128,128]{3,2,1,0:T(8,128)(2,1)} %get-tuple-element.63), channel_id=1, source_target_pairs={{0,48},{1,193},{16,0},{17,209},{32,16},{33,225},{48,32},{49,241},{... | collective-permute-start | bytes 3145736 | tf_op jit(solution)/shard_map/ppermute | solution.py:299
  49.0 1.7 %collective-permute-start.17 = (bf16[2,16,128,128]{3,2,1,0:T(8,128)(2,1)}, bf16[2,16,128,128]{3,2,1,0:T(8,128)(2,1)}, u32[]{:S(2)}, u32[]{:S(2)}) collective-permute-start(bf16[2,16,128,128]{3,2,1,0:T(8,128)(2,1)} %get-tuple-element.60), channel_id=1, source_target_pairs={{0,16},{1,65},{16,32},{17,81},{32,48},{33,97},{48,0},{49,113},{64,... | collective-permute-start | bytes 3145736 | tf_op jit(solution)/shard_map/ppermute | solution.py:299
  52.4 7.0 %all-to-all-start = ((bf16[8,2,128,256]{3,2,1,0:T(8,128)(2,1)}), bf16[8,2,128,256]{3,2,1,0:T(8,128)(2,1)S(1)}, u32[]{:S(2)}, u32[]{:S(2)}) async-start(bf16[8,2,128,256]{3,2,1,0:T(8,128)(2,1)} %add_convert_fusion), calls=%async_computation | async-start | bytes 2097152 | tf_op jit(solution)/shard_map/all_to_all | solution.py:434
  59.4 2.7 %collective-permute-done.15 = bf16[2,16,128,128]{3,2,1,0:T(8,128)(2,1)} collective-permute-done((bf16[2,16,128,128]{3,2,1,0:T(8,128)(2,1)}, bf16[2,16,128,128]{3,2,1,0:T(8,128)(2,1)}, u32[]{:S(2)}, u32[]{:S(2)}) %collective-permute-start.15) | collective-permute-done | bytes 1048608 | tf_op jit(solution)/shard_map/ppermute | solution.py:299
  62.1 1.9 %add_convert_fusion.2 = bf16[2,16,128,128]{3,2,1,0:T(8,128)(2,1)S(1)} fusion(bf16[2,16,128,128]{3,2,1,0:T(8,128)(2,1)} %collective-permute-done.15, bf16[2,16,128,128]{3,2,1,0:T(8,128)(2,1)} %copy-done.4), kind=kLoop, calls=%fused_computation.2 | loop fusion | flops 2097152 | bytes 3145728 | tf_op jit(solution)/shard_map/convert_element_type | solution.py:307
  64.0 1.8 %collective-permute-start.16 = (bf16[2,16,128,128]{3,2,1,0:T(8,128)(2,1)S(1)}, bf16[2,16,128,128]{3,2,1,0:T(8,128)(2,1)S(1)}, u32[]{:S(2)}, u32[]{:S(2)}) collective-permute-start(bf16[2,16,128,128]{3,2,1,0:T(8,128)(2,1)S(1)} %add_convert_fusion.2), channel_id=1, source_target_pairs={{0,16},{1,65},{16,32},{17,81},{32,48},{33,97},{48,0},{49,113},{64,... | collective-permute-start | bytes 3145736 | tf_op jit(solution)/shard_map/ppermute | solution.py:299
  65.8 1.6 %add_convert_fusion.1 = bf16[2,16,128,128]{3,2,1,0:T(8,128)(2,1)S(1)} fusion(bf16[2,16,128,128]{3,2,1,0:T(8,128)(2,1)} %collective-permute-done.19, bf16[2,16,128,128]{3,2,1,0:T(8,128)(2,1)S(1)} %copy-done.3), kind=kLoop, calls=%fused_computation.1 | loop fusion | flops 2097152 | bytes 3145728 | tf_op jit(solution)/shard_map/convert_element_type | solution.py:308
  67.8 7.2 %collective-permute-done.18.right = bf16[2,16,128,128]{3,2,1,0:T(8,128)(2,1)} collective-permute-done((bf16[2,16,128,128]{3,2,1,0:T(8,128)(2,1)}, bf16[2,16,128,128]{3,2,1,0:T(8,128)(2,1)}, u32[]{:S(2)}, u32[]{:S(2)}) %collective-permute-start.18) | collective-permute-done | bytes 1048608 | tf_op jit(solution)/shard_map/ppermute | solution.py:299
  75.1 9.4 %collective-permute-done.16.left = bf16[2,16,128,128]{3,2,1,0:T(8,128)(2,1)S(1)} collective-permute-done((bf16[2,16,128,128]{3,2,1,0:T(8,128)(2,1)S(1)}, bf16[2,16,128,128]{3,2,1,0:T(8,128)(2,1)S(1)}, u32[]{:S(2)}, u32[]{:S(2)}) %collective-permute-start.16) | collective-permute-done | bytes 1048608 | tf_op jit(solution)/shard_map/ppermute | solution.py:299
  84.5 1.7 %collective-permute-done.20.right = bf16[2,16,128,128]{3,2,1,0:T(8,128)(2,1)S(1)} collective-permute-done((bf16[2,16,128,128]{3,2,1,0:T(8,128)(2,1)S(1)}, bf16[2,16,128,128]{3,2,1,0:T(8,128)(2,1)S(1)}, u32[]{:S(2)}, u32[]{:S(2)}) %collective-permute-start.20) | collective-permute-done | bytes 1048608 | tf_op jit(solution)/shard_map/ppermute | solution.py:299
  86.2 2.3 %send_sums.1 = (bf16[2,8,128,128]{3,2,1,0:T(8,128)(2,1)S(1)}, bf16[2,8,128,128]{3,2,1,0:T(8,128)(2,1)}) custom-call(bf16[2,32,128,128]{3,2,1,0:T(8,128)(2,1)S(1)} %get-tuple-element.57.own, bf16[2,16,128,128]{3,2,1,0:T(8,128)(2,1)S(1)} %collective-permute-done.16.left, bf16[2,16,128,128]{3,2,1,0:T(8,128)(2,1)} %collective-permute-done.18.right), custom_call_target="tpu_custom_call" | custom-call | flops 1048576 | bytes 4194304 | tf_op jit(solution)/shard_map/send_sums/pallas_call | solution.py:333
  88.5 1.6 %collective-permute-start.21 = (bf16[2,8,128,128]{3,2,1,0:T(8,128)(2,1)S(1)}, bf16[2,8,128,128]{3,2,1,0:T(8,128)(2,1)}, u32[]{:S(2)}, u32[]{:S(2)}) collective-permute-start(bf16[2,8,128,128]{3,2,1,0:T(8,128)(2,1)S(1)} %get-tuple-element.66), channel_id=1, source_target_pairs={{0,64},{1,17},{16,80},{17,33},{32,96},{33,49},{48,112},{49,1},{64,... | collective-permute-start | bytes 1572872 | tf_op jit(solution)/shard_map/ppermute | solution.py:299
  90.1 1.6 %collective-permute-start.23 = (bf16[2,8,128,128]{3,2,1,0:T(8,128)(2,1)}, bf16[2,8,128,128]{3,2,1,0:T(8,128)(2,1)}, u32[]{:S(2)}, u32[]{:S(2)}) collective-permute-start(bf16[2,8,128,128]{3,2,1,0:T(8,128)(2,1)} %get-tuple-element.80), channel_id=1, source_target_pairs={{0,192},{1,49},{16,208},{17,1},{32,224},{33,17},{48,240},{49,33},{... | collective-permute-start | bytes 1572872 | tf_op jit(solution)/shard_map/ppermute | solution.py:299
  91.7 1.5 %kept_sums.1 = (f32[2,8,128,128]{3,2,1,0:T(8,128)S(1)}, f32[2,8,128,128]{3,2,1,0:T(8,128)S(1)}) custom-call(bf16[2,32,128,128]{3,2,1,0:T(8,128)(2,1)S(1)} %get-tuple-element.57.own, bf16[2,16,128,128]{3,2,1,0:T(8,128)(2,1)} %collective-permute-done.17.left, bf16[2,16,128,128]{3,2,1,0:T(8,128)(2,1)S(1)} %collective-permute-done.20.right), custom_call_target="tpu_custom_call" | custom-call | flops 1048576 | bytes 4194304 | tf_op jit(solution)/shard_map/kept_sums/pallas_call | solution.py:333
  95.2 3.8 %collective-permute-done.21.from_left = bf16[2,8,128,128]{3,2,1,0:T(8,128)(2,1)} collective-permute-done((bf16[2,8,128,128]{3,2,1,0:T(8,128)(2,1)S(1)}, bf16[2,8,128,128]{3,2,1,0:T(8,128)(2,1)}, u32[]{:S(2)}, u32[]{:S(2)}) %collective-permute-start.21) | collective-permute-done | bytes 524320 | tf_op jit(solution)/shard_map/ppermute | solution.py:299
  99.6 1.5 %add_convert_fusion.3 = (bf16[2,4,128,128]{3,2,1,0:T(8,128)(2,1)S(1)}, bf16[2,4,128,128]{3,2,1,0:T(8,128)(2,1)S(1)}) fusion(f32[2,8,128,128]{3,2,1,0:T(8,128)} %copy-done.7, bf16[2,8,128,128]{3,2,1,0:T(8,128)(2,1)} %collective-permute-done.23.from_right, bf16[2,8,128,128]{3,2,1,0:T(8,128)(2,1)} %collective-permute-done.21.from_left), kind=kLoop, calls=%fused_computation.3 | loop fusion | flops 786432 | bytes 2097152 | tf_op jit(solution)/shard_map/convert_element_type | solution.py:317
  101.1 2.9 %collective-permute-start.25 = (bf16[2,4,128,128]{3,2,1,0:T(8,128)(2,1)S(1)}, bf16[2,4,128,128]{3,2,1,0:T(8,128)(2,1)S(1)}, u32[]{:S(2)}, u32[]{:S(2)}) collective-permute-start(bf16[2,4,128,128]{3,2,1,0:T(8,128)(2,1)S(1)} %get-tuple-element.84), channel_id=1, source_target_pairs={{0,192},{1,49},{16,208},{17,1},{32,224},{33,17},{48,240},{49,33},{... | collective-permute-start | bytes 786440 | tf_op jit(solution)/shard_map/ppermute | solution.py:299
  105.9 2.0 %collective-permute-done.25.end_b = bf16[2,4,128,128]{3,2,1,0:T(8,128)(2,1)S(1)} collective-permute-done((bf16[2,4,128,128]{3,2,1,0:T(8,128)(2,1)S(1)}, bf16[2,4,128,128]{3,2,1,0:T(8,128)(2,1)S(1)}, u32[]{:S(2)}, u32[]{:S(2)}) %collective-permute-start.25) | collective-permute-done | bytes 262176 | tf_op jit(solution)/shard_map/ppermute | solution.py:299
  107.9 3.7 %collective-permute-done.24.end_a = bf16[2,4,128,128]{3,2,1,0:T(8,128)(2,1)S(1)} collective-permute-done((bf16[2,4,128,128]{3,2,1,0:T(8,128)(2,1)S(1)}, bf16[2,4,128,128]{3,2,1,0:T(8,128)(2,1)S(1)}, u32[]{:S(2)}, u32[]{:S(2)}) %collective-permute-start.24) | collective-permute-done | bytes 262176 | tf_op jit(solution)/shard_map/ppermute | solution.py:299
  (55 shorter events, 16.7 us)
Async XLA Ops:
  1.5 2.1 %collective-permute-start = (bf16[2,128,256]{2,1,0:T(8,128)(2,1)S(1)}, bf16[2,128,256]{2,1,0:T(8,128)(2,1)S(1)}, u32[]{:S(2)}, u32[]{:S(2)}) collective-permute-start(bf16[2,128,256]{2,1,0:T(8,128)(2,1)S(1)} %pad_maximum_fusion.refs_0_), channel_id=1, source_target_pairs={{0,1},{1,0},{2,3},{3,2},{4,5},{5,4},{6,7},{7,6},{8,9},{9,8},{10,11... | collective-permute-start | bytes 393224 | tf_op jit(solution)/shard_map/ppermute | solution.py:261
  1.6 8.9 %collective-permute-start.1 = (bf16[2,128,256]{2,1,0:T(8,128)(2,1)S(1)}, bf16[2,128,256]{2,1,0:T(8,128)(2,1)S(1)}, u32[]{:S(2)}, u32[]{:S(2)}) collective-permute-start(bf16[2,128,256]{2,1,0:T(8,128)(2,1)S(1)} %pad_maximum_fusion.refs_0_), channel_id=1, source_target_pairs={{0,2},{1,15},{2,4},{3,1},{4,6},{5,3},{6,8},{7,5},{8,10},{9,7},{10,... | collective-permute-start | bytes 393224 | tf_op jit(solution)/shard_map/ppermute | solution.py:257
  3.6 8.3 %collective-permute-start.3 = (bf16[2,128,256]{2,1,0:T(8,128)(2,1)S(1)}, bf16[2,128,256]{2,1,0:T(8,128)(2,1)S(1)}, u32[]{:S(2)}, u32[]{:S(2)}) collective-permute-start(bf16[2,128,256]{2,1,0:T(8,128)(2,1)S(1)} %collective-permute-done.refs_1_), channel_id=1, source_target_pairs={{0,2},{1,15},{2,4},{3,1},{4,6},{5,3},{6,8},{7,5},{8,10},{9,7},{10,... | collective-permute-start | bytes 393224 | tf_op jit(solution)/shard_map/ppermute | solution.py:257
  10.5 6.3 %collective-permute-start.5 = (bf16[2,128,256]{2,1,0:T(8,128)(2,1)S(1)}, bf16[2,128,256]{2,1,0:T(8,128)(2,1)S(1)}, u32[]{:S(2)}, u32[]{:S(2)}) collective-permute-start(bf16[2,128,256]{2,1,0:T(8,128)(2,1)S(1)} %collective-permute-done.1.refs_2_), channel_id=1, source_target_pairs={{0,2},{1,15},{2,4},{3,1},{4,6},{5,3},{6,8},{7,5},{8,10},{9,7},{10,... | collective-permute-start | bytes 393224 | tf_op jit(solution)/shard_map/ppermute | solution.py:257
  11.9 8.1 %collective-permute-start.7 = (bf16[2,128,256]{2,1,0:T(8,128)(2,1)S(1)}, bf16[2,128,256]{2,1,0:T(8,128)(2,1)S(1)}, u32[]{:S(2)}, u32[]{:S(2)}) collective-permute-start(bf16[2,128,256]{2,1,0:T(8,128)(2,1)S(1)} %collective-permute-done.3.refs_4_), channel_id=1, source_target_pairs={{0,2},{1,15},{2,4},{3,1},{4,6},{5,3},{6,8},{7,5},{8,10},{9,7},{10,... | collective-permute-start | bytes 393224 | tf_op jit(solution)/shard_map/ppermute | solution.py:257
  14.8 5.3 %copy-start.1 = (bf16[1,128,128,128]{3,2,1,0:T(8,128)(2,1)S(1)}, bf16[1,128,128,128]{3,2,1,0:T(8,128)(2,1)}, u32[]{:S(2)}) copy-start(bf16[1,128,128,128]{3,2,1,0:T(8,128)(2,1)} %tiles_ref.3) | copy-start | bytes 12582916
  16.8 6.3 %collective-permute-start.9 = (bf16[2,128,256]{2,1,0:T(8,128)(2,1)S(1)}, bf16[2,128,256]{2,1,0:T(8,128)(2,1)S(1)}, u32[]{:S(2)}, u32[]{:S(2)}) collective-permute-start(bf16[2,128,256]{2,1,0:T(8,128)(2,1)S(1)} %collective-permute-done.5.refs_6_), channel_id=1, source_target_pairs={{0,2},{1,15},{2,4},{3,1},{4,6},{5,3},{6,8},{7,5},{8,10},{9,7},{10,... | collective-permute-start | bytes 393224 | tf_op jit(solution)/shard_map/ppermute | solution.py:257
  18.9 6.9 %collective-permute-start.2 = (bf16[2,128,256]{2,1,0:T(8,128)(2,1)S(1)}, bf16[2,128,256]{2,1,0:T(8,128)(2,1)S(1)}, u32[]{:S(2)}, u32[]{:S(2)}) collective-permute-start(bf16[2,128,256]{2,1,0:T(8,128)(2,1)S(1)} %collective-permute-done.1.refs_2_), channel_id=1, source_target_pairs={{0,1},{1,0},{2,3},{3,2},{4,5},{5,4},{6,7},{7,6},{8,9},{9,8},{10,11... | collective-permute-start | bytes 393224 | tf_op jit(solution)/shard_map/ppermute | solution.py:261
  19.5 7.6 %collective-permute-start.6 = (bf16[2,128,256]{2,1,0:T(8,128)(2,1)S(1)}, bf16[2,128,256]{2,1,0:T(8,128)(2,1)S(1)}, u32[]{:S(2)}, u32[]{:S(2)}) collective-permute-start(bf16[2,128,256]{2,1,0:T(8,128)(2,1)S(1)} %collective-permute-done.5.refs_6_), channel_id=1, source_target_pairs={{0,1},{1,0},{2,3},{3,2},{4,5},{5,4},{6,7},{7,6},{8,9},{9,8},{10,11... | collective-permute-start | bytes 393224 | tf_op jit(solution)/shard_map/ppermute | solution.py:261
  19.5 7.6 %collective-permute-start.4 = (bf16[2,128,256]{2,1,0:T(8,128)(2,1)S(1)}, bf16[2,128,256]{2,1,0:T(8,128)(2,1)S(1)}, u32[]{:S(2)}, u32[]{:S(2)}) collective-permute-start(bf16[2,128,256]{2,1,0:T(8,128)(2,1)S(1)} %collective-permute-done.3.refs_4_), channel_id=1, source_target_pairs={{0,1},{1,0},{2,3},{3,2},{4,5},{5,4},{6,7},{7,6},{8,9},{9,8},{10,11... | collective-permute-start | bytes 393224 | tf_op jit(solution)/shard_map/ppermute | solution.py:261
  20.0 7.1 %collective-permute-start.8 = (bf16[2,128,256]{2,1,0:T(8,128)(2,1)S(1)}, bf16[2,128,256]{2,1,0:T(8,128)(2,1)S(1)}, u32[]{:S(2)}, u32[]{:S(2)}) collective-permute-start(bf16[2,128,256]{2,1,0:T(8,128)(2,1)S(1)} %collective-permute-done.7.refs_8_), channel_id=1, source_target_pairs={{0,1},{1,0},{2,3},{3,2},{4,5},{5,4},{6,7},{7,6},{8,9},{9,8},{10,11... | collective-permute-start | bytes 393224 | tf_op jit(solution)/shard_map/ppermute | solution.py:261
  23.1 6.8 %collective-permute-start.13 = (bf16[2,128,256]{2,1,0:T(8,128)(2,1)S(1)}, bf16[2,128,256]{2,1,0:T(8,128)(2,1)S(1)}, u32[]{:S(2)}, u32[]{:S(2)}) collective-permute-start(bf16[2,128,256]{2,1,0:T(8,128)(2,1)S(1)} %collective-permute-done.9.refs_10_), channel_id=1, source_target_pairs={{0,2},{1,15},{2,4},{3,1},{4,6},{5,3},{6,8},{7,5},{8,10},{9,7},{10,... | collective-permute-start | bytes 393224 | tf_op jit(solution)/shard_map/ppermute | solution.py:257
  25.8 6.2 %collective-permute-start.11 = (bf16[2,128,256]{2,1,0:T(8,128)(2,1)S(1)}, bf16[2,128,256]{2,1,0:T(8,128)(2,1)S(1)}, u32[]{:S(2)}, u32[]{:S(2)}) collective-permute-start(bf16[2,128,256]{2,1,0:T(8,128)(2,1)S(1)} %collective-permute-done.7.refs_8_), channel_id=1, source_target_pairs={{0,2},{1,15},{2,4},{3,1},{4,6},{5,3},{6,8},{7,5},{8,10},{9,7},{10,... | collective-permute-start | bytes 393224 | tf_op jit(solution)/shard_map/ppermute | solution.py:257
  27.1 5.3 %collective-permute-start.10 = (bf16[2,128,256]{2,1,0:T(8,128)(2,1)S(1)}, bf16[2,128,256]{2,1,0:T(8,128)(2,1)S(1)}, u32[]{:S(2)}, u32[]{:S(2)}) collective-permute-start(bf16[2,128,256]{2,1,0:T(8,128)(2,1)S(1)} %collective-permute-done.9.refs_10_), channel_id=1, source_target_pairs={{0,1},{1,0},{2,3},{3,2},{4,5},{5,4},{6,7},{7,6},{8,9},{9,8},{10,11... | collective-permute-start | bytes 393224 | tf_op jit(solution)/shard_map/ppermute | solution.py:261
  32.0 1.3 %collective-permute-start.12 = (bf16[2,128,256]{2,1,0:T(8,128)(2,1)S(1)}, bf16[2,128,256]{2,1,0:T(8,128)(2,1)S(1)}, u32[]{:S(2)}, u32[]{:S(2)}) collective-permute-start(bf16[2,128,256]{2,1,0:T(8,128)(2,1)S(1)} %collective-permute-done.11.refs_12_), channel_id=1, source_target_pairs={{0,1},{1,0},{2,3},{3,2},{4,5},{5,4},{6,7},{7,6},{8,9},{9,8},{10,11... | collective-permute-start | bytes 393224 | tf_op jit(solution)/shard_map/ppermute | solution.py:261
  32.0 1.5 %collective-permute-start.14 = (bf16[2,128,256]{2,1,0:T(8,128)(2,1)S(1)}, bf16[2,128,256]{2,1,0:T(8,128)(2,1)S(1)}, u32[]{:S(2)}, u32[]{:S(2)}) collective-permute-start(bf16[2,128,256]{2,1,0:T(8,128)(2,1)S(1)} %collective-permute-done.13.refs_14_), channel_id=1, source_target_pairs={{0,1},{1,0},{2,3},{3,2},{4,5},{5,4},{6,7},{7,6},{8,9},{9,8},{10,11... | collective-permute-start | bytes 393224 | tf_op jit(solution)/shard_map/ppermute | solution.py:261
  42.5 4.1 %copy-start.2 = (bf16[2,16,128,128]{3,2,1,0:T(8,128)(2,1)}, bf16[2,16,128,128]{3,2,1,0:T(8,128)(2,1)S(1)}, u32[]{:S(2)}) copy-start(bf16[2,16,128,128]{3,2,1,0:T(8,128)(2,1)S(1)} %get-tuple-element.62) | copy-start | bytes 3145732
  42.5 4.1 %copy-start.4 = (bf16[2,16,128,128]{3,2,1,0:T(8,128)(2,1)}, bf16[2,16,128,128]{3,2,1,0:T(8,128)(2,1)S(1)}, u32[]{:S(2)}) copy-start(bf16[2,16,128,128]{3,2,1,0:T(8,128)(2,1)S(1)} %get-tuple-element.58) | copy-start | bytes 3145732
  46.6 4.5 %collective-permute-start.22 = (bf16[8,2,128,256]{3,2,1,0:T(8,128)(2,1)S(1)}, bf16[8,2,128,256]{3,2,1,0:T(8,128)(2,1)S(1)}, u32[]{:S(2)}, u32[]{:S(2)}) collective-permute-start(bf16[8,2,128,256]{3,2,1,0:T(8,128)(2,1)S(1)} %get-tuple-element.72), channel_id=1, source_target_pairs={{0,1},{1,0},{2,3},{3,2},{4,5},{5,4},{6,7},{7,6},{8,9},{9,8},{10,11... | collective-permute-start | bytes 3145736 | tf_op jit(solution)/shard_map/ppermute | solution.py:261
  47.0 15.1 %collective-permute-start.15 = (bf16[2,16,128,128]{3,2,1,0:T(8,128)(2,1)}, bf16[2,16,128,128]{3,2,1,0:T(8,128)(2,1)}, u32[]{:S(2)}, u32[]{:S(2)}) collective-permute-start(bf16[2,16,128,128]{3,2,1,0:T(8,128)(2,1)} %get-tuple-element.59), channel_id=1, source_target_pairs={{0,16},{1,65},{16,32},{17,81},{32,48},{33,97},{48,0},{49,113},{64,... | collective-permute-start | bytes 3145736 | tf_op jit(solution)/shard_map/ppermute | solution.py:299
  47.5 18.3 %collective-permute-start.19 = (bf16[2,16,128,128]{3,2,1,0:T(8,128)(2,1)}, bf16[2,16,128,128]{3,2,1,0:T(8,128)(2,1)}, u32[]{:S(2)}, u32[]{:S(2)}) collective-permute-start(bf16[2,16,128,128]{3,2,1,0:T(8,128)(2,1)} %get-tuple-element.63), channel_id=1, source_target_pairs={{0,48},{1,193},{16,0},{17,209},{32,16},{33,225},{48,32},{49,241},{... | collective-permute-start | bytes 3145736 | tf_op jit(solution)/shard_map/ppermute | solution.py:299
  49.0 26.0 %collective-permute-start.17 = (bf16[2,16,128,128]{3,2,1,0:T(8,128)(2,1)}, bf16[2,16,128,128]{3,2,1,0:T(8,128)(2,1)}, u32[]{:S(2)}, u32[]{:S(2)}) collective-permute-start(bf16[2,16,128,128]{3,2,1,0:T(8,128)(2,1)} %get-tuple-element.60), channel_id=1, source_target_pairs={{0,16},{1,65},{16,32},{17,81},{32,48},{33,97},{48,0},{49,113},{64,... | collective-permute-start | bytes 3145736 | tf_op jit(solution)/shard_map/ppermute | solution.py:299
  50.7 24.3 %collective-permute-start.18 = (bf16[2,16,128,128]{3,2,1,0:T(8,128)(2,1)}, bf16[2,16,128,128]{3,2,1,0:T(8,128)(2,1)}, u32[]{:S(2)}, u32[]{:S(2)}) collective-permute-start(bf16[2,16,128,128]{3,2,1,0:T(8,128)(2,1)} %get-tuple-element.61), channel_id=1, source_target_pairs={{0,48},{1,193},{16,0},{17,209},{32,16},{33,225},{48,32},{49,241},{... | collective-permute-start | bytes 3145736 | tf_op jit(solution)/shard_map/ppermute | solution.py:299
  52.4 46.6 %all-to-all-start = ((bf16[8,2,128,256]{3,2,1,0:T(8,128)(2,1)}), bf16[8,2,128,256]{3,2,1,0:T(8,128)(2,1)S(1)}, u32[]{:S(2)}, u32[]{:S(2)}) async-start(bf16[8,2,128,256]{3,2,1,0:T(8,128)(2,1)} %add_convert_fusion), calls=%async_computation | async-start | bytes 2097152 | tf_op jit(solution)/shard_map/all_to_all | solution.py:434
  59.4 6.4 %copy-start.3 = (bf16[2,16,128,128]{3,2,1,0:T(8,128)(2,1)S(1)}, bf16[2,16,128,128]{3,2,1,0:T(8,128)(2,1)}, u32[]{:S(2)}) copy-start(bf16[2,16,128,128]{3,2,1,0:T(8,128)(2,1)} %copy-done.2) | copy-start | bytes 3145732
  64.0 20.5 %collective-permute-start.16 = (bf16[2,16,128,128]{3,2,1,0:T(8,128)(2,1)S(1)}, bf16[2,16,128,128]{3,2,1,0:T(8,128)(2,1)S(1)}, u32[]{:S(2)}, u32[]{:S(2)}) collective-permute-start(bf16[2,16,128,128]{3,2,1,0:T(8,128)(2,1)S(1)} %add_convert_fusion.2), channel_id=1, source_target_pairs={{0,16},{1,65},{16,32},{17,81},{32,48},{33,97},{48,0},{49,113},{64,... | collective-permute-start | bytes 3145736 | tf_op jit(solution)/shard_map/ppermute | solution.py:299
  67.4 18.8 %collective-permute-start.20 = (bf16[2,16,128,128]{3,2,1,0:T(8,128)(2,1)S(1)}, bf16[2,16,128,128]{3,2,1,0:T(8,128)(2,1)S(1)}, u32[]{:S(2)}, u32[]{:S(2)}) collective-permute-start(bf16[2,16,128,128]{3,2,1,0:T(8,128)(2,1)S(1)} %add_convert_fusion.1), channel_id=1, source_target_pairs={{0,48},{1,193},{16,0},{17,209},{32,16},{33,225},{48,32},{49,241},{... | collective-permute-start | bytes 3145736 | tf_op jit(solution)/shard_map/ppermute | solution.py:299
  88.5 10.5 %collective-permute-start.21 = (bf16[2,8,128,128]{3,2,1,0:T(8,128)(2,1)S(1)}, bf16[2,8,128,128]{3,2,1,0:T(8,128)(2,1)}, u32[]{:S(2)}, u32[]{:S(2)}) collective-permute-start(bf16[2,8,128,128]{3,2,1,0:T(8,128)(2,1)S(1)} %get-tuple-element.66), channel_id=1, source_target_pairs={{0,64},{1,17},{16,80},{17,33},{32,96},{33,49},{48,112},{49,1},{64,... | collective-permute-start | bytes 1572872 | tf_op jit(solution)/shard_map/ppermute | solution.py:299
  90.1 9.5 %collective-permute-start.23 = (bf16[2,8,128,128]{3,2,1,0:T(8,128)(2,1)}, bf16[2,8,128,128]{3,2,1,0:T(8,128)(2,1)}, u32[]{:S(2)}, u32[]{:S(2)}) collective-permute-start(bf16[2,8,128,128]{3,2,1,0:T(8,128)(2,1)} %get-tuple-element.80), channel_id=1, source_target_pairs={{0,192},{1,49},{16,208},{17,1},{32,224},{33,17},{48,240},{49,33},{... | collective-permute-start | bytes 1572872 | tf_op jit(solution)/shard_map/ppermute | solution.py:299
  99.0 5.8 %copy-start.6 = (f32[2,8,128,128]{3,2,1,0:T(8,128)S(1)}, f32[2,8,128,128]{3,2,1,0:T(8,128)}, u32[]{:S(2)}) copy-start(f32[2,8,128,128]{3,2,1,0:T(8,128)} %copy-done.5) | copy-start | bytes 3145732
  101.1 6.8 %collective-permute-start.25 = (bf16[2,4,128,128]{3,2,1,0:T(8,128)(2,1)S(1)}, bf16[2,4,128,128]{3,2,1,0:T(8,128)(2,1)S(1)}, u32[]{:S(2)}, u32[]{:S(2)}) collective-permute-start(bf16[2,4,128,128]{3,2,1,0:T(8,128)(2,1)S(1)} %get-tuple-element.84), channel_id=1, source_target_pairs={{0,192},{1,49},{16,208},{17,1},{32,224},{33,17},{48,240},{49,33},{... | collective-permute-start | bytes 786440 | tf_op jit(solution)/shard_map/ppermute | solution.py:299
  104.0 7.6 %collective-permute-start.24 = (bf16[2,4,128,128]{3,2,1,0:T(8,128)(2,1)S(1)}, bf16[2,4,128,128]{3,2,1,0:T(8,128)(2,1)S(1)}, u32[]{:S(2)}, u32[]{:S(2)}) collective-permute-start(bf16[2,4,128,128]{3,2,1,0:T(8,128)(2,1)S(1)} %get-tuple-element.85), channel_id=1, source_target_pairs={{0,64},{1,17},{16,80},{17,33},{32,96},{33,49},{48,112},{49,1},{64,... | collective-permute-start | bytes 786440 | tf_op jit(solution)/shard_map/ppermute | solution.py:299
  (3 other events, 4.2 us)

commit v9 on v7

--- a/solution.py
+++ b/solution.py
@@ -318,37 +318,38 @@
     from_left, terms = lax.optimization_barrier((from_left, terms))
     end_a = hop(add(total(16, 4), from_left[:, :4]).astype(BF), 1, 1)
     end_b = hop(add(total(20, 4), from_right[:, :4]).astype(BF), 1, -1)
-    return (near_sum(own, left_b, right_b), from_left, from_right, end_a, end_b), terms
-
-
-def near_sum_kernel(own, left_b, right_b, out):
+    return (near_sum(own, left_b, right_b, from_left, from_right), end_a, end_b), terms
+
+
+def near_sum_kernel(own, left_b, right_b, from_left, from_right, out):
     for k in range(2):
         for s in range(8):
-            out[k, s] = add(own[k, s], left_b[k, s], right_b[k, s])
-
-
-def near_sum(own, left_b, right_b):
+            one = from_right[k, s] if s < 4 else from_left[k, s - 4]
+            out[k, s] = add(own[k, s], left_b[k, s], right_b[k, s], one)
+
+
+def near_sum(own, left_b, right_b, from_left, from_right):
     def last(block):
         return pl.BlockSpec((2, 8, SIDE, SIDE), lambda i: (0, block, 0, 0))
 
+    half = pl.BlockSpec((2, 4, SIDE, SIDE), lambda i: (0, 1, 0, 0))
     return pl.pallas_call(
         near_sum_kernel,
         grid=(1,),
-        in_specs=[last(3), last(1), last(1)],
+        in_specs=[last(3), last(1), last(1), half, half],
         out_specs=whole(2, 8, SIDE, SIDE),
         out_shape=jax.ShapeDtypeStruct((2, 8, SIDE, SIDE), F32),
         compiler_params=params(16),
         cost_estimate=pl.CostEstimate(flops=1 << 19, bytes_accessed=3 << 20, transcendentals=0),
         name="near_sum",
-    )(own, left_b, right_b)
-
-
-def finish_kernel(count_ref, near, from_left, from_right, end_a, end_b, up_out, down_out):
+    )(own, left_b, right_b, from_left, from_right)
+
+
+def finish_kernel(count_ref, near, end_a, end_b, up_out, down_out):
     first = lax.axis_index(("y", "x")) * 8
     for k in range(2):
         for s in range(8):
-            one, two = (end_a[k, s], from_right[k, 4 + s]) if s < 4 else (from_left[k, s], end_b[k, s - 4])
-            total = add(near[k, s], one, two)
+            total = add(near[k, s], end_a[k, s] if s < 4 else end_b[k, s - 4])
             total = jnp.where(first + s < count_ref[0], total * (1.0 / 16), 0.0)
             if k == 0:
                 up_out[0, s] = total.T
@@ -361,7 +362,7 @@
     return pl.pallas_call(
         finish_kernel,
         grid=(1,),
-        in_specs=[sspec()] + [whole(2, n, SIDE, SIDE) for n in (8, 8, 8, 4, 4)],
+        in_specs=[sspec()] + [whole(2, n, SIDE, SIDE) for n in (8, 4, 4)],
         out_specs=[whole(*shape)] * 2,
         out_shape=[jax.ShapeDtypeStruct(shape, F32)] * 2,
         compiler_params=params(16),

time: 109 us -> 107 us (0.982)
  the two profiles are of different devices: /device:TPU:1 before, /device:TPU:6 now
where the time goes in v9:
time: 107 us
  waiting for transfers between devices  39.1 us (37%)
  starting transfers between devices  31.7 us (30%)
  Pallas kernels  21.9 us (20%)
  other arithmetic  10.2 us (10%)
  local copies, waits for them, and re-layouts  2.19 us (2%)
  between operations  1.4 us (1%)
    ppermute x10, waiting for transfers between devices, hop(): return lax.ppermute(t, ('y', 'x', 'c'), pairs)  28.4 us
    ppermute x7, starting transfers between devices, step_both(): return lax.ppermute(x, ('z', 'c'), pairs)  12.8 us
    ppermute x10, starting transfers between devices, hop(): return lax.ppermute(t, ('y', 'x', 'c'), pairs)  11.5 us
    ppermute x7, waiting for transfers between devices, step_both(): return lax.ppermute(x, ('z', 'c'), pairs)  7.92 us
    pallas_call x1, Pallas kernels, token_parts(): pl.pallas_call(token_kernel, in_specs=[vspec()] * 4, out_specs=[vspec()]...  4.12 us
    pallas_call x1, Pallas kernels, rest_parts(): pl.pallas_call(rest_kernel, in_specs=[sspec()] + [vspec()] * 4, out_specs...  4.05 us
    ppermute x9, starting transfers between devices, swap(): return lax.ppermute(x, 'c', [(0, 1), (1, 0)])  3.88 us
    pallas_call x1, Pallas kernels, forward(): pl.pallas_call(forward_kernel, in_specs=[sspec()] + [pl.BlockSpec(memory_...  3.76 us
  transfers between devices with their start and end apart: 27, of which 15 were waited for; matrix products, arithmetic and copies ran while one was open for 7% of the time, Pallas kernels for 16%

profile of v9, /device:TPU:6, one launch (start us, length us, event | category | flops | bytes accessed | tf_op | source)
XLA Modules:
  0.0 106.5 jit_solution(15917348630357298142)
XLA Ops:
  1.6 2.0 %collective-permute-start.1 = (bf16[2,128,256]{2,1,0:T(8,128)(2,1)S(1)}, bf16[2,128,256]{2,1,0:T(8,128)(2,1)S(1)}, u32[]{:S(2)}, u32[]{:S(2)}) collective-permute-start(bf16[2,128,256]{2,1,0:T(8,128)(2,1)S(1)} %pad_maximum_fusion.refs_0_), channel_id=1, source_target_pairs={{0,2},{1,15},{2,4},{3,1},{4,6},{5,3},{6,8},{7,5},{8,10},{9,7},{10,... | collective-permute-start | bytes 393224 | tf_op jit(solution)/shard_map/ppermute | solution.py:257
  3.6 1.9 %collective-permute-start.3 = (bf16[2,128,256]{2,1,0:T(8,128)(2,1)S(1)}, bf16[2,128,256]{2,1,0:T(8,128)(2,1)S(1)}, u32[]{:S(2)}, u32[]{:S(2)}) collective-permute-start(bf16[2,128,256]{2,1,0:T(8,128)(2,1)S(1)} %collective-permute-done.refs_1_), channel_id=1, source_target_pairs={{0,2},{1,15},{2,4},{3,1},{4,6},{5,3},{6,8},{7,5},{8,10},{9,7},{10,... | collective-permute-start | bytes 393224 | tf_op jit(solution)/shard_map/ppermute | solution.py:257
  6.2 4.3 %collective-permute-done.1.refs_2_ = bf16[2,128,256]{2,1,0:T(8,128)(2,1)S(1)} collective-permute-done((bf16[2,128,256]{2,1,0:T(8,128)(2,1)S(1)}, bf16[2,128,256]{2,1,0:T(8,128)(2,1)S(1)}, u32[]{:S(2)}, u32[]{:S(2)}) %collective-permute-start.1) | collective-permute-done | bytes 131104 | tf_op jit(solution)/shard_map/ppermute | solution.py:257
  12.6 2.2 %copy-done = bf16[1,128,128,128]{3,2,1,0:T(8,128)(2,1)S(1)} copy-done((bf16[1,128,128,128]{3,2,1,0:T(8,128)(2,1)S(1)}, bf16[1,128,128,128]{3,2,1,0:T(8,128)(2,1)}, u32[]{:S(2)}) %copy-start) | copy-done | bytes 4194328
  14.8 1.8 %dense_up.1.refs_10_.refs_16_.wu_ref = bf16[4096,1024]{1,0:T(8,128)(2,1)S(1)} custom-call(s32[128]{0:T(128)S(1)} %add_bitcast_fusion.where, s32[1]{0:T(128)S(6)} %copy.11.count_ref, bf16[1,128,128,128]{3,2,1,0:T(8,128)(2,1)S(1)} %copy-done), custom_call_target="tpu_custom_call" | custom-call | bytes 12582912 | tf_op jit(solution)/shard_map/dense_up/pallas_call | solution.py:86
  16.7 2.0 %collective-permute-start.9 = (bf16[2,128,256]{2,1,0:T(8,128)(2,1)S(1)}, bf16[2,128,256]{2,1,0:T(8,128)(2,1)S(1)}, u32[]{:S(2)}, u32[]{:S(2)}) collective-permute-start(bf16[2,128,256]{2,1,0:T(8,128)(2,1)S(1)} %collective-permute-done.5.refs_6_), channel_id=1, source_target_pairs={{0,2},{1,15},{2,4},{3,1},{4,6},{5,3},{6,8},{7,5},{8,10},{9,7},{10,... | collective-permute-start | bytes 393224 | tf_op jit(solution)/shard_map/ppermute | solution.py:257
  20.6 1.9 %dense_down.1.refs_11_.refs_17_.wd_ref = bf16[1024,4096]{1,0:T(8,128)(2,1)S(1)} custom-call(s32[128]{0:T(128)S(1)} %add_bitcast_fusion.where, s32[1]{0:T(128)S(6)} %copy.11.count_ref, bf16[1,128,128,128]{3,2,1,0:T(8,128)(2,1)S(1)} %copy-done.1), custom_call_target="tpu_custom_call" | custom-call | bytes 12582912 | tf_op jit(solution)/shard_map/dense_down/pallas_call | solution.py:86
  23.2 4.8 %collective-permute-start.13 = (bf16[2,128,256]{2,1,0:T(8,128)(2,1)S(1)}, bf16[2,128,256]{2,1,0:T(8,128)(2,1)S(1)}, u32[]{:S(2)}, u32[]{:S(2)}) collective-permute-start(bf16[2,128,256]{2,1,0:T(8,128)(2,1)S(1)} %collective-permute-done.9.refs_10_), channel_id=1, source_target_pairs={{0,2},{1,15},{2,4},{3,1},{4,6},{5,3},{6,8},{7,5},{8,10},{9,7},{10,... | collective-permute-start | bytes 393224 | tf_op jit(solution)/shard_map/ppermute | solution.py:257
  28.0 2.1 %collective-permute-start.11 = (bf16[2,128,256]{2,1,0:T(8,128)(2,1)S(1)}, bf16[2,128,256]{2,1,0:T(8,128)(2,1)S(1)}, u32[]{:S(2)}, u32[]{:S(2)}) collective-permute-start(bf16[2,128,256]{2,1,0:T(8,128)(2,1)S(1)} %collective-permute-done.7.refs_8_), channel_id=1, source_target_pairs={{0,2},{1,15},{2,4},{3,1},{4,6},{5,3},{6,8},{7,5},{8,10},{9,7},{10,... | collective-permute-start | bytes 393224 | tf_op jit(solution)/shard_map/ppermute | solution.py:257
  30.2 2.7 %early.1 = (f32[128,1024]{1,0:T(8,128)S(1)}, f32[128,1024]{1,0:T(8,128)S(1)}) custom-call(bf16[2,128,256]{2,1,0:T(8,128)(2,1)S(1)} %pad_maximum_fusion.refs_0_, bf16[2,128,256]{2,1,0:T(8,128)(2,1)S(1)} %collective-permute-done.refs_1_, bf16[2,128,256]{2,1,0:T(8,128)(2,1)S(1)} %collective-permute-done.1.refs_2_, ...), custom_call_target="tpu_custom_call" | custom-call | flops 1342177280 | bytes 13631488 | tf_op jit(solution)/shard_map/early/pallas_call | solution.py:137
  35.8 3.8 %forward.1 = (bf16[128,1024]{1,0:T(8,128)(2,1)S(1)}, bf16[128,1024]{1,0:T(8,128)(2,1)S(1)}, bf16[128,4096]{1,0:T(8,128)(2,1)S(1)}, bf16[128,4096]{1,0:T(8,128)(2...) custom-call(s32[128]{0:T(128)S(1)} %add_bitcast_fusion.where, ...), custom_call_target="tpu_custom_call" | custom-call | flops 3221225472 | bytes 23068672 | tf_op jit(solution)/shard_map/forward/pallas_call | solution.py:184
  40.1 1.5 %collective-permute-start.19 = (bf16[2,16,128,128]{3,2,1,0:T(8,128)(2,1)S(1)}, bf16[2,16,128,128]{3,2,1,0:T(8,128)(2,1)S(1)}, u32[]{:S(2)}, u32[]{:S(2)}) collective-permute-start(bf16[2,16,128,128]{3,2,1,0:T(8,128)(2,1)S(1)} %get-tuple-element.59), channel_id=1, source_target_pairs={{0,48},{1,193},{16,0},{17,209},{32,16},{33,225},{48,32},{49,241},{... | collective-permute-start | bytes 3145736 | tf_op jit(solution)/shard_map/ppermute | solution.py:299
  41.6 4.1 %rest_parts.1 = (bf16[2,16,128,128]{3,2,1,0:T(8,128)(2,1)}, bf16[2,16,128,128]{3,2,1,0:T(8,128)(2,1)}, bf16[2,16,128,128]{3,2,1,0:T(8,128)(2,1)S(1)}, bf16[2,16,...) custom-call(s32[128]{0:T(128)S(1)} %add_bitcast_fusion.where, bf16[128,4096]{1,0:T(8,128)(2,1)S(1)} %get-tuple-element.49.x_ref, ...), custom_call_target="tpu_custom_call" | custom-call | flops 1073741824 | bytes 9437184 | tf_op jit(solution)/shard_map/rest_parts/pallas_call | solution.py:204
  45.7 4.1 %token_parts.1 = (bf16[8,2,128,256]{3,2,1,0:T(8,128)(2,1)S(1)}, bf16[8,2,128,256]{3,2,1,0:T(8,128)(2,1)S(1)}) custom-call(bf16[128,1024]{1,0:T(8,128)(2,1)S(1)} %get-tuple-element.64.h_ref, bf16[128,1024]{1,0:T(8,128)(2,1)S(1)} %get-tuple-element.65.d_ref, bf16[4096,1024]{1,0:T(8,128)(2,1)S(1)} %dense_up.1.refs_10_.refs_16_.wu_ref, ...), custom_call_target="tpu_custom_call" | custom-call | flops 2147483648 | bytes 19922944 | tf_op jit(solution)/shard_map/token_parts/pallas_call | solution.py:237
  49.8 1.4 %collective-permute-start.22 = (bf16[8,2,128,256]{3,2,1,0:T(8,128)(2,1)S(1)}, bf16[8,2,128,256]{3,2,1,0:T(8,128)(2,1)S(1)}, u32[]{:S(2)}, u32[]{:S(2)}) collective-permute-start(bf16[8,2,128,256]{3,2,1,0:T(8,128)(2,1)S(1)} %get-tuple-element.67), channel_id=1, source_target_pairs={{0,1},{1,0},{2,3},{3,2},{4,5},{5,4},{6,7},{7,6},{8,9},{9,8},{10,11... | collective-permute-start | bytes 3145736 | tf_op jit(solution)/shard_map/ppermute | solution.py:261
  51.7 1.5 %collective-permute-start.18 = (bf16[2,16,128,128]{3,2,1,0:T(8,128)(2,1)}, bf16[2,16,128,128]{3,2,1,0:T(8,128)(2,1)}, u32[]{:S(2)}, u32[]{:S(2)}) collective-permute-start(bf16[2,16,128,128]{3,2,1,0:T(8,128)(2,1)} %get-tuple-element.57), channel_id=1, source_target_pairs={{0,48},{1,193},{16,0},{17,209},{32,16},{33,225},{48,32},{49,241},{... | collective-permute-start | bytes 3145736 | tf_op jit(solution)/shard_map/ppermute | solution.py:299
  54.4 1.5 %add_convert_fusion.2 = bf16[2,16,128,128]{3,2,1,0:T(8,128)(2,1)} fusion(bf16[2,16,128,128]{3,2,1,0:T(8,128)(2,1)S(1)} %collective-permute-done.15, bf16[2,16,128,128]{3,2,1,0:T(8,128)(2,1)S(1)} %get-tuple-element.54), kind=kLoop, calls=%fused_computation.2 | loop fusion | flops 2097152 | bytes 3145728 | tf_op jit(solution)/shard_map/convert_element_type | solution.py:307
  55.9 1.7 %collective-permute-start.16 = (bf16[2,16,128,128]{3,2,1,0:T(8,128)(2,1)}, bf16[2,16,128,128]{3,2,1,0:T(8,128)(2,1)}, u32[]{:S(2)}, u32[]{:S(2)}) collective-permute-start(bf16[2,16,128,128]{3,2,1,0:T(8,128)(2,1)} %add_convert_fusion.2), channel_id=1, source_target_pairs={{0,16},{1,65},{16,32},{17,81},{32,48},{33,97},{48,0},{49,113},{64,... | collective-permute-start | bytes 3145736 | tf_op jit(solution)/shard_map/ppermute | solution.py:299
  60.6 3.6 %all-to-all-start = ((bf16[8,2,128,256]{3,2,1,0:T(8,128)(2,1)}), bf16[8,2,128,256]{3,2,1,0:T(8,128)(2,1)S(1)}, u32[]{:S(2)}, u32[]{:S(2)}) async-start(bf16[8,2,128,256]{3,2,1,0:T(8,128)(2,1)} %add_convert_fusion), calls=%async_computation | async-start | bytes 2097152 | tf_op jit(solution)/shard_map/all_to_all | solution.py:406
  64.2 3.9 %collective-permute-done.18 = bf16[2,16,128,128]{3,2,1,0:T(8,128)(2,1)} collective-permute-done((bf16[2,16,128,128]{3,2,1,0:T(8,128)(2,1)}, bf16[2,16,128,128]{3,2,1,0:T(8,128)(2,1)}, u32[]{:S(2)}, u32[]{:S(2)}) %collective-permute-start.18) | collective-permute-done | bytes 1048608 | tf_op jit(solution)/shard_map/ppermute | solution.py:299
  68.0 9.5 %collective-permute-done.16 = bf16[2,16,128,128]{3,2,1,0:T(8,128)(2,1)} collective-permute-done((bf16[2,16,128,128]{3,2,1,0:T(8,128)(2,1)}, bf16[2,16,128,128]{3,2,1,0:T(8,128)(2,1)}, u32[]{:S(2)}, u32[]{:S(2)}) %collective-permute-start.16) | collective-permute-done | bytes 1048608 | tf_op jit(solution)/shard_map/ppermute | solution.py:299
  77.6 1.7 %collective-permute-done.20.right_b = bf16[2,16,128,128]{3,2,1,0:T(8,128)(2,1)} collective-permute-done((bf16[2,16,128,128]{3,2,1,0:T(8,128)(2,1)}, bf16[2,16,128,128]{3,2,1,0:T(8,128)(2,1)}, u32[]{:S(2)}, u32[]{:S(2)}) %collective-permute-start.20) | collective-permute-done | bytes 1048608 | tf_op jit(solution)/shard_map/ppermute | solution.py:299
  79.3 2.8 %add_convert_fusion.3 = (bf16[2,8,128,128]{3,2,1,0:T(8,128)(2,1)}, bf16[2,8,128,128]{3,2,1,0:T(8,128)(2,1)S(1)}) fusion(bf16[2,16,128,128]{3,2,1,0:T(8,128)(2,1)} %collective-permute-done.18, bf16[2,16,128,128]{3,2,1,0:T(8,128)(2,1)} %collective-permute-done.16, bf16[2,32,128,128]{3,2,1,0:T(8,128)(2,1)S(1)} %get-tuple-element.53.own), kind=kLoop, calls=%fused_computation.3 | loop fusion | flops 3145728 | bytes 4194304 | tf_op jit(solution)/shard_map/convert_element_type | solution.py:317
  82.1 1.6 %collective-permute-start.21 = (bf16[2,8,128,128]{3,2,1,0:T(8,128)(2,1)S(1)}, bf16[2,8,128,128]{3,2,1,0:T(8,128)(2,1)}, u32[]{:S(2)}, u32[]{:S(2)}) collective-permute-start(bf16[2,8,128,128]{3,2,1,0:T(8,128)(2,1)S(1)} %get-tuple-element.79), channel_id=1, source_target_pairs={{0,64},{1,17},{16,80},{17,33},{32,96},{33,49},{48,112},{49,1},{64,... | collective-permute-start | bytes 1572872 | tf_op jit(solution)/shard_map/ppermute | solution.py:299
  83.6 1.7 %collective-permute-start.23 = (bf16[2,8,128,128]{3,2,1,0:T(8,128)(2,1)}, bf16[2,8,128,128]{3,2,1,0:T(8,128)(2,1)}, u32[]{:S(2)}, u32[]{:S(2)}) collective-permute-start(bf16[2,8,128,128]{3,2,1,0:T(8,128)(2,1)} %get-tuple-element.78), channel_id=1, source_target_pairs={{0,192},{1,49},{16,208},{17,1},{32,224},{33,17},{48,240},{49,33},{... | collective-permute-start | bytes 1572872 | tf_op jit(solution)/shard_map/ppermute | solution.py:299
  85.3 7.3 %collective-permute-done.21.from_left = bf16[2,8,128,128]{3,2,1,0:T(8,128)(2,1)} collective-permute-done((bf16[2,8,128,128]{3,2,1,0:T(8,128)(2,1)S(1)}, bf16[2,8,128,128]{3,2,1,0:T(8,128)(2,1)}, u32[]{:S(2)}, u32[]{:S(2)}) %collective-permute-start.21) | collective-permute-done | bytes 524320 | tf_op jit(solution)/shard_map/ppermute | solution.py:299
  92.5 1.7 %all-to-all-done.terms_ref = bf16[8,2,128,256]{3,2,1,0:T(8,128)(2,1)S(1)} async-done(((bf16[8,2,128,256]{3,2,1,0:T(8,128)(2,1)}), bf16[8,2,128,256]{3,2,1,0:T(8,128)(2,1)S(1)}, u32[]{:S(2)}, u32[]{:S(2)}) %all-to-all-start) | async-done | bytes 1048608 | tf_op jit(solution)/shard_map/all_to_all | solution.py:406
  94.2 1.7 %add_convert_fusion.5 = (bf16[2,4,128,128]{3,2,1,0:T(8,128)(2,1)S(1)}, bf16[2,4,128,128]{3,2,1,0:T(8,128)(2,1)S(1)}) fusion(bf16[2,8,128,128]{3,2,1,0:T(8,128)(2,1)} %collective-permute-done.23.from_right, bf16[2,16,128,128]{3,2,1,0:T(8,128)(2,1)} %collective-permute-done.20.right_b, bf16[2,16,128,128]{3,2,1,0:T(8,128)(2,1)} %collective-permute-done.17.left_b, ...), kind=kLoop, calls=%fused_computation.5 | loop fusion | flops 2097152 | bytes 2621440 | tf_op jit(solution)/shard_map/convert_element_type | solution.py:320
  95.9 1.8 %collective-permute-start.25 = (bf16[2,4,128,128]{3,2,1,0:T(8,128)(2,1)S(1)}, bf16[2,4,128,128]{3,2,1,0:T(8,128)(2,1)S(1)}, u32[]{:S(2)}, u32[]{:S(2)}) collective-permute-start(bf16[2,4,128,128]{3,2,1,0:T(8,128)(2,1)S(1)} %get-tuple-element.76), channel_id=1, source_target_pairs={{0,192},{1,49},{16,208},{17,1},{32,224},{33,17},{48,240},{49,33},{... | collective-permute-start | bytes 786440 | tf_op jit(solution)/shard_map/ppermute | solution.py:299
  98.8 1.6 %near_sum.1.near = f32[2,8,128,128]{3,2,1,0:T(8,128)S(1)} custom-call(bf16[2,32,128,128]{3,2,1,0:T(8,128)(2,1)S(1)} %get-tuple-element.53.own, bf16[2,16,128,128]{3,2,1,0:T(8,128)(2,1)} %collective-permute-done.17.left_b, bf16[2,16,128,128]{3,2,1,0:T(8,128)(2,1)} %collective-permute-done.20.right_b, ...), custom_call_target="tpu_custom_call" | custom-call | flops 524288 | bytes 3145728 | tf_op jit(solution)/shard_map/near_sum/pallas_call | solution.py:336
  100.4 2.0 %collective-permute-done.25.end_b = bf16[2,4,128,128]{3,2,1,0:T(8,128)(2,1)S(1)} collective-permute-done((bf16[2,4,128,128]{3,2,1,0:T(8,128)(2,1)S(1)}, bf16[2,4,128,128]{3,2,1,0:T(8,128)(2,1)S(1)}, u32[]{:S(2)}, u32[]{:S(2)}) %collective-permute-start.25) | collective-permute-done | bytes 262176 | tf_op jit(solution)/shard_map/ppermute | solution.py:299
  102.4 3.0 %collective-permute-done.24.end_a = bf16[2,4,128,128]{3,2,1,0:T(8,128)(2,1)S(1)} collective-permute-done((bf16[2,4,128,128]{3,2,1,0:T(8,128)(2,1)S(1)}, bf16[2,4,128,128]{3,2,1,0:T(8,128)(2,1)S(1)}, u32[]{:S(2)}, u32[]{:S(2)}) %collective-permute-start.24) | collective-permute-done | bytes 262176 | tf_op jit(solution)/shard_map/ppermute | solution.py:299
  (42 shorter events, 16.1 us)
Async XLA Ops:
  1.5 2.1 %collective-permute-start = (bf16[2,128,256]{2,1,0:T(8,128)(2,1)S(1)}, bf16[2,128,256]{2,1,0:T(8,128)(2,1)S(1)}, u32[]{:S(2)}, u32[]{:S(2)}) collective-permute-start(bf16[2,128,256]{2,1,0:T(8,128)(2,1)S(1)} %pad_maximum_fusion.refs_0_), channel_id=1, source_target_pairs={{0,1},{1,0},{2,3},{3,2},{4,5},{5,4},{6,7},{7,6},{8,9},{9,8},{10,11... | collective-permute-start | bytes 393224 | tf_op jit(solution)/shard_map/ppermute | solution.py:261
  1.6 8.9 %collective-permute-start.1 = (bf16[2,128,256]{2,1,0:T(8,128)(2,1)S(1)}, bf16[2,128,256]{2,1,0:T(8,128)(2,1)S(1)}, u32[]{:S(2)}, u32[]{:S(2)}) collective-permute-start(bf16[2,128,256]{2,1,0:T(8,128)(2,1)S(1)} %pad_maximum_fusion.refs_0_), channel_id=1, source_target_pairs={{0,2},{1,15},{2,4},{3,1},{4,6},{5,3},{6,8},{7,5},{8,10},{9,7},{10,... | collective-permute-start | bytes 393224 | tf_op jit(solution)/shard_map/ppermute | solution.py:257
  3.6 8.3 %collective-permute-start.3 = (bf16[2,128,256]{2,1,0:T(8,128)(2,1)S(1)}, bf16[2,128,256]{2,1,0:T(8,128)(2,1)S(1)}, u32[]{:S(2)}, u32[]{:S(2)}) collective-permute-start(bf16[2,128,256]{2,1,0:T(8,128)(2,1)S(1)} %collective-permute-done.refs_1_), channel_id=1, source_target_pairs={{0,2},{1,15},{2,4},{3,1},{4,6},{5,3},{6,8},{7,5},{8,10},{9,7},{10,... | collective-permute-start | bytes 393224 | tf_op jit(solution)/shard_map/ppermute | solution.py:257
  10.5 6.2 %collective-permute-start.5 = (bf16[2,128,256]{2,1,0:T(8,128)(2,1)S(1)}, bf16[2,128,256]{2,1,0:T(8,128)(2,1)S(1)}, u32[]{:S(2)}, u32[]{:S(2)}) collective-permute-start(bf16[2,128,256]{2,1,0:T(8,128)(2,1)S(1)} %collective-permute-done.1.refs_2_), channel_id=1, source_target_pairs={{0,2},{1,15},{2,4},{3,1},{4,6},{5,3},{6,8},{7,5},{8,10},{9,7},{10,... | collective-permute-start | bytes 393224 | tf_op jit(solution)/shard_map/ppermute | solution.py:257
  11.9 8.5 %collective-permute-start.7 = (bf16[2,128,256]{2,1,0:T(8,128)(2,1)S(1)}, bf16[2,128,256]{2,1,0:T(8,128)(2,1)S(1)}, u32[]{:S(2)}, u32[]{:S(2)}) collective-permute-start(bf16[2,128,256]{2,1,0:T(8,128)(2,1)S(1)} %collective-permute-done.3.refs_4_), channel_id=1, source_target_pairs={{0,2},{1,15},{2,4},{3,1},{4,6},{5,3},{6,8},{7,5},{8,10},{9,7},{10,... | collective-permute-start | bytes 393224 | tf_op jit(solution)/shard_map/ppermute | solution.py:257
  12.6 2.2 %copy-start = (bf16[1,128,128,128]{3,2,1,0:T(8,128)(2,1)S(1)}, bf16[1,128,128,128]{3,2,1,0:T(8,128)(2,1)}, u32[]{:S(2)}) copy-start(bf16[1,128,128,128]{3,2,1,0:T(8,128)(2,1)} %tiles_ref.2) | copy-start | bytes 12582916
  14.8 5.8 %copy-start.1 = (bf16[1,128,128,128]{3,2,1,0:T(8,128)(2,1)S(1)}, bf16[1,128,128,128]{3,2,1,0:T(8,128)(2,1)}, u32[]{:S(2)}) copy-start(bf16[1,128,128,128]{3,2,1,0:T(8,128)(2,1)} %tiles_ref.3) | copy-start | bytes 12582916
  16.7 6.6 %collective-permute-start.9 = (bf16[2,128,256]{2,1,0:T(8,128)(2,1)S(1)}, bf16[2,128,256]{2,1,0:T(8,128)(2,1)S(1)}, u32[]{:S(2)}, u32[]{:S(2)}) collective-permute-start(bf16[2,128,256]{2,1,0:T(8,128)(2,1)S(1)} %collective-permute-done.5.refs_6_), channel_id=1, source_target_pairs={{0,2},{1,15},{2,4},{3,1},{4,6},{5,3},{6,8},{7,5},{8,10},{9,7},{10,... | collective-permute-start | bytes 393224 | tf_op jit(solution)/shard_map/ppermute | solution.py:257
  18.7 9.4 %collective-permute-start.2 = (bf16[2,128,256]{2,1,0:T(8,128)(2,1)S(1)}, bf16[2,128,256]{2,1,0:T(8,128)(2,1)S(1)}, u32[]{:S(2)}, u32[]{:S(2)}) collective-permute-start(bf16[2,128,256]{2,1,0:T(8,128)(2,1)S(1)} %collective-permute-done.1.refs_2_), channel_id=1, source_target_pairs={{0,1},{1,0},{2,3},{3,2},{4,5},{5,4},{6,7},{7,6},{8,9},{9,8},{10,11... | collective-permute-start | bytes 393224 | tf_op jit(solution)/shard_map/ppermute | solution.py:261
  19.9 10.2 %collective-permute-start.6 = (bf16[2,128,256]{2,1,0:T(8,128)(2,1)S(1)}, bf16[2,128,256]{2,1,0:T(8,128)(2,1)S(1)}, u32[]{:S(2)}, u32[]{:S(2)}) collective-permute-start(bf16[2,128,256]{2,1,0:T(8,128)(2,1)S(1)} %collective-permute-done.5.refs_6_), channel_id=1, source_target_pairs={{0,1},{1,0},{2,3},{3,2},{4,5},{5,4},{6,7},{7,6},{8,9},{9,8},{10,11... | collective-permute-start | bytes 393224 | tf_op jit(solution)/shard_map/ppermute | solution.py:261
  20.0 10.1 %collective-permute-start.4 = (bf16[2,128,256]{2,1,0:T(8,128)(2,1)S(1)}, bf16[2,128,256]{2,1,0:T(8,128)(2,1)S(1)}, u32[]{:S(2)}, u32[]{:S(2)}) collective-permute-start(bf16[2,128,256]{2,1,0:T(8,128)(2,1)S(1)} %collective-permute-done.3.refs_4_), channel_id=1, source_target_pairs={{0,1},{1,0},{2,3},{3,2},{4,5},{5,4},{6,7},{7,6},{8,9},{9,8},{10,11... | collective-permute-start | bytes 393224 | tf_op jit(solution)/shard_map/ppermute | solution.py:261
  20.5 9.7 %collective-permute-start.8 = (bf16[2,128,256]{2,1,0:T(8,128)(2,1)S(1)}, bf16[2,128,256]{2,1,0:T(8,128)(2,1)S(1)}, u32[]{:S(2)}, u32[]{:S(2)}) collective-permute-start(bf16[2,128,256]{2,1,0:T(8,128)(2,1)S(1)} %collective-permute-done.7.refs_8_), channel_id=1, source_target_pairs={{0,1},{1,0},{2,3},{3,2},{4,5},{5,4},{6,7},{7,6},{8,9},{9,8},{10,11... | collective-permute-start | bytes 393224 | tf_op jit(solution)/shard_map/ppermute | solution.py:261
  23.2 9.6 %collective-permute-start.13 = (bf16[2,128,256]{2,1,0:T(8,128)(2,1)S(1)}, bf16[2,128,256]{2,1,0:T(8,128)(2,1)S(1)}, u32[]{:S(2)}, u32[]{:S(2)}) collective-permute-start(bf16[2,128,256]{2,1,0:T(8,128)(2,1)S(1)} %collective-permute-done.9.refs_10_), channel_id=1, source_target_pairs={{0,2},{1,15},{2,4},{3,1},{4,6},{5,3},{6,8},{7,5},{8,10},{9,7},{10,... | collective-permute-start | bytes 393224 | tf_op jit(solution)/shard_map/ppermute | solution.py:257
  28.0 6.2 %collective-permute-start.11 = (bf16[2,128,256]{2,1,0:T(8,128)(2,1)S(1)}, bf16[2,128,256]{2,1,0:T(8,128)(2,1)S(1)}, u32[]{:S(2)}, u32[]{:S(2)}) collective-permute-start(bf16[2,128,256]{2,1,0:T(8,128)(2,1)S(1)} %collective-permute-done.7.refs_8_), channel_id=1, source_target_pairs={{0,2},{1,15},{2,4},{3,1},{4,6},{5,3},{6,8},{7,5},{8,10},{9,7},{10,... | collective-permute-start | bytes 393224 | tf_op jit(solution)/shard_map/ppermute | solution.py:257
  30.1 4.6 %collective-permute-start.10 = (bf16[2,128,256]{2,1,0:T(8,128)(2,1)S(1)}, bf16[2,128,256]{2,1,0:T(8,128)(2,1)S(1)}, u32[]{:S(2)}, u32[]{:S(2)}) collective-permute-start(bf16[2,128,256]{2,1,0:T(8,128)(2,1)S(1)} %collective-permute-done.9.refs_10_), channel_id=1, source_target_pairs={{0,1},{1,0},{2,3},{3,2},{4,5},{5,4},{6,7},{7,6},{8,9},{9,8},{10,11... | collective-permute-start | bytes 393224 | tf_op jit(solution)/shard_map/ppermute | solution.py:261
  34.2 1.3 %collective-permute-start.12 = (bf16[2,128,256]{2,1,0:T(8,128)(2,1)S(1)}, bf16[2,128,256]{2,1,0:T(8,128)(2,1)S(1)}, u32[]{:S(2)}, u32[]{:S(2)}) collective-permute-start(bf16[2,128,256]{2,1,0:T(8,128)(2,1)S(1)} %collective-permute-done.11.refs_12_), channel_id=1, source_target_pairs={{0,1},{1,0},{2,3},{3,2},{4,5},{5,4},{6,7},{7,6},{8,9},{9,8},{10,11... | collective-permute-start | bytes 393224 | tf_op jit(solution)/shard_map/ppermute | solution.py:261
  34.2 1.5 %collective-permute-start.14 = (bf16[2,128,256]{2,1,0:T(8,128)(2,1)S(1)}, bf16[2,128,256]{2,1,0:T(8,128)(2,1)S(1)}, u32[]{:S(2)}, u32[]{:S(2)}) collective-permute-start(bf16[2,128,256]{2,1,0:T(8,128)(2,1)S(1)} %collective-permute-done.13.refs_14_), channel_id=1, source_target_pairs={{0,1},{1,0},{2,3},{3,2},{4,5},{5,4},{6,7},{7,6},{8,9},{9,8},{10,11... | collective-permute-start | bytes 393224 | tf_op jit(solution)/shard_map/ppermute | solution.py:261
  39.5 14.9 %collective-permute-start.15 = (bf16[2,16,128,128]{3,2,1,0:T(8,128)(2,1)S(1)}, bf16[2,16,128,128]{3,2,1,0:T(8,128)(2,1)S(1)}, u32[]{:S(2)}, u32[]{:S(2)}) collective-permute-start(bf16[2,16,128,128]{3,2,1,0:T(8,128)(2,1)S(1)} %get-tuple-element.55), channel_id=1, source_target_pairs={{0,16},{1,65},{16,32},{17,81},{32,48},{33,97},{48,0},{49,113},{64,... | collective-permute-start | bytes 3145736 | tf_op jit(solution)/shard_map/ppermute | solution.py:299
  40.1 17.5 %collective-permute-start.19 = (bf16[2,16,128,128]{3,2,1,0:T(8,128)(2,1)S(1)}, bf16[2,16,128,128]{3,2,1,0:T(8,128)(2,1)S(1)}, u32[]{:S(2)}, u32[]{:S(2)}) collective-permute-start(bf16[2,16,128,128]{3,2,1,0:T(8,128)(2,1)S(1)} %get-tuple-element.59), channel_id=1, source_target_pairs={{0,48},{1,193},{16,0},{17,209},{32,16},{33,225},{48,32},{49,241},{... | collective-permute-start | bytes 3145736 | tf_op jit(solution)/shard_map/ppermute | solution.py:299
  49.8 9.5 %collective-permute-start.22 = (bf16[8,2,128,256]{3,2,1,0:T(8,128)(2,1)S(1)}, bf16[8,2,128,256]{3,2,1,0:T(8,128)(2,1)S(1)}, u32[]{:S(2)}, u32[]{:S(2)}) collective-permute-start(bf16[8,2,128,256]{3,2,1,0:T(8,128)(2,1)S(1)} %get-tuple-element.67), channel_id=1, source_target_pairs={{0,1},{1,0},{2,3},{3,2},{4,5},{5,4},{6,7},{7,6},{8,9},{9,8},{10,11... | collective-permute-start | bytes 3145736 | tf_op jit(solution)/shard_map/ppermute | solution.py:261
  51.2 16.8 %collective-permute-start.17 = (bf16[2,16,128,128]{3,2,1,0:T(8,128)(2,1)}, bf16[2,16,128,128]{3,2,1,0:T(8,128)(2,1)}, u32[]{:S(2)}, u32[]{:S(2)}) collective-permute-start(bf16[2,16,128,128]{3,2,1,0:T(8,128)(2,1)} %get-tuple-element.56), channel_id=1, source_target_pairs={{0,16},{1,65},{16,32},{17,81},{32,48},{33,97},{48,0},{49,113},{64,... | collective-permute-start | bytes 3145736 | tf_op jit(solution)/shard_map/ppermute | solution.py:299
  51.7 16.3 %collective-permute-start.18 = (bf16[2,16,128,128]{3,2,1,0:T(8,128)(2,1)}, bf16[2,16,128,128]{3,2,1,0:T(8,128)(2,1)}, u32[]{:S(2)}, u32[]{:S(2)}) collective-permute-start(bf16[2,16,128,128]{3,2,1,0:T(8,128)(2,1)} %get-tuple-element.57), channel_id=1, source_target_pairs={{0,48},{1,193},{16,0},{17,209},{32,16},{33,225},{48,32},{49,241},{... | collective-permute-start | bytes 3145736 | tf_op jit(solution)/shard_map/ppermute | solution.py:299
  55.9 21.7 %collective-permute-start.16 = (bf16[2,16,128,128]{3,2,1,0:T(8,128)(2,1)}, bf16[2,16,128,128]{3,2,1,0:T(8,128)(2,1)}, u32[]{:S(2)}, u32[]{:S(2)}) collective-permute-start(bf16[2,16,128,128]{3,2,1,0:T(8,128)(2,1)} %add_convert_fusion.2), channel_id=1, source_target_pairs={{0,16},{1,65},{16,32},{17,81},{32,48},{33,97},{48,0},{49,113},{64,... | collective-permute-start | bytes 3145736 | tf_op jit(solution)/shard_map/ppermute | solution.py:299
  58.9 20.3 %collective-permute-start.20 = (bf16[2,16,128,128]{3,2,1,0:T(8,128)(2,1)}, bf16[2,16,128,128]{3,2,1,0:T(8,128)(2,1)}, u32[]{:S(2)}, u32[]{:S(2)}) collective-permute-start(bf16[2,16,128,128]{3,2,1,0:T(8,128)(2,1)} %add_convert_fusion.1), channel_id=1, source_target_pairs={{0,48},{1,193},{16,0},{17,209},{32,16},{33,225},{48,32},{49,241},{... | collective-permute-start | bytes 3145736 | tf_op jit(solution)/shard_map/ppermute | solution.py:299
  60.6 33.6 %all-to-all-start = ((bf16[8,2,128,256]{3,2,1,0:T(8,128)(2,1)}), bf16[8,2,128,256]{3,2,1,0:T(8,128)(2,1)S(1)}, u32[]{:S(2)}, u32[]{:S(2)}) async-start(bf16[8,2,128,256]{3,2,1,0:T(8,128)(2,1)} %add_convert_fusion), calls=%async_computation | async-start | bytes 2097152 | tf_op jit(solution)/shard_map/all_to_all | solution.py:406
  82.1 10.5 %collective-permute-start.21 = (bf16[2,8,128,128]{3,2,1,0:T(8,128)(2,1)S(1)}, bf16[2,8,128,128]{3,2,1,0:T(8,128)(2,1)}, u32[]{:S(2)}, u32[]{:S(2)}) collective-permute-start(bf16[2,8,128,128]{3,2,1,0:T(8,128)(2,1)S(1)} %get-tuple-element.79), channel_id=1, source_target_pairs={{0,64},{1,17},{16,80},{17,33},{32,96},{33,49},{48,112},{49,1},{64,... | collective-permute-start | bytes 1572872 | tf_op jit(solution)/shard_map/ppermute | solution.py:299
  83.6 10.6 %collective-permute-start.23 = (bf16[2,8,128,128]{3,2,1,0:T(8,128)(2,1)}, bf16[2,8,128,128]{3,2,1,0:T(8,128)(2,1)}, u32[]{:S(2)}, u32[]{:S(2)}) collective-permute-start(bf16[2,8,128,128]{3,2,1,0:T(8,128)(2,1)} %get-tuple-element.78), channel_id=1, source_target_pairs={{0,192},{1,49},{16,208},{17,1},{32,224},{33,17},{48,240},{49,33},{... | collective-permute-start | bytes 1572872 | tf_op jit(solution)/shard_map/ppermute | solution.py:299
  95.9 6.4 %collective-permute-start.25 = (bf16[2,4,128,128]{3,2,1,0:T(8,128)(2,1)S(1)}, bf16[2,4,128,128]{3,2,1,0:T(8,128)(2,1)S(1)}, u32[]{:S(2)}, u32[]{:S(2)}) collective-permute-start(bf16[2,4,128,128]{3,2,1,0:T(8,128)(2,1)S(1)} %get-tuple-element.76), channel_id=1, source_target_pairs={{0,192},{1,49},{16,208},{17,1},{32,224},{33,17},{48,240},{49,33},{... | collective-permute-start | bytes 786440 | tf_op jit(solution)/shard_map/ppermute | solution.py:299
  97.8 7.6 %collective-permute-start.24 = (bf16[2,4,128,128]{3,2,1,0:T(8,128)(2,1)S(1)}, bf16[2,4,128,128]{3,2,1,0:T(8,128)(2,1)S(1)}, u32[]{:S(2)}, u32[]{:S(2)}) collective-permute-start(bf16[2,4,128,128]{3,2,1,0:T(8,128)(2,1)S(1)} %get-tuple-element.77), channel_id=1, source_target_pairs={{0,64},{1,17},{16,80},{17,33},{32,96},{33,49},{48,112},{49,1},{64,... | collective-permute-start | bytes 786440 | tf_op jit(solution)/shard_map/ppermute | solution.py:299
